TPU v7x, 32 devices: a whole 2x2x4 slice. The times are simulated.
32 devices in a mesh: ctx: 8 (over z, x), wt: 4 (over y, core).
Axes of the slice: x: 2, y: 2, z: 4, core: 2. Of those that a mesh axis runs over, the one named last changes fastest.
Arguments:
- tokens: bfloat16 [8192, 768], P(('ctx', 'wt')), may hold values from -6 to 6
- doc_start: int32 [8192], replicated, may hold values from 0 to 8191, as said below
- cotangent: bfloat16 [8192, 768], P(('ctx', 'wt')), may hold values from -6 to 6
- query_weight: bfloat16 [768, 768], P('wt'), may hold values from -0.3125 to 0.3125
- key_weight: bfloat16 [768, 768], P('wt'), may hold values from -0.3125 to 0.3125
- value_weight: bfloat16 [768, 768], P('wt'), may hold values from -0.21875 to 0.21875
- out_weight: bfloat16 [768, 768], P('wt'), may hold values from -0.875 to 0.875
- query_bias: bfloat16 [768], P('wt'), may hold values from -1.5 to 1.5
- value_bias: bfloat16 [768], P('wt'), may hold values from -1 to 1
- out_bias: bfloat16 [768], P('wt'), may hold values from -1.5 to 1.5
- first_gain: bfloat16 [768], P('wt'), may hold values from 0.5 to 1.5
- first_shift: bfloat16 [768], P('wt'), may hold values from -1.5 to 1.5
- inner_weight: bfloat16 [768, 3072], P('wt'), may hold values from -0.21875 to 0.21875
- inner_bias: bfloat16 [3072], P('wt'), may hold values from -1.5 to 1.5
- outer_weight: bfloat16 [3072, 768], P('wt'), may hold values from -0.109375 to 0.109375
- outer_bias: bfloat16 [768], P('wt'), may hold values from -1 to 1
- second_gain: bfloat16 [768], P('wt'), may hold values from 0.5 to 1.5
- second_shift: bfloat16 [768], P('wt'), may hold values from -1.5 to 1.5
Outputs:
- layer_out: bfloat16 [8192, 768], P(('ctx', 'wt'))
- tokens_gradient: float32 [8192, 768], P(('ctx', 'wt'))
- query_weight_gradient: float32 [768, 768], P('wt')
- key_weight_gradient: float32 [768, 768], P('wt')
- value_weight_gradient: float32 [768, 768], P('wt')
- out_weight_gradient: float32 [768, 768], P('wt')
- query_bias_gradient: float32 [768], P('wt')
- value_bias_gradient: float32 [768], P('wt')
- out_bias_gradient: float32 [768], P('wt')
- first_gain_gradient: float32 [768], P('wt')
- first_shift_gradient: float32 [768], P('wt')
- inner_weight_gradient: float32 [768, 3072], P('wt')
- inner_bias_gradient: float32 [3072], P('wt')
- outer_weight_gradient: float32 [3072, 768], P('wt')
- outer_bias_gradient: float32 [768], P('wt')
- second_gain_gradient: float32 [768], P('wt')
- second_shift_gradient: float32 [768], P('wt')
Inputs may be any that keep to these rules, and one draw needn't show every extreme that they name: `doc_start`: each position holds the first position of its document; documents are runs of consecutive positions, each 1 to 2048 long, at least one is exactly 2048 long, and the last position starts a document of its own.
All inputs are finite; a program needn't handle non-finite values.
Results may differ from a plain program's by a relative error of at most 0.02.
The roundings to bfloat16 on the way count: a program that leaves them out, or rounds other values in their place, can miss the bound.
Values may be sent and summed in bfloat16 or wider, within the bound.
No kernel may reach another device: no remote copies, remote signals or barrier semaphores. Data moves between devices by JAX's collectives and lax.ppermute only.
A program may use at most 256 MiB of HBM per device.

v0:
```python
import jax
import jax.numpy as jnp
from jax import lax
from jax.sharding import PartitionSpec as P

HEADS = 12
HEAD_DIM = 64
MAXDOC = 2048


masked_score = -1e30
epsilon = 1e-06


def passed_along(block, axis, distance):
    devices = range(lax.axis_size(axis))
    route = [((i - distance) % len(devices), i) for i in devices]
    return lax.ppermute(block, axis, route)


def shortened(array):

    def short(part):
        return part.astype(jnp.bfloat16) if part.dtype == jnp.float32 else part

    return jax.tree.map(short, array)


def layer_norm(values, gain, shift):
    center = values - jnp.mean(values, axis=-1, keepdims=True)
    spread = jnp.mean(center * center, axis=-1, keepdims=True)
    return center * lax.rsqrt(spread + epsilon) * gain + shift


def matmul(left, right):
    return jnp.dot(left, right, preferred_element_type=jnp.float32)


def left_transposed(left, right):
    return jnp.einsum("td,te->de", left, right, preferred_element_type=jnp.float32)


def right_transposed(left, right):
    return jnp.einsum("te,de->td", left, right, preferred_element_type=jnp.float32)


def column_sums(values):
    return jnp.sum(values.astype(jnp.float32), axis=0)


def on_device(
    tokens,
    doc_start,
    cotangent,
    query_weight,
    key_weight,
    value_weight,
    out_weight,
    query_bias,
    value_bias,
    out_bias,
    first_gain,
    first_shift,
    inner_weight,
    inner_bias,
    outer_weight,
    outer_bias,
    second_gain,
    second_shift,
):
    row_count, feature_count = tokens.shape
    cycle_size = lax.axis_size("ctx")
    shard_count = lax.axis_size("wt")
    block_rows = row_count * shard_count
    reach = (MAXDOC + block_rows - 2) // block_rows
    window = 2 * reach + 1
    cycle_index = lax.axis_index("ctx")
    shard_index = lax.axis_index("wt")
    first_row = (cycle_index * shard_count + shard_index) * row_count
    query_marks = lax.dynamic_slice_in_dim(doc_start, first_row, row_count) + 1
    gathered = (
        lax.all_gather(query_weight, "wt", axis=0, tiled=True),
        lax.all_gather(key_weight, "wt", axis=0, tiled=True),
        lax.all_gather(value_weight, "wt", axis=0, tiled=True),
        lax.all_gather(out_weight, "wt", axis=0, tiled=True),
        lax.all_gather(query_bias, "wt", axis=0, tiled=True),
        lax.all_gather(value_bias, "wt", axis=0, tiled=True),
        lax.all_gather(out_bias, "wt", axis=0, tiled=True),
        lax.all_gather(first_gain, "wt", axis=0, tiled=True),
        lax.all_gather(first_shift, "wt", axis=0, tiled=True),
        lax.all_gather(inner_weight, "wt", axis=0, tiled=True),
        lax.all_gather(inner_bias, "wt", axis=0, tiled=True),
        lax.all_gather(outer_weight, "wt", axis=0, tiled=True),
        lax.all_gather(outer_bias, "wt", axis=0, tiled=True),
        lax.all_gather(second_gain, "wt", axis=0, tiled=True),
        lax.all_gather(second_shift, "wt", axis=0, tiled=True),
    )
    (
        full_query,
        full_key,
        full_value,
        full_out,
        bias_query,
        bias_value,
        bias_out,
        gain_first,
        shift_first,
        full_inner,
        bias_inner,
        full_outer,
        bias_outer,
        gain_second,
        shift_second,
    ) = gathered
    query_rows = (matmul(tokens, full_query) + bias_query.astype(jnp.float32)).astype(jnp.bfloat16)
    key_rows = matmul(tokens, full_key).astype(jnp.bfloat16)
    value_rows = (matmul(tokens, full_value) + bias_value.astype(jnp.float32)).astype(jnp.bfloat16)
    own_shard = jnp.stack((key_rows, value_rows))
    start_pair = lax.all_gather(own_shard, "wt", axis=1, tiled=True)
    query_heads = query_rows.reshape(row_count, HEADS, HEAD_DIM)

    def block_marks(offset):
        target = cycle_index + offset
        inside = (target >= 0) & (target < cycle_size)
        clipped = jnp.clip(target, 0, cycle_size - 1)
        marks = lax.dynamic_slice_in_dim(doc_start, clipped * block_rows, block_rows) + 1
        return jnp.where(inside, marks, 0)

    def scores_of(key_value, marks):
        key_heads = key_value[0].reshape(block_rows, HEADS, HEAD_DIM)
        raw = (
            jnp.einsum("qhd,khd->hqk", query_heads, key_heads, preferred_element_type=jnp.float32)
            * 0.125
        )
        allowed = (query_marks[:, None] == marks[None, :])[None]
        return (raw, allowed)

    def merge(softmax_state, key_value, marks):
        running, total, accum = softmax_state
        raw, allowed = scores_of(key_value, marks)
        masked = jnp.where(allowed, raw, masked_score)
        newest = jnp.maximum(running, jnp.max(masked, axis=-1))
        factor = jnp.exp(running - newest)
        weights = jnp.where(allowed, jnp.exp(masked - newest[:, :, None]), 0.0)
        total = total * factor + jnp.sum(weights, axis=-1)
        value_heads = key_value[1].reshape(block_rows, HEADS, HEAD_DIM)
        mixed = jnp.einsum(
            "hqk,khd->qhd",
            weights.astype(jnp.bfloat16),
            value_heads,
            preferred_element_type=jnp.float32,
        )
        accum = accum * jnp.transpose(factor)[:, :, None] + mixed
        return (newest, total, accum)

    def visit(softmax_state, key_value, offset):
        marks = block_marks(offset)
        return merge(softmax_state, key_value, marks)

    stored_list = [None] * window

    def arrive(softmax_state, pair, offset):
        stored_list[offset + reach] = pair
        return visit(softmax_state, pair, offset)

    softmax_state = (
        jnp.full((HEADS, row_count), masked_score, jnp.float32),
        jnp.zeros((HEADS, row_count), jnp.float32),
        jnp.zeros((row_count, HEADS, HEAD_DIM), jnp.float32),
    )
    traveler = passed_along(start_pair, "ctx", -reach)
    for position in range(2 * reach):
        softmax_state = arrive(softmax_state, traveler, reach - position)
        traveler = passed_along(traveler, "ctx", 1)
    softmax_state = arrive(softmax_state, traveler, -reach)
    stored_pairs = jnp.stack(stored_list)
    running, total, accum = softmax_state
    attention = accum / jnp.transpose(total)[:, :, None]
    log_total = running + jnp.log(total)
    attention_low = attention.reshape(row_count, feature_count).astype(jnp.bfloat16)
    gain_one = gain_first.astype(jnp.float32)
    shift_one = shift_first.astype(jnp.float32)
    gain_two = gain_second.astype(jnp.float32)
    shift_two = shift_second.astype(jnp.float32)
    residual_one = (
        tokens.astype(jnp.float32) + matmul(attention_low, full_out) + bias_out.astype(jnp.float32)
    )
    first_out = layer_norm(residual_one, gain_one, shift_one)
    first_low = first_out.astype(jnp.bfloat16)
    hidden_pre = matmul(first_low, full_inner) + bias_inner.astype(jnp.float32)
    hidden_low = jax.nn.gelu(hidden_pre, approximate=False).astype(jnp.bfloat16)
    residual_two = first_out + matmul(hidden_low, full_outer) + bias_outer.astype(jnp.float32)
    layer_out = layer_norm(residual_two, gain_two, shift_two).astype(jnp.bfloat16)
    upstream = cotangent.astype(jnp.float32)
    unused_two, second_back = jax.vjp(layer_norm, residual_two, gain_two, shift_two)
    grad_two, grad_gain_second, grad_shift_second = second_back(upstream)
    outer_low = grad_two.astype(jnp.bfloat16)
    grad_bias_outer = column_sums(outer_low)
    grad_full_outer = left_transposed(hidden_low, outer_low)
    grad_activated = right_transposed(outer_low, full_outer)
    unused_gelu, gelu_back = jax.vjp(
        lambda values: jax.nn.gelu(values, approximate=False), hidden_pre
    )
    inner_low = gelu_back(grad_activated)[0].astype(jnp.bfloat16)
    grad_bias_inner = column_sums(inner_low)
    grad_full_inner = left_transposed(first_low, inner_low)
    grad_first = grad_two + right_transposed(inner_low, full_inner)
    unused_one, first_back = jax.vjp(layer_norm, residual_one, gain_one, shift_one)
    grad_one, grad_gain_first, grad_shift_first = first_back(grad_first)
    branch_low = grad_one.astype(jnp.bfloat16)
    grad_bias_out = column_sums(branch_low)
    grad_full_out = left_transposed(attention_low, branch_low)
    grad_attention = right_transposed(branch_low, full_out).astype(jnp.bfloat16)
    grad_heads = grad_attention.reshape(row_count, HEADS, HEAD_DIM)
    delta = jnp.transpose(jnp.sum(grad_heads.astype(jnp.float32) * attention, axis=-1))

    def contribution(key_value, marks):
        raw, allowed = scores_of(key_value, marks)
        chances = jnp.where(allowed, jnp.exp(raw - log_total[:, :, None]), 0.0)
        key_heads = key_value[0].reshape(block_rows, HEADS, HEAD_DIM)
        value_heads = key_value[1].reshape(block_rows, HEADS, HEAD_DIM)
        grad_value = jnp.einsum(
            "hqk,qhd->khd",
            chances.astype(jnp.bfloat16),
            grad_heads,
            preferred_element_type=jnp.float32,
        )
        grad_chances = jnp.einsum(
            "qhd,khd->hqk", grad_heads, value_heads, preferred_element_type=jnp.float32
        )
        grad_scores = (chances * (grad_chances - delta[:, :, None])).astype(jnp.bfloat16)
        grad_query = (
            jnp.einsum("hqk,khd->qhd", grad_scores, key_heads, preferred_element_type=jnp.float32)
            * 0.125
        )
        grad_key = (
            jnp.einsum("hqk,qhd->khd", grad_scores, query_heads, preferred_element_type=jnp.float32)
            * 0.125
        )
        return (
            grad_query,
            jnp.stack(
                (
                    grad_key.reshape(block_rows, feature_count),
                    grad_value.reshape(block_rows, feature_count),
                )
            ),
        )

    zero_query = jnp.zeros((row_count, HEADS, HEAD_DIM), jnp.float32)
    zero_moving = jnp.zeros((2, start_pair.shape[1], feature_count), jnp.float32)

    def block_terms(key_value, offset):
        marks = block_marks(offset)
        return contribution(key_value, marks)

    query_sum = zero_query
    moving = zero_moving
    for position in range(2 * reach):
        part_query, part_pair = block_terms(stored_pairs[position], position - reach)
        moving = passed_along(shortened(moving + part_pair), "ctx", -1)
        query_sum = query_sum + part_query
    part_query, part_pair = block_terms(stored_pairs[2 * reach], reach)
    query_sum = query_sum + part_query
    home_pair = passed_along(shortened(moving + part_pair), "ctx", reach)
    own_grads = lax.psum_scatter(
        home_pair.astype(jnp.bfloat16), "wt", scatter_dimension=1, tiled=True
    ).astype(jnp.float32)
    key_low = own_grads[0].astype(jnp.bfloat16)
    value_low = own_grads[1].astype(jnp.bfloat16)
    query_low = query_sum.reshape(row_count, feature_count).astype(jnp.bfloat16)
    tokens_gradient = (
        grad_one
        + right_transposed(query_low, full_query)
        + right_transposed(key_low, full_key)
        + right_transposed(value_low, full_value)
    )
    grad_full_query = left_transposed(tokens, query_low)
    grad_full_key = left_transposed(tokens, key_low)
    grad_full_value = left_transposed(tokens, value_low)
    grad_bias_query = column_sums(query_low)
    grad_bias_value = column_sums(value_low)
    shards = (
        lax.psum_scatter(
            grad_full_query.astype(jnp.bfloat16), "wt", scatter_dimension=0, tiled=True
        ).astype(jnp.float32),
        lax.psum_scatter(
            grad_full_key.astype(jnp.bfloat16), "wt", scatter_dimension=0, tiled=True
        ).astype(jnp.float32),
        lax.psum_scatter(
            grad_full_value.astype(jnp.bfloat16), "wt", scatter_dimension=0, tiled=True
        ).astype(jnp.float32),
        lax.psum_scatter(
            grad_full_out.astype(jnp.bfloat16), "wt", scatter_dimension=0, tiled=True
        ).astype(jnp.float32),
        lax.psum_scatter(
            grad_bias_query.astype(jnp.bfloat16), "wt", scatter_dimension=0, tiled=True
        ).astype(jnp.float32),
        lax.psum_scatter(
            grad_bias_value.astype(jnp.bfloat16), "wt", scatter_dimension=0, tiled=True
        ).astype(jnp.float32),
        lax.psum_scatter(
            grad_bias_out.astype(jnp.bfloat16), "wt", scatter_dimension=0, tiled=True
        ).astype(jnp.float32),
        lax.psum_scatter(
            grad_gain_first.astype(jnp.bfloat16), "wt", scatter_dimension=0, tiled=True
        ).astype(jnp.float32),
        lax.psum_scatter(
            grad_shift_first.astype(jnp.bfloat16), "wt", scatter_dimension=0, tiled=True
        ).astype(jnp.float32),
        lax.psum_scatter(
            grad_full_inner.astype(jnp.bfloat16), "wt", scatter_dimension=0, tiled=True
        ).astype(jnp.float32),
        lax.psum_scatter(
            grad_bias_inner.astype(jnp.bfloat16), "wt", scatter_dimension=0, tiled=True
        ).astype(jnp.float32),
        lax.psum_scatter(
            grad_full_outer.astype(jnp.bfloat16), "wt", scatter_dimension=0, tiled=True
        ).astype(jnp.float32),
        lax.psum_scatter(
            grad_bias_outer.astype(jnp.bfloat16), "wt", scatter_dimension=0, tiled=True
        ).astype(jnp.float32),
        lax.psum_scatter(
            grad_gain_second.astype(jnp.bfloat16), "wt", scatter_dimension=0, tiled=True
        ).astype(jnp.float32),
        lax.psum_scatter(
            grad_shift_second.astype(jnp.bfloat16), "wt", scatter_dimension=0, tiled=True
        ).astype(jnp.float32),
    )
    totals = lax.psum(
        (
            shards[0],
            shards[1],
            shards[2],
            shards[3],
            shards[4],
            shards[5],
            shards[6],
            shards[7],
            shards[8],
            shards[9],
            shards[10],
            shards[11],
            shards[12],
            shards[13],
            shards[14],
        ),
        "ctx",
    )
    return (layer_out, tokens_gradient) + tuple(totals)


def solution(mesh):
    in_specs = (
        P(("ctx", "wt"), None),
        P(),
        P(("ctx", "wt"), None),
        P("wt", None),
        P("wt", None),
        P("wt", None),
        P("wt", None),
        P("wt"),
        P("wt"),
        P("wt"),
        P("wt"),
        P("wt"),
        P("wt", None),
        P("wt"),
        P("wt", None),
        P("wt"),
        P("wt"),
        P("wt"),
    )
    out_specs = (
        P(("ctx", "wt"), None),
        P(("ctx", "wt"), None),
        P("wt", None),
        P("wt", None),
        P("wt", None),
        P("wt", None),
        P("wt"),
        P("wt"),
        P("wt"),
        P("wt"),
        P("wt"),
        P("wt", None),
        P("wt"),
        P("wt", None),
        P("wt"),
        P("wt"),
        P("wt"),
    )
    return jax.shard_map(
        on_device, mesh=mesh, in_specs=in_specs, out_specs=out_specs, check_vma=False
    )
```

profile of v0, /device:TPU:0, one launch (start us, length us, event | category | flops | bytes accessed | tf_op | source)
XLA Modules:
  0.0 1477.9 jit_solution(848376466840517226)
XLA Ops:
  16.6 13.3 all-reduce.19
  31.9 17.2 %all-gather.13.cloned.1.call-done = bf16[768,768]{1,0:T(8,128)(2,1)} async-done(((bf16[192,768]{1,0:T(8,128)(2,1)}), bf16[768,768]{1,0:T(8,128)(2,1)}) %all-gather.13.cloned.1.call-update) | async-done | bytes 1179664 | tf_op jit(solution)/shard_map/all_gather | solution.py:84
  52.0 28.6 %all-gather.15.cloned.1.call-done = bf16[2,1024,768]{2,1,0:T(8,128)(2,1)} async-done(((bf16[2,256,768]{2,1,0:T(8,128)(2,1)}), bf16[2,1024,768]{2,1,0:T(8,128)(2,1)}) %all-gather.15.cloned.1.call-update) | async-done | bytes 3145744 | tf_op jit(solution)/shard_map/all_gather | solution.py:119
  84.6 67.4 %collective-permute-done = bf16[2,1024,768]{2,1,0:T(8,128)(2,1)} collective-permute-done((bf16[2,1024,768]{2,1,0:T(8,128)(2,1)}, bf16[2,1024,768]{2,1,0:T(8,128)(2,1)}, u32[]{:S(2)}, u32[]{:S(2)}) %collective-permute-start) | collective-permute-done | bytes 3145760 | tf_op jit(solution)/shard_map/ppermute | solution.py:18
  153.6 71.6 %collective-permute-done.1 = bf16[2,1024,768]{2,1,0:T(8,128)(2,1)} collective-permute-done((bf16[2,1024,768]{2,1,0:T(8,128)(2,1)}, bf16[2,1024,768]{2,1,0:T(8,128)(2,1)}, u32[]{:S(2)}, u32[]{:S(2)}) %collective-permute-start.1) | collective-permute-done | bytes 3145760 | tf_op jit(solution)/shard_map/ppermute | solution.py:18
  225.2 71.8 %collective-permute-done.2 = bf16[2,1024,768]{2,1,0:T(8,128)(2,1)} collective-permute-done((bf16[2,1024,768]{2,1,0:T(8,128)(2,1)}, bf16[2,1024,768]{2,1,0:T(8,128)(2,1)}, u32[]{:S(2)}, u32[]{:S(2)}) %collective-permute-start.2) | collective-permute-done | bytes 3145760 | tf_op jit(solution)/shard_map/ppermute | solution.py:18
  316.2 51.8 %collective-permute-done.3 = bf16[2,1024,768]{2,1,0:T(8,128)(2,1)} collective-permute-done((bf16[2,1024,768]{2,1,0:T(8,128)(2,1)}, bf16[2,1024,768]{2,1,0:T(8,128)(2,1)}, u32[]{:S(2)}, u32[]{:S(2)}) %collective-permute-start.3) | collective-permute-done | bytes 3145760 | tf_op jit(solution)/shard_map/ppermute | solution.py:18
  419.5 18.4 %collective-permute-done.4 = bf16[2,1024,768]{2,1,0:T(8,128)(2,1)} collective-permute-done((bf16[2,1024,768]{2,1,0:T(8,128)(2,1)}, bf16[2,1024,768]{2,1,0:T(8,128)(2,1)}, u32[]{:S(2)}, u32[]{:S(2)}) %collective-permute-start.4) | collective-permute-done | bytes 3145760 | tf_op jit(solution)/shard_map/ppermute | solution.py:18
  453.1 10.8 fusion.5
  464.0 13.5 fusion.9
  512.2 11.5 multiply_convert_fusion.6
  574.7 52.1 %collective-permute-done.5 = bf16[2,1024,768]{1,2,0:T(8,128)(2,1)} collective-permute-done((bf16[2,1024,768]{1,2,0:T(8,128)(2,1)}, bf16[2,1024,768]{1,2,0:T(8,128)(2,1)}, u32[]{:S(2)}, u32[]{:S(2)}) %collective-permute-start.5) | collective-permute-done | bytes 3145760 | tf_op jit(solution)/shard_map/ppermute | solution.py:18
  643.2 8.0 fusion.23
  651.3 47.6 %collective-permute-done.6 = bf16[2,1024,768]{1,2,0:T(8,128)(2,1)} collective-permute-done((bf16[2,1024,768]{1,2,0:T(8,128)(2,1)}, bf16[2,1024,768]{1,2,0:T(8,128)(2,1)}, u32[]{:S(2)}, u32[]{:S(2)}) %collective-permute-start.6) | collective-permute-done | bytes 3145760 | tf_op jit(solution)/shard_map/ppermute | solution.py:18
  722.7 49.6 %collective-permute-done.7 = bf16[2,1024,768]{1,2,0:T(8,128)(2,1)} collective-permute-done((bf16[2,1024,768]{1,2,0:T(8,128)(2,1)}, bf16[2,1024,768]{1,2,0:T(8,128)(2,1)}, u32[]{:S(2)}, u32[]{:S(2)}) %collective-permute-start.7) | collective-permute-done | bytes 3145760 | tf_op jit(solution)/shard_map/ppermute | solution.py:18
  794.9 53.6 %collective-permute-done.8 = bf16[2,1024,768]{1,2,0:T(8,128)(2,1)S(1)} collective-permute-done((bf16[2,1024,768]{1,2,0:T(8,128)(2,1)}, bf16[2,1024,768]{1,2,0:T(8,128)(2,1)S(1)}, u32[]{:S(2)}, u32[]{:S(2)}) %collective-permute-start.8) | collective-permute-done | bytes 3145760 | tf_op jit(solution)/shard_map/ppermute | solution.py:18
  851.6 60.8 %collective-permute-done.9 = bf16[2,1024,768]{1,2,0:T(8,128)(2,1)} collective-permute-done((bf16[2,1024,768]{1,2,0:T(8,128)(2,1)S(1)}, bf16[2,1024,768]{1,2,0:T(8,128)(2,1)}, u32[]{:S(2)}, u32[]{:S(2)}) %collective-permute-start.9) | collective-permute-done | bytes 3145760 | tf_op jit(solution)/shard_map/ppermute | solution.py:18
  965.6 13.8 reduce-scatter.22.cloned.1.call-done
  981.3 26.3 %reduce-scatter.16.cloned.1.call-done = bf16[192,768]{1,0:T(8,128)(2,1)} async-done(((bf16[768,768]{1,0:T(8,128)(2,1)}), bf16[192,768]{1,0:T(8,128)(2,1)}) %reduce-scatter.16.cloned.1.call-update) | async-done | bytes 294928 | tf_op jit(solution)/shard_map/reduce_scatter | solution.py:293
  1007.6 50.6 %reduce-scatter.18.cloned.1.call-done = bf16[192,3072]{1,0:T(8,128)(2,1)} async-done(((bf16[768,3072]{1,0:T(8,128)(2,1)}), bf16[192,3072]{1,0:T(8,128)(2,1)}) %reduce-scatter.18.cloned.1.call-update) | async-done | bytes 1179664 | tf_op jit(solution)/shard_map/reduce_scatter | solution.py:311
  1058.2 50.3 %reduce-scatter.20.cloned.1.call-done = bf16[768,768]{1,0:T(8,128)(2,1)} async-done(((bf16[3072,768]{1,0:T(8,128)(2,1)}), bf16[768,768]{1,0:T(8,128)(2,1)}) %reduce-scatter.20.cloned.1.call-update) | async-done | bytes 1179664 | tf_op jit(solution)/shard_map/reduce_scatter | solution.py:317
  1108.7 11.5 all-reduce.18
  1138.1 27.0 %reduce-scatter.24.cloned.1.call-done = bf16[192,768]{1,0:T(8,128)(2,1)} async-done(((bf16[768,768]{1,0:T(8,128)(2,1)}), bf16[192,768]{1,0:T(8,128)(2,1)}) %reduce-scatter.24.cloned.1.call-update) | async-done | bytes 294928
  1166.3 301.4 %all-reduce.21 = (f32[192,768]{0,1:T(8,128)S(1)}, f32[192,768]{0,1:T(8,128)S(1)}, f32[192,768]{0,1:T(8,128)S(1)}, f32[192,768]{1,0:T(8,128)}, f32[192]{0:T(256)}...) all-reduce(bf16[192,768]{0,1:T(8,128)(2,1)S(1)} %copy-done.57, ...), channel_id=1, replica_groups=mesh['ctx'=8,'wt'=4] {'ctx'}, use_global_device_ids=true, to_apply=%region_21.22 | all-reduce | flops 1771776 | bytes 10635264 | tf_op jit(solution)/shard_map/psum | solution.py:330
  (456 shorter events, 331.1 us)
Async XLA Ops:
  7.2 22.8 %all-gather.11.cloned.1.call-start = ((), (), s32[]{:S(2)}) async-start(), calls=%async_computation.8 | async-start | bytes 1474560 | tf_op jit(solution)/shard_map/all_gather | solution.py:83
  7.9 41.1 %all-gather.13.cloned.1.call-start = ((), (), s32[]{:S(2)}) async-start(), calls=%async_computation.9 | async-start | bytes 1474560 | tf_op jit(solution)/shard_map/all_gather | solution.py:84
  8.7 72.0 %all-gather.15.cloned.1.call-start = ((), (), s32[]{:S(2)}) async-start(), calls=%async_computation.10 | async-start | bytes 3932160 | tf_op jit(solution)/shard_map/all_gather | solution.py:119
  51.9 253.2 %all-gather.9.cloned.1.call-start = ((), (), s32[]{:S(2)}) async-start(), calls=%async_computation.7 | async-start | bytes 1474560 | tf_op jit(solution)/shard_map/all_gather | solution.py:82
  80.6 71.4 %collective-permute-start = (bf16[2,1024,768]{2,1,0:T(8,128)(2,1)}, bf16[2,1024,768]{2,1,0:T(8,128)(2,1)}, u32[]{:S(2)}, u32[]{:S(2)}) collective-permute-start(bf16[2,1024,768]{2,1,0:T(8,128)(2,1)} %all-gather.15.cloned.1.call-done), channel_id=1, source_target_pairs={{8,0},{12,4},{16,8},{20,12},{24,16},{28,20},{0,24},{4,28},{9,1},{1... | collective-permute-start | bytes 9437192 | tf_op jit(solution)/shard_map/ppermute | solution.py:18
  84.0 425.8 %all-gather.17.cloned.1.call-start = ((), (), s32[]{:S(2)}) async-start(), calls=%async_computation.11 | async-start | bytes 1474560 | tf_op jit(solution)/shard_map/all_gather | solution.py:85
  84.6 427.6 %all-gather.19.cloned.1.call-start = ((), (), s32[]{:S(2)}) async-start(), calls=%async_computation.12 | async-start | bytes 5898240 | tf_op jit(solution)/shard_map/all_gather | solution.py:91
  152.0 73.2 %collective-permute-start.1 = (bf16[2,1024,768]{2,1,0:T(8,128)(2,1)}, bf16[2,1024,768]{2,1,0:T(8,128)(2,1)}, u32[]{:S(2)}, u32[]{:S(2)}) collective-permute-start(bf16[2,1024,768]{2,1,0:T(8,128)(2,1)} %collective-permute-done), channel_id=1, source_target_pairs={{28,0},{0,4},{4,8},{8,12},{12,16},{16,20},{20,24},{24,28},{29,1},{... | collective-permute-start | bytes 9437192 | tf_op jit(solution)/shard_map/ppermute | solution.py:18
  153.5 370.2 %all-gather.21.cloned.1.call-start = ((), (), s32[]{:S(2)}) async-start(), calls=%async_computation.13 | async-start | bytes 5898240 | tf_op jit(solution)/shard_map/all_gather | solution.py:93
  225.2 71.8 %collective-permute-start.2 = (bf16[2,1024,768]{2,1,0:T(8,128)(2,1)}, bf16[2,1024,768]{2,1,0:T(8,128)(2,1)}, u32[]{:S(2)}, u32[]{:S(2)}) collective-permute-start(bf16[2,1024,768]{2,1,0:T(8,128)(2,1)} %collective-permute-done.1), channel_id=1, source_target_pairs={{28,0},{0,4},{4,8},{8,12},{12,16},{16,20},{20,24},{24,28},{29,1},{... | collective-permute-start | bytes 9437192 | tf_op jit(solution)/shard_map/ppermute | solution.py:18
  297.1 70.9 %collective-permute-start.3 = (bf16[2,1024,768]{2,1,0:T(8,128)(2,1)}, bf16[2,1024,768]{2,1,0:T(8,128)(2,1)}, u32[]{:S(2)}, u32[]{:S(2)}) collective-permute-start(bf16[2,1024,768]{2,1,0:T(8,128)(2,1)} %collective-permute-done.2), channel_id=1, source_target_pairs={{28,0},{0,4},{4,8},{8,12},{12,16},{16,20},{20,24},{24,28},{29,1},{... | collective-permute-start | bytes 9437192 | tf_op jit(solution)/shard_map/ppermute | solution.py:18
  297.1 653.3 %reduce-scatter.14.cloned.1.call-start = ((), (), s32[]{:S(2)}) async-start(), calls=%async_computation.14 | async-start | bytes 3932160 | tf_op jit(solution)/shard_map/reduce_scatter | solution.py:266
  368.0 70.0 %collective-permute-start.4 = (bf16[2,1024,768]{2,1,0:T(8,128)(2,1)}, bf16[2,1024,768]{2,1,0:T(8,128)(2,1)}, u32[]{:S(2)}, u32[]{:S(2)}) collective-permute-start(bf16[2,1024,768]{2,1,0:T(8,128)(2,1)} %collective-permute-done.3), channel_id=1, source_target_pairs={{28,0},{0,4},{4,8},{8,12},{12,16},{16,20},{20,24},{24,28},{29,1},{... | collective-permute-start | bytes 9437192 | tf_op jit(solution)/shard_map/ppermute | solution.py:18
  560.4 66.4 %collective-permute-start.5 = (bf16[2,1024,768]{1,2,0:T(8,128)(2,1)}, bf16[2,1024,768]{1,2,0:T(8,128)(2,1)}, u32[]{:S(2)}, u32[]{:S(2)}) collective-permute-start(bf16[2,1024,768]{1,2,0:T(8,128)(2,1)} %pad_maximum_fusion), channel_id=1, source_target_pairs={{4,0},{8,4},{12,8},{16,12},{20,16},{24,20},{28,24},{0,28},{5,1},{9... | collective-permute-start | bytes 9437192 | tf_op jit(solution)/shard_map/ppermute | solution.py:18
  632.7 66.2 %collective-permute-start.6 = (bf16[2,1024,768]{1,2,0:T(8,128)(2,1)}, bf16[2,1024,768]{1,2,0:T(8,128)(2,1)}, u32[]{:S(2)}, u32[]{:S(2)}) collective-permute-start(bf16[2,1024,768]{1,2,0:T(8,128)(2,1)} %fusion.15), channel_id=1, source_target_pairs={{4,0},{8,4},{12,8},{16,12},{20,16},{24,20},{28,24},{0,28},{5,1},{9... | collective-permute-start | bytes 9437192 | tf_op jit(solution)/shard_map/ppermute | solution.py:18
  704.8 67.5 %collective-permute-start.7 = (bf16[2,1024,768]{1,2,0:T(8,128)(2,1)}, bf16[2,1024,768]{1,2,0:T(8,128)(2,1)}, u32[]{:S(2)}, u32[]{:S(2)}) collective-permute-start(bf16[2,1024,768]{1,2,0:T(8,128)(2,1)} %fusion.16), channel_id=1, source_target_pairs={{4,0},{8,4},{12,8},{16,12},{20,16},{24,20},{28,24},{0,28},{5,1},{9... | collective-permute-start | bytes 9437192 | tf_op jit(solution)/shard_map/ppermute | solution.py:18
  778.1 70.4 %collective-permute-start.8 = (bf16[2,1024,768]{1,2,0:T(8,128)(2,1)}, bf16[2,1024,768]{1,2,0:T(8,128)(2,1)S(1)}, u32[]{:S(2)}, u32[]{:S(2)}) collective-permute-start(bf16[2,1024,768]{1,2,0:T(8,128)(2,1)} %fusion.17), channel_id=1, source_target_pairs={{4,0},{8,4},{12,8},{16,12},{20,16},{24,20},{28,24},{0,28},{5,1},{9... | collective-permute-start | bytes 9437192 | tf_op jit(solution)/shard_map/ppermute | solution.py:18
  851.5 60.8 %collective-permute-start.9 = (bf16[2,1024,768]{1,2,0:T(8,128)(2,1)S(1)}, bf16[2,1024,768]{1,2,0:T(8,128)(2,1)}, u32[]{:S(2)}, u32[]{:S(2)}) collective-permute-start(bf16[2,1024,768]{1,2,0:T(8,128)(2,1)S(1)} %fusion.18), channel_id=1, source_target_pairs={{24,0},{28,4},{0,8},{4,12},{8,16},{12,20},{16,24},{20,28},{25,1},{... | collective-permute-start | bytes 9437192 | tf_op jit(solution)/shard_map/ppermute | solution.py:18
  912.4 67.1 %reduce-scatter.22.cloned.1.call-start = ((), (), s32[]{:S(2)}) async-start(), calls=%async_computation.18 | async-start | bytes 1474560
  935.1 72.5 %reduce-scatter.16.cloned.1.call-start = ((), (), s32[]{:S(2)}) async-start(), calls=%async_computation.15 | async-start | bytes 1474560 | tf_op jit(solution)/shard_map/reduce_scatter | solution.py:293
  936.7 121.5 %reduce-scatter.18.cloned.1.call-start = ((), (), s32[]{:S(2)}) async-start(), calls=%async_computation.16 | async-start | bytes 5898240 | tf_op jit(solution)/shard_map/reduce_scatter | solution.py:311
  942.0 166.5 %reduce-scatter.20.cloned.1.call-start = ((), (), s32[]{:S(2)}) async-start(), calls=%async_computation.17 | async-start | bytes 5898240 | tf_op jit(solution)/shard_map/reduce_scatter | solution.py:317
  947.2 189.8 %reduce-scatter.26.cloned.1.call-start = ((), (), s32[]{:S(2)}) async-start(), calls=%async_computation.20 | async-start | bytes 1474560
  955.4 209.7 %reduce-scatter.24.cloned.1.call-start = ((), (), s32[]{:S(2)}) async-start(), calls=%async_computation.19 | async-start | bytes 1474560
  (129 other events, 3705.5 us)
Sparse Core Ops, SparseCore 0:
  9.6 20.3 all-gather.10
  31.6 17.4 all-gather.12
  52.1 28.5 all-gather.14
  84.1 15.3 all-gather.8
  100.9 17.4 all-gather.16
  153.7 37.4 all-gather.18
  297.2 37.9 all-gather.20
  912.5 37.8 reduce-scatter.13
  953.7 25.7 reduce-scatter.21
  981.9 25.7 reduce-scatter.15
  1010.3 47.8 reduce-scatter.17
  1060.6 47.8 reduce-scatter.19
  1111.2 25.7 reduce-scatter.25
  1139.4 25.7 reduce-scatter.23
where the time goes:
time: 1490 us; the launch traced here: 1480 us
  waiting for transfers between devices  764 us (51%)
  blocking collectives  331 us (22%)
  matrix products  192 us (13%)
  local copies, waits for them, and re-layouts  79 us (5%)
  other arithmetic  73.7 us (5%)
  starting transfers between devices  19.2 us (1%)
  between operations  18.2 us (1%)
    ppermute x10, waiting for transfers between devices, passed_along(): return lax.ppermute(block, axis, route)  545 us
    psum x1, blocking collectives, on_device(): lax.psum((shards[0], shards[1], shards[2], shards[3], shards[4], shards[5...  301 us
    reduce_scatter x1, waiting for transfers between devices, on_device(): lax.psum_scatter(grad_full_inner.astype(jnp.bfloat16), 'wt', scatter_dime...  50.6 us
    reduce_scatter x1, waiting for transfers between devices, on_device(): lax.psum_scatter(grad_full_outer.astype(jnp.bfloat16), 'wt', scatter_dime...  50.3 us
    unnamed x17, waiting for transfers between devices  43.2 us
    unnamed x285, local copies, waits for them, and re-layouts  37.5 us
    dot_general x5, matrix products, scores_of(): jnp.einsum('qhd,khd->hqk', query_heads, key_heads, preferred_element_type...  30.7 us
  transfers between devices with their start and end apart: 24, of which 20 were waited for; matrix products, arithmetic and copies ran while one was open for 18% of the time, Pallas kernels for 0%

commit v1 on v0

v1 whole, which is shorter than its diff:
```python
import functools

import jax
import jax.numpy as jnp
from jax import lax
from jax.experimental import pallas as pl
from jax.experimental.pallas import tpu as pltpu
from jax.sharding import PartitionSpec as P

HEADS = 12
HEAD_DIM = 64
MAXDOC = 2048
TILE = 256

masked_score = -1e30
epsilon = 1e-06
bf16 = jnp.bfloat16
f32 = jnp.float32


def swapped(block, axis, bit):
    count = lax.axis_size(axis)
    return lax.ppermute(block, axis, [(i, i ^ bit) for i in range(count)])


def shifted(block, axis, distance):
    count = lax.axis_size(axis)
    route = [(i, i + distance) for i in range(count) if 0 <= i + distance < count]
    return lax.ppermute(block, axis, route)


def matmul(left, right):
    return jnp.dot(left, right, preferred_element_type=f32)


def left_transposed(left, right):
    return jnp.einsum("td,te->de", left, right, preferred_element_type=f32)


def right_transposed(left, right):
    return jnp.einsum("te,de->td", left, right, preferred_element_type=f32)


def column_sums(values):
    return jnp.sum(values.astype(f32), axis=0)


def rows_nt(left, right):
    return lax.dot_general(left, right, (((1,), (1,)), ((), ())), preferred_element_type=f32)


def rows_nn(left, right):
    return lax.dot_general(left, right, (((1,), (0,)), ((), ())), preferred_element_type=f32)


def load_window(pieces, target, sem, block):
    copies = [
        pltpu.make_async_copy(piece, target.at[pl.ds(i * block, block), :], sem.at[i])
        for i, piece in enumerate(pieces)
    ]
    for copy in copies:
        copy.start()
    return copies


def tile_loops(bounds, step, run):
    low, full_low, full_high, high = (bounds[4 * step + i] for i in range(4))
    front = full_low - low

    def edge(i, carry):
        tile = jnp.where(i < front, low + i, full_high + i - front)
        run(tile, True)
        return carry

    def inner(i, carry):
        run(i, False)
        return carry

    lax.fori_loop(0, front + high - full_high, edge, 0)
    lax.fori_loop(full_low, full_high, inner, 0)


def allowed_rows(span_ref, first, tile):
    keys = tile * TILE + lax.broadcasted_iota(jnp.int32, (TILE, TILE), 1)
    start = span_ref[pl.ds(first, TILE), 0:1]
    stop = span_ref[pl.ds(first, TILE), 1:2]
    return (keys >= start) & (keys < stop)


def head_of(tile0, tile1, head):
    lane = lax.broadcasted_iota(jnp.int32, tile0.shape, 1)
    if head == 0:
        return jnp.where(lane < HEAD_DIM, tile0, jnp.zeros_like(tile0))
    if head == 1:
        return jnp.where(lane >= HEAD_DIM, tile0, jnp.zeros_like(tile0))
    return tile1


def forward_kernel(bounds, q_ref, span_ref, *rest):
    pieces, (out_ref, wide_ref, stat_ref, kv, top, total, accum, sem) = rest[:-8], rest[-8:]
    step = pl.program_id(0)
    block = pieces[0].shape[0]

    @pl.when(step == 0)
    def _():
        for copy in load_window(pieces, kv, sem, block):
            copy.wait()

    first = pl.multiple_of(step * TILE, TILE)
    top[...] = jnp.full_like(top, masked_score)
    total[...] = jnp.zeros_like(total)
    accum[...] = jnp.zeros_like(accum)
    q_tile = q_ref[pl.ds(first, TILE), :]
    heads = [head_of(q_tile[:, :128], q_tile[:, 128:], h) for h in range(3)]

    def run(tile, edge):
        rows = pl.ds(pl.multiple_of(tile * TILE, TILE), TILE)
        allowed = allowed_rows(span_ref, first, tile) if edge else None
        for h in range(3):
            keys = kv[rows, 0:128] if h < 2 else kv[rows, 128:192]
            values = kv[rows, 128:256] if h == 0 else kv[rows, 256:384]
            score = rows_nt(heads[h], keys)
            if edge:
                score = jnp.where(allowed, score, masked_score)
            before = top[h]
            newest = jnp.maximum(before, jnp.max(score, axis=1, keepdims=True))
            factor = jnp.exp(before - newest)
            weight = jnp.exp(score - jnp.tile(newest, (1, TILE // 128)))
            if edge:
                weight = jnp.where(allowed, weight, 0.0)
            part = weight[:, 0:128]
            for i in range(1, TILE // 128):
                part = part + weight[:, 128 * i : 128 * i + 128]
            total[h] = total[h] * factor + part
            accum[h] = accum[h] * factor + rows_nn(weight.astype(bf16), values)
            top[h] = newest

    tile_loops(bounds, step, run)
    lane = lax.broadcasted_iota(jnp.int32, (TILE, 128), 1)
    mixed, stats = [], jnp.zeros((TILE, 128), f32)
    for h in range(3):
        mass = jnp.sum(total[h], axis=1, keepdims=True)
        mixed.append(pltpu.roll(accum[h] / mass, HEAD_DIM, 1))
        stats = jnp.where(lane == h, top[h] + jnp.log(mass), stats)
    here = pl.ds(first, TILE)
    pair = jnp.where(lane < HEAD_DIM, mixed[0], mixed[1])
    wide_ref[here, 0:128] = pair
    wide_ref[here, 128:192] = mixed[2][:, :HEAD_DIM]
    out_ref[here, 0:128] = pair.astype(bf16)
    out_ref[here, 128:192] = mixed[2][:, :HEAD_DIM].astype(bf16)
    stat_ref[here, :] = stats


def whole_spec(shape):
    return pl.BlockSpec(shape, lambda i, *_: (0,) * len(shape))


def attention_forward(bounds, queries, spans, pieces):
    block = queries.shape[0]
    window = len(pieces) * block
    return pl.pallas_call(
        forward_kernel,
        grid_spec=pltpu.PrefetchScalarGridSpec(
            num_scalar_prefetch=1,
            grid=(block // TILE,),
            in_specs=[whole_spec(queries.shape), whole_spec(spans.shape)]
            + [pl.BlockSpec(memory_space=pl.ANY)] * len(pieces),
            out_specs=[
                whole_spec((block, 192)),
                whole_spec((block, 192)),
                whole_spec((block, 128)),
            ],
            scratch_shapes=[
                pltpu.VMEM((window, 384), bf16),
                pltpu.VMEM((3, TILE, 128), f32),
                pltpu.VMEM((3, TILE, 128), f32),
                pltpu.VMEM((3, TILE, 128), f32),
                pltpu.SemaphoreType.DMA((len(pieces),)),
            ],
        ),
        out_shape=[
            jax.ShapeDtypeStruct((block, 192), bf16),
            jax.ShapeDtypeStruct((block, 192), f32),
            jax.ShapeDtypeStruct((block, 128), f32),
        ],
        compiler_params=pltpu.CompilerParams(vmem_limit_bytes=40 * 2**20),
        cost_estimate=pl.CostEstimate(
            flops=4 * block * 2304 * 192, bytes_accessed=6 * 2**20, transcendentals=block * 2304 * 3
        ),
        name="attention_forward",
    )(bounds, queries, spans, *pieces)


def query_kernel(bounds, q_ref, span_ref, grad_ref, wide_ref, stat_ref, *rest):
    pieces, (out_ref, kv, accum, sem) = rest[:-4], rest[-4:]
    step = pl.program_id(0)
    block = pieces[0].shape[0]

    @pl.when(step == 0)
    def _():
        for copy in load_window(pieces, kv, sem, block):
            copy.wait()

    first = pl.multiple_of(step * TILE, TILE)
    here = pl.ds(first, TILE)
    accum[...] = jnp.zeros_like(accum)
    q_tile = q_ref[here, :]
    heads = [head_of(q_tile[:, :128], q_tile[:, 128:], h) for h in range(3)]
    g_tile = grad_ref[here, :]
    lane = lax.broadcasted_iota(jnp.int32, (TILE, 128), 1)
    g_pair = g_tile[:, :128]
    g_last = jnp.concatenate([g_tile[:, 128:], jnp.zeros((TILE, HEAD_DIM), bf16)], axis=1)
    none = jnp.zeros((TILE, 128), bf16)
    r_pair = pltpu.roll(g_pair.astype(f32), HEAD_DIM, 1).astype(bf16)
    r_last = pltpu.roll(g_last.astype(f32), HEAD_DIM, 1).astype(bf16)
    grads = [
        jnp.where(lane >= HEAD_DIM, r_pair, none),
        jnp.where(lane < HEAD_DIM, r_pair, none),
        jnp.where(lane >= HEAD_DIM, r_last, none),
    ]
    product_pair = g_pair.astype(f32) * wide_ref[here, 0:128]
    product_last = g_tile[:, 128:].astype(f32) * wide_ref[here, 128:192]
    deltas = [
        jnp.sum(jnp.where(lane < HEAD_DIM, product_pair, 0.0), axis=1, keepdims=True),
        jnp.sum(jnp.where(lane < HEAD_DIM, 0.0, product_pair), axis=1, keepdims=True),
        jnp.sum(product_last, axis=1, keepdims=True),
    ]
    logs = [stat_ref[here, h : h + 1] for h in range(3)]
    deltas = [jnp.broadcast_to(d, (TILE, 128)) for d in deltas]
    logs = [jnp.broadcast_to(d, (TILE, 128)) for d in logs]

    def run(tile, edge):
        rows = pl.ds(pl.multiple_of(tile * TILE, TILE), TILE)
        allowed = allowed_rows(span_ref, first, tile) if edge else None
        for h in range(3):
            keys = kv[rows, 0:128] if h < 2 else kv[rows, 128:192]
            values = kv[rows, 128:256] if h == 0 else kv[rows, 256:384]
            score = rows_nt(heads[h], keys) - jnp.tile(logs[h], (1, TILE // 128))
            if edge:
                score = jnp.where(allowed, score, masked_score)
            chance = jnp.exp(score)
            back = rows_nt(grads[h], values) - jnp.tile(deltas[h], (1, TILE // 128))
            change = (chance * back).astype(bf16)
            accum[h] += rows_nn(change, kv[rows, 0:128] if h < 2 else kv[rows, 128:256])

    tile_loops(bounds, step, run)
    out_ref[here, 0:128] = (jnp.where(lane < HEAD_DIM, accum[0], accum[1]) * 0.125).astype(bf16)
    out_ref[here, 128:192] = (accum[2][:, :HEAD_DIM] * 0.125).astype(bf16)


def attention_queries(bounds, queries, spans, grads, wide, stats, pieces):
    block = queries.shape[0]
    window = len(pieces) * block
    return pl.pallas_call(
        query_kernel,
        grid_spec=pltpu.PrefetchScalarGridSpec(
            num_scalar_prefetch=1,
            grid=(block // TILE,),
            in_specs=[whole_spec(x.shape) for x in (queries, spans, grads, wide, stats)]
            + [pl.BlockSpec(memory_space=pl.ANY)] * len(pieces),
            out_specs=whole_spec((block, 192)),
            scratch_shapes=[
                pltpu.VMEM((window, 384), bf16),
                pltpu.VMEM((3, TILE, 128), f32),
                pltpu.SemaphoreType.DMA((len(pieces),)),
            ],
        ),
        out_shape=jax.ShapeDtypeStruct((block, 192), bf16),
        compiler_params=pltpu.CompilerParams(vmem_limit_bytes=40 * 2**20),
        cost_estimate=pl.CostEstimate(
            flops=6 * block * 2304 * 192, bytes_accessed=6 * 2**20, transcendentals=block * 2304 * 3
        ),
        name="attention_queries",
    )(bounds, queries, spans, grads, wide, stats, *pieces)


def key_kernel(reach, bounds, kv_ref, span_ref, stat_ref, *rest):
    window = 2 * reach + 1
    q_pieces, g_pieces = rest[:window], rest[window : 2 * window]
    out_ref, qs, gs, key_sum, value_sum, sem = rest[2 * window :]
    step = pl.program_id(0)
    block = q_pieces[0].shape[0]

    @pl.when(step == 0)
    def _():
        copies = load_window(q_pieces, qs, sem.at[0], block)
        copies += load_window(g_pieces, gs, sem.at[1], block)
        for copy in copies:
            copy.wait()

    first = pl.multiple_of(step * TILE, TILE)
    here = pl.ds(first, TILE)
    key_sum[...] = jnp.zeros_like(key_sum)
    value_sum[...] = jnp.zeros_like(value_sum)
    keys_pair = kv_ref[here, 0:128]
    keys = [head_of(keys_pair, kv_ref[here, 128:192], h) for h in range(3)]
    lane = lax.broadcasted_iota(jnp.int32, (TILE, 128), 1)
    zero = jnp.zeros((TILE, 128), f32)
    v_one = pltpu.roll(kv_ref[here, 128:256].astype(f32), HEAD_DIM, 1)
    v_two = pltpu.roll(kv_ref[here, 256:384].astype(f32), HEAD_DIM, 1)
    values = [
        jnp.where(lane < HEAD_DIM, v_one, zero).astype(bf16),
        jnp.where(lane < HEAD_DIM, zero, v_two).astype(bf16),
        v_two.astype(bf16)[:, :HEAD_DIM],
    ]

    def run(tile, edge):
        columns = pl.ds(pl.multiple_of(tile * TILE, TILE), TILE)
        if edge:
            place = reach * block + first + lax.broadcasted_iota(jnp.int32, (TILE, TILE), 0)
            allowed = (place >= span_ref[0:1, columns]) & (place < span_ref[1:2, columns])
        for h in range(3):
            lanes = slice(0, 128) if h < 2 else slice(128, 192)
            q_tile, g_tile = qs[columns, lanes], gs[columns, lanes]
            score = rows_nt(keys[h], q_tile) - stat_ref[h : h + 1, columns]
            if edge:
                score = jnp.where(allowed, score, masked_score)
            chance = jnp.exp(score)
            back = rows_nt(values[h], g_tile) - stat_ref[h + 3 : h + 4, columns]
            change = (chance * back).astype(bf16)
            size = 128 if h < 2 else HEAD_DIM
            key_sum[h, :, 0:size] += rows_nn(change, q_tile)
            value_sum[h, :, 0:size] += rows_nn(chance.astype(bf16), g_tile)

    tile_loops(bounds, step, run)
    k_pair = jnp.where(lane < HEAD_DIM, key_sum[0], key_sum[1])
    v_pair = jnp.where(lane < HEAD_DIM, value_sum[0], value_sum[1])
    k_last = key_sum[2]
    v_last = value_sum[2]
    v_turn = pltpu.roll(v_pair, HEAD_DIM, 1)
    last_turn = pltpu.roll(v_last, HEAD_DIM, 1)
    out_ref[here, 0:128] = k_pair.astype(bf16)
    out_ref[here, 128:256] = jnp.where(lane < HEAD_DIM, k_last, v_turn).astype(bf16)
    out_ref[here, 256:384] = jnp.where(lane < HEAD_DIM, v_turn, last_turn).astype(bf16)


def attention_keys(bounds, pair, spans, stats, q_pieces, g_pieces):
    block = pair.shape[0]
    count = len(q_pieces)
    return pl.pallas_call(
        functools.partial(key_kernel, count // 2),
        grid_spec=pltpu.PrefetchScalarGridSpec(
            num_scalar_prefetch=1,
            grid=(block // TILE,),
            in_specs=[whole_spec(x.shape) for x in (pair, spans, stats)]
            + [pl.BlockSpec(memory_space=pl.ANY)] * (2 * count),
            out_specs=whole_spec((block, 384)),
            scratch_shapes=[
                pltpu.VMEM((count * block, 192), bf16),
                pltpu.VMEM((count * block, 192), bf16),
                pltpu.VMEM((3, TILE, 128), f32),
                pltpu.VMEM((3, TILE, 128), f32),
                pltpu.SemaphoreType.DMA((2, count)),
            ],
        ),
        out_shape=jax.ShapeDtypeStruct((block, 384), bf16),
        compiler_params=pltpu.CompilerParams(vmem_limit_bytes=40 * 2**20),
        cost_estimate=pl.CostEstimate(
            flops=8 * block * 2304 * 192, bytes_accessed=8 * 2**20, transcendentals=block * 2304 * 3
        ),
        name="attention_keys",
    )(bounds, pair, spans, stats, *q_pieces, *g_pieces)


def norm_parts(values):
    center = values - jnp.mean(values, axis=-1, keepdims=True)
    inverse = lax.rsqrt(jnp.mean(center * center, axis=-1, keepdims=True) + epsilon)
    return center * inverse, inverse


def norm_back(upstream, normal, inverse, gain):
    scaled = upstream * gain
    mean_scaled = jnp.mean(scaled, axis=-1, keepdims=True)
    mean_product = jnp.mean(scaled * normal, axis=-1, keepdims=True)
    grad = (scaled - mean_scaled - normal * mean_product) * inverse
    return grad, jnp.sum(upstream * normal, axis=0), jnp.sum(upstream, axis=0)


def both(left, right):
    return (left.astype(f32) + right.astype(f32)).astype(bf16)


def halves(block, bit, axis):
    size = block.shape[axis] // 2
    kept = lax.dynamic_slice_in_dim(block, bit * size, size, axis)
    sent = lax.dynamic_slice_in_dim(block, (1 - bit) * size, size, axis)
    return kept, sent


def scatter_sum(block, axis_name, order, axis):
    index = lax.axis_index(axis_name)
    for step in order:
        kept, sent = halves(block, (index // step) % 2, axis)
        block = both(kept, swapped(sent, axis_name, step))
    return block


def gather_back(block, axis_name, order, axis):
    index = lax.axis_index(axis_name)
    for step in reversed(order):
        other = swapped(block, axis_name, step)
        late = (index // step) % 2 == 1
        block = jnp.where(
            late,
            jnp.concatenate([other, block], axis),
            jnp.concatenate([block, other], axis),
        )
    return block


def on_device(
    tokens,
    doc_start,
    cotangent,
    query_weight,
    key_weight,
    value_weight,
    out_weight,
    query_bias,
    value_bias,
    out_bias,
    first_gain,
    first_shift,
    inner_weight,
    inner_bias,
    outer_weight,
    outer_bias,
    second_gain,
    second_shift,
):
    rows, width = tokens.shape
    cycle = lax.axis_size("ctx")
    shards = lax.axis_size("wt")
    block = rows * shards
    reach = (MAXDOC + block - 2) // block
    window = (2 * reach + 1) * block
    c = lax.axis_index("ctx")
    w = lax.axis_index("wt")
    part = width // shards
    hidden_size = inner_weight.shape[1]
    others = [w ^ r for r in range(shards)]

    def placed(pieces):
        buffer = jnp.zeros((shards,) + pieces[0].shape, pieces[0].dtype)
        for r, piece in enumerate(pieces):
            buffer = lax.dynamic_update_slice_in_dim(buffer, piece[None], others[r], 0)
        return buffer

    def spread(own):
        far = swapped(own, "wt", 2)
        near = swapped(jnp.stack((own, far)), "wt", 1)
        return [own, near[0], far, near[1]]

    token_pieces = spread(tokens)

    def columns(r):
        start = others[r] * part
        return jnp.concatenate(
            [
                lax.dynamic_slice_in_dim(x, start, part, 1)
                for x in (query_weight, key_weight, value_weight)
            ],
            axis=1,
        )

    projection = placed(
        [columns(0)] + [swapped(columns(r), "wt", r) for r in range(1, shards)]
    ).reshape(width, 3 * part)
    block_tokens = placed(token_pieces).reshape(block, width)

    small_own = jnp.concatenate(
        [out_bias, first_gain, first_shift, outer_bias, second_gain, second_shift, inner_bias]
    ).reshape(-1, part)
    small = lax.all_gather(small_own, "wt", axis=0)
    out_bias_row, gain_one, shift_one, outer_bias_row, gain_two, shift_two = (
        small[:, i].reshape(width).astype(f32) for i in range(6)
    )
    inner_bias_row = small[:, 6:].reshape(hidden_size).astype(f32)

    pad = reach * block
    padded = jnp.pad(doc_start, (pad, pad), constant_values=-1)
    base = c * block - pad
    marks = lax.dynamic_slice_in_dim(padded, c * block, window)
    place = jnp.arange(window, dtype=jnp.int32)
    begins = jnp.where((marks == base + place) | (marks < 0), place, window)
    next_begin = lax.cummin(begins, axis=0, reverse=True)
    stops = jnp.concatenate([next_begin[1:], jnp.full((1,), window, jnp.int32)])
    starts = marks - base
    spans_row = jnp.stack([starts, stops] + [jnp.zeros_like(starts)] * 6)
    spans_column = spans_row[:, pad : pad + block].T
    own_starts = starts[pad : pad + block].reshape(-1, TILE)
    own_stops = stops[pad : pad + block].reshape(-1, TILE)
    lowest, highest = own_starts[:, 0], own_stops[:, -1]
    low, high = lowest // TILE, (highest + TILE - 1) // TILE
    full_low, full_high = (lowest + TILE - 1) // TILE, highest // TILE
    single = (own_starts[:, -1] == lowest) & (full_low < full_high)
    full_low = jnp.where(single, full_low, low)
    full_high = jnp.where(single, full_high, low)
    bounds = jnp.stack([low, full_low, full_high, high], axis=1).reshape(-1)

    projected = matmul(block_tokens, projection)
    own_query_bias = query_bias.astype(f32)
    own_value_bias = value_bias.astype(f32)
    queries = (
        (projected[:, :part] + own_query_bias).astype(bf16).astype(f32) * 0.125
    ).astype(bf16)
    pair = jnp.concatenate(
        [projected[:, part : 2 * part], projected[:, 2 * part :] + own_value_bias], axis=1
    ).astype(bf16)

    distances = [d for d in range(reach, -reach - 1, -1)]

    def halo(own):
        return [own if d == 0 else shifted(own, "ctx", d) for d in distances]

    pairs = halo(pair)
    inner_pieces = spread(inner_weight)
    outer_pieces = spread(jnp.concatenate([outer_weight, out_weight], axis=0))
    out_pieces = [x[hidden_size // shards :] for x in outer_pieces]
    full_inner = placed(inner_pieces).reshape(width, hidden_size)
    full_outer = placed([x[: hidden_size // shards] for x in outer_pieces]).reshape(
        hidden_size, width
    )

    mixed, mixed_wide, stat_columns = attention_forward(bounds, queries, spans_column, pairs)
    query_halo = halo(queries)

    mixed_rows = mixed.reshape(shards, rows, part)
    mixed_pieces = [
        lax.dynamic_index_in_dim(mixed_rows, others[r], 0, keepdims=False) for r in range(shards)
    ]
    mixed_pieces = [mixed_pieces[0]] + [
        swapped(mixed_pieces[r], "wt", r) for r in range(1, shards)
    ]
    branch = sum(matmul(mixed_pieces[r], out_pieces[r]) for r in range(shards))
    residual_one = tokens.astype(f32) + branch + out_bias_row
    normal_one, inverse_one = norm_parts(residual_one)
    first = normal_one * gain_one + shift_one
    first_low = first.astype(bf16)
    hidden = matmul(first_low, full_inner) + inner_bias_row
    cdf = 0.5 * (1.0 + lax.erf(hidden * (2.0**-0.5)))
    slope = cdf + hidden * jnp.exp(-0.5 * hidden * hidden) * ((2.0 * jnp.pi) ** -0.5)
    activated = (hidden * cdf).astype(bf16)
    residual_two = first + matmul(activated, full_outer) + outer_bias_row
    normal_two, inverse_two = norm_parts(residual_two)
    layer_out = (normal_two * gain_two + shift_two).astype(bf16)

    upstream = cotangent.astype(f32)
    grad_two, gain_two_grad, shift_two_grad = norm_back(
        upstream, normal_two, inverse_two, gain_two
    )
    grad_two_low = grad_two.astype(bf16)
    outer_bias_grad = column_sums(grad_two_low)
    outer_grad = left_transposed(activated, grad_two_low).astype(bf16)
    grad_hidden = (right_transposed(grad_two_low, full_outer) * slope).astype(bf16)
    inner_bias_grad = column_sums(grad_hidden)
    inner_grad = left_transposed(first_low, grad_hidden).astype(bf16)
    grad_first = grad_two + right_transposed(grad_hidden, full_inner)
    grad_one, gain_one_grad, shift_one_grad = norm_back(
        grad_first, normal_one, inverse_one, gain_one
    )
    grad_one_low = grad_one.astype(bf16)
    out_bias_grad = column_sums(grad_one_low)

    back_pieces = [right_transposed(grad_one_low, out_pieces[r]).astype(bf16) for r in range(shards)]
    back_pieces = [back_pieces[0]] + [swapped(back_pieces[r], "wt", r) for r in range(1, shards)]
    grad_mixed = placed(back_pieces).reshape(block, part)

    selector = (
        jnp.arange(part)[:, None] // HEAD_DIM == jnp.arange(3)[None, :]
    ).astype(f32)
    delta = jnp.einsum(
        "ij,jh->hi",
        grad_mixed.astype(f32) * mixed_wide,
        selector,
        precision=lax.Precision.HIGHEST,
    )
    stat_rows = jnp.concatenate([stat_columns[:, :3].T, delta], axis=0)
    parts, rest = [], stat_rows
    for _ in range(3):
        piece = lax.reduce_precision(rest, 8, 7)
        parts.append(piece.astype(bf16))
        rest = rest - piece
    packed = jnp.concatenate(parts, axis=0).reshape(-1, part)
    grad_halo = halo(jnp.concatenate([grad_mixed, packed], axis=0))
    grad_blocks = [x[:block] for x in grad_halo]
    stat_parts = jnp.concatenate(
        [x[block:].reshape(3, -1, block) for x in grad_halo], axis=2
    ).astype(f32)
    stat_window = stat_parts[0] + stat_parts[1] + stat_parts[2]
    stat_window = jnp.concatenate([stat_window, jnp.zeros((2, window), f32)], axis=0)

    def shard_sum(grad):
        kept, sent = halves(grad.reshape((2, 2) + grad.shape[1:]), w % 2, 1)
        grad = both(kept, swapped(sent, "wt", 1))
        kept, sent = halves(grad, w // 2, 0)
        return both(kept, swapped(sent, "wt", 2))[0, 0]

    near_first = [1 << i for i in range(cycle.bit_length() - 1)]
    far_first = [2, 1] + near_first[2:]
    outer_shard = shard_sum(outer_grad.reshape(shards, -1, width))
    outer_total = gather_back(scatter_sum(outer_shard, "ctx", near_first, 0), "ctx", near_first, 0)
    inner_shard = shard_sum(inner_grad.reshape(shards, part, hidden_size))
    inner_total = gather_back(scatter_sum(inner_shard, "ctx", far_first, 0), "ctx", far_first, 0)

    grad_query = attention_queries(
        bounds, queries, spans_column, grad_mixed, mixed_wide, stat_columns, pairs
    )
    grad_pair = attention_keys(bounds, pair, spans_row, stat_window, query_halo, grad_blocks)

    grad_one_block = placed(spread(grad_one_low)).reshape(block, width)
    out_grad = left_transposed(mixed, grad_one_block).astype(bf16)
    query_grad = left_transposed(block_tokens, grad_query).astype(bf16)
    pair_grad = left_transposed(block_tokens, grad_pair).astype(bf16)
    early = jnp.concatenate([query_grad.reshape(shards, part, part)], axis=2)
    late = pair_grad.reshape(shards, part, 2 * part)

    def head_sum(grad, order):
        grad = scatter_sum(grad, "ctx", order, 1)
        pieces = [
            lax.dynamic_index_in_dim(grad, others[r], 0, keepdims=False) for r in range(shards)
        ]
        pieces = [pieces[0]] + [swapped(pieces[r], "wt", r) for r in range(1, shards)]
        return gather_back(placed(pieces), "ctx", order, 1)

    out_total = gather_back(scatter_sum(out_grad, "ctx", far_first, 0), "ctx", far_first, 0)
    query_total = head_sum(early, near_first)
    pair_total = head_sum(late, near_first)

    def columns_joined(grad):
        return jnp.transpose(grad, (1, 0, 2)).reshape(part, width).astype(f32)

    token_partial = (
        right_transposed(grad_query, projection[:, :part])
        + right_transposed(grad_pair, projection[:, part:])
    ).astype(bf16)
    token_sum = shard_sum(token_partial.reshape(shards, rows, width))
    tokens_gradient = grad_one + token_sum.astype(f32)

    query_bias_grad = column_sums(grad_query)
    value_bias_grad = column_sums(grad_pair[:, part:])
    own_bias = jnp.stack([query_bias_grad, value_bias_grad])
    small_grads = jnp.concatenate(
        [
            jnp.stack(
                [
                    x.reshape(shards, part)
                    for x in (
                        out_bias_grad,
                        gain_one_grad,
                        shift_one_grad,
                        outer_bias_grad,
                        gain_two_grad,
                        shift_two_grad,
                    )
                ],
                axis=1,
            ),
            inner_bias_grad.reshape(shards, -1, part),
            jnp.where((jnp.arange(shards) == w)[:, None, None], own_bias[None], 0.0),
        ],
        axis=1,
    )
    small_sums = lax.psum(small_grads, ("ctx", "wt"))
    mine = lax.dynamic_index_in_dim(small_sums, w, 0, keepdims=False)

    return (
        layer_out,
        tokens_gradient,
        columns_joined(query_total),
        columns_joined(pair_total[:, :, :part]),
        columns_joined(pair_total[:, :, part:]),
        out_total.astype(f32),
        mine[-2],
        mine[-1],
        mine[0],
        mine[1],
        mine[2],
        inner_total.astype(f32),
        mine[6:-2].reshape(-1),
        outer_total.astype(f32),
        mine[3],
        mine[4],
        mine[5],
    )


def solution(mesh):
    matrix, vector = P("wt", None), P("wt")
    stream = P(("ctx", "wt"), None)
    in_specs = (stream, P(), stream) + (matrix,) * 4 + (vector,) * 5
    in_specs += (matrix, vector, matrix, vector, vector, vector)
    out_specs = (stream, stream) + (matrix,) * 4 + (vector,) * 5
    out_specs += (matrix, vector, matrix, vector, vector, vector)
    return jax.shard_map(
        on_device, mesh=mesh, in_specs=in_specs, out_specs=out_specs, check_vma=False
    )
```

time: 1490 us -> 630 us (0.42)
  waiting for transfers between devices: 764 us -> 148 us
  blocking collectives: 331 us -> 82.9 us
  matrix products: 192 us -> 37.8 us
  starting transfers between devices: 19.2 us -> 139 us
  Pallas kernels: 0 us -> 58.3 us
  other arithmetic: 73.7 us -> 49.3 us
  local copies, waits for them, and re-layouts: 79 us -> 100 us
  between operations: 18.2 us -> 3.02 us
    ppermute x10 -> x71, waiting for transfers between devices: 545 us -> 148 us  [the longest x59 137 us: swapped(): return lax.ppermute(block, axis, [(i, i ^ bit) for i in range(count)])]
    psum x1, blocking collectives: 301 us -> 45.1 us  [on_device(): small_sums = lax.psum(small_grads, ('ctx', 'wt'))]
    dot_general x48 -> x21, matrix products: 192 us -> 37.8 us  [the longest x8 15 us: right_transposed(): return jnp.einsum('te,de->td', left, right, preferred_element_type=f32)]
    reduce_scatter x4 -> x0, waiting for transfers between devices: 130 us -> none  [the longest x1 50.6 us: on_device(): lax.psum_scatter(grad_full_inner.astype(jnp.bfloat16), 'wt', scatter_dime...]
    ppermute x10 -> x71, starting transfers between devices: 18.2 us -> 139 us  [the longest x59 111 us: swapped(): return lax.ppermute(block, axis, [(i, i ^ bit) for i in range(count)])]
    pallas_call x0 -> x3, Pallas kernels: none -> 58.3 us  [the longest x1 20.6 us: attention_forward(): pl.pallas_call(forward_kernel, grid_spec=pltpu.PrefetchScalarGridSpec(num...]
    all_gather x7 -> x0, waiting for transfers between devices: 46 us -> none  [the longest x1 28.6 us: on_device(): start_pair = lax.all_gather(own_shard, 'wt', axis=1, tiled=True)]
    unnamed x17 -> x0, waiting for transfers between devices: 43.2 us -> none
  transfers between devices with their start and end apart: 24 -> 71, of which waited for: 20 -> 26; matrix products, arithmetic and copies ran while one was open for 18% -> 27% of each run, Pallas kernels for 0% -> 9%
where the time goes in v1:
time: 630 us; the launch traced here: 619 us
  waiting for transfers between devices  148 us (23%)
  starting transfers between devices  139 us (22%)
  local copies, waits for them, and re-layouts  100 us (16%)
  blocking collectives  82.9 us (13%)
  Pallas kernels  58.3 us (9%)
  other arithmetic  49.3 us (8%)
  matrix products  37.8 us (6%)
    ppermute x59, waiting for transfers between devices, swapped(): return lax.ppermute(block, axis, [(i, i ^ bit) for i in range(count)])  137 us
    ppermute x59, starting transfers between devices, swapped(): return lax.ppermute(block, axis, [(i, i ^ bit) for i in range(count)])  111 us
    psum x1, blocking collectives, on_device(): small_sums = lax.psum(small_grads, ('ctx', 'wt'))  45.1 us
    all_gather x1, blocking collectives, on_device(): small = lax.all_gather(small_own, 'wt', axis=0)  37.8 us
    ppermute x12, starting transfers between devices, shifted(): return lax.ppermute(block, axis, route)  28.2 us
    unnamed x144, local copies, waits for them, and re-layouts  26 us
    dynamic_update_slice x33, local copies, waits for them, and re-layouts, placed(): buffer = lax.dynamic_update_slice_in_dim(buffer, piece[None], others[r], 0)  25.7 us
    pallas_call x1, Pallas kernels, attention_forward(): pl.pallas_call(forward_kernel, grid_spec=pltpu.PrefetchScalarGridSpec(num...  20.6 us
  transfers between devices with their start and end apart: 71, of which 26 were waited for; matrix products, arithmetic and copies ran while one was open for 27% of the time, Pallas kernels for 9%

profile of v1, /device:TPU:0, one launch (start us, length us, event | category | flops | bytes accessed | tf_op | source)
XLA Modules:
  0.0 618.7 jit_solution(15773296176342783880)
XLA Ops:
  12.1 37.8 %all_gather.3 = bf16[4,10,192]{2,1,0:T(8,128)(2,1)S(1)} all-gather(bf16[1,10,192]{2,1,0:T(8,128)(2,1)S(1)} %all_gather_reshape.3), channel_id=1, replica_groups=mesh['ctx'=8,'wt'=4] {'wt'}, dimensions={0}, use_global_device_ids=true | all-gather | bytes 19200 | tf_op jit(solution)/shard_map/all_gather | solution.py:474
  86.0 13.5 %collective-permute-done.10 = bf16[960,768]{1,0:T(8,128)(2,1)} collective-permute-done((bf16[960,768]{1,0:T(8,128)(2,1)}, bf16[960,768]{1,0:T(8,128)(2,1)}, u32[]{:S(2)}, u32[]{:S(2)}) %collective-permute-start.10) | collective-permute-done | bytes 1474592 | tf_op jit(solution)/shard_map/ppermute | solution.py:23
  117.2 5.8 collective-permute-start.23
  126.2 20.6 %attention_forward.1 = (bf16[1024,192]{1,0:T(8,128)(2,1)S(1)}, f32[1024,192]{1,0:T(8,128)S(1)}, f32[1024,128]{1,0:T(8,128)S(1)}) custom-call(s32[16]{0:T(128)S(1)} %reshape.293.bounds, bf16[1024,192]{1,0:T(8,128)(2,1)} %multiply_convert_fusion.1.q_ref.rest_2_, s32[1024,8]{1,0:T(8,128)S(1)} %copy.154.span_ref, bf16[1024,384]{1,0:T(8,128)(2,1)S(1)} %copy-done.8, ...), custom_call_target="tpu_custom_call" | custom-call | flops 1811939328 | bytes 6291456 | tf_op jit(solution)/shard_map/attention_forward/pallas_call | solution.py:161
  177.7 4.1 multiply_reduce_fusion
  186.0 3.8 convolution_convert_fusion.1
  213.2 19.3 %attention_queries.1 = bf16[1024,192]{1,0:T(8,128)(2,1)S(1)} custom-call(s32[16]{0:T(128)S(1)} %reshape.293.bounds, bf16[1024,192]{1,0:T(8,128)(2,1)} %multiply_convert_fusion.1.q_ref.rest_2_, s32[1024,8]{1,0:T(8,128)S(1)} %copy.154.span_ref, bf16[1024,192]{1,0:T(8,128)(2,1)S(1)} %bitcast.153, f32[1024,192]{1,0:T(8,128)S(1)} %get-tuple-element.21.wide_ref, ...), custom_call_target="tpu_custom_call" | custom-call | flops 2717908992 | bytes 6291456 | tf_op jit(solution)/shard_map/attention_queries/pallas_call | solution.py:254
  235.7 6.4 %collective-permute-done.29 = bf16[4,96,192]{2,1,0:T(8,128)(2,1)S(1)} collective-permute-done((bf16[4,96,192]{2,1,0:T(8,128)(2,1)S(1)}, bf16[4,96,192]{2,1,0:T(8,128)(2,1)S(1)}, u32[]{:S(2)}, u32[]{:S(2)}) %collective-permute-start.29) | collective-permute-done | bytes 147488 | tf_op jit(solution)/shard_map/ppermute | solution.py:23
  242.2 23.7 %collective-permute-start.30 = (bf16[4,48,192]{2,1,0:T(8,128)(2,1)S(1)}, bf16[4,48,192]{2,1,0:T(8,128)(2,1)S(1)}, u32[]{:S(2)}, u32[]{:S(2)}) collective-permute-start(bf16[4,48,192]{2,1,0:T(8,128)(2,1)S(1)} %constant_dynamic-slice_fusion.32), channel_id=1, source_target_pairs={{0,8},{4,12},{8,0},{12,4},{16,24},{20,28},{24,16},{28,20},{1,9},{5... | collective-permute-start | bytes 221192 | tf_op jit(solution)/shard_map/ppermute | solution.py:23
  268.8 13.8 %collective-permute-start.31 = (bf16[4,24,192]{2,1,0:T(8,128)(2,1)S(1)}, bf16[4,24,192]{2,1,0:T(8,128)(2,1)S(1)}, u32[]{:S(2)}, u32[]{:S(2)}) collective-permute-start(bf16[4,24,192]{2,1,0:T(8,128)(2,1)S(1)} %constant_dynamic-slice_fusion.31), channel_id=1, source_target_pairs={{0,16},{4,20},{8,24},{12,28},{16,0},{20,4},{24,8},{28,12},{1,17},{... | collective-permute-start | bytes 110600 | tf_op jit(solution)/shard_map/ppermute | solution.py:23
  302.9 13.3 %collective-permute-start.36 = (bf16[4,48,192]{2,1,0:T(8,128)(2,1)S(1)}, bf16[4,48,192]{2,1,0:T(8,128)(2,1)S(1)}, u32[]{:S(2)}, u32[]{:S(2)}) collective-permute-start(bf16[4,48,192]{2,1,0:T(8,128)(2,1)S(1)} %copy.183), channel_id=1, source_target_pairs={{0,8},{4,12},{8,0},{12,4},{16,24},{20,28},{24,16},{28,20},{1,9},{5... | collective-permute-start | bytes 221192 | tf_op jit(solution)/shard_map/ppermute | solution.py:23
  318.2 9.5 %collective-permute-done.36 = bf16[4,48,192]{2,1,0:T(8,128)(2,1)S(1)} collective-permute-done((bf16[4,48,192]{2,1,0:T(8,128)(2,1)S(1)}, bf16[4,48,192]{2,1,0:T(8,128)(2,1)S(1)}, u32[]{:S(2)}, u32[]{:S(2)}) %collective-permute-start.36) | collective-permute-done | bytes 73760 | tf_op jit(solution)/shard_map/ppermute | solution.py:23
  337.0 5.3 collective-permute-done.22
  356.7 6.2 %collective-permute-done.26.rest_4_ = bf16[1024,192]{1,0:T(8,128)(2,1)} collective-permute-done((bf16[1024,192]{1,0:T(8,128)(2,1)}, bf16[1024,192]{1,0:T(8,128)(2,1)}, u32[]{:S(2)}, u32[]{:S(2)}) %collective-permute-start.26) | collective-permute-done | bytes 393248 | tf_op jit(solution)/shard_map/ppermute | solution.py:29
  364.9 18.4 %attention_keys.1 = bf16[1024,384]{1,0:T(8,128)(2,1)S(1)} custom-call(s32[16]{0:T(128)S(1)} %reshape.293.bounds, bf16[1024,384]{1,0:T(8,128)(2,1)S(1)} %pad_maximum_fusion.3.rest_2_.kv_ref, s32[8,5120]{1,0:T(8,128)S(1)} %copy-done.6, f32[8,5120]{1,0:T(8,128)S(1)} %concatenate.145.stat_ref, bf16[1024,192]{1,0:T(8,128)(2,1)} %collective-permute-done.23.rest_0_, ...), custom_call_target="tpu_custom_call" | custom-call | flops 3623878656 | bytes 8388608 | tf_op jit(solution)/shard_map/attention_keys/pallas_call | solution.py:340
  386.7 6.5 %collective-permute-done.38 = bf16[4,96,384]{2,1,0:T(8,128)(2,1)S(1)} collective-permute-done((bf16[4,96,384]{2,1,0:T(8,128)(2,1)S(1)}, bf16[4,96,384]{2,1,0:T(8,128)(2,1)S(1)}, u32[]{:S(2)}, u32[]{:S(2)}) %collective-permute-start.38) | collective-permute-done | bytes 294944 | tf_op jit(solution)/shard_map/ppermute | solution.py:23
  393.4 10.0 %collective-permute-start.39 = (bf16[4,48,384]{2,1,0:T(8,128)(2,1)S(1)}, bf16[4,48,384]{2,1,0:T(8,128)(2,1)S(1)}, u32[]{:S(2)}, u32[]{:S(2)}) collective-permute-start(bf16[4,48,384]{2,1,0:T(8,128)(2,1)S(1)} %constant_dynamic-slice_fusion.25), channel_id=1, source_target_pairs={{0,8},{4,12},{8,0},{12,4},{16,24},{20,28},{24,16},{28,20},{1,9},{5... | collective-permute-start | bytes 442376 | tf_op jit(solution)/shard_map/ppermute | solution.py:23
  403.6 45.1 %psum.7 = f32[4,12,192]{2,1,0:T(8,128)S(1)} all-reduce(f32[4,12,192]{2,1,0:T(8,128)S(1)} %concatenate.164), channel_id=1, replica_groups=mesh['ctx'=8,'wt'=4] {'ctx','wt'}, use_global_device_ids=true, to_apply=%region_19.20 | all-reduce | flops 9216 | bytes 73728 | tf_op jit(solution)/shard_map/psum | solution.py:664
  509.1 17.6 %collective-permute-done.56 = bf16[1,1,192,3072]{3,2,1,0:T(8,128)(2,1)S(1)} collective-permute-done((bf16[1,1,192,3072]{3,2,1,0:T(8,128)(2,1)S(1)}, bf16[1,1,192,3072]{3,2,1,0:T(8,128)(2,1)S(1)}, u32[]{:S(2)}, u32[]{:S(2)}) %collective-permute-start.56) | collective-permute-done | bytes 1179680 | tf_op jit(solution)/shard_map/ppermute | solution.py:23
  530.1 24.7 %collective-permute-done.64 = bf16[1,1,768,768]{3,2,1,0:T(8,128)(2,1)S(1)} collective-permute-done((bf16[1,1,768,768]{3,2,1,0:T(8,128)(2,1)S(1)}, bf16[1,1,768,768]{3,2,1,0:T(8,128)(2,1)S(1)}, u32[]{:S(2)}, u32[]{:S(2)}) %collective-permute-start.64) | collective-permute-done | bytes 1179680 | tf_op jit(solution)/shard_map/ppermute | solution.py:23
  557.6 10.7 %collective-permute-done.65 = bf16[384,768]{1,0:T(8,128)(2,1)S(1)} collective-permute-done((bf16[384,768]{1,0:T(8,128)(2,1)S(1)}, bf16[384,768]{1,0:T(8,128)(2,1)S(1)}, u32[]{:S(2)}, u32[]{:S(2)}) %collective-permute-start.65) | collective-permute-done | bytes 589856 | tf_op jit(solution)/shard_map/ppermute | solution.py:23
  573.2 5.1 collective-permute-done.66
  578.4 6.6 %collective-permute-done.59 = bf16[24,3072]{1,0:T(8,128)(2,1)S(1)} collective-permute-done((bf16[24,3072]{1,0:T(8,128)(2,1)S(1)}, bf16[24,3072]{1,0:T(8,128)(2,1)S(1)}, u32[]{:S(2)}, u32[]{:S(2)}) %collective-permute-start.59) | collective-permute-done | bytes 147488 | tf_op jit(solution)/shard_map/ppermute | solution.py:23
  588.3 3.8 collective-permute-done.60
  (532 shorter events, 284.4 us)
Async XLA Ops:
  0.7 70.0 %collective-permute-start.14 = (bf16[192,3072]{1,0:T(8,128)(2,1)}, bf16[192,3072]{1,0:T(8,128)(2,1)S(1)}, u32[]{:S(2)}, u32[]{:S(2)}) collective-permute-start(bf16[192,3072]{1,0:T(8,128)(2,1)} %param.30), channel_id=1, source_target_pairs={{0,2},{1,3},{2,0},{3,1},{4,6},{5,7},{6,4},{7,5},{8,10},{9,11},{10,... | collective-permute-start | bytes 3538952 | tf_op jit(solution)/shard_map/ppermute | solution.py:23
  3.8 63.7 %collective-permute-start = (bf16[256,768]{1,0:T(8,128)(2,1)}, bf16[256,768]{1,0:T(8,128)(2,1)}, u32[]{:S(2)}, u32[]{:S(2)}) collective-permute-start(bf16[256,768]{1,0:T(8,128)(2,1)} %param.18), channel_id=1, source_target_pairs={{0,2},{1,3},{2,0},{3,1},{4,6},{5,7},{6,4},{7,5},{8,10},{9,11},{10,... | collective-permute-start | bytes 1179656 | tf_op jit(solution)/shard_map/ppermute | solution.py:23
  8.2 56.5 %collective-permute-start.2 = (bf16[192,576]{1,0:T(8,128)(2,1)}, bf16[192,576]{1,0:T(8,128)(2,1)}, u32[]{:S(2)}, u32[]{:S(2)}) collective-permute-start(bf16[192,576]{1,0:T(8,128)(2,1)} %pad_maximum_fusion.9), channel_id=1, source_target_pairs={{0,1},{1,0},{2,3},{3,2},{4,5},{5,4},{6,7},{7,6},{8,9},{9,8},{10,11... | collective-permute-start | bytes 663560 | tf_op jit(solution)/shard_map/ppermute | solution.py:23
  9.0 59.7 %collective-permute-start.3 = (bf16[192,576]{1,0:T(8,128)(2,1)}, bf16[192,576]{1,0:T(8,128)(2,1)}, u32[]{:S(2)}, u32[]{:S(2)}) collective-permute-start(bf16[192,576]{1,0:T(8,128)(2,1)} %pad_maximum_fusion.10), channel_id=1, source_target_pairs={{0,2},{1,3},{2,0},{3,1},{4,6},{5,7},{6,4},{7,5},{8,10},{9,11},{10,... | collective-permute-start | bytes 663560 | tf_op jit(solution)/shard_map/ppermute | solution.py:23
  11.8 58.0 %collective-permute-start.4 = (bf16[192,576]{1,0:T(8,128)(2,1)}, bf16[192,576]{1,0:T(8,128)(2,1)}, u32[]{:S(2)}, u32[]{:S(2)}) collective-permute-start(bf16[192,576]{1,0:T(8,128)(2,1)} %pad_maximum_fusion.11), channel_id=1, source_target_pairs={{0,3},{1,2},{2,1},{3,0},{4,7},{5,6},{6,5},{7,4},{8,11},{9,10},{10,... | collective-permute-start | bytes 663560 | tf_op jit(solution)/shard_map/ppermute | solution.py:23
  72.6 80.5 %collective-permute-start.15 = (bf16[2,192,3072]{2,1,0:T(8,128)(2,1)}, bf16[2,192,3072]{2,1,0:T(8,128)(2,1)}, u32[]{:S(2)}, u32[]{:S(2)}) collective-permute-start(bf16[2,192,3072]{2,1,0:T(8,128)(2,1)} %pad_maximum_fusion.1), channel_id=1, source_target_pairs={{0,1},{1,0},{2,3},{3,2},{4,5},{5,4},{6,7},{7,6},{8,9},{9,8},{10,11... | collective-permute-start | bytes 7077896 | tf_op jit(solution)/shard_map/ppermute | solution.py:23
  77.7 38.6 %collective-permute-start.5 = (bf16[1024,384]{1,0:T(8,128)(2,1)S(1)}, bf16[1024,384]{1,0:T(8,128)(2,1)S(1)}, u32[]{:S(2)}, u32[]{:S(2)}) collective-permute-start(bf16[1024,384]{1,0:T(8,128)(2,1)S(1)} %pad_maximum_fusion.3.rest_2_.kv_ref), channel_id=1, source_target_pairs={{0,8},{4,12},{8,16},{12,20},{16,24},{20,28},{1,9},{5,13},{9,17},{1... | collective-permute-start | bytes 2359304 | tf_op jit(solution)/shard_map/ppermute | solution.py:29
  81.3 41.7 %collective-permute-start.6 = (bf16[1024,384]{1,0:T(8,128)(2,1)S(1)}, bf16[1024,384]{1,0:T(8,128)(2,1)S(1)}, u32[]{:S(2)}, u32[]{:S(2)}) collective-permute-start(bf16[1024,384]{1,0:T(8,128)(2,1)S(1)} %pad_maximum_fusion.3.rest_2_.kv_ref), channel_id=1, source_target_pairs={{0,4},{4,8},{8,12},{12,16},{16,20},{20,24},{24,28},{1,5},{5,9},{9,... | collective-permute-start | bytes 2359304 | tf_op jit(solution)/shard_map/ppermute | solution.py:29
  84.7 39.2 %collective-permute-start.7 = (bf16[1024,384]{1,0:T(8,128)(2,1)S(1)}, bf16[1024,384]{1,0:T(8,128)(2,1)}, u32[]{:S(2)}, u32[]{:S(2)}) collective-permute-start(bf16[1024,384]{1,0:T(8,128)(2,1)S(1)} %pad_maximum_fusion.3.rest_2_.kv_ref), channel_id=1, source_target_pairs={{4,0},{8,4},{12,8},{16,12},{20,16},{24,20},{28,24},{5,1},{9,5},{13... | collective-permute-start | bytes 2359304 | tf_op jit(solution)/shard_map/ppermute | solution.py:29
  117.2 239.4 %collective-permute-start.23 = (bf16[1024,192]{1,0:T(8,128)(2,1)}, bf16[1024,192]{1,0:T(8,128)(2,1)}, u32[]{:S(2)}, u32[]{:S(2)}) collective-permute-start(bf16[1024,192]{1,0:T(8,128)(2,1)} %multiply_convert_fusion.1.q_ref.rest_2_), channel_id=1, source_target_pairs={{0,8},{4,12},{8,16},{12,20},{16,24},{20,28},{1,9},{5,13},{9,17},{1... | collective-permute-start | bytes 1179656 | tf_op jit(solution)/shard_map/ppermute | solution.py:29
  123.9 35.6 %collective-permute-start.11 = (bf16[2,960,768]{2,1,0:T(8,128)(2,1)}, bf16[2,960,768]{2,1,0:T(8,128)(2,1)}, u32[]{:S(2)}, u32[]{:S(2)}) collective-permute-start(bf16[2,960,768]{2,1,0:T(8,128)(2,1)} %pad_maximum_fusion), channel_id=1, source_target_pairs={{0,1},{1,0},{2,3},{3,2},{4,5},{5,4},{6,7},{7,6},{8,9},{9,8},{10,11... | collective-permute-start | bytes 8847368 | tf_op jit(solution)/shard_map/ppermute | solution.py:23
  184.4 118.6 %collective-permute-start.47 = (bf16[256,768]{1,0:T(8,128)(2,1)}, bf16[256,768]{1,0:T(8,128)(2,1)}, u32[]{:S(2)}, u32[]{:S(2)}) collective-permute-start(bf16[256,768]{1,0:T(8,128)(2,1)} %get-tuple-element.40), channel_id=1, source_target_pairs={{0,2},{1,3},{2,0},{3,1},{4,6},{5,7},{6,4},{7,5},{8,10},{9,11},{10,... | collective-permute-start | bytes 1179656 | tf_op jit(solution)/shard_map/ppermute | solution.py:23
  288.1 42.0 %collective-permute-start.19 = (bf16[1120,192]{0,1:T(8,128)(2,1)}, bf16[1120,192]{0,1:T(8,128)(2,1)S(1)}, u32[]{:S(2)}, u32[]{:S(2)}) collective-permute-start(bf16[1120,192]{0,1:T(8,128)(2,1)} %copy.161), channel_id=1, source_target_pairs={{0,8},{4,12},{8,16},{12,20},{16,24},{20,28},{1,9},{5,13},{9,17},{1... | collective-permute-start | bytes 1290248 | tf_op jit(solution)/shard_map/ppermute | solution.py:29
  290.1 42.3 %collective-permute-start.20 = (bf16[1120,192]{0,1:T(8,128)(2,1)}, bf16[1120,192]{0,1:T(8,128)(2,1)S(1)}, u32[]{:S(2)}, u32[]{:S(2)}) collective-permute-start(bf16[1120,192]{0,1:T(8,128)(2,1)} %copy.161), channel_id=1, source_target_pairs={{0,4},{4,8},{8,12},{12,16},{16,20},{20,24},{24,28},{1,5},{5,9},{9,... | collective-permute-start | bytes 1290248 | tf_op jit(solution)/shard_map/ppermute | solution.py:29
  342.2 129.8 %collective-permute-start.48 = (bf16[2,256,768]{2,1,0:T(8,128)(2,1)}, bf16[2,256,768]{2,1,0:T(8,128)(2,1)}, u32[]{:S(2)}, u32[]{:S(2)}) collective-permute-start(bf16[2,256,768]{2,1,0:T(8,128)(2,1)} %pad_maximum_fusion.4), channel_id=1, source_target_pairs={{0,1},{1,0},{2,3},{3,2},{4,5},{5,4},{6,7},{7,6},{8,9},{9,8},{10,11... | collective-permute-start | bytes 2359304 | tf_op jit(solution)/shard_map/ppermute | solution.py:23
  356.6 101.6 %collective-permute-start.37 = (bf16[4,96,192]{2,1,0:T(8,128)(2,1)}, bf16[4,96,192]{2,1,0:T(8,128)(2,1)}, u32[]{:S(2)}, u32[]{:S(2)}) collective-permute-start(bf16[4,96,192]{2,1,0:T(8,128)(2,1)} %copy.187), channel_id=1, source_target_pairs={{0,4},{4,0},{8,12},{12,8},{16,20},{20,16},{24,28},{28,24},{1,5},{5... | collective-permute-start | bytes 442376 | tf_op jit(solution)/shard_map/ppermute | solution.py:23
  393.4 56.2 %collective-permute-start.39 = (bf16[4,48,384]{2,1,0:T(8,128)(2,1)S(1)}, bf16[4,48,384]{2,1,0:T(8,128)(2,1)S(1)}, u32[]{:S(2)}, u32[]{:S(2)}) collective-permute-start(bf16[4,48,384]{2,1,0:T(8,128)(2,1)S(1)} %constant_dynamic-slice_fusion.25), channel_id=1, source_target_pairs={{0,8},{4,12},{8,0},{12,4},{16,24},{20,28},{24,16},{28,20},{1,9},{5... | collective-permute-start | bytes 442376 | tf_op jit(solution)/shard_map/ppermute | solution.py:23
  458.2 36.1 %collective-permute-start.55 = (bf16[2,1,192,3072]{3,2,1,0:T(8,128)(2,1)}, bf16[2,1,192,3072]{3,2,1,0:T(8,128)(2,1)}, u32[]{:S(2)}, u32[]{:S(2)}) collective-permute-start(bf16[2,1,192,3072]{3,2,1,0:T(8,128)(2,1)} %constant_dynamic-slice_fusion.15), channel_id=1, source_target_pairs={{0,1},{1,0},{2,3},{3,2},{4,5},{5,4},{6,7},{7,6},{8,9},{9,8},{10,11... | collective-permute-start | bytes 7077896 | tf_op jit(solution)/shard_map/ppermute | solution.py:23
  460.2 45.6 %collective-permute-start.63 = (bf16[2,1,768,768]{3,2,1,0:T(8,128)(2,1)}, bf16[2,1,768,768]{3,2,1,0:T(8,128)(2,1)}, u32[]{:S(2)}, u32[]{:S(2)}) collective-permute-start(bf16[2,1,768,768]{3,2,1,0:T(8,128)(2,1)} %constant_dynamic-slice_fusion.11), channel_id=1, source_target_pairs={{0,1},{1,0},{2,3},{3,2},{4,5},{5,4},{6,7},{7,6},{8,9},{9,8},{10,11... | collective-permute-start | bytes 7077896 | tf_op jit(solution)/shard_map/ppermute | solution.py:23
  460.7 38.2 %collective-permute-start.27 = (bf16[2,1,256,768]{3,2,1,0:T(8,128)(2,1)}, bf16[2,1,256,768]{3,2,1,0:T(8,128)(2,1)S(1)}, u32[]{:S(2)}, u32[]{:S(2)}) collective-permute-start(bf16[2,1,256,768]{3,2,1,0:T(8,128)(2,1)} %constant_dynamic-slice_fusion.35), channel_id=1, source_target_pairs={{0,1},{1,0},{2,3},{3,2},{4,5},{5,4},{6,7},{7,6},{8,9},{9,8},{10,11... | collective-permute-start | bytes 2359304 | tf_op jit(solution)/shard_map/ppermute | solution.py:23
  488.7 41.2 %collective-permute-start.46 = (bf16[4,96,384]{2,1,0:T(8,128)(2,1)S(1)}, bf16[4,96,384]{2,1,0:T(8,128)(2,1)S(1)}, u32[]{:S(2)}, u32[]{:S(2)}) collective-permute-start(bf16[4,96,384]{2,1,0:T(8,128)(2,1)S(1)} %copy.203), channel_id=1, source_target_pairs={{0,4},{4,0},{8,12},{12,8},{16,20},{20,16},{24,28},{28,24},{1,5},{5... | collective-permute-start | bytes 884744 | tf_op jit(solution)/shard_map/ppermute | solution.py:23
  501.3 107.1 %collective-permute-start.28 = (bf16[1,1,256,768]{3,2,1,0:T(8,128)(2,1)}, bf16[1,1,256,768]{3,2,1,0:T(8,128)(2,1)}, u32[]{:S(2)}, u32[]{:S(2)}) collective-permute-start(bf16[1,1,256,768]{3,2,1,0:T(8,128)(2,1)} %constant_dynamic-slice_fusion.34), channel_id=1, source_target_pairs={{0,2},{1,3},{2,0},{3,1},{4,6},{5,7},{6,4},{7,5},{8,10},{9,11},{10,... | collective-permute-start | bytes 1179656 | tf_op jit(solution)/shard_map/ppermute | solution.py:23
  508.2 46.7 %collective-permute-start.64 = (bf16[1,1,768,768]{3,2,1,0:T(8,128)(2,1)S(1)}, bf16[1,1,768,768]{3,2,1,0:T(8,128)(2,1)S(1)}, u32[]{:S(2)}, u32[]{:S(2)}) collective-permute-start(bf16[1,1,768,768]{3,2,1,0:T(8,128)(2,1)S(1)} %constant_dynamic-slice_fusion.10), channel_id=1, source_target_pairs={{0,2},{1,3},{2,0},{3,1},{4,6},{5,7},{6,4},{7,5},{8,10},{9,11},{10,... | collective-permute-start | bytes 3538952 | tf_op jit(solution)/shard_map/ppermute | solution.py:23
  528.6 74.3 %collective-permute-start.54 = (bf16[96,768]{1,0:T(8,128)(2,1)}, bf16[96,768]{1,0:T(8,128)(2,1)}, u32[]{:S(2)}, u32[]{:S(2)}) collective-permute-start(bf16[96,768]{1,0:T(8,128)(2,1)} %maximum_select_fusion.12), channel_id=1, source_target_pairs={{0,8},{4,12},{8,0},{12,4},{16,24},{20,28},{24,16},{28,20},{1,9},{5... | collective-permute-start | bytes 442376 | tf_op jit(solution)/shard_map/ppermute | solution.py:23
  (113 other events, 1314.2 us)

commit v2 on v1

v2 whole, which is shorter than its diff:
```python
import functools

import jax
import jax.numpy as jnp
from jax import lax
from jax.experimental import pallas as pl
from jax.experimental.pallas import tpu as pltpu
from jax.sharding import PartitionSpec as P

HEADS = 12
HEAD_DIM = 64
MAXDOC = 2048
TILE_Q = 256
SPAN_K = 768
TILE_K = 256
SPAN_Q = 768

masked_score = -1e30
epsilon = 1e-06
bf16 = jnp.bfloat16
f32 = jnp.float32


def swapped(block, axis, bit):
    count = lax.axis_size(axis)
    return lax.ppermute(block, axis, [(i, i ^ bit) for i in range(count)])


def shifted(block, axis, distance):
    count = lax.axis_size(axis)
    route = [(i, i + distance) for i in range(count) if 0 <= i + distance < count]
    return lax.ppermute(block, axis, route)


def rows_nt(left, right):
    return lax.dot_general(left, right, (((1,), (1,)), ((), ())), preferred_element_type=f32)


def rows_nn(left, right):
    return lax.dot_general(left, right, (((1,), (0,)), ((), ())), preferred_element_type=f32)


def load_window(pieces, target, sem, block):
    copies = [
        pltpu.make_async_copy(piece, target.at[pl.ds(i * block, block), :], sem.at[i])
        for i, piece in enumerate(pieces)
    ]
    for copy in copies:
        copy.start()
    return copies


def lanes_of(values, size):
    return jnp.tile(values, (1, size // 128))


def head_of(tile0, tile1, head):
    lane = lax.broadcasted_iota(jnp.int32, tile0.shape, 1)
    if head == 0:
        return jnp.where(lane < HEAD_DIM, tile0, jnp.zeros_like(tile0))
    if head == 1:
        return jnp.where(lane >= HEAD_DIM, tile0, jnp.zeros_like(tile0))
    return tile1


def forward_kernel(bounds, q_ref, span_ref, *rest):
    pieces, (out_ref, wide_ref, stat_ref, kv, top, total, accum, sem) = rest[:-8], rest[-8:]
    step = pl.program_id(0)
    block = pieces[0].shape[0]

    @pl.when(step == 0)
    def _():
        for copy in load_window(pieces, kv, sem, block):
            copy.wait()

    first = pl.multiple_of(step * TILE_Q, TILE_Q)
    here = pl.ds(first, TILE_Q)
    top[...] = jnp.full_like(top, masked_score)
    total[...] = jnp.zeros_like(total)
    accum[...] = jnp.zeros_like(accum)
    q_tile = q_ref[here, :]
    heads = [head_of(q_tile[:, :128], q_tile[:, 128:], h) for h in range(3)]
    lower, count = bounds[2 * step], bounds[2 * step + 1]

    def run(i, carry):
        begin = pl.multiple_of(lower + i * SPAN_K, 128)
        rows = pl.ds(begin, SPAN_K)
        keys = lax.broadcasted_iota(jnp.int32, (TILE_Q, SPAN_K), 1)
        allowed = (keys >= span_ref[here, 0:1] - begin) & (keys < span_ref[here, 1:2] - begin)
        scores = [rows_nt(heads[h], kv[rows, 0:128] if h < 2 else kv[rows, 128:192]) for h in range(3)]
        for h in range(3):
            score = scores[h]
            score = jnp.where(allowed, score, masked_score)
            before = top[h]
            newest = jnp.maximum(before, jnp.max(score, axis=1, keepdims=True))
            factor = jnp.exp(before - newest)
            weight = jnp.exp(score - lanes_of(newest, SPAN_K))
            part = weight[:, 0:128]
            for j in range(1, SPAN_K // 128):
                part = part + weight[:, 128 * j : 128 * j + 128]
            total[h] = total[h] * factor + part
            values = kv[rows, 128:256] if h == 0 else kv[rows, 256:384]
            accum[h] = accum[h] * factor + rows_nn(weight.astype(bf16), values)
            top[h] = newest
        return carry

    lax.fori_loop(0, count, run, 0)
    lane = lax.broadcasted_iota(jnp.int32, (TILE_Q, 128), 1)
    mixed, stats = [], jnp.zeros((TILE_Q, 128), f32)
    for h in range(3):
        mass = jnp.sum(total[h], axis=1, keepdims=True)
        mixed.append(pltpu.roll(accum[h] / mass, HEAD_DIM, 1))
        stats = jnp.where(lane == h, top[h] + jnp.log(mass), stats)
    pair = jnp.where(lane < HEAD_DIM, mixed[0], mixed[1])
    wide_ref[here, 0:128] = pair
    wide_ref[here, 128:192] = mixed[2][:, :HEAD_DIM]
    out_ref[here, 0:128] = pair.astype(bf16)
    out_ref[here, 128:192] = mixed[2][:, :HEAD_DIM].astype(bf16)
    stat_ref[here, :] = stats


def whole_spec(shape):
    return pl.BlockSpec(shape, lambda i, *_: (0,) * len(shape))


def attention_forward(bounds, queries, spans, pieces):
    block = queries.shape[0]
    window = len(pieces) * block
    return pl.pallas_call(
        forward_kernel,
        grid_spec=pltpu.PrefetchScalarGridSpec(
            num_scalar_prefetch=1,
            grid=(block // TILE_Q,),
            in_specs=[whole_spec(queries.shape), whole_spec(spans.shape)]
            + [pl.BlockSpec(memory_space=pl.ANY)] * len(pieces),
            out_specs=[
                whole_spec((block, 192)),
                whole_spec((block, 192)),
                whole_spec((block, 128)),
            ],
            scratch_shapes=[
                pltpu.VMEM((window, 384), bf16),
                pltpu.VMEM((3, TILE_Q, 128), f32),
                pltpu.VMEM((3, TILE_Q, 128), f32),
                pltpu.VMEM((3, TILE_Q, 128), f32),
                pltpu.SemaphoreType.DMA((len(pieces),)),
            ],
        ),
        out_shape=[
            jax.ShapeDtypeStruct((block, 192), bf16),
            jax.ShapeDtypeStruct((block, 192), f32),
            jax.ShapeDtypeStruct((block, 128), f32),
        ],
        compiler_params=pltpu.CompilerParams(vmem_limit_bytes=40 * 2**20),
        cost_estimate=pl.CostEstimate(
            flops=4 * block * 2304 * 192, bytes_accessed=6 * 2**20, transcendentals=block * 2304 * 3
        ),
        name="attention_forward",
    )(bounds, queries, spans, *pieces)


def query_kernel(bounds, q_ref, span_ref, grad_ref, wide_ref, stat_ref, *rest):
    pieces, (out_ref, kv, accum, sem) = rest[:-4], rest[-4:]
    step = pl.program_id(0)
    block = pieces[0].shape[0]

    @pl.when(step == 0)
    def _():
        for copy in load_window(pieces, kv, sem, block):
            copy.wait()

    first = pl.multiple_of(step * TILE_Q, TILE_Q)
    here = pl.ds(first, TILE_Q)
    accum[...] = jnp.zeros_like(accum)
    q_tile = q_ref[here, :]
    heads = [head_of(q_tile[:, :128], q_tile[:, 128:], h) for h in range(3)]
    g_tile = grad_ref[here, :]
    lane = lax.broadcasted_iota(jnp.int32, (TILE_Q, 128), 1)
    g_pair = g_tile[:, :128]
    g_last = g_tile[:, 128:256]
    none = jnp.zeros((TILE_Q, 128), bf16)
    r_pair = pltpu.roll(g_pair.astype(f32), HEAD_DIM, 1).astype(bf16)
    r_last = pltpu.roll(g_last.astype(f32), HEAD_DIM, 1).astype(bf16)
    grads = [
        jnp.where(lane >= HEAD_DIM, r_pair, none),
        jnp.where(lane < HEAD_DIM, r_pair, none),
        jnp.where(lane >= HEAD_DIM, r_last, none),
    ]
    product_pair = g_pair.astype(f32) * wide_ref[here, 0:128]
    product_last = g_tile[:, 128:192].astype(f32) * wide_ref[here, 128:192]
    deltas = [
        jnp.sum(jnp.where(lane < HEAD_DIM, product_pair, 0.0), axis=1, keepdims=True),
        jnp.sum(jnp.where(lane < HEAD_DIM, 0.0, product_pair), axis=1, keepdims=True),
        jnp.sum(product_last, axis=1, keepdims=True),
    ]
    logs = [stat_ref[here, h : h + 1] for h in range(3)]
    lower, count = bounds[2 * step], bounds[2 * step + 1]

    def run(i, carry):
        begin = pl.multiple_of(lower + i * SPAN_K, 128)
        rows = pl.ds(begin, SPAN_K)
        keys = lax.broadcasted_iota(jnp.int32, (TILE_Q, SPAN_K), 1)
        allowed = (keys >= span_ref[here, 0:1] - begin) & (keys < span_ref[here, 1:2] - begin)
        S = [rows_nt(heads[h], kv[rows, 0:128] if h < 2 else kv[rows, 128:192]) for h in range(3)]
        B = [rows_nt(grads[h], kv[rows, 128:256] if h == 0 else kv[rows, 256:384]) for h in range(3)]
        for h in range(3):
            chance = jnp.exp(jnp.where(allowed, S[h] - logs[h], masked_score))
            change = (chance * (B[h] - deltas[h])).astype(bf16)
            accum[h] += rows_nn(change, kv[rows, 0:128] if h < 2 else kv[rows, 128:256])
        return carry

    lax.fori_loop(0, count, run, 0)
    out_ref[here, 0:128] = (jnp.where(lane < HEAD_DIM, accum[0], accum[1]) * 0.125).astype(bf16)
    out_ref[here, 128:192] = (accum[2][:, :HEAD_DIM] * 0.125).astype(bf16)


def attention_queries(bounds, queries, spans, grads, wide, stats, pieces):
    block = queries.shape[0]
    window = len(pieces) * block
    return pl.pallas_call(
        query_kernel,
        grid_spec=pltpu.PrefetchScalarGridSpec(
            num_scalar_prefetch=1,
            grid=(block // TILE_Q,),
            in_specs=[whole_spec(x.shape) for x in (queries, spans, grads, wide, stats)]
            + [pl.BlockSpec(memory_space=pl.ANY)] * len(pieces),
            out_specs=whole_spec((block, 192)),
            scratch_shapes=[
                pltpu.VMEM((window, 384), bf16),
                pltpu.VMEM((3, TILE_Q, 128), f32),
                pltpu.SemaphoreType.DMA((len(pieces),)),
            ],
        ),
        out_shape=jax.ShapeDtypeStruct((block, 192), bf16),
        compiler_params=pltpu.CompilerParams(vmem_limit_bytes=40 * 2**20),
        cost_estimate=pl.CostEstimate(
            flops=6 * block * 2304 * 192, bytes_accessed=6 * 2**20, transcendentals=block * 2304 * 3
        ),
        name="attention_queries",
    )(bounds, queries, spans, grads, wide, stats, *pieces)


def key_kernel(reach, bounds, kv_ref, span_ref, *rest):
    window = 2 * reach + 1
    q_pieces, g_pieces = rest[:window], rest[window : 2 * window]
    out_ref, qs, gs, key_sum, value_sum, sem = rest[2 * window :]
    step = pl.program_id(0)
    block = q_pieces[0].shape[0]

    @pl.when(step == 0)
    def _():
        copies = load_window(q_pieces, qs, sem.at[0], block)
        copies += load_window(g_pieces, gs, sem.at[1], block)
        for copy in copies:
            copy.wait()

    first = pl.multiple_of(step * TILE_K, TILE_K)
    here = pl.ds(first, TILE_K)
    key_sum[...] = jnp.zeros_like(key_sum)
    value_sum[...] = jnp.zeros_like(value_sum)
    keys_pair = kv_ref[here, 0:128]
    keys = [head_of(keys_pair, kv_ref[here, 128:192], h) for h in range(3)]
    lane = lax.broadcasted_iota(jnp.int32, (TILE_K, 128), 1)
    zero = jnp.zeros((TILE_K, 128), f32)
    v_one = pltpu.roll(kv_ref[here, 128:256].astype(f32), HEAD_DIM, 1)
    v_two = pltpu.roll(kv_ref[here, 256:384].astype(f32), HEAD_DIM, 1)
    values = [
        jnp.where(lane < HEAD_DIM, v_one, zero).astype(bf16),
        jnp.where(lane < HEAD_DIM, zero, v_two).astype(bf16),
        v_two.astype(bf16)[:, :HEAD_DIM],
    ]
    line = lax.broadcasted_iota(jnp.int32, (16, HEAD_DIM), 0)
    slot = lax.broadcasted_iota(jnp.int32, (16, HEAD_DIM), 1)
    selector = jnp.where((slot // 3 == line) & (slot < 18), 1.0, 0.0).astype(bf16)
    lower, count = bounds[2 * step], bounds[2 * step + 1]

    def run(i, carry):
        begin = pl.multiple_of(lower + i * SPAN_Q, 128)
        columns = pl.ds(begin, SPAN_Q)
        place = reach * block + first + lax.broadcasted_iota(jnp.int32, (TILE_K, SPAN_Q), 0)
        allowed = (place >= span_ref[0:1, columns]) & (place < span_ref[1:2, columns])
        lanes = [slice(0, 128), slice(0, 128), slice(128, 192)]
        parts = gs[columns, 192:256]
        stats = rows_nt(selector, parts)
        S = [rows_nt(keys[h], qs[columns, lanes[h]]) for h in range(3)]
        B = [rows_nt(values[h], gs[columns, lanes[h]]) for h in range(3)]
        for h in range(3):
            score = S[h] - stats[h : h + 1, :]
            chance = jnp.exp(jnp.where(allowed, score, masked_score))
            change = (chance * (B[h] - stats[h + 3 : h + 4, :])).astype(bf16)
            size = 128 if h < 2 else HEAD_DIM
            key_sum[h, :, 0:size] += rows_nn(change, qs[columns, lanes[h]])
            value_sum[h, :, 0:size] += rows_nn(chance.astype(bf16), gs[columns, lanes[h]])
        return carry

    lax.fori_loop(0, count, run, 0)
    k_pair = jnp.where(lane < HEAD_DIM, key_sum[0], key_sum[1])
    v_pair = jnp.where(lane < HEAD_DIM, value_sum[0], value_sum[1])
    v_turn = pltpu.roll(v_pair, HEAD_DIM, 1)
    last_turn = pltpu.roll(value_sum[2], HEAD_DIM, 1)
    out_ref[here, 0:128] = k_pair.astype(bf16)
    out_ref[here, 128:256] = jnp.where(lane < HEAD_DIM, key_sum[2], v_turn).astype(bf16)
    out_ref[here, 256:384] = jnp.where(lane < HEAD_DIM, v_turn, last_turn).astype(bf16)


def attention_keys(bounds, pair, spans, q_pieces, g_pieces):
    block = pair.shape[0]
    count = len(q_pieces)
    return pl.pallas_call(
        functools.partial(key_kernel, count // 2),
        grid_spec=pltpu.PrefetchScalarGridSpec(
            num_scalar_prefetch=1,
            grid=(block // TILE_K,),
            in_specs=[whole_spec(x.shape) for x in (pair, spans)]
            + [pl.BlockSpec(memory_space=pl.ANY)] * (2 * count),
            out_specs=whole_spec((block, 384)),
            scratch_shapes=[
                pltpu.VMEM((count * block, 192), bf16),
                pltpu.VMEM((count * block, 256), bf16),
                pltpu.VMEM((3, TILE_K, 128), f32),
                pltpu.VMEM((3, TILE_K, 128), f32),
                pltpu.SemaphoreType.DMA((2, count)),
            ],
        ),
        out_shape=jax.ShapeDtypeStruct((block, 384), bf16),
        compiler_params=pltpu.CompilerParams(vmem_limit_bytes=40 * 2**20),
        cost_estimate=pl.CostEstimate(
            flops=8 * block * 2304 * 192, bytes_accessed=8 * 2**20, transcendentals=block * 2304 * 3
        ),
        name="attention_keys",
    )(bounds, pair, spans, *q_pieces, *g_pieces)


def projection_kernel(place_ref, own, near, far, corner, w_own, w_near, w_far, w_corner, bias_ref, *rest):
    tokens_ref, query_ref, pair_ref, weight, sem = rest
    rows, part = own.shape[0], w_own.shape[0]
    pieces = (w_own, w_near, w_far, w_corner)
    copies = []
    for r, piece in enumerate(pieces):
        where = pl.multiple_of(place_ref[r] * part, part)
        copies.append(pltpu.make_async_copy(piece, weight.at[pl.ds(where, part), :], sem.at[r]))
        copies[-1].start()
    for copy in copies:
        copy.wait()
    for r, piece in enumerate((own, near, far, corner)):
        here = pl.ds(pl.multiple_of(place_ref[r] * rows, rows), rows)
        tile = piece[...]
        tokens_ref[here, :] = tile
        made = rows_nn(tile, weight[...]) + bias_ref[0:1, :]
        pair_ref[here, :] = made[:, : 2 * part].astype(bf16)
        query_ref[here, :] = (made[:, 2 * part :].astype(bf16).astype(f32) * 0.125).astype(bf16)


def project(places, token_pieces, weight_pieces, bias):
    rows, width = token_pieces[0].shape
    part = weight_pieces[0].shape[0]
    block = rows * len(token_pieces)
    vmem = pl.BlockSpec(memory_space=pltpu.VMEM)
    return pl.pallas_call(
        projection_kernel,
        in_specs=[pl.BlockSpec(memory_space=pltpu.SMEM)]
        + [vmem] * 4
        + [pl.BlockSpec(memory_space=pl.ANY)] * 4
        + [vmem],
        out_specs=[vmem] * 3,
        out_shape=[
            jax.ShapeDtypeStruct((block, width), bf16),
            jax.ShapeDtypeStruct((block, part), bf16),
            jax.ShapeDtypeStruct((block, 2 * part), bf16),
        ],
        scratch_shapes=[pltpu.VMEM((width, 3 * part), bf16), pltpu.SemaphoreType.DMA((4,))],
        compiler_params=pltpu.CompilerParams(vmem_limit_bytes=32 * 2**20),
        cost_estimate=pl.CostEstimate(
            flops=2 * block * width * 3 * part, bytes_accessed=5 * 2**20, transcendentals=0
        ),
        name="layer_projection",
    )(places, *token_pieces, *weight_pieces, bias)


def normal_of(values):
    center = values - jnp.mean(values, axis=1, keepdims=True)
    inverse = lax.rsqrt(jnp.mean(center * center, axis=1, keepdims=True) + epsilon)
    return center * inverse, inverse


def normal_back(upstream, normal, inverse, gain):
    scaled = upstream * gain
    mean_scaled = jnp.mean(scaled, axis=1, keepdims=True)
    mean_product = jnp.mean(scaled * normal, axis=1, keepdims=True)
    return (scaled - mean_scaled - normal * mean_product) * inverse


def rows_tn(left, right):
    return lax.dot_general(left, right, (((0,), (0,)), ((), ())), preferred_element_type=f32)


def dense_kernel(place_ref, *refs):
    mixed = refs[0:4]
    tokens_ref, up_ref, small_ref, inner_bias_ref = refs[4:8]
    inner_pieces, outer_pieces = refs[8:12], refs[12:16]
    out_ref, grad_ref, back_ref, outer_grad, inner_grad = refs[16:21]
    w_out, w_inner, w_outer, hidden, activated, slopes, sem = refs[21:]
    rows, width = tokens_ref.shape
    groups = w_inner.shape[0]
    part = width // groups
    copies = []
    for r in range(groups):
        copies.append(
            pltpu.make_async_copy(outer_pieces[r].at[pl.ds(width, part), :], w_out.at[r], sem.at[0, r])
        )
    for r in range(groups):
        here = pl.ds(pl.multiple_of(place_ref[r] * part, part), part)
        for g in range(groups):
            copies.append(
                pltpu.make_async_copy(
                    inner_pieces[r].at[:, pl.ds(g * width, width)],
                    w_inner.at[g, here, :],
                    sem.at[1 + g, r],
                )
            )
    for r in range(groups):
        copies.append(
            pltpu.make_async_copy(
                outer_pieces[r].at[pl.ds(0, width), :], w_outer.at[place_ref[r]], sem.at[1 + groups, r]
            )
        )
    for copy in copies:
        copy.start()

    out_bias, gain_one, shift_one = small_ref[0:1], small_ref[1:2], small_ref[2:3]
    outer_bias, gain_two, shift_two = small_ref[3:4], small_ref[4:5], small_ref[5:6]

    for copy in copies[:groups]:
        copy.wait()
    residual = tokens_ref[...].astype(f32) + out_bias
    for r in range(groups):
        residual = residual + rows_nn(mixed[r][...], w_out[r])
    normal_one, inverse_one = normal_of(residual)
    first = normal_one * gain_one + shift_one
    first_low = first.astype(bf16)
    for copy in copies[groups:]:
        copy.wait()

    def ahead(g, total):
        value = rows_nn(first_low, w_inner[g]) + inner_bias_ref[pl.ds(g, 1), :]
        chance = 0.5 * (1.0 + lax.erf(value * (2.0**-0.5)))
        density = jnp.exp(-0.5 * value * value) * (2.0 * jnp.pi) ** -0.5
        slopes[g] = chance + value * density
        low = (value * chance).astype(bf16)
        activated[g] = low
        return total + rows_nn(low, w_outer[g])

    residual = lax.fori_loop(0, groups, ahead, first + outer_bias)
    normal_two, inverse_two = normal_of(residual)
    out_ref[...] = (normal_two * gain_two + shift_two).astype(bf16)
    upstream = up_ref[...].astype(f32)
    grad_two = normal_back(upstream, normal_two, inverse_two, gain_two)
    grad_two_low = grad_two.astype(bf16)
    shift_two_sum = jnp.sum(upstream, axis=0, keepdims=True)
    gain_two_sum = jnp.sum(upstream * normal_two, axis=0, keepdims=True)
    outer_bias_sum = jnp.sum(grad_two_low.astype(f32), axis=0, keepdims=True)

    def behind(g, total):
        outer_grad[g] = rows_tn(activated[g], grad_two_low).astype(bf16)
        value = (rows_nt(grad_two_low, w_outer[g]) * slopes[g]).astype(bf16)
        hidden[g] = value
        return total + rows_nt(value, w_inner[g])

    grad_first = lax.fori_loop(0, groups, behind, grad_two)
    grad_one = normal_back(grad_first, normal_one, inverse_one, gain_one)
    grad_ref[...] = grad_one
    grad_one_low = grad_one.astype(bf16)
    for r in range(groups):
        back_ref[r] = rows_nt(grad_one_low, w_out[r]).astype(bf16)

    for g in range(groups):
        made = rows_tn(first_low, hidden[g]).astype(bf16)
        for k in range(groups):
            inner_grad[k, g * part : (g + 1) * part, :] = made[k * part : (k + 1) * part, :]
    for r in range(groups):
        made = rows_tn(mixed[r][...], grad_one_low).astype(bf16)
        inner_grad[place_ref[r], width : width + part, :] = made

    sums = [
        jnp.sum(grad_one_low.astype(f32), axis=0, keepdims=True),
        jnp.sum(grad_first * normal_one, axis=0, keepdims=True),
        jnp.sum(grad_first, axis=0, keepdims=True),
        outer_bias_sum,
        gain_two_sum,
        shift_two_sum,
    ]
    line = lax.broadcasted_iota(jnp.int32, (16, part), 0)
    inner_grad[:, width + part : width + part + 64, :] = jnp.zeros((groups, 64, width), bf16)
    for k in range(groups):
        tail = jnp.zeros((16, part), f32)
        for i, line_sum in enumerate(sums):
            tail = jnp.where(line == i, line_sum[:, k * part : (k + 1) * part], tail)
        bias_sum = jnp.sum(hidden[k].astype(f32), axis=0, keepdims=True)
        for i in range(groups):
            tail = jnp.where(
                line == len(sums) + i, bias_sum[:, i * part : (i + 1) * part], tail
            )
        inner_grad[k, width + part : width + part + 16, 0:part] = tail.astype(bf16)


def dense(places, mixed_pieces, tokens, cotangent, small, inner_bias, inner_pieces, outer_pieces):
    rows, width = tokens.shape
    groups = len(inner_pieces)
    part = width // groups
    vmem = pl.BlockSpec(memory_space=pltpu.VMEM)
    hbm = pl.BlockSpec(memory_space=pl.ANY)
    return pl.pallas_call(
        dense_kernel,
        in_specs=[pl.BlockSpec(memory_space=pltpu.SMEM)] + [vmem] * (groups + 4) + [hbm] * (2 * groups),
        out_specs=[vmem] * 5,
        out_shape=[
            jax.ShapeDtypeStruct((rows, width), bf16),
            jax.ShapeDtypeStruct((rows, width), f32),
            jax.ShapeDtypeStruct((groups, rows, part), bf16),
            jax.ShapeDtypeStruct((groups, width, width), bf16),
            jax.ShapeDtypeStruct((groups, width + part + 64, width), bf16),
        ],
        scratch_shapes=[
            pltpu.VMEM((groups, part, width), bf16),
            pltpu.VMEM((groups, width, width), bf16),
            pltpu.VMEM((groups, width, width), bf16),
            pltpu.VMEM((groups, rows, width), bf16),
            pltpu.VMEM((groups, rows, width), bf16),
            pltpu.VMEM((groups, rows, width), f32),
            pltpu.SemaphoreType.DMA((groups + 2, groups)),
        ],
        compiler_params=pltpu.CompilerParams(vmem_limit_bytes=56 * 2**20),
        cost_estimate=pl.CostEstimate(
            flops=36 * rows * width * width * groups // 3 * 2,
            bytes_accessed=24 * 2**20,
            transcendentals=2 * rows * width * groups,
        ),
        name="layer_dense",
    )(places, *mixed_pieces, tokens, cotangent, small, inner_bias, *inner_pieces, *outer_pieces)

def gather_kernel(place_ref, p0, p1, p2, p3, wide_ref, stat_ref, out_ref):
    rows, part = p0.shape
    lane = lax.broadcasted_iota(jnp.int32, (rows, 128), 1)
    slot = lax.broadcasted_iota(jnp.int32, (rows, HEAD_DIM), 1)
    for r, piece in enumerate((p0, p1, p2, p3)):
        here = pl.ds(pl.multiple_of(place_ref[r] * rows, rows), rows)
        tile = piece[...]
        product = tile.astype(f32) * wide_ref[here, :]
        pair, last = product[:, 0:128], product[:, 128:192]
        values = [stat_ref[here, h : h + 1] for h in range(3)] + [
            jnp.sum(jnp.where(lane < HEAD_DIM, pair, 0.0), axis=1, keepdims=True),
            jnp.sum(jnp.where(lane < HEAD_DIM, 0.0, pair), axis=1, keepdims=True),
            jnp.sum(last, axis=1, keepdims=True),
        ]
        tail = jnp.zeros((rows, HEAD_DIM), f32)
        for i, left in enumerate(values):
            for j in range(3):
                high = left.astype(bf16).astype(f32)
                tail = jnp.where(slot == 3 * i + j, high, tail)
                left = left - high
        out_ref[here, 0:192] = tile
        out_ref[here, 192:256] = tail.astype(bf16)


def gathered(places, pieces, wide, stats):
    block = wide.shape[0]
    vmem = pl.BlockSpec(memory_space=pltpu.VMEM)
    return pl.pallas_call(
        gather_kernel,
        in_specs=[pl.BlockSpec(memory_space=pltpu.SMEM)] + [vmem] * 6,
        out_specs=vmem,
        out_shape=jax.ShapeDtypeStruct((block, 256), bf16),
        compiler_params=pltpu.CompilerParams(vmem_limit_bytes=16 * 2**20),
        cost_estimate=pl.CostEstimate(flops=2**20, bytes_accessed=3 * 2**20, transcendentals=0),
        name="layer_gather",
    )(places, *pieces, wide, stats)


def heads_kernel(place_ref, tokens_ref, query_ref, pair_ref, w0, w1, w2, w3, grad_ref, back_ref, weight, sem):
    groups, part = grad_ref.shape[0], w0.shape[0]
    rows = back_ref.shape[1]
    copies = []
    for r, piece in enumerate((w0, w1, w2, w3)):
        where = pl.multiple_of(place_ref[r] * part, part)
        copies.append(pltpu.make_async_copy(piece, weight.at[pl.ds(where, part), :], sem.at[r]))
        copies[-1].start()
    tokens = tokens_ref[...]
    pair_grad = rows_tn(tokens, pair_ref[...]).astype(bf16)
    query_grad = rows_tn(tokens, query_ref[...]).astype(bf16)
    for k in range(groups):
        here = slice(k * part, (k + 1) * part)
        grad_ref[k, :, 0 : 2 * part] = pair_grad[here]
        grad_ref[k, :, 2 * part : 3 * part] = query_grad[here]
    ones = jnp.ones((tokens.shape[0], HEAD_DIM), bf16)
    query_sum = rows_tn(query_ref[...], ones)
    value_sum = rows_tn(pair_ref[:, part:], ones)
    lane = lax.broadcasted_iota(jnp.int32, (part, HEAD_DIM), 1)
    sums = jnp.where(lane == 0, query_sum, jnp.where(lane == 1, value_sum, 0.0))
    grad_ref[:, :, 3 * part : 3 * part + HEAD_DIM] = jnp.zeros((groups, part, HEAD_DIM), bf16)
    grad_ref[place_ref[0], :, 3 * part : 3 * part + HEAD_DIM] = sums.astype(bf16)
    for copy in copies:
        copy.wait()
    for k in range(groups):
        here = slice(k * rows, (k + 1) * rows)
        made = rows_nt(pair_ref[here, :], weight[:, : 2 * part])
        made = made + rows_nt(query_ref[here, :], weight[:, 2 * part :])
        back_ref[k] = made.astype(bf16)


def head_grads(places, tokens, grad_query, grad_pair, weight_pieces):
    block, width = tokens.shape
    groups, part = len(weight_pieces), weight_pieces[0].shape[0]
    vmem = pl.BlockSpec(memory_space=pltpu.VMEM)
    return pl.pallas_call(
        heads_kernel,
        in_specs=[pl.BlockSpec(memory_space=pltpu.SMEM)]
        + [vmem] * 3
        + [pl.BlockSpec(memory_space=pl.ANY)] * groups,
        out_specs=[vmem] * 2,
        out_shape=[
            jax.ShapeDtypeStruct((groups, part, 3 * part + HEAD_DIM), bf16),
            jax.ShapeDtypeStruct((groups, block // groups, width), bf16),
        ],
        scratch_shapes=[pltpu.VMEM((width, 3 * part), bf16), pltpu.SemaphoreType.DMA((groups,))],
        compiler_params=pltpu.CompilerParams(vmem_limit_bytes=32 * 2**20),
        cost_estimate=pl.CostEstimate(
            flops=4 * block * width * 3 * part, bytes_accessed=8 * 2**20, transcendentals=0
        ),
        name="layer_heads",
    )(places, tokens, grad_query, grad_pair, *weight_pieces)


def both(left, right):
    return (left.astype(f32) + right.astype(f32)).astype(bf16)


def halves(block, bit, axis):
    size = block.shape[axis] // 2
    kept = lax.dynamic_slice_in_dim(block, bit * size, size, axis)
    sent = lax.dynamic_slice_in_dim(block, (1 - bit) * size, size, axis)
    return kept, sent


def scatter_sum(block, axis_name, order, axis):
    index = lax.axis_index(axis_name)
    for step in order:
        kept, sent = halves(block, (index // step) % 2, axis)
        block = both(kept, swapped(sent, axis_name, step))
    return block


def gather_back(block, axis_name, order, axis):
    index = lax.axis_index(axis_name)
    for step in reversed(order):
        other = swapped(block, axis_name, step)
        late = (index // step) % 2 == 1
        block = jnp.where(
            late,
            jnp.concatenate([other, block], axis),
            jnp.concatenate([block, other], axis),
        )
    return block


def on_device(
    tokens,
    doc_start,
    cotangent,
    query_weight,
    key_weight,
    value_weight,
    out_weight,
    query_bias,
    value_bias,
    out_bias,
    first_gain,
    first_shift,
    inner_weight,
    inner_bias,
    outer_weight,
    outer_bias,
    second_gain,
    second_shift,
):
    rows, width = tokens.shape
    cycle = lax.axis_size("ctx")
    shards = lax.axis_size("wt")
    block = rows * shards
    reach = (MAXDOC + block - 2) // block
    window = (2 * reach + 1) * block
    c = lax.axis_index("ctx")
    w = lax.axis_index("wt")
    part = width // shards
    places = jnp.stack([w ^ r for r in range(shards)]).astype(jnp.int32)

    def spread(own, near):
        far = swapped(own, "wt", 2)
        return [own, near, far, swapped(far, "wt", 1)]

    def columns(r):
        start = (w ^ r) * part
        return jnp.concatenate(
            [
                lax.dynamic_slice_in_dim(x, start, part, 1)
                for x in (key_weight, value_weight, query_weight)
            ],
            axis=1,
        )

    token_pieces = spread(tokens, swapped(tokens, "wt", 1))
    weight_pieces = [columns(0)] + [swapped(columns(r), "wt", r) for r in range(1, shards)]
    head_bias = jnp.concatenate([jnp.zeros((part,), f32), value_bias.astype(f32), query_bias.astype(f32)])
    head_bias = jnp.broadcast_to(head_bias[None], (8, 3 * part))

    pad = reach * block
    padded = jnp.pad(doc_start, (pad, pad), constant_values=-1)
    base = c * block - pad
    marks = lax.dynamic_slice_in_dim(padded, c * block, window)
    place = jnp.arange(window, dtype=jnp.int32)
    begins = jnp.where((marks == base + place) | (marks < 0), place, window)
    next_begin = lax.cummin(begins, axis=0, reverse=True)
    stops = jnp.concatenate([next_begin[1:], jnp.full((1,), window, jnp.int32)])
    starts = marks - base
    spans_row = jnp.stack([starts, stops] + [jnp.zeros_like(starts)] * 6)
    spans_column = spans_row[:, pad : pad + block].T
    own_starts = starts[pad : pad + block]
    own_stops = stops[pad : pad + block]

    def bounds_of(tile, span):
        lowest = own_starts.reshape(-1, tile)[:, 0] // 128 * 128
        highest = own_stops.reshape(-1, tile)[:, -1]
        count = (highest - lowest + span - 1) // span
        lowest = jnp.minimum(lowest, (window - count * span) // 128 * 128)
        return jnp.stack([lowest, count], axis=1).reshape(-1)

    query_bounds = bounds_of(TILE_Q, SPAN_K)
    key_bounds = bounds_of(TILE_K, SPAN_Q)

    block_tokens, queries, pair = project(places, token_pieces, weight_pieces, head_bias)

    distances = [d for d in range(reach, -reach - 1, -1)]

    def halo(own):
        return [own if d == 0 else shifted(own, "ctx", d) for d in distances]

    pairs = halo(pair)

    small_own = jnp.stack(
        [out_bias, first_gain, first_shift, outer_bias, second_gain, second_shift]
    )
    small_own = jnp.concatenate([small_own, inner_bias.reshape(-1, part)], axis=0)
    small_own = jnp.pad(small_own, ((0, 16 - small_own.shape[0]), (0, width - part)))
    outer_own = jnp.concatenate([outer_weight, out_weight, small_own], axis=0)
    inner_own, outer_own, _ = lax.optimization_barrier((inner_weight, outer_own, token_pieces[2]))
    inner_pieces = spread(inner_own, swapped(inner_own, "wt", 1))
    outer_pieces = spread(outer_own, swapped(outer_own, "wt", 1))
    small = jnp.stack([x[width + part :, :part] for x in outer_pieces]).astype(f32)
    small = [lax.dynamic_index_in_dim(small, w ^ k, 0, keepdims=False) for k in range(shards)]
    small_rows = jnp.concatenate([x[:8] for x in small], axis=1)
    inner_bias_rows = jnp.stack([x[6:10].reshape(-1) for x in small])

    mixed, mixed_wide, stat_columns = attention_forward(query_bounds, queries, spans_column, pairs)
    queries_sent, _ = lax.optimization_barrier((queries, pairs))
    query_halo = [
        queries if d == 0 else shifted(queries_sent, "ctx", d) for d in distances
    ]

    mixed_rows = mixed.reshape(shards, rows, part)
    mixed_pieces = [
        lax.dynamic_index_in_dim(mixed_rows, w ^ r, 0, keepdims=False) for r in range(shards)
    ]
    mixed_pieces = [mixed_pieces[0]] + [
        swapped(mixed_pieces[r], "wt", r) for r in range(1, shards)
    ]
    mixed_pieces, query_halo = lax.optimization_barrier((mixed_pieces, query_halo))
    layer_out, grad_one, back, outer_grad, inner_grad = dense(
        places,
        mixed_pieces,
        tokens,
        cotangent,
        small_rows,
        inner_bias_rows,
        inner_pieces,
        outer_pieces,
    )

    back_pieces = [back[0]] + [swapped(back[r], "wt", r) for r in range(1, shards)]

    def near_sum(grad):
        kept, sent = halves(grad.reshape((2, 2) + grad.shape[1:]), w % 2, 1)
        return both(kept, swapped(sent, "wt", 1))

    def far_sum(grad):
        kept, sent = halves(grad, w // 2, 0)
        return both(kept, swapped(sent, "wt", 2))[0, 0]

    outer_near = near_sum(outer_grad)
    inner_near = near_sum(inner_grad)
    grads = gathered(places, back_pieces, mixed_wide, stat_columns)
    grad_halo = halo(grads)
    outer_far = far_sum(outer_near)
    grad_query = attention_queries(
        query_bounds, queries, spans_column, grads, mixed_wide, stat_columns, pairs
    )
    grad_query, grad_halo, outer_far, inner_near = lax.optimization_barrier(
        (grad_query, grad_halo, outer_far, inner_near)
    )

    near_first = [1 << i for i in range(cycle.bit_length() - 1)]
    far_first = [2, 1] + near_first[2:]
    outer_part = scatter_sum(outer_far, "ctx", near_first[:1], 0)
    inner_far = far_sum(inner_near)
    grad_pair = attention_keys(key_bounds, pair, spans_row, query_halo, grad_halo)
    grad_pair, outer_part, inner_far = lax.optimization_barrier(
        (grad_pair, outer_part, inner_far)
    )

    head_grad, token_partial = head_grads(places, block_tokens, grad_query, grad_pair, weight_pieces)
    outer_part = scatter_sum(outer_part, "ctx", near_first[1:], 0)
    inner_part = scatter_sum(inner_far, "ctx", far_first, 0)
    head_part = scatter_sum(head_grad, "ctx", near_first, 1)
    token_sum = far_sum(near_sum(token_partial))
    outer_total = gather_back(outer_part, "ctx", near_first, 0)
    inner_total = gather_back(inner_part, "ctx", far_first, 0)
    head_pieces = [
        lax.dynamic_index_in_dim(head_part, w ^ r, 0, keepdims=False) for r in range(shards)
    ]
    head_pieces = [head_pieces[0]] + [swapped(head_pieces[r], "wt", r) for r in range(1, shards)]
    head_parts = jnp.stack(
        [
            lax.dynamic_index_in_dim(jnp.stack(head_pieces), w ^ k, 0, keepdims=False)
            for k in range(shards)
        ]
    )
    head_total = gather_back(head_parts, "ctx", near_first, 1)

    tokens_gradient = grad_one + token_sum.astype(f32)
    key_total, value_total, query_total = (
        jnp.concatenate(
            [head_total[k, :, i * part : (i + 1) * part] for k in range(shards)], axis=1
        ).astype(f32)
        for i in range(3)
    )
    own_total = lax.dynamic_index_in_dim(head_total, w, 0, keepdims=False)
    inner_rows = inner_total[:width].reshape(shards, part, width)
    inner_rows = jnp.concatenate([inner_rows[k] for k in range(shards)], axis=1).astype(f32)
    lines = inner_total[width + part : width + part + 16, :part].astype(f32)

    return (
        layer_out,
        tokens_gradient,
        query_total,
        key_total,
        value_total,
        inner_total[width : width + part].astype(f32),
        own_total[:, 3 * part].astype(f32),
        own_total[:, 3 * part + 1].astype(f32),
        lines[0],
        lines[1],
        lines[2],
        inner_rows,
        lines[6:10].reshape(-1),
        outer_total.astype(f32),
        lines[3],
        lines[4],
        lines[5],
    )


def solution(mesh):
    matrix, vector = P("wt", None), P("wt")
    stream = P(("ctx", "wt"), None)
    in_specs = (stream, P(), stream) + (matrix,) * 4 + (vector,) * 5
    in_specs += (matrix, vector, matrix, vector, vector, vector)
    out_specs = (stream, stream) + (matrix,) * 4 + (vector,) * 5
    out_specs += (matrix, vector, matrix, vector, vector, vector)
    return jax.shard_map(
        on_device, mesh=mesh, in_specs=in_specs, out_specs=out_specs, check_vma=False
    )
```

time: 630 us -> 463 us (0.73); the launches traced: 619 us -> 463 us
  blocking collectives: 82.9 us -> 0 us
  waiting for transfers between devices: 148 us -> 211 us
  local copies, waits for them, and re-layouts: 100 us -> 44.3 us
  starting transfers between devices: 139 us -> 85.3 us
  matrix products: 37.8 us -> 0 us
  Pallas kernels: 58.3 us -> 82.2 us
  other arithmetic: 49.3 us -> 38 us
    ppermute x59 -> x45, starting transfers between devices: 111 us -> 54.8 us  [swapped(): return lax.ppermute(block, axis, [(i, i ^ bit) for i in range(count)])]
    ppermute x12, waiting for transfers between devices: 11.5 us -> 60.3 us  [shifted(): return lax.ppermute(block, axis, route)]
    psum x1 -> x0, blocking collectives: 45.1 us -> none  [on_device(): small_sums = lax.psum(small_grads, ('ctx', 'wt'))]
    all_gather x1 -> x0, blocking collectives: 37.8 us -> none  [on_device(): small = lax.all_gather(small_own, 'wt', axis=0)]
    dot_general x21 -> x0, matrix products: 37.8 us -> none  [the longest x8 15 us: right_transposed(): return jnp.einsum('te,de->td', left, right, preferred_element_type=f32)]
    pallas_call x0 -> x4, Pallas kernels: none -> 32.4 us  [the longest x1 21 us: dense(): pl.pallas_call(dense_kernel, in_specs=[pl.BlockSpec(memory_space=pltpu.SM...]
    dynamic_update_slice x33 -> x0, local copies, waits for them, and re-layouts: 25.7 us -> none  [placed(): buffer = lax.dynamic_update_slice_in_dim(buffer, piece[None], others[r], 0)]
    ppermute x59 -> x45, waiting for transfers between devices: 137 us -> 151 us  [swapped(): return lax.ppermute(block, axis, [(i, i ^ bit) for i in range(count)])]
  transfers between devices with their start and end apart: 71 -> 57, of which waited for: 26 -> 30; matrix products, arithmetic and copies ran while one was open for 27% -> 11% of each run, Pallas kernels for 9% -> 12%
where the time goes in v2:
time: 463 us
  waiting for transfers between devices  211 us (46%)
  starting transfers between devices  85.3 us (18%)
  Pallas kernels  82.2 us (18%)
  local copies, waits for them, and re-layouts  44.3 us (10%)
  other arithmetic  38 us (8%)
    ppermute x45, waiting for transfers between devices, swapped(): return lax.ppermute(block, axis, [(i, i ^ bit) for i in range(count)])  151 us
    ppermute x12, waiting for transfers between devices, shifted(): return lax.ppermute(block, axis, route)  60.3 us
    ppermute x45, starting transfers between devices, swapped(): return lax.ppermute(block, axis, [(i, i ^ bit) for i in range(count)])  54.8 us
    ppermute x12, starting transfers between devices, shifted(): return lax.ppermute(block, axis, route)  30.5 us
    pallas_call x1, Pallas kernels, dense(): pl.pallas_call(dense_kernel, in_specs=[pl.BlockSpec(memory_space=pltpu.SM...  21 us
    unnamed x134, local copies, waits for them, and re-layouts  19.2 us
    pallas_call x1, Pallas kernels, attention_keys(): pl.pallas_call(functools.partial(key_kernel, count // 2), grid_spec=pltpu...  17.3 us
    pallas_call x1, Pallas kernels, attention_forward(): pl.pallas_call(forward_kernel, grid_spec=pltpu.PrefetchScalarGridSpec(num...  16.6 us
  transfers between devices with their start and end apart: 57, of which 30 were waited for; matrix products, arithmetic and copies ran while one was open for 11% of the time, Pallas kernels for 12%

profile of v2, /device:TPU:0, one launch (start us, length us, event | category | flops | bytes accessed | tf_op | source)
XLA Modules:
  0.0 462.8 jit_solution(1395964697603066641)
XLA Ops:
  7.6 6.2 %collective-permute-done.1.far = bf16[256,768]{1,0:T(8,128)(2,1)S(1)} collective-permute-done((bf16[256,768]{1,0:T(8,128)(2,1)}, bf16[256,768]{1,0:T(8,128)(2,1)S(1)}, u32[]{:S(2)}, u32[]{:S(2)}) %collective-permute-start.1) | collective-permute-done | bytes 393248 | tf_op jit(solution)/shard_map/ppermute | solution.py:26
  43.4 6.0 %collective-permute-done.6.rest_0_ = bf16[1024,384]{1,0:T(8,128)(2,1)S(1)} collective-permute-done((bf16[1024,384]{1,0:T(8,128)(2,1)S(1)}, bf16[1024,384]{1,0:T(8,128)(2,1)S(1)}, u32[]{:S(2)}, u32[]{:S(2)}) %collective-permute-start.6) | collective-permute-done | bytes 786464 | tf_op jit(solution)/shard_map/ppermute | solution.py:32
  55.1 21.8 %collective-permute-done.18.refs_14_ = bf16[976,768]{1,0:T(8,128)(2,1)} collective-permute-done((bf16[976,768]{1,0:T(8,128)(2,1)}, bf16[976,768]{1,0:T(8,128)(2,1)}, u32[]{:S(2)}, u32[]{:S(2)}) %collective-permute-start.18) | collective-permute-done | bytes 1499168 | tf_op jit(solution)/shard_map/ppermute | solution.py:26
  77.3 12.9 %collective-permute-done.9.rest_4_ = bf16[1024,384]{1,0:T(8,128)(2,1)} collective-permute-done((bf16[1024,384]{1,0:T(8,128)(2,1)S(1)}, bf16[1024,384]{1,0:T(8,128)(2,1)}, u32[]{:S(2)}, u32[]{:S(2)}) %collective-permute-start.9) | collective-permute-done | bytes 786464 | tf_op jit(solution)/shard_map/ppermute | solution.py:32
  93.6 16.6 %attention_forward.1 = (bf16[1024,192]{1,0:T(8,128)(2,1)S(1)}, f32[1024,192]{1,0:T(8,128)S(1)}, f32[1024,128]{1,0:T(8,128)S(1)}) custom-call(s32[8]{0:T(128)S(1)} %reshape.115.bounds, bf16[1024,192]{1,0:T(8,128)(2,1)} %get-tuple-element.74.q_ref.rest_2_, s32[1024,8]{1,0:T(8,128)S(1)} %copy.39.span_ref, bf16[1024,384]{1,0:T(8,128)(2,1)S(1)} %copy-done.10, ...), custom_call_target="tpu_custom_call" | custom-call | flops 1811939328 | bytes 6291456 | tf_op jit(solution)/shard_map/attention_forward/pallas_call | solution.py:129
  111.0 6.5 %collective-permute-start.13 = (bf16[1024,192]{1,0:T(8,128)(2,1)}, bf16[1024,192]{1,0:T(8,128)(2,1)S(1)}, u32[]{:S(2)}, u32[]{:S(2)}) collective-permute-start(bf16[1024,192]{1,0:T(8,128)(2,1)} %get-tuple-element.74.q_ref.rest_2_), channel_id=1, source_target_pairs={{0,8},{4,12},{8,16},{12,20},{16,24},{20,28},{1,9},{5,13},{9,17},{1... | collective-permute-start | bytes 1179656 | tf_op jit(solution)/shard_map/ppermute | solution.py:32
  117.5 5.2 %collective-permute-start.14 = (bf16[1024,192]{1,0:T(8,128)(2,1)}, bf16[1024,192]{1,0:T(8,128)(2,1)}, u32[]{:S(2)}, u32[]{:S(2)}) collective-permute-start(bf16[1024,192]{1,0:T(8,128)(2,1)} %get-tuple-element.74.q_ref.rest_2_), channel_id=1, source_target_pairs={{0,4},{4,8},{8,12},{12,16},{16,20},{20,24},{24,28},{1,5},{5,9},{9,... | collective-permute-start | bytes 1179656 | tf_op jit(solution)/shard_map/ppermute | solution.py:32
  129.0 4.8 %collective-permute-done.12.refs_3_ = bf16[256,192]{1,0:T(8,128)(2,1)S(1)} collective-permute-done((bf16[256,192]{1,0:T(8,128)(2,1)S(1)}, bf16[256,192]{1,0:T(8,128)(2,1)S(1)}, u32[]{:S(2)}, u32[]{:S(2)}) %collective-permute-start.12) | collective-permute-done | bytes 98336 | tf_op jit(solution)/shard_map/ppermute | solution.py:26
  138.6 15.3 %collective-permute-done.15.rest_3_ = bf16[1024,192]{1,0:T(8,128)(2,1)S(1)} collective-permute-done((bf16[1024,192]{1,0:T(8,128)(2,1)}, bf16[1024,192]{1,0:T(8,128)(2,1)S(1)}, u32[]{:S(2)}, u32[]{:S(2)}) %collective-permute-start.15) | collective-permute-done | bytes 393248 | tf_op jit(solution)/shard_map/ppermute | solution.py:32
  154.7 11.6 %collective-permute-done.16.rest_4_ = bf16[1024,192]{1,0:T(8,128)(2,1)S(1)} collective-permute-done((bf16[1024,192]{1,0:T(8,128)(2,1)}, bf16[1024,192]{1,0:T(8,128)(2,1)S(1)}, u32[]{:S(2)}, u32[]{:S(2)}) %collective-permute-start.16) | collective-permute-done | bytes 393248 | tf_op jit(solution)/shard_map/ppermute | solution.py:32
  169.5 21.0 %layer_dense.1 = (bf16[256,768]{1,0:T(8,128)(2,1)}, f32[256,768]{1,0:T(8,128)}, bf16[4,256,192]{2,1,0:T(8,128)(2,1)}, bf16[4,768,768]{2,1,0:T(8,128)(2,1)}, bf16[4,1024,768]{2,1,0:T(8,128)(2,1)}) custom-call(s32[4]{0:T(128)} %copy-done, bf16[256,192]{1,0:T(8,128)(2,1)} %get-tuple-element.57.refs_0_, bf16[256,192]{1,0:T(8,128)(2,1)} %copy-done.56, ...), custom_call_target="tpu_custom_call" | custom-call | flops 14495514624 | bytes 25165824 | tf_op jit(solution)/shard_map/layer_dense/pallas_call | solution.py:512
  206.2 28.2 %collective-permute-done.24.p2 = bf16[256,192]{1,0:T(8,128)(2,1)S(1)} collective-permute-done((bf16[256,192]{1,0:T(8,128)(2,1)}, bf16[256,192]{1,0:T(8,128)(2,1)S(1)}, u32[]{:S(2)}, u32[]{:S(2)}) %collective-permute-start.24) | collective-permute-done | bytes 98336 | tf_op jit(solution)/shard_map/ppermute | solution.py:26
  244.3 15.9 %attention_queries.1.query_ref = bf16[1024,192]{1,0:T(8,128)(2,1)S(1)} custom-call(s32[8]{0:T(128)S(1)} %copy-done.4, bf16[1024,192]{1,0:T(8,128)(2,1)} %get-tuple-element.74.q_ref.rest_2_, s32[1024,8]{1,0:T(8,128)S(1)} %copy.39.span_ref, bf16[1024,256]{1,0:T(8,128)(2,1)S(1)} %layer_gather.1.grad_ref.rest_7_, f32[1024,192]{1,0:T(8,128)S(1)} %get-tuple-element.67.wide_ref, ...), custom_call_target="tpu_custom_call" | custom-call | flops 2717908992 | bytes 6291456 | tf_op jit(solution)/shard_map/attention_queries/pallas_call | solution.py:220
  268.1 13.4 %collective-permute-done.29.rest_9_ = bf16[1024,256]{1,0:T(8,128)(2,1)S(1)} collective-permute-done((bf16[1024,256]{1,0:T(8,128)(2,1)S(1)}, bf16[1024,256]{1,0:T(8,128)(2,1)S(1)}, u32[]{:S(2)}, u32[]{:S(2)}) %collective-permute-start.29) | collective-permute-done | bytes 524320 | tf_op jit(solution)/shard_map/ppermute | solution.py:32
  293.5 17.3 %attention_keys.1.pair_ref = bf16[1024,384]{1,0:T(8,128)(2,1)S(1)} custom-call(s32[8]{0:T(128)S(1)} %copy-done.4, bf16[1024,384]{1,0:T(8,128)(2,1)S(1)} %copy-done.8, s32[8,5120]{1,0:T(8,128)S(1)} %add_add_fusion.span_ref, bf16[1024,192]{1,0:T(8,128)(2,1)S(1)} %copy-done.16, bf16[1024,192]{1,0:T(8,128)(2,1)} %collective-permute-done.14.rest_1_, ...), custom_call_target="tpu_custom_call" | custom-call | flops 3623878656 | bytes 8388608 | tf_op jit(solution)/shard_map/attention_keys/pallas_call | solution.py:309
  312.4 6.7 %collective-permute-done.34 = bf16[1,1,1024,768]{3,2,1,0:T(8,128)(2,1)} collective-permute-done((bf16[1,1,1024,768]{3,2,1,0:T(8,128)(2,1)}, bf16[1,1,1024,768]{3,2,1,0:T(8,128)(2,1)}, u32[]{:S(2)}, u32[]{:S(2)}) %collective-permute-start.34) | collective-permute-done | bytes 1572896 | tf_op jit(solution)/shard_map/ppermute | solution.py:26
  322.7 5.3 %collective-permute-start.52 = (bf16[192,768]{1,0:T(8,128)(2,1)}, bf16[192,768]{1,0:T(8,128)(2,1)}, u32[]{:S(2)}, u32[]{:S(2)}) collective-permute-start(bf16[192,768]{1,0:T(8,128)(2,1)} %constant_dynamic-slice_fusion.5), channel_id=1, source_target_pairs={{0,8},{4,12},{8,0},{12,4},{16,24},{20,28},{24,16},{28,20},{1,9},{5... | collective-permute-start | bytes 884744 | tf_op jit(solution)/shard_map/ppermute | solution.py:26
  332.6 5.0 %layer_heads.1 = (bf16[4,192,640]{2,1,0:T(8,128)(2,1)S(1)}, bf16[4,256,768]{2,1,0:T(8,128)(2,1)S(1)}) custom-call(s32[4]{0:T(128)S(1)} %copy-done.2, bf16[1024,768]{1,0:T(8,128)(2,1)S(1)} %copy-done.37, bf16[1024,192]{1,0:T(8,128)(2,1)S(1)} %copy-done.41, bf16[1024,384]{1,0:T(8,128)(2,1)S(1)} %copy-done.39, bf16[192,576]{1,0:T(8,128)(2,1)S(1)} %pad_maximum_fusion.w_own.w0, ...), custom_call_target="tpu_custom_call" | custom-call | flops 1811939328 | bytes 8388608 | tf_op jit(solution)/shard_map/layer_heads/pallas_call | solution.py:614
  354.3 12.7 %collective-permute-done.54 = bf16[96,768]{1,0:T(8,128)(2,1)S(1)} collective-permute-done((bf16[96,768]{1,0:T(8,128)(2,1)S(1)}, bf16[96,768]{1,0:T(8,128)(2,1)S(1)}, u32[]{:S(2)}, u32[]{:S(2)}) %collective-permute-start.54) | collective-permute-done | bytes 147488 | tf_op jit(solution)/shard_map/ppermute | solution.py:26
  389.6 9.0 %collective-permute-done.43 = bf16[4,24,640]{2,1,0:T(8,128)(2,1)S(1)} collective-permute-done((bf16[4,24,640]{2,1,0:T(8,128)(2,1)S(1)}, bf16[4,24,640]{2,1,0:T(8,128)(2,1)S(1)}, u32[]{:S(2)}, u32[]{:S(2)}) %collective-permute-start.43) | collective-permute-done | bytes 122912 | tf_op jit(solution)/shard_map/ppermute | solution.py:26
  404.9 5.1 %collective-permute-done.44 = bf16[4,48,640]{2,1,0:T(8,128)(2,1)S(1)} collective-permute-done((bf16[4,48,640]{2,1,0:T(8,128)(2,1)S(1)}, bf16[4,48,640]{2,1,0:T(8,128)(2,1)S(1)}, u32[]{:S(2)}, u32[]{:S(2)}) %collective-permute-start.44) | collective-permute-done | bytes 245792 | tf_op jit(solution)/shard_map/ppermute | solution.py:26
  422.4 7.2 %collective-permute-done.45 = bf16[4,96,640]{2,1,0:T(8,128)(2,1)S(1)} collective-permute-done((bf16[4,96,640]{2,1,0:T(8,128)(2,1)S(1)}, bf16[4,96,640]{2,1,0:T(8,128)(2,1)S(1)}, u32[]{:S(2)}, u32[]{:S(2)}) %collective-permute-start.45) | collective-permute-done | bytes 491552 | tf_op jit(solution)/shard_map/ppermute | solution.py:26
  430.0 6.8 %collective-permute-done.50 = bf16[256,768]{1,0:T(8,128)(2,1)S(1)} collective-permute-done((bf16[256,768]{1,0:T(8,128)(2,1)S(1)}, bf16[256,768]{1,0:T(8,128)(2,1)S(1)}, u32[]{:S(2)}, u32[]{:S(2)}) %collective-permute-start.50) | collective-permute-done | bytes 393248 | tf_op jit(solution)/shard_map/ppermute | solution.py:26
  445.3 12.9 %collective-permute-done.51 = bf16[512,768]{1,0:T(8,128)(2,1)S(1)} collective-permute-done((bf16[512,768]{1,0:T(8,128)(2,1)S(1)}, bf16[512,768]{1,0:T(8,128)(2,1)S(1)}, u32[]{:S(2)}, u32[]{:S(2)}) %collective-permute-start.51) | collective-permute-done | bytes 786464 | tf_op jit(solution)/shard_map/ppermute | solution.py:26
  (343 shorter events, 187.5 us)
Async XLA Ops:
  40.9 36.0 %collective-permute-start.18 = (bf16[976,768]{1,0:T(8,128)(2,1)}, bf16[976,768]{1,0:T(8,128)(2,1)}, u32[]{:S(2)}, u32[]{:S(2)}) collective-permute-start(bf16[976,768]{1,0:T(8,128)(2,1)} %fusion.2.refs_12_), channel_id=1, source_target_pairs={{0,2},{1,3},{2,0},{3,1},{4,6},{5,7},{6,4},{7,5},{8,10},{9,11},{10,... | collective-permute-start | bytes 4497416 | tf_op jit(solution)/shard_map/ppermute | solution.py:26
  42.8 91.1 %collective-permute-start.17 = (bf16[976,768]{1,0:T(8,128)(2,1)}, bf16[976,768]{1,0:T(8,128)(2,1)}, u32[]{:S(2)}, u32[]{:S(2)}) collective-permute-start(bf16[976,768]{1,0:T(8,128)(2,1)} %fusion.2.refs_12_), channel_id=1, source_target_pairs={{0,1},{1,0},{2,3},{3,2},{4,5},{5,4},{6,7},{7,6},{8,9},{9,8},{10,11... | collective-permute-start | bytes 4497416 | tf_op jit(solution)/shard_map/ppermute | solution.py:26
  42.8 74.6 %collective-permute-start.21 = (bf16[192,3072]{1,0:T(8,128)(2,1)}, bf16[192,3072]{1,0:T(8,128)(2,1)}, u32[]{:S(2)}, u32[]{:S(2)}) collective-permute-start(bf16[192,3072]{1,0:T(8,128)(2,1)} %refs_8_), channel_id=1, source_target_pairs={{0,2},{1,3},{2,0},{3,1},{4,6},{5,7},{6,4},{7,5},{8,10},{9,11},{10,... | collective-permute-start | bytes 3538952 | tf_op jit(solution)/shard_map/ppermute | solution.py:26
  50.3 27.0 %collective-permute-start.8 = (bf16[1024,384]{1,0:T(8,128)(2,1)S(1)}, bf16[1024,384]{1,0:T(8,128)(2,1)}, u32[]{:S(2)}, u32[]{:S(2)}) collective-permute-start(bf16[1024,384]{1,0:T(8,128)(2,1)S(1)} %get-tuple-element.54.rest_2_.kv_ref), channel_id=1, source_target_pairs={{4,0},{8,4},{12,8},{16,12},{20,16},{24,20},{28,24},{5,1},{9,5},{13... | collective-permute-start | bytes 2359304 | tf_op jit(solution)/shard_map/ppermute | solution.py:32
  53.6 36.7 %collective-permute-start.9 = (bf16[1024,384]{1,0:T(8,128)(2,1)S(1)}, bf16[1024,384]{1,0:T(8,128)(2,1)}, u32[]{:S(2)}, u32[]{:S(2)}) collective-permute-start(bf16[1024,384]{1,0:T(8,128)(2,1)S(1)} %get-tuple-element.54.rest_2_.kv_ref), channel_id=1, source_target_pairs={{8,0},{12,4},{16,8},{20,12},{24,16},{28,20},{9,1},{13,5},{17,9},{2... | collective-permute-start | bytes 2359304 | tf_op jit(solution)/shard_map/ppermute | solution.py:32
  76.9 90.2 %collective-permute-start.19 = (bf16[976,768]{1,0:T(8,128)(2,1)}, bf16[976,768]{1,0:T(8,128)(2,1)}, u32[]{:S(2)}, u32[]{:S(2)}) collective-permute-start(bf16[976,768]{1,0:T(8,128)(2,1)} %collective-permute-done.18.refs_14_), channel_id=1, source_target_pairs={{0,1},{1,0},{2,3},{3,2},{4,5},{5,4},{6,7},{7,6},{8,9},{9,8},{10,11... | collective-permute-start | bytes 4497416 | tf_op jit(solution)/shard_map/ppermute | solution.py:26
  111.0 24.2 %collective-permute-start.13 = (bf16[1024,192]{1,0:T(8,128)(2,1)}, bf16[1024,192]{1,0:T(8,128)(2,1)S(1)}, u32[]{:S(2)}, u32[]{:S(2)}) collective-permute-start(bf16[1024,192]{1,0:T(8,128)(2,1)} %get-tuple-element.74.q_ref.rest_2_), channel_id=1, source_target_pairs={{0,8},{4,12},{8,16},{12,20},{16,24},{20,28},{1,9},{5,13},{9,17},{1... | collective-permute-start | bytes 1179656 | tf_op jit(solution)/shard_map/ppermute | solution.py:32
  133.8 35.7 %collective-permute-start.20 = (bf16[192,3072]{1,0:T(8,128)(2,1)}, bf16[192,3072]{1,0:T(8,128)(2,1)}, u32[]{:S(2)}, u32[]{:S(2)}) collective-permute-start(bf16[192,3072]{1,0:T(8,128)(2,1)} %refs_8_), channel_id=1, source_target_pairs={{0,1},{1,0},{2,3},{3,2},{4,5},{5,4},{6,7},{7,6},{8,9},{9,8},{10,11... | collective-permute-start | bytes 3538952 | tf_op jit(solution)/shard_map/ppermute | solution.py:26
  135.2 31.1 %collective-permute-start.16 = (bf16[1024,192]{1,0:T(8,128)(2,1)}, bf16[1024,192]{1,0:T(8,128)(2,1)S(1)}, u32[]{:S(2)}, u32[]{:S(2)}) collective-permute-start(bf16[1024,192]{1,0:T(8,128)(2,1)} %get-tuple-element.74.q_ref.rest_2_), channel_id=1, source_target_pairs={{8,0},{12,4},{16,8},{20,12},{24,16},{28,20},{9,1},{13,5},{17,9},{2... | collective-permute-start | bytes 1179656 | tf_op jit(solution)/shard_map/ppermute | solution.py:32
  136.7 32.7 %collective-permute-start.22 = (bf16[192,3072]{1,0:T(8,128)(2,1)}, bf16[192,3072]{1,0:T(8,128)(2,1)}, u32[]{:S(2)}, u32[]{:S(2)}) collective-permute-start(bf16[192,3072]{1,0:T(8,128)(2,1)} %collective-permute-done.21.refs_10_), channel_id=1, source_target_pairs={{0,1},{1,0},{2,3},{3,2},{4,5},{5,4},{6,7},{7,6},{8,9},{9,8},{10,11... | collective-permute-start | bytes 3538952 | tf_op jit(solution)/shard_map/ppermute | solution.py:26
  197.4 62.8 %collective-permute-start.32 = (bf16[2,1,1024,768]{3,2,1,0:T(8,128)(2,1)}, bf16[2,1,1024,768]{3,2,1,0:T(8,128)(2,1)}, u32[]{:S(2)}, u32[]{:S(2)}) collective-permute-start(bf16[2,1,1024,768]{3,2,1,0:T(8,128)(2,1)} %constant_dynamic-slice_fusion.21), channel_id=1, source_target_pairs={{0,1},{1,0},{2,3},{3,2},{4,5},{5,4},{6,7},{7,6},{8,9},{9,8},{10,11... | collective-permute-start | bytes 9437192 | tf_op jit(solution)/shard_map/ppermute | solution.py:26
  202.6 61.9 %collective-permute-start.31 = (bf16[1,1,768,768]{3,2,1,0:T(8,128)(2,1)}, bf16[1,1,768,768]{3,2,1,0:T(8,128)(2,1)}, u32[]{:S(2)}, u32[]{:S(2)}) collective-permute-start(bf16[1,1,768,768]{3,2,1,0:T(8,128)(2,1)} %constant_dynamic-slice_fusion.22), channel_id=1, source_target_pairs={{0,2},{1,3},{2,0},{3,1},{4,6},{5,7},{6,4},{7,5},{8,10},{9,11},{10,... | collective-permute-start | bytes 3538952 | tf_op jit(solution)/shard_map/ppermute | solution.py:26
  204.3 30.1 %collective-permute-start.24 = (bf16[256,192]{1,0:T(8,128)(2,1)}, bf16[256,192]{1,0:T(8,128)(2,1)S(1)}, u32[]{:S(2)}, u32[]{:S(2)}) collective-permute-start(bf16[256,192]{1,0:T(8,128)(2,1)} %get-tuple-element.111), channel_id=1, source_target_pairs={{0,2},{1,3},{2,0},{3,1},{4,6},{5,7},{6,4},{7,5},{8,10},{9,11},{10,... | collective-permute-start | bytes 294920 | tf_op jit(solution)/shard_map/ppermute | solution.py:26
  205.4 30.2 %collective-permute-start.25 = (bf16[256,192]{1,0:T(8,128)(2,1)}, bf16[256,192]{1,0:T(8,128)(2,1)S(1)}, u32[]{:S(2)}, u32[]{:S(2)}) collective-permute-start(bf16[256,192]{1,0:T(8,128)(2,1)} %get-tuple-element.110), channel_id=1, source_target_pairs={{0,3},{1,2},{2,1},{3,0},{4,7},{5,6},{6,5},{7,4},{8,11},{9,10},{10,... | collective-permute-start | bytes 294920 | tf_op jit(solution)/shard_map/ppermute | solution.py:26
  238.7 29.3 %collective-permute-start.26 = (bf16[1024,256]{1,0:T(8,128)(2,1)S(1)}, bf16[1024,256]{1,0:T(8,128)(2,1)S(1)}, u32[]{:S(2)}, u32[]{:S(2)}) collective-permute-start(bf16[1024,256]{1,0:T(8,128)(2,1)S(1)} %layer_gather.1.grad_ref.rest_7_), channel_id=1, source_target_pairs={{0,8},{4,12},{8,16},{12,20},{16,24},{20,28},{1,9},{5,13},{9,17},{1... | collective-permute-start | bytes 1572872 | tf_op jit(solution)/shard_map/ppermute | solution.py:32
  241.0 27.1 %collective-permute-start.27 = (bf16[1024,256]{1,0:T(8,128)(2,1)S(1)}, bf16[1024,256]{1,0:T(8,128)(2,1)S(1)}, u32[]{:S(2)}, u32[]{:S(2)}) collective-permute-start(bf16[1024,256]{1,0:T(8,128)(2,1)S(1)} %layer_gather.1.grad_ref.rest_7_), channel_id=1, source_target_pairs={{0,4},{4,8},{8,12},{12,16},{16,20},{20,24},{24,28},{1,5},{5,9},{9,... | collective-permute-start | bytes 1572872 | tf_op jit(solution)/shard_map/ppermute | solution.py:32
  242.3 25.8 %collective-permute-start.28 = (bf16[1024,256]{1,0:T(8,128)(2,1)S(1)}, bf16[1024,256]{1,0:T(8,128)(2,1)S(1)}, u32[]{:S(2)}, u32[]{:S(2)}) collective-permute-start(bf16[1024,256]{1,0:T(8,128)(2,1)S(1)} %layer_gather.1.grad_ref.rest_7_), channel_id=1, source_target_pairs={{4,0},{8,4},{12,8},{16,12},{20,16},{24,20},{28,24},{5,1},{9,5},{13... | collective-permute-start | bytes 1572872 | tf_op jit(solution)/shard_map/ppermute | solution.py:32
  282.8 36.2 %collective-permute-start.34 = (bf16[1,1,1024,768]{3,2,1,0:T(8,128)(2,1)}, bf16[1,1,1024,768]{3,2,1,0:T(8,128)(2,1)}, u32[]{:S(2)}, u32[]{:S(2)}) collective-permute-start(bf16[1,1,1024,768]{3,2,1,0:T(8,128)(2,1)} %constant_dynamic-slice_fusion.19), channel_id=1, source_target_pairs={{0,2},{1,3},{2,0},{3,1},{4,6},{5,7},{6,4},{7,5},{8,10},{9,11},{10,... | collective-permute-start | bytes 4718600 | tf_op jit(solution)/shard_map/ppermute | solution.py:26
  286.1 24.8 %collective-permute-start.33 = (bf16[384,768]{1,0:T(8,128)(2,1)}, bf16[384,768]{1,0:T(8,128)(2,1)}, u32[]{:S(2)}, u32[]{:S(2)}) collective-permute-start(bf16[384,768]{1,0:T(8,128)(2,1)} %constant_dynamic-slice_fusion.20), channel_id=1, source_target_pairs={{0,4},{4,0},{8,12},{12,8},{16,20},{20,16},{24,28},{28,24},{1,5},{5... | collective-permute-start | bytes 1769480 | tf_op jit(solution)/shard_map/ppermute | solution.py:26
  343.7 31.3 %collective-permute-start.46 = (bf16[512,768]{1,0:T(8,128)(2,1)S(1)}, bf16[512,768]{1,0:T(8,128)(2,1)S(1)}, u32[]{:S(2)}, u32[]{:S(2)}) collective-permute-start(bf16[512,768]{1,0:T(8,128)(2,1)S(1)} %constant_dynamic-slice_fusion.8), channel_id=1, source_target_pairs={{0,8},{4,12},{8,0},{12,4},{16,24},{20,28},{24,16},{28,20},{1,9},{5... | collective-permute-start | bytes 2359304 | tf_op jit(solution)/shard_map/ppermute | solution.py:26
  351.3 21.9 %collective-permute-start.38 = (bf16[4,48,640]{2,1,0:T(8,128)(2,1)S(1)}, bf16[4,48,640]{2,1,0:T(8,128)(2,1)S(1)}, u32[]{:S(2)}, u32[]{:S(2)}) collective-permute-start(bf16[4,48,640]{2,1,0:T(8,128)(2,1)S(1)} %constant_dynamic-slice_fusion.15), channel_id=1, source_target_pairs={{0,8},{4,12},{8,0},{12,4},{16,24},{20,28},{24,16},{28,20},{1,9},{5... | collective-permute-start | bytes 737288 | tf_op jit(solution)/shard_map/ppermute | solution.py:26
  354.2 26.5 %collective-permute-start.35 = (bf16[2,1,256,768]{3,2,1,0:T(8,128)(2,1)S(1)}, bf16[2,1,256,768]{3,2,1,0:T(8,128)(2,1)S(1)}, u32[]{:S(2)}, u32[]{:S(2)}) collective-permute-start(bf16[2,1,256,768]{3,2,1,0:T(8,128)(2,1)S(1)} %constant_dynamic-slice_fusion.18), channel_id=1, source_target_pairs={{0,1},{1,0},{2,3},{3,2},{4,5},{5,4},{6,7},{7,6},{8,9},{9,8},{10,11... | collective-permute-start | bytes 2359304 | tf_op jit(solution)/shard_map/ppermute | solution.py:26
  367.0 35.5 %collective-permute-start.55 = (bf16[192,768]{1,0:T(8,128)(2,1)S(1)}, bf16[192,768]{1,0:T(8,128)(2,1)S(1)}, u32[]{:S(2)}, u32[]{:S(2)}) collective-permute-start(bf16[192,768]{1,0:T(8,128)(2,1)S(1)} %maximum_select_fusion.7), channel_id=1, source_target_pairs={{0,8},{4,12},{8,0},{12,4},{16,24},{20,28},{24,16},{28,20},{1,9},{5... | collective-permute-start | bytes 884744 | tf_op jit(solution)/shard_map/ppermute | solution.py:26
  388.7 28.9 %collective-permute-start.36 = (bf16[1,1,256,768]{3,2,1,0:T(8,128)(2,1)}, bf16[1,1,256,768]{3,2,1,0:T(8,128)(2,1)}, u32[]{:S(2)}, u32[]{:S(2)}) collective-permute-start(bf16[1,1,256,768]{3,2,1,0:T(8,128)(2,1)} %constant_dynamic-slice_fusion.17), channel_id=1, source_target_pairs={{0,2},{1,3},{2,0},{3,1},{4,6},{5,7},{6,4},{7,5},{8,10},{9,11},{10,... | collective-permute-start | bytes 1179656 | tf_op jit(solution)/shard_map/ppermute | solution.py:26
  (100 other events, 1185.9 us)

commit v3 on v2

--- a/solution.py
+++ b/solution.py
@@ -40,11 +40,11 @@
     return lax.dot_general(left, right, (((1,), (0,)), ((), ())), preferred_element_type=f32)
 
 
-def load_window(pieces, target, sem, block):
-    copies = [
-        pltpu.make_async_copy(piece, target.at[pl.ds(i * block, block), :], sem.at[i])
-        for i, piece in enumerate(pieces)
-    ]
+def load_window(pieces, target, sem, starts):
+    copies = []
+    for i, piece in enumerate(pieces):
+        rows = pl.ds(pl.multiple_of(starts[i], 128), piece.shape[0])
+        copies.append(pltpu.make_async_copy(piece, target.at[rows, :], sem.at[i]))
     for copy in copies:
         copy.start()
     return copies
@@ -66,11 +66,10 @@
 def forward_kernel(bounds, q_ref, span_ref, *rest):
     pieces, (out_ref, wide_ref, stat_ref, kv, top, total, accum, sem) = rest[:-8], rest[-8:]
     step = pl.program_id(0)
-    block = pieces[0].shape[0]
 
     @pl.when(step == 0)
     def _():
-        for copy in load_window(pieces, kv, sem, block):
+        for copy in load_window(pieces, kv, sem, [bounds[8 + i] for i in range(len(pieces))]):
             copy.wait()
 
     first = pl.multiple_of(step * TILE_Q, TILE_Q)
@@ -125,7 +124,7 @@
 
 def attention_forward(bounds, queries, spans, pieces):
     block = queries.shape[0]
-    window = len(pieces) * block
+    window = sum(x.shape[0] for x in pieces)
     return pl.pallas_call(
         forward_kernel,
         grid_spec=pltpu.PrefetchScalarGridSpec(
@@ -162,11 +161,10 @@
 def query_kernel(bounds, q_ref, span_ref, grad_ref, wide_ref, stat_ref, *rest):
     pieces, (out_ref, kv, accum, sem) = rest[:-4], rest[-4:]
     step = pl.program_id(0)
-    block = pieces[0].shape[0]
 
     @pl.when(step == 0)
     def _():
-        for copy in load_window(pieces, kv, sem, block):
+        for copy in load_window(pieces, kv, sem, [bounds[8 + i] for i in range(len(pieces))]):
             copy.wait()
 
     first = pl.multiple_of(step * TILE_Q, TILE_Q)
@@ -216,7 +214,7 @@
 
 def attention_queries(bounds, queries, spans, grads, wide, stats, pieces):
     block = queries.shape[0]
-    window = len(pieces) * block
+    window = sum(x.shape[0] for x in pieces)
     return pl.pallas_call(
         query_kernel,
         grid_spec=pltpu.PrefetchScalarGridSpec(
@@ -249,8 +247,8 @@
 
     @pl.when(step == 0)
     def _():
-        copies = load_window(q_pieces, qs, sem.at[0], block)
-        copies += load_window(g_pieces, gs, sem.at[1], block)
+        copies = load_window(q_pieces, qs, sem.at[0], [i * block for i in range(window)])
+        copies += load_window(g_pieces, gs, sem.at[1], [i * block for i in range(window)])
         for copy in copies:
             copy.wait()
 
@@ -397,23 +395,24 @@
 def dense_kernel(place_ref, *refs):
     mixed = refs[0:4]
     tokens_ref, up_ref, small_ref, inner_bias_ref = refs[4:8]
-    inner_pieces, outer_pieces = refs[8:12], refs[12:16]
-    out_ref, grad_ref, back_ref, outer_grad, inner_grad = refs[16:21]
-    w_out, w_inner, w_outer, hidden, activated, slopes, sem = refs[21:]
+    packs = refs[8:12]
+    out_ref, grad_ref, back_ref = refs[12:15]
+    outer_keep, outer_send, inner_keep, inner_send = refs[15:19]
+    w_out, w_inner, w_outer, hidden, activated, slopes, inner_grad, sem = refs[19:]
     rows, width = tokens_ref.shape
     groups = w_inner.shape[0]
     part = width // groups
     copies = []
     for r in range(groups):
         copies.append(
-            pltpu.make_async_copy(outer_pieces[r].at[pl.ds(width, part), :], w_out.at[r], sem.at[0, r])
+            pltpu.make_async_copy(packs[r].at[pl.ds(width, part), :], w_out.at[r], sem.at[0, r])
         )
     for r in range(groups):
         here = pl.ds(pl.multiple_of(place_ref[r] * part, part), part)
         for g in range(groups):
             copies.append(
                 pltpu.make_async_copy(
-                    inner_pieces[r].at[:, pl.ds(g * width, width)],
+                    packs[r].at[pl.ds(width + part + 16 + g * part, part), :],
                     w_inner.at[g, here, :],
                     sem.at[1 + g, r],
                 )
@@ -421,7 +420,7 @@
     for r in range(groups):
         copies.append(
             pltpu.make_async_copy(
-                outer_pieces[r].at[pl.ds(0, width), :], w_outer.at[place_ref[r]], sem.at[1 + groups, r]
+                packs[r].at[pl.ds(0, width), :], w_outer.at[place_ref[r]], sem.at[1 + groups, r]
             )
         )
     for copy in copies:
@@ -461,7 +460,17 @@
     outer_bias_sum = jnp.sum(grad_two_low.astype(f32), axis=0, keepdims=True)
 
     def behind(g, total):
-        outer_grad[g] = rows_tn(activated[g], grad_two_low).astype(bf16)
+        made = rows_tn(activated[g], grad_two_low).astype(bf16)
+        r = place_ref[g]
+
+        @pl.when(r % 2 == 0)
+        def _():
+            outer_keep[r // 2] = made
+
+        @pl.when(r % 2 == 1)
+        def _():
+            outer_send[r // 2] = made
+
         value = (rows_nt(grad_two_low, w_outer[g]) * slopes[g]).astype(bf16)
         hidden[g] = value
         return total + rows_nt(value, w_inner[g])
@@ -476,10 +485,10 @@
     for g in range(groups):
         made = rows_tn(first_low, hidden[g]).astype(bf16)
         for k in range(groups):
-            inner_grad[k, g * part : (g + 1) * part, :] = made[k * part : (k + 1) * part, :]
+            inner_grad[place_ref[k], g * part : (g + 1) * part, :] = made[k * part : (k + 1) * part, :]
     for r in range(groups):
         made = rows_tn(mixed[r][...], grad_one_low).astype(bf16)
-        inner_grad[place_ref[r], width : width + part, :] = made
+        inner_grad[r, width : width + part, :] = made
 
     sums = [
         jnp.sum(grad_one_low.astype(f32), axis=0, keepdims=True),
@@ -500,26 +509,29 @@
             tail = jnp.where(
                 line == len(sums) + i, bias_sum[:, i * part : (i + 1) * part], tail
             )
-        inner_grad[k, width + part : width + part + 16, 0:part] = tail.astype(bf16)
-
-
-def dense(places, mixed_pieces, tokens, cotangent, small, inner_bias, inner_pieces, outer_pieces):
+        inner_grad[place_ref[k], width + part : width + part + 16, 0:part] = tail.astype(bf16)
+    for i in range(groups // 2):
+        inner_keep[i] = inner_grad[2 * i]
+        inner_send[i] = inner_grad[2 * i + 1]
+
+
+def dense(places, mixed_pieces, tokens, cotangent, small, inner_bias, packs):
     rows, width = tokens.shape
-    groups = len(inner_pieces)
+    groups = len(packs)
     part = width // groups
     vmem = pl.BlockSpec(memory_space=pltpu.VMEM)
     hbm = pl.BlockSpec(memory_space=pl.ANY)
     return pl.pallas_call(
         dense_kernel,
-        in_specs=[pl.BlockSpec(memory_space=pltpu.SMEM)] + [vmem] * (groups + 4) + [hbm] * (2 * groups),
-        out_specs=[vmem] * 5,
+        in_specs=[pl.BlockSpec(memory_space=pltpu.SMEM)] + [vmem] * (groups + 4) + [hbm] * groups,
+        out_specs=[vmem] * 7,
         out_shape=[
             jax.ShapeDtypeStruct((rows, width), bf16),
             jax.ShapeDtypeStruct((rows, width), f32),
             jax.ShapeDtypeStruct((groups, rows, part), bf16),
-            jax.ShapeDtypeStruct((groups, width, width), bf16),
-            jax.ShapeDtypeStruct((groups, width + part + 64, width), bf16),
-        ],
+        ]
+        + [jax.ShapeDtypeStruct((groups // 2, width, width), bf16)] * 2
+        + [jax.ShapeDtypeStruct((groups // 2, width + part + 64, width), bf16)] * 2,
         scratch_shapes=[
             pltpu.VMEM((groups, part, width), bf16),
             pltpu.VMEM((groups, width, width), bf16),
@@ -527,6 +539,7 @@
             pltpu.VMEM((groups, rows, width), bf16),
             pltpu.VMEM((groups, rows, width), bf16),
             pltpu.VMEM((groups, rows, width), f32),
+            pltpu.VMEM((groups, width + part + 64, width), bf16),
             pltpu.SemaphoreType.DMA((groups + 2, groups)),
         ],
         compiler_params=pltpu.CompilerParams(vmem_limit_bytes=56 * 2**20),
@@ -536,7 +549,7 @@
             transcendentals=2 * rows * width * groups,
         ),
         name="layer_dense",
-    )(places, *mixed_pieces, tokens, cotangent, small, inner_bias, *inner_pieces, *outer_pieces)
+    )(places, *mixed_pieces, tokens, cotangent, small, inner_bias, *packs)
 
 def gather_kernel(place_ref, p0, p1, p2, p3, wide_ref, stat_ref, out_ref):
     rows, part = p0.shape
@@ -604,7 +617,7 @@
         here = slice(k * rows, (k + 1) * rows)
         made = rows_nt(pair_ref[here, :], weight[:, : 2 * part])
         made = made + rows_nt(query_ref[here, :], weight[:, 2 * part :])
-        back_ref[k] = made.astype(bf16)
+        back_ref[place_ref[k]] = made.astype(bf16)
 
 
 def head_grads(places, tokens, grad_query, grad_pair, weight_pieces):
@@ -634,19 +647,19 @@
     return (left.astype(f32) + right.astype(f32)).astype(bf16)
 
 
-def halves(block, bit, axis):
+def half_of(block, bit, axis):
     size = block.shape[axis] // 2
-    kept = lax.dynamic_slice_in_dim(block, bit * size, size, axis)
-    sent = lax.dynamic_slice_in_dim(block, (1 - bit) * size, size, axis)
-    return kept, sent
-
-
-def scatter_sum(block, axis_name, order, axis):
+    return lax.dynamic_slice_in_dim(block, bit * size, size, axis)
+
+
+def scatter_sum(terms, axis_name, order, axis):
     index = lax.axis_index(axis_name)
     for step in order:
-        kept, sent = halves(block, (index // step) % 2, axis)
-        block = both(kept, swapped(sent, axis_name, step))
-    return block
+        bit = (index // step) % 2
+        sent = functools.reduce(both, [half_of(x, 1 - bit, axis) for x in terms])
+        kept = functools.reduce(both, [half_of(x, bit, axis) for x in terms])
+        terms = [kept, swapped(sent, axis_name, step)]
+    return terms
 
 
 def gather_back(block, axis_name, order, axis):
@@ -743,27 +756,44 @@
     def halo(own):
         return [own if d == 0 else shifted(own, "ctx", d) for d in distances]
 
-    pairs = halo(pair)
+    even = c % 2 == 0
+    beside = swapped(pair, "ctx", 1)
+    before, after = shifted(pair, "ctx", 2), shifted(pair, "ctx", -2)
+    half = block // 2
+    route = [(i, i + 2 if i % 2 == 0 else i - 2) for i in range(cycle)]
+    route = [(i, j) for i, j in route if 0 <= j < cycle]
+    upper = swapped(jnp.where(even, after[:half], before[:half]), "ctx", 1)
+    lower = lax.ppermute(beside[half:], "ctx", route)
+    pairs = [before, after, pair, beside, upper, lower]
+    beside_at = jnp.where(even, reach + 1, reach - 1) * block
+    missing_at = jnp.where(even, reach - 1, reach + 1) * block
+    load_at = jnp.stack(
+        [0 * missing_at, 2 * reach * block + 0 * missing_at, reach * block + 0 * missing_at]
+        + [beside_at, missing_at, missing_at + half]
+    )
+    query_bounds = jnp.concatenate([query_bounds, load_at]).astype(jnp.int32)
 
     small_own = jnp.stack(
         [out_bias, first_gain, first_shift, outer_bias, second_gain, second_shift]
     )
     small_own = jnp.concatenate([small_own, inner_bias.reshape(-1, part)], axis=0)
     small_own = jnp.pad(small_own, ((0, 16 - small_own.shape[0]), (0, width - part)))
-    outer_own = jnp.concatenate([outer_weight, out_weight, small_own], axis=0)
-    inner_own, outer_own, _ = lax.optimization_barrier((inner_weight, outer_own, token_pieces[2]))
-    inner_pieces = spread(inner_own, swapped(inner_own, "wt", 1))
-    outer_pieces = spread(outer_own, swapped(outer_own, "wt", 1))
-    small = jnp.stack([x[width + part :, :part] for x in outer_pieces]).astype(f32)
+    inner_parts = [inner_weight[:, i * width : (i + 1) * width] for i in range(shards)]
+    pack = jnp.concatenate([outer_weight, out_weight, small_own] + inner_parts, axis=0)
+    pack, _ = lax.optimization_barrier((pack, token_pieces[2:] + weight_pieces[1:]))
+    pack_near, pack_far = swapped(pack, "wt", 1), swapped(pack, "wt", 2)
+    mixed, mixed_wide, stat_columns = attention_forward(query_bounds, queries, spans_column, pairs)
+    ready, _ = lax.optimization_barrier((queries, pairs))
+    query_halo = [queries if d == 0 else shifted(ready, "ctx", d) if d * d == 1 else None for d in distances]
+    close = [x for x, d in zip(query_halo, distances) if d * d == 1]
+    mixed, mixed_wide, stat_columns, close, pack_far = lax.optimization_barrier(
+        (mixed, mixed_wide, stat_columns, close, pack_far)
+    )
+    packs = [pack, pack_near, pack_far, swapped(pack_far, "wt", 1)]
+    small = jnp.stack([x[width + part : width + part + 16, :part] for x in packs]).astype(f32)
     small = [lax.dynamic_index_in_dim(small, w ^ k, 0, keepdims=False) for k in range(shards)]
     small_rows = jnp.concatenate([x[:8] for x in small], axis=1)
     inner_bias_rows = jnp.stack([x[6:10].reshape(-1) for x in small])
-
-    mixed, mixed_wide, stat_columns = attention_forward(query_bounds, queries, spans_column, pairs)
-    queries_sent, _ = lax.optimization_barrier((queries, pairs))
-    query_halo = [
-        queries if d == 0 else shifted(queries_sent, "ctx", d) for d in distances
-    ]
 
     mixed_rows = mixed.reshape(shards, rows, part)
     mixed_pieces = [
@@ -772,56 +802,49 @@
     mixed_pieces = [mixed_pieces[0]] + [
         swapped(mixed_pieces[r], "wt", r) for r in range(1, shards)
     ]
-    mixed_pieces, query_halo = lax.optimization_barrier((mixed_pieces, query_halo))
-    layer_out, grad_one, back, outer_grad, inner_grad = dense(
-        places,
-        mixed_pieces,
-        tokens,
-        cotangent,
-        small_rows,
-        inner_bias_rows,
-        inner_pieces,
-        outer_pieces,
-    )
+    far_ready, mixed_pieces = lax.optimization_barrier((queries, mixed_pieces))
+    results = dense(
+        places, mixed_pieces, tokens, cotangent, small_rows, inner_bias_rows, packs
+    )
+    remote = [shifted(far_ready, "ctx", d) for d in distances if d * d > 1]
+    results, remote = lax.optimization_barrier((results, remote))
+    layer_out, grad_one, back, outer_keep, outer_send, inner_keep, inner_send = results
+    query_halo = [remote[0], close[0], queries, close[1], remote[1]]
 
     back_pieces = [back[0]] + [swapped(back[r], "wt", r) for r in range(1, shards)]
-
-    def near_sum(grad):
-        kept, sent = halves(grad.reshape((2, 2) + grad.shape[1:]), w % 2, 1)
-        return both(kept, swapped(sent, "wt", 1))
-
-    def far_sum(grad):
-        kept, sent = halves(grad, w // 2, 0)
-        return both(kept, swapped(sent, "wt", 2))[0, 0]
-
-    outer_near = near_sum(outer_grad)
-    inner_near = near_sum(inner_grad)
+    outer_got = swapped(outer_send, "wt", 1)
+    inner_got = swapped(inner_send, "wt", 1)
     grads = gathered(places, back_pieces, mixed_wide, stat_columns)
+    grads, outer_got, inner_got = lax.optimization_barrier((grads, outer_got, inner_got))
+
+    def far_terms(keep, got):
+        return [both(keep[0], got[0]), swapped(both(keep[1], got[1]), "wt", 2)]
+
     grad_halo = halo(grads)
-    outer_far = far_sum(outer_near)
+    outer_terms = far_terms(outer_keep, outer_got)
     grad_query = attention_queries(
         query_bounds, queries, spans_column, grads, mixed_wide, stat_columns, pairs
     )
-    grad_query, grad_halo, outer_far, inner_near = lax.optimization_barrier(
-        (grad_query, grad_halo, outer_far, inner_near)
+    grad_query, grad_halo, outer_terms, inner_keep, inner_got = lax.optimization_barrier(
+        (grad_query, grad_halo, outer_terms, inner_keep, inner_got)
     )
 
     near_first = [1 << i for i in range(cycle.bit_length() - 1)]
-    far_first = [2, 1] + near_first[2:]
-    outer_part = scatter_sum(outer_far, "ctx", near_first[:1], 0)
-    inner_far = far_sum(inner_near)
+    outer_terms = scatter_sum(outer_terms, "ctx", near_first[:1], 0)
+    inner_terms = far_terms(inner_keep, inner_got)
     grad_pair = attention_keys(key_bounds, pair, spans_row, query_halo, grad_halo)
-    grad_pair, outer_part, inner_far = lax.optimization_barrier(
-        (grad_pair, outer_part, inner_far)
+    grad_pair, outer_terms, inner_terms = lax.optimization_barrier(
+        (grad_pair, outer_terms, inner_terms)
     )
 
     head_grad, token_partial = head_grads(places, block_tokens, grad_query, grad_pair, weight_pieces)
-    outer_part = scatter_sum(outer_part, "ctx", near_first[1:], 0)
-    inner_part = scatter_sum(inner_far, "ctx", far_first, 0)
-    head_part = scatter_sum(head_grad, "ctx", near_first, 1)
-    token_sum = far_sum(near_sum(token_partial))
+    outer_part = both(*scatter_sum(outer_terms, "ctx", near_first[1:], 0))
+    inner_part = both(*scatter_sum(inner_terms, "ctx", near_first, 0))
+    head_part = both(*scatter_sum([head_grad], "ctx", near_first, 1))
+    token_got = swapped(token_partial[1::2], "wt", 1)
+    token_sum = both(*far_terms(token_partial[0::2], token_got))
     outer_total = gather_back(outer_part, "ctx", near_first, 0)
-    inner_total = gather_back(inner_part, "ctx", far_first, 0)
+    inner_total = gather_back(inner_part, "ctx", near_first, 0)
     head_pieces = [
         lax.dynamic_index_in_dim(head_part, w ^ r, 0, keepdims=False) for r in range(shards)
     ]

time: 463 us -> 348 us (0.75)
  waiting for transfers between devices: 211 us -> 108 us
  local copies, waits for them, and re-layouts: 44.3 us -> 25.3 us
    ppermute x45 -> x44, waiting for transfers between devices: 151 us -> 81.2 us  [swapped(): return lax.ppermute(block, axis, [(i, i ^ bit) for i in range(count)])]
    ppermute x12 -> x10, waiting for transfers between devices: 60.3 us -> 23.6 us  [shifted(): return lax.ppermute(block, axis, route)]
    dynamic_slice x15 -> x1, local copies, waits for them, and re-layouts: 15 us -> 0.05 us  [half_of(): return lax.dynamic_slice_in_dim(block, bit * size, size, axis)]
    unnamed x134 -> x116, local copies, waits for them, and re-layouts: 19.2 us -> 12.1 us
    squeeze x2 -> x0, other arithmetic: 6.44 us -> none  [far_sum(): return both(kept, swapped(sent, 'wt', 2))[0, 0]]
    convert_element_type x12 -> x14, other arithmetic: 9.92 us -> 15.7 us  [both(): return (left.astype(f32) + right.astype(f32)).astype(bf16)]
    ppermute x45 -> x44, starting transfers between devices: 54.8 us -> 52 us  [swapped(): return lax.ppermute(block, axis, [(i, i ^ bit) for i in range(count)])]
    ppermute x12 -> x10, starting transfers between devices: 30.5 us -> 33.3 us  [shifted(): return lax.ppermute(block, axis, route)]
  transfers between devices with their start and end apart: 57 -> 55, of which waited for: 30 -> 27; matrix products, arithmetic and copies ran while one was open for 11% -> 14% of each run, Pallas kernels for 12% -> 22%
where the time goes in v3:
time: 348 us
  waiting for transfers between devices  108 us (31%)
  starting transfers between devices  89.5 us (26%)
  Pallas kernels  85.8 us (25%)
  other arithmetic  37.5 us (11%)
  local copies, waits for them, and re-layouts  25.3 us (7%)
    ppermute x44, waiting for transfers between devices, swapped(): return lax.ppermute(block, axis, [(i, i ^ bit) for i in range(count)])  81.2 us
    ppermute x44, starting transfers between devices, swapped(): return lax.ppermute(block, axis, [(i, i ^ bit) for i in range(count)])  52 us
    ppermute x10, starting transfers between devices, shifted(): return lax.ppermute(block, axis, route)  33.3 us
    ppermute x10, waiting for transfers between devices, shifted(): return lax.ppermute(block, axis, route)  23.6 us
    pallas_call x1, Pallas kernels, dense(): pl.pallas_call(dense_kernel, in_specs=[pl.BlockSpec(memory_space=pltpu.SM...  23.2 us
    pallas_call x1, Pallas kernels, attention_keys(): pl.pallas_call(functools.partial(key_kernel, count // 2), grid_spec=pltpu...  18.5 us
    pallas_call x1, Pallas kernels, attention_forward(): pl.pallas_call(forward_kernel, grid_spec=pltpu.PrefetchScalarGridSpec(num...  16.5 us
    pallas_call x1, Pallas kernels, attention_queries(): pl.pallas_call(query_kernel, grid_spec=pltpu.PrefetchScalarGridSpec(num_s...  15.8 us
  transfers between devices with their start and end apart: 55, of which 27 were waited for; matrix products, arithmetic and copies ran while one was open for 14% of the time, Pallas kernels for 22%

profile of v3, /device:TPU:0, one launch (start us, length us, event | category | flops | bytes accessed | tf_op | source)
XLA Modules:
  0.0 347.7 jit_solution(2289320946498093124)
XLA Ops:
  23.0 4.3 %layer_projection.1 = (bf16[1024,768]{1,0:T(8,128)(2,1)S(1)}, bf16[1024,192]{1,0:T(8,128)(2,1)}, bf16[1024,384]{1,0:T(8,128)(2,1)}) custom-call(s32[4]{0:T(128)S(1)} %pad_add_fusion.2.place_ref, bf16[256,768]{1,0:T(8,128)(2,1)S(1)} %copy-done.21, bf16[256,768]{1,0:T(8,128)(2,1)S(1)} %collective-permute-done.near, ...), custom_call_target="tpu_custom_call" | custom-call | flops 905969664 | bytes 5242880 | tf_op jit(solution)/shard_map/layer_projection/pallas_call | solution.py:357
  39.8 10.0 %collective-permute-done.6.rest_0_ = bf16[1024,384]{1,0:T(8,128)(2,1)S(1)} collective-permute-done((bf16[1024,384]{1,0:T(8,128)(2,1)}, bf16[1024,384]{1,0:T(8,128)(2,1)S(1)}, u32[]{:S(2)}, u32[]{:S(2)}) %collective-permute-start.6) | collective-permute-done | bytes 786464 | tf_op jit(solution)/shard_map/ppermute | solution.py:32
  49.8 4.1 %collective-permute-done.7.rest_1_ = bf16[1024,384]{1,0:T(8,128)(2,1)S(1)} collective-permute-done((bf16[1024,384]{1,0:T(8,128)(2,1)}, bf16[1024,384]{1,0:T(8,128)(2,1)S(1)}, u32[]{:S(2)}, u32[]{:S(2)}) %collective-permute-start.7) | collective-permute-done | bytes 786464 | tf_op jit(solution)/shard_map/ppermute | solution.py:32
  57.1 4.2 %collective-permute-start.10 = (bf16[512,384]{1,0:T(8,128)(2,1)}, bf16[512,384]{1,0:T(8,128)(2,1)}, u32[]{:S(2)}, u32[]{:S(2)}) collective-permute-start(bf16[512,384]{1,0:T(8,128)(2,1)} %slice.342), channel_id=1, source_target_pairs={{0,8},{8,16},{12,4},{16,24},{20,12},{28,20},{1,9},{9,17},{13,5},{1... | collective-permute-start | bytes 1179656 | tf_op jit(solution)/shard_map/ppermute | solution.py:766
  61.5 4.2 %collective-permute-done.9.rest_4_ = bf16[512,384]{1,0:T(8,128)(2,1)S(1)} collective-permute-done((bf16[512,384]{1,0:T(8,128)(2,1)}, bf16[512,384]{1,0:T(8,128)(2,1)S(1)}, u32[]{:S(2)}, u32[]{:S(2)}) %collective-permute-start.9) | collective-permute-done | bytes 393248 | tf_op jit(solution)/shard_map/ppermute | solution.py:26
  68.8 4.8 %collective-permute-start.11 = (bf16[1024,192]{1,0:T(8,128)(2,1)}, bf16[1024,192]{1,0:T(8,128)(2,1)}, u32[]{:S(2)}, u32[]{:S(2)}) collective-permute-start(bf16[1024,192]{1,0:T(8,128)(2,1)} %get-tuple-element.92.q_ref.rest_2_), channel_id=1, source_target_pairs={{0,4},{4,8},{8,12},{12,16},{16,20},{20,24},{24,28},{1,5},{5,9},{9,... | collective-permute-start | bytes 1179656 | tf_op jit(solution)/shard_map/ppermute | solution.py:32
  78.9 16.5 %attention_forward.1 = (bf16[1024,192]{1,0:T(8,128)(2,1)S(1)}, f32[1024,192]{1,0:T(8,128)S(1)}, f32[1024,128]{1,0:T(8,128)S(1)}) custom-call(s32[14]{0:T(128)S(1)} %concatenate.101.bounds, bf16[1024,192]{1,0:T(8,128)(2,1)} %get-tuple-element.92.q_ref.rest_2_, s32[1024,8]{1,0:T(8,128)S(1)} %copy.39.span_ref, bf16[1024,384]{1,0:T(8,128)(2,1)S(1)} %copy-done.4, ...), custom_call_target="tpu_custom_call" | custom-call | flops 1811939328 | bytes 6291456 | tf_op jit(solution)/shard_map/attention_forward/pallas_call | solution.py:128
  106.4 12.2 %collective-permute-start.19 = (bf16[1024,192]{1,0:T(8,128)(2,1)}, bf16[1024,192]{1,0:T(8,128)(2,1)S(1)}, u32[]{:S(2)}, u32[]{:S(2)}) collective-permute-start(bf16[1024,192]{1,0:T(8,128)(2,1)} %get-tuple-element.92.q_ref.rest_2_), channel_id=1, source_target_pairs={{0,8},{4,12},{8,16},{12,20},{16,24},{20,28},{1,9},{5,13},{9,17},{1... | collective-permute-start | bytes 1179656 | tf_op jit(solution)/shard_map/ppermute | solution.py:32
  122.5 23.2 %layer_dense.1 = (bf16[256,768]{1,0:T(8,128)(2,1)}, f32[256,768]{1,0:T(8,128)}, bf16[4,256,192]{2,1,0:T(8,128)(2,1)}, bf16[2,768,768]{2,1,0:T(8,128)(2,1)}, bf16...) custom-call(s32[4]{0:T(128)} %copy-done.9, ...), custom_call_target="tpu_custom_call" | custom-call | flops 14495514624 | bytes 25165824 | tf_op jit(solution)/shard_map/layer_dense/pallas_call | solution.py:524
  161.9 4.6 %collective-permute-start.26 = (bf16[1024,256]{1,0:T(8,128)(2,1)S(1)}, bf16[1024,256]{1,0:T(8,128)(2,1)S(1)}, u32[]{:S(2)}, u32[]{:S(2)}) collective-permute-start(bf16[1024,256]{1,0:T(8,128)(2,1)S(1)} %layer_gather.1.grad_ref.rest_7_), channel_id=1, source_target_pairs={{0,8},{4,12},{8,16},{12,20},{16,24},{20,28},{1,9},{5,13},{9,17},{1... | collective-permute-start | bytes 1572872 | tf_op jit(solution)/shard_map/ppermute | solution.py:32
  170.7 15.8 %attention_queries.1.query_ref = bf16[1024,192]{1,0:T(8,128)(2,1)S(1)} custom-call(s32[14]{0:T(128)S(1)} %concatenate.101.bounds, bf16[1024,192]{1,0:T(8,128)(2,1)} %get-tuple-element.92.q_ref.rest_2_, s32[1024,8]{1,0:T(8,128)S(1)} %copy.39.span_ref, bf16[1024,256]{1,0:T(8,128)(2,1)S(1)} %layer_gather.1.grad_ref.rest_7_, ...), custom_call_target="tpu_custom_call" | custom-call | flops 2717908992 | bytes 6291456 | tf_op jit(solution)/shard_map/attention_queries/pallas_call | solution.py:218
  186.6 3.8 %collective-permute-done.27.rest_6_ = bf16[1024,256]{1,0:T(8,128)(2,1)S(1)} collective-permute-done((bf16[1024,256]{1,0:T(8,128)(2,1)S(1)}, bf16[1024,256]{1,0:T(8,128)(2,1)S(1)}, u32[]{:S(2)}, u32[]{:S(2)}) %collective-permute-start.27) | collective-permute-done | bytes 524320 | tf_op jit(solution)/shard_map/ppermute | solution.py:32
  190.4 5.7 %collective-permute-done.29.rest_9_ = bf16[1024,256]{1,0:T(8,128)(2,1)S(1)} collective-permute-done((bf16[1024,256]{1,0:T(8,128)(2,1)S(1)}, bf16[1024,256]{1,0:T(8,128)(2,1)S(1)}, u32[]{:S(2)}, u32[]{:S(2)}) %collective-permute-start.29) | collective-permute-done | bytes 524320 | tf_op jit(solution)/shard_map/ppermute | solution.py:32
  203.6 18.5 %attention_keys.1.pair_ref = bf16[1024,384]{1,0:T(8,128)(2,1)S(1)} custom-call(s32[8]{0:T(128)S(1)} %reshape.130.bounds, bf16[1024,384]{1,0:T(8,128)(2,1)} %get-tuple-element.73.rest_2_.kv_ref, s32[8,5120]{1,0:T(8,128)S(1)} %add_add_fusion.span_ref, bf16[1024,192]{1,0:T(8,128)(2,1)S(1)} %copy-done.12, bf16[1024,192]{1,0:T(8,128)(2,1)} %collective-permute-done.11.rest_1_, ...), custom_call_target="tpu_custom_call" | custom-call | flops 3623878656 | bytes 8388608 | tf_op jit(solution)/shard_map/attention_keys/pallas_call | solution.py:307
  222.2 12.1 %collective-permute-done.32 = bf16[1024,768]{1,0:T(8,128)(2,1)} collective-permute-done((bf16[1024,768]{1,0:T(8,128)(2,1)}, bf16[1024,768]{1,0:T(8,128)(2,1)}, u32[]{:S(2)}, u32[]{:S(2)}) %collective-permute-start.32) | collective-permute-done | bytes 1572896 | tf_op jit(solution)/shard_map/ppermute | solution.py:26
  234.2 5.1 %layer_heads.1 = (bf16[4,192,640]{2,1,0:T(8,128)(2,1)S(1)}, bf16[4,256,768]{2,1,0:T(8,128)(2,1)S(1)}) custom-call(s32[4]{0:T(128)S(1)} %copy-done.10, bf16[1024,768]{1,0:T(8,128)(2,1)S(1)} %copy-done.29, bf16[1024,192]{1,0:T(8,128)(2,1)S(1)} %copy-done.31, bf16[1024,384]{1,0:T(8,128)(2,1)S(1)} %attention_keys.1.pair_ref, ...), custom_call_target="tpu_custom_call" | custom-call | flops 1811939328 | bytes 8388608 | tf_op jit(solution)/shard_map/layer_heads/pallas_call | solution.py:627
  263.2 4.3 %collective-permute-start.37 = (bf16[4,24,640]{2,1,0:T(8,128)(2,1)S(1)}, bf16[4,24,640]{2,1,0:T(8,128)(2,1)S(1)}, u32[]{:S(2)}, u32[]{:S(2)}) collective-permute-start(bf16[4,24,640]{2,1,0:T(8,128)(2,1)S(1)} %add_convert_fusion.23), channel_id=1, source_target_pairs={{0,16},{4,20},{8,24},{12,28},{16,0},{20,4},{24,8},{28,12},{1,17},{... | collective-permute-start | bytes 368648 | tf_op jit(solution)/shard_map/ppermute | solution.py:26
  267.8 3.7 %collective-permute-start.45 = (bf16[256,768]{1,0:T(8,128)(2,1)S(1)}, bf16[256,768]{1,0:T(8,128)(2,1)S(1)}, u32[]{:S(2)}, u32[]{:S(2)}) collective-permute-start(bf16[256,768]{1,0:T(8,128)(2,1)S(1)} %get-tuple-element.145), channel_id=1, source_target_pairs={{0,8},{4,12},{8,0},{12,4},{16,24},{20,28},{24,16},{28,20},{1,9},{5... | collective-permute-start | bytes 1179656 | tf_op jit(solution)/shard_map/ppermute | solution.py:26
  271.5 4.2 %collective-permute-done.37 = bf16[4,24,640]{2,1,0:T(8,128)(2,1)S(1)} collective-permute-done((bf16[4,24,640]{2,1,0:T(8,128)(2,1)S(1)}, bf16[4,24,640]{2,1,0:T(8,128)(2,1)S(1)}, u32[]{:S(2)}, u32[]{:S(2)}) %collective-permute-start.37) | collective-permute-done | bytes 122912 | tf_op jit(solution)/shard_map/ppermute | solution.py:26
  288.3 6.0 %collective-permute-start.42 = (bf16[4,48,640]{2,1,0:T(8,128)(2,1)S(1)}, bf16[4,48,640]{2,1,0:T(8,128)(2,1)S(1)}, u32[]{:S(2)}, u32[]{:S(2)}) collective-permute-start(bf16[4,48,640]{2,1,0:T(8,128)(2,1)S(1)} %maximum_select_fusion.8), channel_id=1, source_target_pairs={{0,8},{4,12},{8,0},{12,4},{16,24},{20,28},{24,16},{28,20},{1,9},{5... | collective-permute-start | bytes 737288 | tf_op jit(solution)/shard_map/ppermute | solution.py:26
  294.3 4.3 %collective-permute-done.46 = bf16[128,768]{1,0:T(8,128)(2,1)S(1)} collective-permute-done((bf16[128,768]{1,0:T(8,128)(2,1)S(1)}, bf16[128,768]{1,0:T(8,128)(2,1)S(1)}, u32[]{:S(2)}, u32[]{:S(2)}) %collective-permute-start.46) | collective-permute-done | bytes 196640 | tf_op jit(solution)/shard_map/ppermute | solution.py:26
  301.9 8.3 %collective-permute-done.47 = bf16[128,768]{1,0:T(8,128)(2,1)S(1)} collective-permute-done((bf16[128,768]{1,0:T(8,128)(2,1)S(1)}, bf16[128,768]{1,0:T(8,128)(2,1)S(1)}, u32[]{:S(2)}, u32[]{:S(2)}) %collective-permute-start.47) | collective-permute-done | bytes 196640 | tf_op jit(solution)/shard_map/ppermute | solution.py:26
  318.3 6.1 %collective-permute-done.43 = bf16[4,96,640]{2,1,0:T(8,128)(2,1)S(1)} collective-permute-done((bf16[4,96,640]{2,1,0:T(8,128)(2,1)S(1)}, bf16[4,96,640]{2,1,0:T(8,128)(2,1)S(1)}, u32[]{:S(2)}, u32[]{:S(2)}) %collective-permute-start.43) | collective-permute-done | bytes 491552 | tf_op jit(solution)/shard_map/ppermute | solution.py:26
  329.5 13.7 %collective-permute-done.49 = bf16[512,768]{1,0:T(8,128)(2,1)S(1)} collective-permute-done((bf16[512,768]{1,0:T(8,128)(2,1)S(1)}, bf16[512,768]{1,0:T(8,128)(2,1)S(1)}, u32[]{:S(2)}, u32[]{:S(2)}) %collective-permute-start.49) | collective-permute-done | bytes 786464 | tf_op jit(solution)/shard_map/ppermute | solution.py:26
  (311 shorter events, 146.4 us)
Async XLA Ops:
  3.7 19.2 %collective-permute-start = (bf16[256,768]{1,0:T(8,128)(2,1)}, bf16[256,768]{1,0:T(8,128)(2,1)S(1)}, u32[]{:S(2)}, u32[]{:S(2)}) collective-permute-start(bf16[256,768]{1,0:T(8,128)(2,1)} %refs_4_.1), channel_id=1, source_target_pairs={{0,1},{1,0},{2,3},{3,2},{4,5},{5,4},{6,7},{7,6},{8,9},{9,8},{10,11... | collective-permute-start | bytes 1179656 | tf_op jit(solution)/shard_map/ppermute | solution.py:26
  28.4 21.4 %collective-permute-start.6 = (bf16[1024,384]{1,0:T(8,128)(2,1)}, bf16[1024,384]{1,0:T(8,128)(2,1)S(1)}, u32[]{:S(2)}, u32[]{:S(2)}) collective-permute-start(bf16[1024,384]{1,0:T(8,128)(2,1)} %get-tuple-element.73.rest_2_.kv_ref), channel_id=1, source_target_pairs={{0,8},{4,12},{8,16},{12,20},{16,24},{20,28},{1,9},{5,13},{9,17},{1... | collective-permute-start | bytes 2359304 | tf_op jit(solution)/shard_map/ppermute | solution.py:32
  32.0 21.9 %collective-permute-start.7 = (bf16[1024,384]{1,0:T(8,128)(2,1)}, bf16[1024,384]{1,0:T(8,128)(2,1)S(1)}, u32[]{:S(2)}, u32[]{:S(2)}) collective-permute-start(bf16[1024,384]{1,0:T(8,128)(2,1)} %get-tuple-element.73.rest_2_.kv_ref), channel_id=1, source_target_pairs={{8,0},{12,4},{16,8},{20,12},{24,16},{28,20},{9,1},{13,5},{17,9},{2... | collective-permute-start | bytes 2359304 | tf_op jit(solution)/shard_map/ppermute | solution.py:32
  34.0 61.5 %collective-permute-start.13 = (bf16[1744,768]{1,0:T(8,128)(2,1)}, bf16[1744,768]{1,0:T(8,128)(2,1)}, u32[]{:S(2)}, u32[]{:S(2)}) collective-permute-start(bf16[1744,768]{1,0:T(8,128)(2,1)} %slice_dynamic-update-slice_fusion.refs_8_), channel_id=1, source_target_pairs={{0,2},{1,3},{2,0},{3,1},{4,6},{5,7},{6,4},{7,5},{8,10},{9,11},{10,... | collective-permute-start | bytes 8036360 | tf_op jit(solution)/shard_map/ppermute | solution.py:26
  35.2 21.1 %collective-permute-start.8 = (bf16[1024,384]{1,0:T(8,128)(2,1)}, bf16[1024,384]{1,0:T(8,128)(2,1)S(1)}, u32[]{:S(2)}, u32[]{:S(2)}) collective-permute-start(bf16[1024,384]{1,0:T(8,128)(2,1)} %get-tuple-element.73.rest_2_.kv_ref), channel_id=1, source_target_pairs={{0,4},{4,0},{8,12},{12,8},{16,20},{20,16},{24,28},{28,24},{1,5},{5... | collective-permute-start | bytes 2359304 | tf_op jit(solution)/shard_map/ppermute | solution.py:26
  68.8 26.7 %collective-permute-start.11 = (bf16[1024,192]{1,0:T(8,128)(2,1)}, bf16[1024,192]{1,0:T(8,128)(2,1)}, u32[]{:S(2)}, u32[]{:S(2)}) collective-permute-start(bf16[1024,192]{1,0:T(8,128)(2,1)} %get-tuple-element.92.q_ref.rest_2_), channel_id=1, source_target_pairs={{0,4},{4,8},{8,12},{12,16},{16,20},{20,24},{24,28},{1,5},{5,9},{9,... | collective-permute-start | bytes 1179656 | tf_op jit(solution)/shard_map/ppermute | solution.py:32
  73.6 21.9 %collective-permute-start.12 = (bf16[1024,192]{1,0:T(8,128)(2,1)}, bf16[1024,192]{1,0:T(8,128)(2,1)}, u32[]{:S(2)}, u32[]{:S(2)}) collective-permute-start(bf16[1024,192]{1,0:T(8,128)(2,1)} %get-tuple-element.92.q_ref.rest_2_), channel_id=1, source_target_pairs={{4,0},{8,4},{12,8},{16,12},{20,16},{24,20},{28,24},{5,1},{9,5},{13... | collective-permute-start | bytes 1179656 | tf_op jit(solution)/shard_map/ppermute | solution.py:32
  75.0 25.0 %collective-permute-start.17 = (bf16[1744,768]{1,0:T(8,128)(2,1)}, bf16[1744,768]{1,0:T(8,128)(2,1)}, u32[]{:S(2)}, u32[]{:S(2)}) collective-permute-start(bf16[1744,768]{1,0:T(8,128)(2,1)} %slice_dynamic-update-slice_fusion.refs_8_), channel_id=1, source_target_pairs={{0,1},{1,0},{2,3},{3,2},{4,5},{5,4},{6,7},{7,6},{8,9},{9,8},{10,11... | collective-permute-start | bytes 8036360 | tf_op jit(solution)/shard_map/ppermute | solution.py:26
  95.5 24.6 %collective-permute-start.18 = (bf16[1744,768]{1,0:T(8,128)(2,1)}, bf16[1744,768]{1,0:T(8,128)(2,1)}, u32[]{:S(2)}, u32[]{:S(2)}) collective-permute-start(bf16[1744,768]{1,0:T(8,128)(2,1)} %collective-permute-done.13.refs_10_), channel_id=1, source_target_pairs={{0,1},{1,0},{2,3},{3,2},{4,5},{5,4},{6,7},{7,6},{8,9},{9,8},{10,11... | collective-permute-start | bytes 8036360 | tf_op jit(solution)/shard_map/ppermute | solution.py:26
  106.4 39.3 %collective-permute-start.19 = (bf16[1024,192]{1,0:T(8,128)(2,1)}, bf16[1024,192]{1,0:T(8,128)(2,1)S(1)}, u32[]{:S(2)}, u32[]{:S(2)}) collective-permute-start(bf16[1024,192]{1,0:T(8,128)(2,1)} %get-tuple-element.92.q_ref.rest_2_), channel_id=1, source_target_pairs={{0,8},{4,12},{8,16},{12,20},{16,24},{20,28},{1,9},{5,13},{9,17},{1... | collective-permute-start | bytes 1179656 | tf_op jit(solution)/shard_map/ppermute | solution.py:32
  118.6 27.2 %collective-permute-start.20 = (bf16[1024,192]{1,0:T(8,128)(2,1)}, bf16[1024,192]{1,0:T(8,128)(2,1)}, u32[]{:S(2)}, u32[]{:S(2)}) collective-permute-start(bf16[1024,192]{1,0:T(8,128)(2,1)} %get-tuple-element.92.q_ref.rest_2_), channel_id=1, source_target_pairs={{8,0},{12,4},{16,8},{20,12},{24,16},{28,20},{9,1},{13,5},{17,9},{2... | collective-permute-start | bytes 1179656 | tf_op jit(solution)/shard_map/ppermute | solution.py:32
  160.3 35.8 %collective-permute-start.30 = (bf16[768,768]{1,0:T(8,128)(2,1)S(1)}, bf16[768,768]{1,0:T(8,128)(2,1)S(1)}, u32[]{:S(2)}, u32[]{:S(2)}) collective-permute-start(bf16[768,768]{1,0:T(8,128)(2,1)S(1)} %get-tuple-element.133), channel_id=1, source_target_pairs={{0,2},{1,3},{2,0},{3,1},{4,6},{5,7},{6,4},{7,5},{8,10},{9,11},{10,... | collective-permute-start | bytes 3538952 | tf_op jit(solution)/shard_map/ppermute | solution.py:26
  161.9 24.6 %collective-permute-start.26 = (bf16[1024,256]{1,0:T(8,128)(2,1)S(1)}, bf16[1024,256]{1,0:T(8,128)(2,1)S(1)}, u32[]{:S(2)}, u32[]{:S(2)}) collective-permute-start(bf16[1024,256]{1,0:T(8,128)(2,1)S(1)} %layer_gather.1.grad_ref.rest_7_), channel_id=1, source_target_pairs={{0,8},{4,12},{8,16},{12,20},{16,24},{20,28},{1,9},{5,13},{9,17},{1... | collective-permute-start | bytes 1572872 | tf_op jit(solution)/shard_map/ppermute | solution.py:32
  166.5 23.9 %collective-permute-start.27 = (bf16[1024,256]{1,0:T(8,128)(2,1)S(1)}, bf16[1024,256]{1,0:T(8,128)(2,1)S(1)}, u32[]{:S(2)}, u32[]{:S(2)}) collective-permute-start(bf16[1024,256]{1,0:T(8,128)(2,1)S(1)} %layer_gather.1.grad_ref.rest_7_), channel_id=1, source_target_pairs={{0,4},{4,8},{8,12},{12,16},{16,20},{20,24},{24,28},{1,5},{5,9},{9,... | collective-permute-start | bytes 1572872 | tf_op jit(solution)/shard_map/ppermute | solution.py:32
  167.9 22.5 %collective-permute-start.28 = (bf16[1024,256]{1,0:T(8,128)(2,1)S(1)}, bf16[1024,256]{1,0:T(8,128)(2,1)S(1)}, u32[]{:S(2)}, u32[]{:S(2)}) collective-permute-start(bf16[1024,256]{1,0:T(8,128)(2,1)S(1)} %layer_gather.1.grad_ref.rest_7_), channel_id=1, source_target_pairs={{4,0},{8,4},{12,8},{16,12},{20,16},{24,20},{28,24},{5,1},{9,5},{13... | collective-permute-start | bytes 1572872 | tf_op jit(solution)/shard_map/ppermute | solution.py:32
  169.2 26.9 %collective-permute-start.29 = (bf16[1024,256]{1,0:T(8,128)(2,1)S(1)}, bf16[1024,256]{1,0:T(8,128)(2,1)S(1)}, u32[]{:S(2)}, u32[]{:S(2)}) collective-permute-start(bf16[1024,256]{1,0:T(8,128)(2,1)S(1)} %layer_gather.1.grad_ref.rest_7_), channel_id=1, source_target_pairs={{8,0},{12,4},{16,8},{20,12},{24,16},{28,20},{9,1},{13,5},{17,9},{2... | collective-permute-start | bytes 1572872 | tf_op jit(solution)/shard_map/ppermute | solution.py:32
  198.7 35.6 %collective-permute-start.32 = (bf16[1024,768]{1,0:T(8,128)(2,1)}, bf16[1024,768]{1,0:T(8,128)(2,1)}, u32[]{:S(2)}, u32[]{:S(2)}) collective-permute-start(bf16[1024,768]{1,0:T(8,128)(2,1)} %get-tuple-element.131), channel_id=1, source_target_pairs={{0,2},{1,3},{2,0},{3,1},{4,6},{5,7},{6,4},{7,5},{8,10},{9,11},{10,... | collective-permute-start | bytes 4718600 | tf_op jit(solution)/shard_map/ppermute | solution.py:26
  202.5 19.6 %collective-permute-start.31 = (bf16[384,768]{1,0:T(8,128)(2,1)}, bf16[384,768]{1,0:T(8,128)(2,1)}, u32[]{:S(2)}, u32[]{:S(2)}) collective-permute-start(bf16[384,768]{1,0:T(8,128)(2,1)} %get-tuple-element.137), channel_id=1, source_target_pairs={{0,4},{4,0},{8,12},{12,8},{16,20},{20,16},{24,28},{28,24},{1,5},{5... | collective-permute-start | bytes 1769480 | tf_op jit(solution)/shard_map/ppermute | solution.py:26
  246.9 20.7 %collective-permute-start.44 = (bf16[512,768]{1,0:T(8,128)(2,1)S(1)}, bf16[512,768]{1,0:T(8,128)(2,1)S(1)}, u32[]{:S(2)}, u32[]{:S(2)}) collective-permute-start(bf16[512,768]{1,0:T(8,128)(2,1)S(1)} %get-tuple-element.136), channel_id=1, source_target_pairs={{0,4},{4,0},{8,12},{12,8},{16,20},{20,16},{24,28},{28,24},{1,5},{5... | collective-permute-start | bytes 2359304 | tf_op jit(solution)/shard_map/ppermute | solution.py:26
  258.4 26.4 %collective-permute-start.33 = (bf16[2,256,768]{2,1,0:T(8,128)(2,1)S(1)}, bf16[2,256,768]{2,1,0:T(8,128)(2,1)S(1)}, u32[]{:S(2)}, u32[]{:S(2)}) collective-permute-start(bf16[2,256,768]{2,1,0:T(8,128)(2,1)S(1)} %get-tuple-element.147), channel_id=1, source_target_pairs={{0,1},{1,0},{2,3},{3,2},{4,5},{5,4},{6,7},{7,6},{8,9},{9,8},{10,11... | collective-permute-start | bytes 2359304 | tf_op jit(solution)/shard_map/ppermute | solution.py:26
  277.8 21.0 %collective-permute-start.53 = (bf16[192,768]{1,0:T(8,128)(2,1)S(1)}, bf16[192,768]{1,0:T(8,128)(2,1)S(1)}, u32[]{:S(2)}, u32[]{:S(2)}) collective-permute-start(bf16[192,768]{1,0:T(8,128)(2,1)S(1)} %maximum_select_fusion.7), channel_id=1, source_target_pairs={{0,8},{4,12},{8,0},{12,4},{16,24},{20,28},{24,16},{28,20},{1,9},{5... | collective-permute-start | bytes 884744 | tf_op jit(solution)/shard_map/ppermute | solution.py:26
  285.8 24.6 %collective-permute-start.34 = (bf16[256,768]{1,0:T(8,128)(2,1)}, bf16[256,768]{1,0:T(8,128)(2,1)}, u32[]{:S(2)}, u32[]{:S(2)}) collective-permute-start(bf16[256,768]{1,0:T(8,128)(2,1)} %fusion.7), channel_id=1, source_target_pairs={{0,2},{1,3},{2,0},{3,1},{4,6},{5,7},{6,4},{7,5},{8,10},{9,11},{10,... | collective-permute-start | bytes 1179656 | tf_op jit(solution)/shard_map/ppermute | solution.py:26
  301.3 23.0 %collective-permute-start.43 = (bf16[4,96,640]{2,1,0:T(8,128)(2,1)S(1)}, bf16[4,96,640]{2,1,0:T(8,128)(2,1)S(1)}, u32[]{:S(2)}, u32[]{:S(2)}) collective-permute-start(bf16[4,96,640]{2,1,0:T(8,128)(2,1)S(1)} %maximum_select_fusion.5), channel_id=1, source_target_pairs={{0,4},{4,0},{8,12},{12,8},{16,20},{20,16},{24,28},{28,24},{1,5},{5... | collective-permute-start | bytes 1474568 | tf_op jit(solution)/shard_map/ppermute | solution.py:26
  325.1 18.1 %collective-permute-start.49 = (bf16[512,768]{1,0:T(8,128)(2,1)S(1)}, bf16[512,768]{1,0:T(8,128)(2,1)S(1)}, u32[]{:S(2)}, u32[]{:S(2)}) collective-permute-start(bf16[512,768]{1,0:T(8,128)(2,1)S(1)} %maximum_select_fusion.3), channel_id=1, source_target_pairs={{0,4},{4,0},{8,12},{12,8},{16,20},{20,16},{24,28},{28,24},{1,5},{5... | collective-permute-start | bytes 2359304 | tf_op jit(solution)/shard_map/ppermute | solution.py:26
  (86 other events, 897.9 us)

commit v4 on v3

--- a/solution.py
+++ b/solution.py
@@ -150,7 +150,7 @@
             jax.ShapeDtypeStruct((block, 192), f32),
             jax.ShapeDtypeStruct((block, 128), f32),
         ],
-        compiler_params=pltpu.CompilerParams(vmem_limit_bytes=40 * 2**20),
+        compiler_params=pltpu.CompilerParams(vmem_limit_bytes=60 * 2**20),
         cost_estimate=pl.CostEstimate(
             flops=4 * block * 2304 * 192, bytes_accessed=6 * 2**20, transcendentals=block * 2304 * 3
         ),
@@ -230,7 +230,7 @@
             ],
         ),
         out_shape=jax.ShapeDtypeStruct((block, 192), bf16),
-        compiler_params=pltpu.CompilerParams(vmem_limit_bytes=40 * 2**20),
+        compiler_params=pltpu.CompilerParams(vmem_limit_bytes=60 * 2**20),
         cost_estimate=pl.CostEstimate(
             flops=6 * block * 2304 * 192, bytes_accessed=6 * 2**20, transcendentals=block * 2304 * 3
         ),
@@ -321,7 +321,7 @@
             ],
         ),
         out_shape=jax.ShapeDtypeStruct((block, 384), bf16),
-        compiler_params=pltpu.CompilerParams(vmem_limit_bytes=40 * 2**20),
+        compiler_params=pltpu.CompilerParams(vmem_limit_bytes=60 * 2**20),
         cost_estimate=pl.CostEstimate(
             flops=8 * block * 2304 * 192, bytes_accessed=8 * 2**20, transcendentals=block * 2304 * 3
         ),
@@ -821,30 +821,30 @@
         return [both(keep[0], got[0]), swapped(both(keep[1], got[1]), "wt", 2)]
 
     grad_halo = halo(grads)
-    outer_terms = far_terms(outer_keep, outer_got)
+    inner_terms = far_terms(inner_keep, inner_got)
     grad_query = attention_queries(
         query_bounds, queries, spans_column, grads, mixed_wide, stat_columns, pairs
     )
-    grad_query, grad_halo, outer_terms, inner_keep, inner_got = lax.optimization_barrier(
-        (grad_query, grad_halo, outer_terms, inner_keep, inner_got)
+    grad_query, grad_halo, inner_terms, outer_keep, outer_got = lax.optimization_barrier(
+        (grad_query, grad_halo, inner_terms, outer_keep, outer_got)
     )
 
     near_first = [1 << i for i in range(cycle.bit_length() - 1)]
-    outer_terms = scatter_sum(outer_terms, "ctx", near_first[:1], 0)
-    inner_terms = far_terms(inner_keep, inner_got)
+    inner_terms = scatter_sum(inner_terms, "ctx", near_first[:1], 0)
+    outer_terms = far_terms(outer_keep, outer_got)
     grad_pair = attention_keys(key_bounds, pair, spans_row, query_halo, grad_halo)
-    grad_pair, outer_terms, inner_terms = lax.optimization_barrier(
-        (grad_pair, outer_terms, inner_terms)
+    grad_pair, inner_terms, outer_terms = lax.optimization_barrier(
+        (grad_pair, inner_terms, outer_terms)
     )
 
     head_grad, token_partial = head_grads(places, block_tokens, grad_query, grad_pair, weight_pieces)
-    outer_part = both(*scatter_sum(outer_terms, "ctx", near_first[1:], 0))
-    inner_part = both(*scatter_sum(inner_terms, "ctx", near_first, 0))
+    inner_part = both(*scatter_sum(inner_terms, "ctx", near_first[1:], 0))
+    outer_part = both(*scatter_sum(outer_terms, "ctx", near_first, 0))
     head_part = both(*scatter_sum([head_grad], "ctx", near_first, 1))
     token_got = swapped(token_partial[1::2], "wt", 1)
     token_sum = both(*far_terms(token_partial[0::2], token_got))
+    inner_total = gather_back(inner_part, "ctx", near_first, 0)
     outer_total = gather_back(outer_part, "ctx", near_first, 0)
-    inner_total = gather_back(inner_part, "ctx", near_first, 0)
     head_pieces = [
         lax.dynamic_index_in_dim(head_part, w ^ r, 0, keepdims=False) for r in range(shards)
     ]

time: 348 us -> 375 us (1.078)
  starting transfers between devices: 89.5 us -> 108 us
  local copies, waits for them, and re-layouts: 25.3 us -> 33.7 us
  other arithmetic: 37.5 us -> 33.4 us
  waiting for transfers between devices: 108 us -> 112 us
    ppermute x44, starting transfers between devices: 52 us -> 65.1 us  [swapped(): return lax.ppermute(block, axis, [(i, i ^ bit) for i in range(count)])]
    ppermute x44, waiting for transfers between devices: 81.2 us -> 91 us  [swapped(): return lax.ppermute(block, axis, [(i, i ^ bit) for i in range(count)])]
    unnamed x116 -> x100, local copies, waits for them, and re-layouts: 12.1 us -> 19.2 us
    ppermute x10, starting transfers between devices: 33.3 us -> 38 us  [shifted(): return lax.ppermute(block, axis, route)]
    ppermute x10, waiting for transfers between devices: 23.6 us -> 19 us  [shifted(): return lax.ppermute(block, axis, route)]
  transfers between devices with their start and end apart: 55 -> 55, of which waited for: 27 -> 29; matrix products, arithmetic and copies ran while one was open for 14% -> 12% of each run, Pallas kernels for 22% -> 21%
where the time goes in v4:
time: 375 us
  waiting for transfers between devices  112 us (30%)
  starting transfers between devices  108 us (29%)
  Pallas kernels  86.7 us (23%)
  local copies, waits for them, and re-layouts  33.7 us (9%)
  other arithmetic  33.4 us (9%)
    ppermute x44, waiting for transfers between devices, swapped(): return lax.ppermute(block, axis, [(i, i ^ bit) for i in range(count)])  91 us
    ppermute x44, starting transfers between devices, swapped(): return lax.ppermute(block, axis, [(i, i ^ bit) for i in range(count)])  65.1 us
    ppermute x10, starting transfers between devices, shifted(): return lax.ppermute(block, axis, route)  38 us
    pallas_call x1, Pallas kernels, dense(): pl.pallas_call(dense_kernel, in_specs=[pl.BlockSpec(memory_space=pltpu.SM...  23.3 us
    unnamed x100, local copies, waits for them, and re-layouts  19.2 us
    ppermute x10, waiting for transfers between devices, shifted(): return lax.ppermute(block, axis, route)  19 us
    pallas_call x1, Pallas kernels, attention_keys(): pl.pallas_call(functools.partial(key_kernel, count // 2), grid_spec=pltpu...  18.7 us
    pallas_call x1, Pallas kernels, attention_forward(): pl.pallas_call(forward_kernel, grid_spec=pltpu.PrefetchScalarGridSpec(num...  17.4 us
  transfers between devices with their start and end apart: 55, of which 29 were waited for; matrix products, arithmetic and copies ran while one was open for 12% of the time, Pallas kernels for 21%

profile of v4, /device:TPU:0, one launch (start us, length us, event | category | flops | bytes accessed | tf_op | source)
XLA Modules:
  0.0 375.5 jit_solution(16134768929572936298)
XLA Ops:
  42.3 8.8 %collective-permute-done.6.rest_0_ = bf16[1024,384]{1,0:T(8,128)(2,1)S(1)} collective-permute-done((bf16[1024,384]{1,0:T(8,128)(2,1)S(1)}, bf16[1024,384]{1,0:T(8,128)(2,1)S(1)}, u32[]{:S(2)}, u32[]{:S(2)}) %collective-permute-start.6) | collective-permute-done | bytes 786464 | tf_op jit(solution)/shard_map/ppermute | solution.py:32
  58.2 4.5 %collective-permute-start.10 = (bf16[512,384]{1,0:T(8,128)(2,1)S(1)}, bf16[512,384]{1,0:T(8,128)(2,1)}, u32[]{:S(2)}, u32[]{:S(2)}) collective-permute-start(bf16[512,384]{1,0:T(8,128)(2,1)S(1)} %slice.342), channel_id=1, source_target_pairs={{0,8},{8,16},{12,4},{16,24},{20,12},{28,20},{1,9},{9,17},{13,5},{1... | collective-permute-start | bytes 1179656 | tf_op jit(solution)/shard_map/ppermute | solution.py:766
  62.9 4.5 %collective-permute-done.9.rest_4_ = bf16[512,384]{1,0:T(8,128)(2,1)} collective-permute-done((bf16[512,384]{1,0:T(8,128)(2,1)S(1)}, bf16[512,384]{1,0:T(8,128)(2,1)}, u32[]{:S(2)}, u32[]{:S(2)}) %collective-permute-start.9) | collective-permute-done | bytes 393248 | tf_op jit(solution)/shard_map/ppermute | solution.py:26
  69.9 4.3 %collective-permute-start.11 = (bf16[1024,192]{1,0:T(8,128)(2,1)S(1)}, bf16[1024,192]{1,0:T(8,128)(2,1)S(1)}, u32[]{:S(2)}, u32[]{:S(2)}) collective-permute-start(bf16[1024,192]{1,0:T(8,128)(2,1)S(1)} %get-tuple-element.92.q_ref.rest_2_), channel_id=1, source_target_pairs={{0,4},{4,8},{8,12},{12,16},{16,20},{20,24},{24,28},{1,5},{5,9},{9,... | collective-permute-start | bytes 1179656 | tf_op jit(solution)/shard_map/ppermute | solution.py:32
  77.4 17.4 %attention_forward.1 = (bf16[1024,192]{1,0:T(8,128)(2,1)}, f32[1024,192]{1,0:T(8,128)}, f32[1024,128]{1,0:T(8,128)}) custom-call(s32[14]{0:T(128)} %concatenate.101.bounds, bf16[1024,192]{1,0:T(8,128)(2,1)} %copy-done.6, s32[1024,8]{1,0:T(8,128)} %copy.39.span_ref, bf16[1024,384]{1,0:T(8,128)(2,1)} %copy-done.28, ...), custom_call_target="tpu_custom_call" | custom-call | flops 1811939328 | bytes 6291456 | tf_op jit(solution)/shard_map/attention_forward/pallas_call | solution.py:128
  107.5 13.2 %collective-permute-start.19 = (bf16[1024,192]{1,0:T(8,128)(2,1)}, bf16[1024,192]{1,0:T(8,128)(2,1)}, u32[]{:S(2)}, u32[]{:S(2)}) collective-permute-start(bf16[1024,192]{1,0:T(8,128)(2,1)} %copy-done.6), channel_id=1, source_target_pairs={{0,8},{4,12},{8,16},{12,20},{16,24},{20,28},{1,9},{5,13},{9,17},{1... | collective-permute-start | bytes 1179656 | tf_op jit(solution)/shard_map/ppermute | solution.py:32
  125.4 23.3 %layer_dense.1 = (bf16[256,768]{1,0:T(8,128)(2,1)}, f32[256,768]{1,0:T(8,128)}, bf16[4,256,192]{2,1,0:T(8,128)(2,1)}, bf16[2,768,768]{2,1,0:T(8,128)(2,1)}, bf16...) custom-call(s32[4]{0:T(128)} %copy-done.3, ...), custom_call_target="tpu_custom_call" | custom-call | flops 14495514624 | bytes 25165824 | tf_op jit(solution)/shard_map/layer_dense/pallas_call | solution.py:524
  152.7 5.2 %collective-permute-done.21.p1 = bf16[256,192]{1,0:T(8,128)(2,1)S(1)} collective-permute-done((bf16[256,192]{1,0:T(8,128)(2,1)S(1)}, bf16[256,192]{1,0:T(8,128)(2,1)S(1)}, u32[]{:S(2)}, u32[]{:S(2)}) %collective-permute-start.21) | collective-permute-done | bytes 98336 | tf_op jit(solution)/shard_map/ppermute | solution.py:26
  165.4 4.6 %collective-permute-start.26 = (bf16[1024,256]{1,0:T(8,128)(2,1)S(1)}, bf16[1024,256]{1,0:T(8,128)(2,1)S(1)}, u32[]{:S(2)}, u32[]{:S(2)}) collective-permute-start(bf16[1024,256]{1,0:T(8,128)(2,1)S(1)} %layer_gather.1.grad_ref.rest_7_), channel_id=1, source_target_pairs={{0,8},{4,12},{8,16},{12,20},{16,24},{20,28},{1,9},{5,13},{9,17},{1... | collective-permute-start | bytes 1572872 | tf_op jit(solution)/shard_map/ppermute | solution.py:32
  169.9 5.6 %collective-permute-start.27 = (bf16[1024,256]{1,0:T(8,128)(2,1)S(1)}, bf16[1024,256]{1,0:T(8,128)(2,1)}, u32[]{:S(2)}, u32[]{:S(2)}) collective-permute-start(bf16[1024,256]{1,0:T(8,128)(2,1)S(1)} %layer_gather.1.grad_ref.rest_7_), channel_id=1, source_target_pairs={{0,4},{4,8},{8,12},{12,16},{16,20},{20,24},{24,28},{1,5},{5,9},{9,... | collective-permute-start | bytes 1572872 | tf_op jit(solution)/shard_map/ppermute | solution.py:32
  178.4 16.6 %attention_queries.1.query_ref = bf16[1024,192]{1,0:T(8,128)(2,1)} custom-call(s32[14]{0:T(128)} %concatenate.101.bounds, bf16[1024,192]{1,0:T(8,128)(2,1)} %copy-done.6, s32[1024,8]{1,0:T(8,128)} %copy.39.span_ref, bf16[1024,256]{1,0:T(8,128)(2,1)} %copy-done.2, f32[1024,192]{1,0:T(8,128)} %get-tuple-element.97.wide_ref, ...), custom_call_target="tpu_custom_call" | custom-call | flops 2717908992 | bytes 6291456 | tf_op jit(solution)/shard_map/attention_queries/pallas_call | solution.py:218
  202.2 4.4 %fusion.3 = (bf16[768,768]{1,0:T(8,128)(2,1)}, bf16[768,768]{1,0:T(8,128)(2,1)}) fusion(bf16[2,768,768]{2,1,0:T(8,128)(2,1)} %collective-permute-done.24, bf16[2,768,768]{2,1,0:T(8,128)(2,1)} %get-tuple-element.118), kind=kLoop, calls=%fused_computation.10 | loop fusion | flops 4718592 | bytes 7077888 | tf_op jit(solution)/shard_map/convert_element_type | solution.py:647
  213.3 18.7 %attention_keys.1.pair_ref = bf16[1024,384]{1,0:T(8,128)(2,1)} custom-call(s32[8]{0:T(128)} %copy-done.31, bf16[1024,384]{1,0:T(8,128)(2,1)} %copy-done.5, s32[8,5120]{1,0:T(8,128)} %copy-done.26, bf16[1024,192]{1,0:T(8,128)(2,1)} %collective-permute-done.19.rest_0_, bf16[1024,192]{1,0:T(8,128)(2,1)} %copy-done.33, bf16[1024,192]{1,0:T(8,128)(2,1)} %copy-done.6, ...), custom_call_target="tpu_custom_call" | custom-call | flops 3623878656 | bytes 8388608 | tf_op jit(solution)/shard_map/attention_keys/pallas_call | solution.py:307
  237.8 5.0 %layer_heads.1 = (bf16[4,192,640]{2,1,0:T(8,128)(2,1)S(1)}, bf16[4,256,768]{2,1,0:T(8,128)(2,1)S(1)}) custom-call(s32[4]{0:T(128)S(1)} %copy-done.4, bf16[1024,768]{1,0:T(8,128)(2,1)S(1)} %copy-done.15, bf16[1024,192]{1,0:T(8,128)(2,1)S(1)} %copy-done.17, bf16[1024,384]{1,0:T(8,128)(2,1)S(1)} %copy-done.16, bf16[192,576]{1,0:T(8,128)(2,1)S(1)} %pad_maximum_fusion.w_own.w0, ...), custom_call_target="tpu_custom_call" | custom-call | flops 1811939328 | bytes 8388608 | tf_op jit(solution)/shard_map/layer_heads/pallas_call | solution.py:627
  242.9 5.7 %collective-permute-start.35 = (bf16[4,96,640]{2,1,0:T(8,128)(2,1)S(1)}, bf16[4,96,640]{2,1,0:T(8,128)(2,1)S(1)}, u32[]{:S(2)}, u32[]{:S(2)}) collective-permute-start(bf16[4,96,640]{2,1,0:T(8,128)(2,1)S(1)} %constant_dynamic-slice_fusion.8), channel_id=1, source_target_pairs={{0,4},{4,0},{8,12},{12,8},{16,20},{20,16},{24,28},{28,24},{1,5},{5... | collective-permute-start | bytes 1474568 | tf_op jit(solution)/shard_map/ppermute | solution.py:26
  252.3 11.7 %collective-permute-start.44 = (bf16[256,768]{1,0:T(8,128)(2,1)S(1)}, bf16[256,768]{1,0:T(8,128)(2,1)S(1)}, u32[]{:S(2)}, u32[]{:S(2)}) collective-permute-start(bf16[256,768]{1,0:T(8,128)(2,1)S(1)} %get-tuple-element.145), channel_id=1, source_target_pairs={{0,8},{4,12},{8,0},{12,4},{16,24},{20,28},{24,16},{28,20},{1,9},{5... | collective-permute-start | bytes 1179656 | tf_op jit(solution)/shard_map/ppermute | solution.py:26
  264.2 8.5 %collective-permute-start.36 = (bf16[4,48,640]{2,1,0:T(8,128)(2,1)S(1)}, bf16[4,48,640]{2,1,0:T(8,128)(2,1)S(1)}, u32[]{:S(2)}, u32[]{:S(2)}) collective-permute-start(bf16[4,48,640]{2,1,0:T(8,128)(2,1)S(1)} %get-tuple-element.149), channel_id=1, source_target_pairs={{0,8},{4,12},{8,0},{12,4},{16,24},{20,28},{24,16},{28,20},{1,9},{5... | collective-permute-start | bytes 737288 | tf_op jit(solution)/shard_map/ppermute | solution.py:26
  273.9 5.0 %collective-permute-done.36 = bf16[4,48,640]{2,1,0:T(8,128)(2,1)S(1)} collective-permute-done((bf16[4,48,640]{2,1,0:T(8,128)(2,1)S(1)}, bf16[4,48,640]{2,1,0:T(8,128)(2,1)S(1)}, u32[]{:S(2)}, u32[]{:S(2)}) %collective-permute-start.36) | collective-permute-done | bytes 245792 | tf_op jit(solution)/shard_map/ppermute | solution.py:26
  283.1 7.2 %collective-permute-done.37 = bf16[4,24,640]{2,1,0:T(8,128)(2,1)S(1)} collective-permute-done((bf16[4,24,640]{2,1,0:T(8,128)(2,1)S(1)}, bf16[4,24,640]{2,1,0:T(8,128)(2,1)S(1)}, u32[]{:S(2)}, u32[]{:S(2)}) %collective-permute-start.37) | collective-permute-done | bytes 122912 | tf_op jit(solution)/shard_map/ppermute | solution.py:26
  297.9 10.2 %collective-permute-done.46 = bf16[128,768]{1,0:T(8,128)(2,1)S(1)} collective-permute-done((bf16[128,768]{1,0:T(8,128)(2,1)S(1)}, bf16[128,768]{1,0:T(8,128)(2,1)S(1)}, u32[]{:S(2)}, u32[]{:S(2)}) %collective-permute-start.46) | collective-permute-done | bytes 196640 | tf_op jit(solution)/shard_map/ppermute | solution.py:26
  316.7 8.9 %collective-permute-done.52 = bf16[96,768]{1,0:T(8,128)(2,1)S(1)} collective-permute-done((bf16[96,768]{1,0:T(8,128)(2,1)S(1)}, bf16[96,768]{1,0:T(8,128)(2,1)S(1)}, u32[]{:S(2)}, u32[]{:S(2)}) %collective-permute-start.52) | collective-permute-done | bytes 147488 | tf_op jit(solution)/shard_map/ppermute | solution.py:26
  339.3 5.8 %collective-permute-done.43 = bf16[4,96,640]{2,1,0:T(8,128)(2,1)S(1)} collective-permute-done((bf16[4,96,640]{2,1,0:T(8,128)(2,1)S(1)}, bf16[4,96,640]{2,1,0:T(8,128)(2,1)S(1)}, u32[]{:S(2)}, u32[]{:S(2)}) %collective-permute-start.43) | collective-permute-done | bytes 491552 | tf_op jit(solution)/shard_map/ppermute | solution.py:26
  349.3 12.6 %collective-permute-done.48 = bf16[512,768]{1,0:T(8,128)(2,1)S(1)} collective-permute-done((bf16[512,768]{1,0:T(8,128)(2,1)S(1)}, bf16[512,768]{1,0:T(8,128)(2,1)S(1)}, u32[]{:S(2)}, u32[]{:S(2)}) %collective-permute-start.48) | collective-permute-done | bytes 786464 | tf_op jit(solution)/shard_map/ppermute | solution.py:26
  366.5 7.4 %collective-permute-done.54 = bf16[384,768]{1,0:T(8,128)(2,1)S(1)} collective-permute-done((bf16[384,768]{1,0:T(8,128)(2,1)S(1)}, bf16[384,768]{1,0:T(8,128)(2,1)S(1)}, u32[]{:S(2)}, u32[]{:S(2)}) %collective-permute-start.54) | collective-permute-done | bytes 589856 | tf_op jit(solution)/shard_map/ppermute | solution.py:26
  (295 shorter events, 155.1 us)
Async XLA Ops:
  30.0 21.1 %collective-permute-start.6 = (bf16[1024,384]{1,0:T(8,128)(2,1)S(1)}, bf16[1024,384]{1,0:T(8,128)(2,1)S(1)}, u32[]{:S(2)}, u32[]{:S(2)}) collective-permute-start(bf16[1024,384]{1,0:T(8,128)(2,1)S(1)} %get-tuple-element.73.rest_2_.kv_ref), channel_id=1, source_target_pairs={{0,8},{4,12},{8,16},{12,20},{16,24},{20,28},{1,9},{5,13},{9,17},{1... | collective-permute-start | bytes 2359304 | tf_op jit(solution)/shard_map/ppermute | solution.py:32
  33.5 21.9 %collective-permute-start.7 = (bf16[1024,384]{1,0:T(8,128)(2,1)S(1)}, bf16[1024,384]{1,0:T(8,128)(2,1)}, u32[]{:S(2)}, u32[]{:S(2)}) collective-permute-start(bf16[1024,384]{1,0:T(8,128)(2,1)S(1)} %get-tuple-element.73.rest_2_.kv_ref), channel_id=1, source_target_pairs={{8,0},{12,4},{16,8},{20,12},{24,16},{28,20},{9,1},{13,5},{17,9},{2... | collective-permute-start | bytes 2359304 | tf_op jit(solution)/shard_map/ppermute | solution.py:32
  36.5 60.7 %collective-permute-start.13 = (bf16[1744,768]{1,0:T(8,128)(2,1)}, bf16[1744,768]{1,0:T(8,128)(2,1)}, u32[]{:S(2)}, u32[]{:S(2)}) collective-permute-start(bf16[1744,768]{1,0:T(8,128)(2,1)} %slice_dynamic-update-slice_fusion.refs_8_), channel_id=1, source_target_pairs={{0,2},{1,3},{2,0},{3,1},{4,6},{5,7},{6,4},{7,5},{8,10},{9,11},{10,... | collective-permute-start | bytes 8036360 | tf_op jit(solution)/shard_map/ppermute | solution.py:26
  37.7 20.4 %collective-permute-start.8 = (bf16[1024,384]{1,0:T(8,128)(2,1)S(1)}, bf16[1024,384]{1,0:T(8,128)(2,1)S(1)}, u32[]{:S(2)}, u32[]{:S(2)}) collective-permute-start(bf16[1024,384]{1,0:T(8,128)(2,1)S(1)} %get-tuple-element.73.rest_2_.kv_ref), channel_id=1, source_target_pairs={{0,4},{4,0},{8,12},{12,8},{16,20},{20,16},{24,28},{28,24},{1,5},{5... | collective-permute-start | bytes 2359304 | tf_op jit(solution)/shard_map/ppermute | solution.py:26
  69.9 25.6 %collective-permute-start.11 = (bf16[1024,192]{1,0:T(8,128)(2,1)S(1)}, bf16[1024,192]{1,0:T(8,128)(2,1)S(1)}, u32[]{:S(2)}, u32[]{:S(2)}) collective-permute-start(bf16[1024,192]{1,0:T(8,128)(2,1)S(1)} %get-tuple-element.92.q_ref.rest_2_), channel_id=1, source_target_pairs={{0,4},{4,8},{8,12},{12,16},{16,20},{20,24},{24,28},{1,5},{5,9},{9,... | collective-permute-start | bytes 1179656 | tf_op jit(solution)/shard_map/ppermute | solution.py:32
  74.1 21.4 %collective-permute-start.12 = (bf16[1024,192]{1,0:T(8,128)(2,1)S(1)}, bf16[1024,192]{1,0:T(8,128)(2,1)S(1)}, u32[]{:S(2)}, u32[]{:S(2)}) collective-permute-start(bf16[1024,192]{1,0:T(8,128)(2,1)S(1)} %get-tuple-element.92.q_ref.rest_2_), channel_id=1, source_target_pairs={{4,0},{8,4},{12,8},{16,12},{20,16},{24,20},{28,24},{5,1},{9,5},{13... | collective-permute-start | bytes 1179656 | tf_op jit(solution)/shard_map/ppermute | solution.py:32
  75.5 26.9 %collective-permute-start.17 = (bf16[1744,768]{1,0:T(8,128)(2,1)}, bf16[1744,768]{1,0:T(8,128)(2,1)}, u32[]{:S(2)}, u32[]{:S(2)}) collective-permute-start(bf16[1744,768]{1,0:T(8,128)(2,1)} %slice_dynamic-update-slice_fusion.refs_8_), channel_id=1, source_target_pairs={{0,1},{1,0},{2,3},{3,2},{4,5},{5,4},{6,7},{7,6},{8,9},{9,8},{10,11... | collective-permute-start | bytes 8036360 | tf_op jit(solution)/shard_map/ppermute | solution.py:26
  97.2 24.9 %collective-permute-start.18 = (bf16[1744,768]{1,0:T(8,128)(2,1)}, bf16[1744,768]{1,0:T(8,128)(2,1)S(1)}, u32[]{:S(2)}, u32[]{:S(2)}) collective-permute-start(bf16[1744,768]{1,0:T(8,128)(2,1)} %collective-permute-done.13.refs_10_), channel_id=1, source_target_pairs={{0,1},{1,0},{2,3},{3,2},{4,5},{5,4},{6,7},{7,6},{8,9},{9,8},{10,11... | collective-permute-start | bytes 8036360 | tf_op jit(solution)/shard_map/ppermute | solution.py:26
  107.5 41.2 %collective-permute-start.19 = (bf16[1024,192]{1,0:T(8,128)(2,1)}, bf16[1024,192]{1,0:T(8,128)(2,1)}, u32[]{:S(2)}, u32[]{:S(2)}) collective-permute-start(bf16[1024,192]{1,0:T(8,128)(2,1)} %copy-done.6), channel_id=1, source_target_pairs={{0,8},{4,12},{8,16},{12,20},{16,24},{20,28},{1,9},{5,13},{9,17},{1... | collective-permute-start | bytes 1179656 | tf_op jit(solution)/shard_map/ppermute | solution.py:32
  120.7 28.0 %collective-permute-start.20 = (bf16[1024,192]{1,0:T(8,128)(2,1)}, bf16[1024,192]{1,0:T(8,128)(2,1)}, u32[]{:S(2)}, u32[]{:S(2)}) collective-permute-start(bf16[1024,192]{1,0:T(8,128)(2,1)} %copy-done.6), channel_id=1, source_target_pairs={{8,0},{12,4},{16,8},{20,12},{24,16},{28,20},{9,1},{13,5},{17,9},{2... | collective-permute-start | bytes 1179656 | tf_op jit(solution)/shard_map/ppermute | solution.py:32
  164.1 37.0 %collective-permute-start.30 = (bf16[1024,768]{1,0:T(8,128)(2,1)}, bf16[1024,768]{1,0:T(8,128)(2,1)S(1)}, u32[]{:S(2)}, u32[]{:S(2)}) collective-permute-start(bf16[1024,768]{1,0:T(8,128)(2,1)} %get-tuple-element.131), channel_id=1, source_target_pairs={{0,2},{1,3},{2,0},{3,1},{4,6},{5,7},{6,4},{7,5},{8,10},{9,11},{10,... | collective-permute-start | bytes 4718600 | tf_op jit(solution)/shard_map/ppermute | solution.py:26
  165.4 29.7 %collective-permute-start.26 = (bf16[1024,256]{1,0:T(8,128)(2,1)S(1)}, bf16[1024,256]{1,0:T(8,128)(2,1)S(1)}, u32[]{:S(2)}, u32[]{:S(2)}) collective-permute-start(bf16[1024,256]{1,0:T(8,128)(2,1)S(1)} %layer_gather.1.grad_ref.rest_7_), channel_id=1, source_target_pairs={{0,8},{4,12},{8,16},{12,20},{16,24},{20,28},{1,9},{5,13},{9,17},{1... | collective-permute-start | bytes 1572872 | tf_op jit(solution)/shard_map/ppermute | solution.py:32
  169.9 27.1 %collective-permute-start.27 = (bf16[1024,256]{1,0:T(8,128)(2,1)S(1)}, bf16[1024,256]{1,0:T(8,128)(2,1)}, u32[]{:S(2)}, u32[]{:S(2)}) collective-permute-start(bf16[1024,256]{1,0:T(8,128)(2,1)S(1)} %layer_gather.1.grad_ref.rest_7_), channel_id=1, source_target_pairs={{0,4},{4,8},{8,12},{12,16},{16,20},{20,24},{24,28},{1,5},{5,9},{9,... | collective-permute-start | bytes 1572872 | tf_op jit(solution)/shard_map/ppermute | solution.py:32
  175.6 21.5 %collective-permute-start.28 = (bf16[1024,256]{1,0:T(8,128)(2,1)S(1)}, bf16[1024,256]{1,0:T(8,128)(2,1)}, u32[]{:S(2)}, u32[]{:S(2)}) collective-permute-start(bf16[1024,256]{1,0:T(8,128)(2,1)S(1)} %layer_gather.1.grad_ref.rest_7_), channel_id=1, source_target_pairs={{4,0},{8,4},{12,8},{16,12},{20,16},{24,20},{28,24},{5,1},{9,5},{13... | collective-permute-start | bytes 1572872 | tf_op jit(solution)/shard_map/ppermute | solution.py:32
  176.9 24.2 %collective-permute-start.29 = (bf16[1024,256]{1,0:T(8,128)(2,1)S(1)}, bf16[1024,256]{1,0:T(8,128)(2,1)}, u32[]{:S(2)}, u32[]{:S(2)}) collective-permute-start(bf16[1024,256]{1,0:T(8,128)(2,1)S(1)} %layer_gather.1.grad_ref.rest_7_), channel_id=1, source_target_pairs={{8,0},{12,4},{16,8},{20,12},{24,16},{28,20},{9,1},{13,5},{17,9},{2... | collective-permute-start | bytes 1572872 | tf_op jit(solution)/shard_map/ppermute | solution.py:32
  206.7 27.5 %collective-permute-start.32 = (bf16[768,768]{1,0:T(8,128)(2,1)}, bf16[768,768]{1,0:T(8,128)(2,1)}, u32[]{:S(2)}, u32[]{:S(2)}) collective-permute-start(bf16[768,768]{1,0:T(8,128)(2,1)} %get-tuple-element.133), channel_id=1, source_target_pairs={{0,2},{1,3},{2,0},{3,1},{4,6},{5,7},{6,4},{7,5},{8,10},{9,11},{10,... | collective-permute-start | bytes 3538952 | tf_op jit(solution)/shard_map/ppermute | solution.py:26
  210.5 21.5 %collective-permute-start.31 = (bf16[512,768]{1,0:T(8,128)(2,1)S(1)}, bf16[512,768]{1,0:T(8,128)(2,1)S(1)}, u32[]{:S(2)}, u32[]{:S(2)}) collective-permute-start(bf16[512,768]{1,0:T(8,128)(2,1)S(1)} %get-tuple-element.135), channel_id=1, source_target_pairs={{0,4},{4,0},{8,12},{12,8},{16,20},{20,16},{24,28},{28,24},{1,5},{5... | collective-permute-start | bytes 2359304 | tf_op jit(solution)/shard_map/ppermute | solution.py:26
  242.9 21.0 %collective-permute-start.35 = (bf16[4,96,640]{2,1,0:T(8,128)(2,1)S(1)}, bf16[4,96,640]{2,1,0:T(8,128)(2,1)S(1)}, u32[]{:S(2)}, u32[]{:S(2)}) collective-permute-start(bf16[4,96,640]{2,1,0:T(8,128)(2,1)S(1)} %constant_dynamic-slice_fusion.8), channel_id=1, source_target_pairs={{0,4},{4,0},{8,12},{12,8},{16,20},{20,16},{24,28},{28,24},{1,5},{5... | collective-permute-start | bytes 1474568 | tf_op jit(solution)/shard_map/ppermute | solution.py:26
  250.5 28.5 %collective-permute-start.49 = (bf16[384,768]{1,0:T(8,128)(2,1)S(1)}, bf16[384,768]{1,0:T(8,128)(2,1)S(1)}, u32[]{:S(2)}, u32[]{:S(2)}) collective-permute-start(bf16[384,768]{1,0:T(8,128)(2,1)S(1)} %get-tuple-element.138), channel_id=1, source_target_pairs={{0,4},{4,0},{8,12},{12,8},{16,20},{20,16},{24,28},{28,24},{1,5},{5... | collective-permute-start | bytes 1769480 | tf_op jit(solution)/shard_map/ppermute | solution.py:26
  252.3 21.5 %collective-permute-start.44 = (bf16[256,768]{1,0:T(8,128)(2,1)S(1)}, bf16[256,768]{1,0:T(8,128)(2,1)S(1)}, u32[]{:S(2)}, u32[]{:S(2)}) collective-permute-start(bf16[256,768]{1,0:T(8,128)(2,1)S(1)} %get-tuple-element.145), channel_id=1, source_target_pairs={{0,8},{4,12},{8,0},{12,4},{16,24},{20,28},{24,16},{28,20},{1,9},{5... | collective-permute-start | bytes 1179656 | tf_op jit(solution)/shard_map/ppermute | solution.py:26
  272.7 42.1 %collective-permute-start.33 = (bf16[2,256,768]{2,1,0:T(8,128)(2,1)S(1)}, bf16[2,256,768]{2,1,0:T(8,128)(2,1)S(1)}, u32[]{:S(2)}, u32[]{:S(2)}) collective-permute-start(bf16[2,256,768]{2,1,0:T(8,128)(2,1)S(1)} %get-tuple-element.147), channel_id=1, source_target_pairs={{0,1},{1,0},{2,3},{3,2},{4,5},{5,4},{6,7},{7,6},{8,9},{9,8},{10,11... | collective-permute-start | bytes 2359304 | tf_op jit(solution)/shard_map/ppermute | solution.py:26
  308.2 24.8 %collective-permute-start.47 = (bf16[256,768]{1,0:T(8,128)(2,1)S(1)}, bf16[256,768]{1,0:T(8,128)(2,1)S(1)}, u32[]{:S(2)}, u32[]{:S(2)}) collective-permute-start(bf16[256,768]{1,0:T(8,128)(2,1)S(1)} %maximum_select_fusion.6), channel_id=1, source_target_pairs={{0,8},{4,12},{8,0},{12,4},{16,24},{20,28},{24,16},{28,20},{1,9},{5... | collective-permute-start | bytes 1179656 | tf_op jit(solution)/shard_map/ppermute | solution.py:26
  333.4 28.6 %collective-permute-start.48 = (bf16[512,768]{1,0:T(8,128)(2,1)S(1)}, bf16[512,768]{1,0:T(8,128)(2,1)S(1)}, u32[]{:S(2)}, u32[]{:S(2)}) collective-permute-start(bf16[512,768]{1,0:T(8,128)(2,1)S(1)} %maximum_select_fusion.3), channel_id=1, source_target_pairs={{0,4},{4,0},{8,12},{12,8},{16,20},{20,16},{24,28},{28,24},{1,5},{5... | collective-permute-start | bytes 2359304 | tf_op jit(solution)/shard_map/ppermute | solution.py:26
  337.2 36.6 %collective-permute-start.54 = (bf16[384,768]{1,0:T(8,128)(2,1)S(1)}, bf16[384,768]{1,0:T(8,128)(2,1)S(1)}, u32[]{:S(2)}, u32[]{:S(2)}) collective-permute-start(bf16[384,768]{1,0:T(8,128)(2,1)S(1)} %maximum_select_fusion.4), channel_id=1, source_target_pairs={{0,4},{4,0},{8,12},{12,8},{16,20},{20,16},{24,28},{28,24},{1,5},{5... | collective-permute-start | bytes 1769480 | tf_op jit(solution)/shard_map/ppermute | solution.py:26
  (78 other events, 881.0 us)

commit v5 on v3

--- a/solution.py
+++ b/solution.py
@@ -64,7 +64,8 @@
 
 
 def forward_kernel(bounds, q_ref, span_ref, *rest):
-    pieces, (out_ref, wide_ref, stat_ref, kv, top, total, accum, sem) = rest[:-8], rest[-8:]
+    pieces, rest = rest[:-11], rest[-11:]
+    outs, (wide_ref, stat_ref, kv, top, total, accum, sem) = rest[:4], rest[4:]
     step = pl.program_id(0)
 
     @pl.when(step == 0)
@@ -113,9 +114,13 @@
     pair = jnp.where(lane < HEAD_DIM, mixed[0], mixed[1])
     wide_ref[here, 0:128] = pair
     wide_ref[here, 128:192] = mixed[2][:, :HEAD_DIM]
-    out_ref[here, 0:128] = pair.astype(bf16)
-    out_ref[here, 128:192] = mixed[2][:, :HEAD_DIM].astype(bf16)
     stat_ref[here, :] = stats
+    for r, out_ref in enumerate(outs):
+
+        @pl.when(bounds[14 + step] == r)
+        def _(out_ref=out_ref):
+            out_ref[:, 0:128] = pair.astype(bf16)
+            out_ref[:, 128:192] = mixed[2][:, :HEAD_DIM].astype(bf16)
 
 
 def whole_spec(shape):
@@ -132,11 +137,8 @@
             grid=(block // TILE_Q,),
             in_specs=[whole_spec(queries.shape), whole_spec(spans.shape)]
             + [pl.BlockSpec(memory_space=pl.ANY)] * len(pieces),
-            out_specs=[
-                whole_spec((block, 192)),
-                whole_spec((block, 192)),
-                whole_spec((block, 128)),
-            ],
+            out_specs=[whole_spec((TILE_Q, 192))] * 4
+            + [whole_spec((block, 192)), whole_spec((block, 128))],
             scratch_shapes=[
                 pltpu.VMEM((window, 384), bf16),
                 pltpu.VMEM((3, TILE_Q, 128), f32),
@@ -145,11 +147,8 @@
                 pltpu.SemaphoreType.DMA((len(pieces),)),
             ],
         ),
-        out_shape=[
-            jax.ShapeDtypeStruct((block, 192), bf16),
-            jax.ShapeDtypeStruct((block, 192), f32),
-            jax.ShapeDtypeStruct((block, 128), f32),
-        ],
+        out_shape=[jax.ShapeDtypeStruct((TILE_Q, 192), bf16)] * 4
+        + [jax.ShapeDtypeStruct((block, 192), f32), jax.ShapeDtypeStruct((block, 128), f32)],
         compiler_params=pltpu.CompilerParams(vmem_limit_bytes=40 * 2**20),
         cost_estimate=pl.CostEstimate(
             flops=4 * block * 2304 * 192, bytes_accessed=6 * 2**20, transcendentals=block * 2304 * 3
@@ -396,40 +395,42 @@
     mixed = refs[0:4]
     tokens_ref, up_ref, small_ref, inner_bias_ref = refs[4:8]
     packs = refs[8:12]
-    out_ref, grad_ref, back_ref = refs[12:15]
-    outer_keep, outer_send, inner_keep, inner_send = refs[15:19]
-    w_out, w_inner, w_outer, hidden, activated, slopes, inner_grad, sem = refs[19:]
+    out_ref, grad_ref = refs[12:14]
+    back_refs = refs[14:18]
+    outer_refs, inner_refs = refs[18:20], refs[20:22]
+    w_out, w_inner, w_outer, hidden, activated, slopes = refs[22:28]
+    outer_made, inner_made, tail_made, sem, sent = refs[28:]
     rows, width = tokens_ref.shape
     groups = w_inner.shape[0]
     part = width // groups
-    copies = []
-    for r in range(groups):
-        copies.append(
-            pltpu.make_async_copy(packs[r].at[pl.ds(width, part), :], w_out.at[r], sem.at[0, r])
+
+    def inner_copies(g):
+        return [
+            pltpu.make_async_copy(
+                packs[r].at[pl.ds(pl.multiple_of(width + part + 16 + g * part, 16), part), :],
+                w_inner.at[g, pl.ds(pl.multiple_of(place_ref[r] * part, part), part), :],
+                sem.at[1 + g, r],
+            )
+            for r in range(groups)
+        ]
+
+    out_copies = [
+        pltpu.make_async_copy(packs[r].at[pl.ds(width, part), :], w_out.at[r], sem.at[0, r])
+        for r in range(groups)
+    ]
+    outer_copies = [
+        pltpu.make_async_copy(
+            packs[r].at[pl.ds(0, width), :], w_outer.at[place_ref[r]], sem.at[1 + groups, r]
         )
-    for r in range(groups):
-        here = pl.ds(pl.multiple_of(place_ref[r] * part, part), part)
-        for g in range(groups):
-            copies.append(
-                pltpu.make_async_copy(
-                    packs[r].at[pl.ds(width + part + 16 + g * part, part), :],
-                    w_inner.at[g, here, :],
-                    sem.at[1 + g, r],
-                )
-            )
-    for r in range(groups):
-        copies.append(
-            pltpu.make_async_copy(
-                packs[r].at[pl.ds(0, width), :], w_outer.at[place_ref[r]], sem.at[1 + groups, r]
-            )
-        )
-    for copy in copies:
+        for r in range(groups)
+    ]
+    for copy in out_copies + [x for g in range(groups) for x in inner_copies(g)] + outer_copies:
         copy.start()
 
     out_bias, gain_one, shift_one = small_ref[0:1], small_ref[1:2], small_ref[2:3]
     outer_bias, gain_two, shift_two = small_ref[3:4], small_ref[4:5], small_ref[5:6]
 
-    for copy in copies[:groups]:
+    for copy in out_copies:
         copy.wait()
     residual = tokens_ref[...].astype(f32) + out_bias
     for r in range(groups):
@@ -437,19 +438,25 @@
     normal_one, inverse_one = normal_of(residual)
     first = normal_one * gain_one + shift_one
     first_low = first.astype(bf16)
-    for copy in copies[groups:]:
-        copy.wait()
-
-    def ahead(g, total):
+
+    def ahead(g, carry):
+        for copy in inner_copies(g):
+            copy.wait()
         value = rows_nn(first_low, w_inner[g]) + inner_bias_ref[pl.ds(g, 1), :]
         chance = 0.5 * (1.0 + lax.erf(value * (2.0**-0.5)))
         density = jnp.exp(-0.5 * value * value) * (2.0 * jnp.pi) ** -0.5
         slopes[g] = chance + value * density
-        low = (value * chance).astype(bf16)
-        activated[g] = low
-        return total + rows_nn(low, w_outer[g])
-
-    residual = lax.fori_loop(0, groups, ahead, first + outer_bias)
+        activated[g] = (value * chance).astype(bf16)
+        return carry
+
+    lax.fori_loop(0, groups, ahead, 0)
+    for copy in outer_copies:
+        copy.wait()
+
+    def combine(g, total):
+        return total + rows_nn(activated[g], w_outer[g])
+
+    residual = lax.fori_loop(0, groups, combine, first + outer_bias)
     normal_two, inverse_two = normal_of(residual)
     out_ref[...] = (normal_two * gain_two + shift_two).astype(bf16)
     upstream = up_ref[...].astype(f32)
@@ -459,37 +466,44 @@
     gain_two_sum = jnp.sum(upstream * normal_two, axis=0, keepdims=True)
     outer_bias_sum = jnp.sum(grad_two_low.astype(f32), axis=0, keepdims=True)
 
-    def behind(g, total):
-        made = rows_tn(activated[g], grad_two_low).astype(bf16)
-        r = place_ref[g]
-
-        @pl.when(r % 2 == 0)
-        def _():
-            outer_keep[r // 2] = made
-
-        @pl.when(r % 2 == 1)
-        def _():
-            outer_send[r // 2] = made
-
-        value = (rows_nt(grad_two_low, w_outer[g]) * slopes[g]).astype(bf16)
-        hidden[g] = value
-        return total + rows_nt(value, w_inner[g])
-
-    grad_first = lax.fori_loop(0, groups, behind, grad_two)
+    def outer_copy(i, odd):
+        r = 2 * i + odd
+        return pltpu.make_async_copy(outer_made.at[r], outer_refs[odd].at[i], sent.at[0, r])
+
+    def behind(i, total):
+        for odd in range(2):
+            g = place_ref[2 * i + odd]
+            outer_made[2 * i + odd] = rows_tn(activated[g], grad_two_low).astype(bf16)
+            outer_copy(i, odd).start()
+            value = (rows_nt(grad_two_low, w_outer[g]) * slopes[g]).astype(bf16)
+            hidden[g] = value
+            total = total + rows_nt(value, w_inner[g])
+        return total
+
+    grad_first = lax.fori_loop(0, groups // 2, behind, grad_two)
     grad_one = normal_back(grad_first, normal_one, inverse_one, gain_one)
     grad_ref[...] = grad_one
     grad_one_low = grad_one.astype(bf16)
     for r in range(groups):
-        back_ref[r] = rows_nt(grad_one_low, w_out[r]).astype(bf16)
-
-    for g in range(groups):
-        made = rows_tn(first_low, hidden[g]).astype(bf16)
-        for k in range(groups):
-            inner_grad[place_ref[k], g * part : (g + 1) * part, :] = made[k * part : (k + 1) * part, :]
-    for r in range(groups):
-        made = rows_tn(mixed[r][...], grad_one_low).astype(bf16)
-        inner_grad[r, width : width + part, :] = made
-
+        back_refs[r][...] = rows_nt(grad_one_low, w_out[r]).astype(bf16)
+
+    def inner_sends(g):
+        return [
+            pltpu.make_async_copy(
+                inner_made.at[g, pl.ds(pl.multiple_of(place_ref[r] * part, part), part), :],
+                inner_refs[r % 2].at[r // 2, pl.ds(pl.multiple_of(g * part, part), part), :],
+                sent.at[1 + g, r],
+            )
+            for r in range(groups)
+        ]
+
+    def weigh(g, carry):
+        inner_made[g] = rows_tn(first_low, hidden[g]).astype(bf16)
+        for copy in inner_sends(g):
+            copy.start()
+        return carry
+
+    lax.fori_loop(0, groups, weigh, 0)
     sums = [
         jnp.sum(grad_one_low.astype(f32), axis=0, keepdims=True),
         jnp.sum(grad_first * normal_one, axis=0, keepdims=True),
@@ -499,7 +513,9 @@
         shift_two_sum,
     ]
     line = lax.broadcasted_iota(jnp.int32, (16, part), 0)
-    inner_grad[:, width + part : width + part + 64, :] = jnp.zeros((groups, 64, width), bf16)
+    tail_made[:, part:, :] = jnp.zeros((groups, 64, width), bf16)
+    for r in range(groups):
+        tail_made[r, 0:part, :] = rows_tn(mixed[r][...], grad_one_low).astype(bf16)
     for k in range(groups):
         tail = jnp.zeros((16, part), f32)
         for i, line_sum in enumerate(sums):
@@ -509,10 +525,23 @@
             tail = jnp.where(
                 line == len(sums) + i, bias_sum[:, i * part : (i + 1) * part], tail
             )
-        inner_grad[place_ref[k], width + part : width + part + 16, 0:part] = tail.astype(bf16)
+        tail_made[place_ref[k], part : part + 16, 0:part] = tail.astype(bf16)
+    tail_copies = [
+        pltpu.make_async_copy(
+            tail_made.at[r], inner_refs[r % 2].at[r // 2, pl.ds(width, part + 64), :], sent.at[1 + groups, r]
+        )
+        for r in range(groups)
+    ]
+    for copy in tail_copies:
+        copy.start()
     for i in range(groups // 2):
-        inner_keep[i] = inner_grad[2 * i]
-        inner_send[i] = inner_grad[2 * i + 1]
+        for odd in range(2):
+            outer_copy(i, odd).wait()
+    for g in range(groups):
+        for copy in inner_sends(g):
+            copy.wait()
+    for copy in tail_copies:
+        copy.wait()
 
 
 def dense(places, mixed_pieces, tokens, cotangent, small, inner_bias, packs):
@@ -524,12 +553,12 @@
     return pl.pallas_call(
         dense_kernel,
         in_specs=[pl.BlockSpec(memory_space=pltpu.SMEM)] + [vmem] * (groups + 4) + [hbm] * groups,
-        out_specs=[vmem] * 7,
+        out_specs=[vmem] * (2 + groups) + [hbm] * 4,
         out_shape=[
             jax.ShapeDtypeStruct((rows, width), bf16),
             jax.ShapeDtypeStruct((rows, width), f32),
-            jax.ShapeDtypeStruct((groups, rows, part), bf16),
         ]
+        + [jax.ShapeDtypeStruct((rows, part), bf16)] * groups
         + [jax.ShapeDtypeStruct((groups // 2, width, width), bf16)] * 2
         + [jax.ShapeDtypeStruct((groups // 2, width + part + 64, width), bf16)] * 2,
         scratch_shapes=[
@@ -539,17 +568,21 @@
             pltpu.VMEM((groups, rows, width), bf16),
             pltpu.VMEM((groups, rows, width), bf16),
             pltpu.VMEM((groups, rows, width), f32),
-            pltpu.VMEM((groups, width + part + 64, width), bf16),
+            pltpu.VMEM((groups, width, width), bf16),
+            pltpu.VMEM((groups, width, width), bf16),
+            pltpu.VMEM((groups, part + 64, width), bf16),
+            pltpu.SemaphoreType.DMA((groups + 2, groups)),
             pltpu.SemaphoreType.DMA((groups + 2, groups)),
         ],
-        compiler_params=pltpu.CompilerParams(vmem_limit_bytes=56 * 2**20),
+        compiler_params=pltpu.CompilerParams(vmem_limit_bytes=48 * 2**20),
         cost_estimate=pl.CostEstimate(
-            flops=36 * rows * width * width * groups // 3 * 2,
+            flops=24 * rows * width * width * groups,
             bytes_accessed=24 * 2**20,
             transcendentals=2 * rows * width * groups,
         ),
         name="layer_dense",
     )(places, *mixed_pieces, tokens, cotangent, small, inner_bias, *packs)
+
 
 def gather_kernel(place_ref, p0, p1, p2, p3, wide_ref, stat_ref, out_ref):
     rows, part = p0.shape
@@ -660,6 +693,11 @@
         kept = functools.reduce(both, [half_of(x, bit, axis) for x in terms])
         terms = [kept, swapped(sent, axis_name, step)]
     return terms
+
+
+def full_sum(terms, axis_name, step):
+    block = functools.reduce(both, terms)
+    return both(block, swapped(block, axis_name, step))
 
 
 def gather_back(block, axis_name, order, axis):
@@ -771,7 +809,7 @@
         [0 * missing_at, 2 * reach * block + 0 * missing_at, reach * block + 0 * missing_at]
         + [beside_at, missing_at, missing_at + half]
     )
-    query_bounds = jnp.concatenate([query_bounds, load_at]).astype(jnp.int32)
+    query_bounds = jnp.concatenate([query_bounds, load_at, places]).astype(jnp.int32)
 
     small_own = jnp.stack(
         [out_bias, first_gain, first_shift, outer_bias, second_gain, second_shift]
@@ -782,12 +820,14 @@
     pack = jnp.concatenate([outer_weight, out_weight, small_own] + inner_parts, axis=0)
     pack, _ = lax.optimization_barrier((pack, token_pieces[2:] + weight_pieces[1:]))
     pack_near, pack_far = swapped(pack, "wt", 1), swapped(pack, "wt", 2)
-    mixed, mixed_wide, stat_columns = attention_forward(query_bounds, queries, spans_column, pairs)
+    *mixed_pieces, mixed_wide, stat_columns = attention_forward(
+        query_bounds, queries, spans_column, pairs
+    )
     ready, _ = lax.optimization_barrier((queries, pairs))
     query_halo = [queries if d == 0 else shifted(ready, "ctx", d) if d * d == 1 else None for d in distances]
     close = [x for x, d in zip(query_halo, distances) if d * d == 1]
-    mixed, mixed_wide, stat_columns, close, pack_far = lax.optimization_barrier(
-        (mixed, mixed_wide, stat_columns, close, pack_far)
+    mixed_pieces, mixed_wide, stat_columns, close, pack_far = lax.optimization_barrier(
+        (mixed_pieces, mixed_wide, stat_columns, close, pack_far)
     )
     packs = [pack, pack_near, pack_far, swapped(pack_far, "wt", 1)]
     small = jnp.stack([x[width + part : width + part + 16, :part] for x in packs]).astype(f32)
@@ -795,10 +835,6 @@
     small_rows = jnp.concatenate([x[:8] for x in small], axis=1)
     inner_bias_rows = jnp.stack([x[6:10].reshape(-1) for x in small])
 
-    mixed_rows = mixed.reshape(shards, rows, part)
-    mixed_pieces = [
-        lax.dynamic_index_in_dim(mixed_rows, w ^ r, 0, keepdims=False) for r in range(shards)
-    ]
     mixed_pieces = [mixed_pieces[0]] + [
         swapped(mixed_pieces[r], "wt", r) for r in range(1, shards)
     ]
@@ -808,14 +844,16 @@
     )
     remote = [shifted(far_ready, "ctx", d) for d in distances if d * d > 1]
     results, remote = lax.optimization_barrier((results, remote))
-    layer_out, grad_one, back, outer_keep, outer_send, inner_keep, inner_send = results
+    layer_out, grad_one, *back = results[: 2 + shards]
+    outer_keep, outer_send, inner_keep, inner_send = results[2 + shards :]
     query_halo = [remote[0], close[0], queries, close[1], remote[1]]
 
     back_pieces = [back[0]] + [swapped(back[r], "wt", r) for r in range(1, shards)]
     outer_got = swapped(outer_send, "wt", 1)
     inner_got = swapped(inner_send, "wt", 1)
     grads = gathered(places, back_pieces, mixed_wide, stat_columns)
-    grads, outer_got, inner_got = lax.optimization_barrier((grads, outer_got, inner_got))
+    outer_got, _ = lax.optimization_barrier((outer_got, back_pieces[1:]))
+    grads, inner_got = lax.optimization_barrier((grads, inner_got))
 
     def far_terms(keep, got):
         return [both(keep[0], got[0]), swapped(both(keep[1], got[1]), "wt", 2)]
@@ -838,13 +876,14 @@
     )
 
     head_grad, token_partial = head_grads(places, block_tokens, grad_query, grad_pair, weight_pieces)
-    outer_part = both(*scatter_sum(outer_terms, "ctx", near_first[1:], 0))
-    inner_part = both(*scatter_sum(inner_terms, "ctx", near_first, 0))
-    head_part = both(*scatter_sum([head_grad], "ctx", near_first, 1))
+    halved, last = near_first[:-1], near_first[-1]
+    outer_part = full_sum(scatter_sum(outer_terms, "ctx", halved[1:], 0), "ctx", last)
+    inner_part = full_sum(scatter_sum(inner_terms, "ctx", halved, 0), "ctx", last)
+    head_part = full_sum(scatter_sum([head_grad], "ctx", halved, 1), "ctx", last)
     token_got = swapped(token_partial[1::2], "wt", 1)
     token_sum = both(*far_terms(token_partial[0::2], token_got))
-    outer_total = gather_back(outer_part, "ctx", near_first, 0)
-    inner_total = gather_back(inner_part, "ctx", near_first, 0)
+    outer_total = gather_back(outer_part, "ctx", halved, 0)
+    inner_total = gather_back(inner_part, "ctx", halved, 0)
     head_pieces = [
         lax.dynamic_index_in_dim(head_part, w ^ r, 0, keepdims=False) for r in range(shards)
     ]
@@ -855,7 +894,7 @@
             for k in range(shards)
         ]
     )
-    head_total = gather_back(head_parts, "ctx", near_first, 1)
+    head_total = gather_back(head_parts, "ctx", halved, 1)
 
     tokens_gradient = grad_one + token_sum.astype(f32)
     key_total, value_total, query_total = (

time: 348 us -> 355 us (1.020)
  waiting for transfers between devices: 108 us -> 122 us
  other arithmetic: 37.5 us -> 31.7 us
    ppermute x44 -> x41, waiting for transfers between devices: 81.2 us -> 96.9 us  [swapped(): return lax.ppermute(block, axis, [(i, i ^ bit) for i in range(count)])]
    ppermute x10, starting transfers between devices: 33.3 us -> 37.5 us  [shifted(): return lax.ppermute(block, axis, route)]
    unnamed x116, local copies, waits for them, and re-layouts: 12.1 us -> 15.8 us
    ppermute x44 -> x41, starting transfers between devices: 52 us -> 49.3 us  [swapped(): return lax.ppermute(block, axis, [(i, i ^ bit) for i in range(count)])]
  transfers between devices with their start and end apart: 55 -> 52, of which waited for: 27 -> 26; matrix products, arithmetic and copies ran while one was open for 14% -> 11% of each run, Pallas kernels for 22% -> 21%
where the time goes in v5:
time: 355 us; the launch traced here: 356 us
  waiting for transfers between devices  122 us (34%)
  starting transfers between devices  90.9 us (26%)
  Pallas kernels  83.4 us (23%)
  other arithmetic  31.7 us (9%)
  local copies, waits for them, and re-layouts  27.1 us (8%)
    ppermute x41, waiting for transfers between devices, swapped(): return lax.ppermute(block, axis, [(i, i ^ bit) for i in range(count)])  96.9 us
    ppermute x41, starting transfers between devices, swapped(): return lax.ppermute(block, axis, [(i, i ^ bit) for i in range(count)])  49.3 us
    ppermute x10, starting transfers between devices, shifted(): return lax.ppermute(block, axis, route)  37.5 us
    ppermute x10, waiting for transfers between devices, shifted(): return lax.ppermute(block, axis, route)  21.5 us
    pallas_call x1, Pallas kernels, dense(): pl.pallas_call(dense_kernel, in_specs=[pl.BlockSpec(memory_space=pltpu.SM...  19.8 us
    pallas_call x1, Pallas kernels, attention_keys(): pl.pallas_call(functools.partial(key_kernel, count // 2), grid_spec=pltpu...  18.7 us
    pallas_call x1, Pallas kernels, attention_forward(): pl.pallas_call(forward_kernel, grid_spec=pltpu.PrefetchScalarGridSpec(num...  17.3 us
    pallas_call x1, Pallas kernels, attention_queries(): pl.pallas_call(query_kernel, grid_spec=pltpu.PrefetchScalarGridSpec(num_s...  15.8 us
  transfers between devices with their start and end apart: 52, of which 26 were waited for; matrix products, arithmetic and copies ran while one was open for 11% of the time, Pallas kernels for 21%

profile of v5, /device:TPU:0, one launch (start us, length us, event | category | flops | bytes accessed | tf_op | source)
XLA Modules:
  0.0 356.4 jit_solution(10065541488757858696)
XLA Ops:
  22.9 4.3 %layer_projection.1 = (bf16[1024,768]{1,0:T(8,128)(2,1)S(1)}, bf16[1024,192]{1,0:T(8,128)(2,1)}, bf16[1024,384]{1,0:T(8,128)(2,1)}) custom-call(s32[4]{0:T(128)S(1)} %pad_add_fusion.2.place_ref, bf16[256,768]{1,0:T(8,128)(2,1)S(1)} %copy-done.20, bf16[256,768]{1,0:T(8,128)(2,1)S(1)} %collective-permute-done.near, ...), custom_call_target="tpu_custom_call" | custom-call | flops 905969664 | bytes 5242880 | tf_op jit(solution)/shard_map/layer_projection/pallas_call | solution.py:356
  39.8 10.0 %collective-permute-done.6.rest_0_ = bf16[1024,384]{1,0:T(8,128)(2,1)S(1)} collective-permute-done((bf16[1024,384]{1,0:T(8,128)(2,1)}, bf16[1024,384]{1,0:T(8,128)(2,1)S(1)}, u32[]{:S(2)}, u32[]{:S(2)}) %collective-permute-start.6) | collective-permute-done | bytes 786464 | tf_op jit(solution)/shard_map/ppermute | solution.py:32
  57.1 4.2 %collective-permute-start.10 = (bf16[512,384]{1,0:T(8,128)(2,1)}, bf16[512,384]{1,0:T(8,128)(2,1)}, u32[]{:S(2)}, u32[]{:S(2)}) collective-permute-start(bf16[512,384]{1,0:T(8,128)(2,1)} %slice.326), channel_id=1, source_target_pairs={{0,8},{8,16},{12,4},{16,24},{20,12},{28,20},{1,9},{9,17},{13,5},{1... | collective-permute-start | bytes 1179656 | tf_op jit(solution)/shard_map/ppermute | solution.py:804
  61.5 4.2 %collective-permute-done.9.rest_4_ = bf16[512,384]{1,0:T(8,128)(2,1)S(1)} collective-permute-done((bf16[512,384]{1,0:T(8,128)(2,1)}, bf16[512,384]{1,0:T(8,128)(2,1)S(1)}, u32[]{:S(2)}, u32[]{:S(2)}) %collective-permute-start.9) | collective-permute-done | bytes 393248 | tf_op jit(solution)/shard_map/ppermute | solution.py:26
  68.8 4.8 %collective-permute-start.11 = (bf16[1024,192]{1,0:T(8,128)(2,1)}, bf16[1024,192]{1,0:T(8,128)(2,1)}, u32[]{:S(2)}, u32[]{:S(2)}) collective-permute-start(bf16[1024,192]{1,0:T(8,128)(2,1)} %get-tuple-element.113.q_ref.rest_2_), channel_id=1, source_target_pairs={{0,4},{4,8},{8,12},{12,16},{16,20},{20,24},{24,28},{1,5},{5,9},{9,... | collective-permute-start | bytes 1179656 | tf_op jit(solution)/shard_map/ppermute | solution.py:32
  78.8 17.3 %attention_forward.1 = (bf16[256,192]{1,0:T(8,128)(2,1)S(1)}, bf16[256,192]{1,0:T(8,128)(2,1)}, bf16[256,192]{1,0:T(8,128)(2,1)S(1)}, bf16[256,192]{1,0:T(8,128)...) custom-call(s32[18]{0:T(128)S(1)} %concatenate.84.bounds, ...), custom_call_target="tpu_custom_call" | custom-call | flops 1811939328 | bytes 6291456 | tf_op jit(solution)/shard_map/attention_forward/pallas_call | solution.py:133
  106.4 11.5 %collective-permute-start.19 = (bf16[1024,192]{1,0:T(8,128)(2,1)}, bf16[1024,192]{1,0:T(8,128)(2,1)}, u32[]{:S(2)}, u32[]{:S(2)}) collective-permute-start(bf16[1024,192]{1,0:T(8,128)(2,1)} %get-tuple-element.113.q_ref.rest_2_), channel_id=1, source_target_pairs={{0,8},{4,12},{8,16},{12,20},{16,24},{20,28},{1,9},{5,13},{9,17},{1... | collective-permute-start | bytes 1179656 | tf_op jit(solution)/shard_map/ppermute | solution.py:32
  124.4 19.8 %layer_dense.1 = (bf16[256,768]{1,0:T(8,128)(2,1)}, f32[256,768]{1,0:T(8,128)S(1)}, bf16[256,192]{1,0:T(8,128)(2,1)S(1)}, bf16[256,192]{1,0:T(8,128)(2,1)S(1)}, ...) custom-call(s32[4]{0:T(128)S(1)} %pad_add_fusion.2.place_ref, ...), custom_call_target="tpu_custom_call" | custom-call | flops 14495514624 | bytes 25165824 | tf_op jit(solution)/shard_map/layer_dense/pallas_call | solution.py:553
  158.9 4.6 %collective-permute-start.25 = (bf16[1024,256]{1,0:T(8,128)(2,1)S(1)}, bf16[1024,256]{1,0:T(8,128)(2,1)S(1)}, u32[]{:S(2)}, u32[]{:S(2)}) collective-permute-start(bf16[1024,256]{1,0:T(8,128)(2,1)S(1)} %layer_gather.1.grad_ref.rest_7_), channel_id=1, source_target_pairs={{0,8},{4,12},{8,16},{12,20},{16,24},{20,28},{1,9},{5,13},{9,17},{1... | collective-permute-start | bytes 1572872 | tf_op jit(solution)/shard_map/ppermute | solution.py:32
  163.5 6.3 %collective-permute-start.26 = (bf16[1024,256]{1,0:T(8,128)(2,1)S(1)}, bf16[1024,256]{1,0:T(8,128)(2,1)S(1)}, u32[]{:S(2)}, u32[]{:S(2)}) collective-permute-start(bf16[1024,256]{1,0:T(8,128)(2,1)S(1)} %layer_gather.1.grad_ref.rest_7_), channel_id=1, source_target_pairs={{0,4},{4,8},{8,12},{12,16},{16,20},{20,24},{24,28},{1,5},{5,9},{9,... | collective-permute-start | bytes 1572872 | tf_op jit(solution)/shard_map/ppermute | solution.py:32
  172.7 15.8 %attention_queries.1.query_ref = bf16[1024,192]{1,0:T(8,128)(2,1)S(1)} custom-call(s32[18]{0:T(128)S(1)} %concatenate.84.bounds, bf16[1024,192]{1,0:T(8,128)(2,1)} %get-tuple-element.113.q_ref.rest_2_, s32[1024,8]{1,0:T(8,128)S(1)} %copy.39.span_ref, bf16[1024,256]{1,0:T(8,128)(2,1)S(1)} %layer_gather.1.grad_ref.rest_7_, ...), custom_call_target="tpu_custom_call" | custom-call | flops 2717908992 | bytes 6291456 | tf_op jit(solution)/shard_map/attention_queries/pallas_call | solution.py:217
  207.4 18.7 %attention_keys.1.pair_ref = bf16[1024,384]{1,0:T(8,128)(2,1)S(1)} custom-call(s32[8]{0:T(128)S(1)} %reshape.127.bounds, bf16[1024,384]{1,0:T(8,128)(2,1)} %get-tuple-element.85.rest_2_.kv_ref, s32[8,5120]{1,0:T(8,128)S(1)} %add_add_fusion.span_ref, bf16[1024,192]{1,0:T(8,128)(2,1)} %collective-permute-done.19.rest_0_, ...), custom_call_target="tpu_custom_call" | custom-call | flops 3623878656 | bytes 8388608 | tf_op jit(solution)/shard_map/attention_keys/pallas_call | solution.py:306
  226.1 8.2 %collective-permute-done.32 = bf16[1024,768]{1,0:T(8,128)(2,1)} collective-permute-done((bf16[1024,768]{1,0:T(8,128)(2,1)}, bf16[1024,768]{1,0:T(8,128)(2,1)}, u32[]{:S(2)}, u32[]{:S(2)}) %collective-permute-start.32) | collective-permute-done | bytes 1572896 | tf_op jit(solution)/shard_map/ppermute | solution.py:26
  234.3 5.1 %layer_heads.1 = (bf16[4,192,640]{2,1,0:T(8,128)(2,1)S(1)}, bf16[4,256,768]{2,1,0:T(8,128)(2,1)S(1)}) custom-call(s32[4]{0:T(128)S(1)} %pad_add_fusion.2.place_ref, bf16[1024,768]{1,0:T(8,128)(2,1)S(1)} %copy-done.35, bf16[1024,192]{1,0:T(8,128)(2,1)S(1)} %copy-done.37, bf16[1024,384]{1,0:T(8,128)(2,1)S(1)} %attention_keys.1.pair_ref, ...), custom_call_target="tpu_custom_call" | custom-call | flops 1811939328 | bytes 8388608 | tf_op jit(solution)/shard_map/layer_heads/pallas_call | solution.py:660
  240.2 4.3 %collective-permute-start.35 = (bf16[4,96,640]{2,1,0:T(8,128)(2,1)}, bf16[4,96,640]{2,1,0:T(8,128)(2,1)}, u32[]{:S(2)}, u32[]{:S(2)}) collective-permute-start(bf16[4,96,640]{2,1,0:T(8,128)(2,1)} %constant_dynamic-slice_fusion.7), channel_id=1, source_target_pairs={{0,4},{4,0},{8,12},{12,8},{16,20},{20,16},{24,28},{28,24},{1,5},{5... | collective-permute-start | bytes 1474568 | tf_op jit(solution)/shard_map/ppermute | solution.py:26
  251.8 4.7 %collective-permute-done.35 = bf16[4,96,640]{2,1,0:T(8,128)(2,1)} collective-permute-done((bf16[4,96,640]{2,1,0:T(8,128)(2,1)}, bf16[4,96,640]{2,1,0:T(8,128)(2,1)}, u32[]{:S(2)}, u32[]{:S(2)}) %collective-permute-start.35) | collective-permute-done | bytes 491552 | tf_op jit(solution)/shard_map/ppermute | solution.py:26
  257.5 4.3 %collective-permute-start.36 = (bf16[4,48,640]{2,1,0:T(8,128)(2,1)S(1)}, bf16[4,48,640]{2,1,0:T(8,128)(2,1)S(1)}, u32[]{:S(2)}, u32[]{:S(2)}) collective-permute-start(bf16[4,48,640]{2,1,0:T(8,128)(2,1)S(1)} %add_convert_fusion.20), channel_id=1, source_target_pairs={{0,8},{4,12},{8,0},{12,4},{16,24},{20,28},{24,16},{28,20},{1,9},{5... | collective-permute-start | bytes 737288 | tf_op jit(solution)/shard_map/ppermute | solution.py:26
  262.0 5.0 %collective-permute-done.36 = bf16[4,48,640]{2,1,0:T(8,128)(2,1)S(1)} collective-permute-done((bf16[4,48,640]{2,1,0:T(8,128)(2,1)S(1)}, bf16[4,48,640]{2,1,0:T(8,128)(2,1)S(1)}, u32[]{:S(2)}, u32[]{:S(2)}) %collective-permute-start.36) | collective-permute-done | bytes 245792 | tf_op jit(solution)/shard_map/ppermute | solution.py:26
  275.6 8.8 %collective-permute-done.37 = bf16[4,48,640]{2,1,0:T(8,128)(2,1)S(1)} collective-permute-done((bf16[4,48,640]{2,1,0:T(8,128)(2,1)S(1)}, bf16[4,48,640]{2,1,0:T(8,128)(2,1)S(1)}, u32[]{:S(2)}, u32[]{:S(2)}) %collective-permute-start.37) | collective-permute-done | bytes 245792 | tf_op jit(solution)/shard_map/ppermute | solution.py:26
  285.7 4.7 %collective-permute-done.49 = bf16[192,768]{1,0:T(8,128)(2,1)S(1)} collective-permute-done((bf16[192,768]{1,0:T(8,128)(2,1)S(1)}, bf16[192,768]{1,0:T(8,128)(2,1)S(1)}, u32[]{:S(2)}, u32[]{:S(2)}) %collective-permute-start.49) | collective-permute-done | bytes 294944 | tf_op jit(solution)/shard_map/ppermute | solution.py:26
  297.0 10.6 %collective-permute-done.50 = bf16[192,768]{1,0:T(8,128)(2,1)S(1)} collective-permute-done((bf16[192,768]{1,0:T(8,128)(2,1)S(1)}, bf16[192,768]{1,0:T(8,128)(2,1)S(1)}, u32[]{:S(2)}, u32[]{:S(2)}) %collective-permute-start.50) | collective-permute-done | bytes 294944 | tf_op jit(solution)/shard_map/ppermute | solution.py:26
  316.9 7.2 %collective-permute-done.51 = bf16[384,768]{1,0:T(8,128)(2,1)S(1)} collective-permute-done((bf16[384,768]{1,0:T(8,128)(2,1)S(1)}, bf16[384,768]{1,0:T(8,128)(2,1)S(1)}, u32[]{:S(2)}, u32[]{:S(2)}) %collective-permute-start.51) | collective-permute-done | bytes 589856 | tf_op jit(solution)/shard_map/ppermute | solution.py:26
  325.8 7.3 %collective-permute-done.42 = bf16[4,96,640]{2,1,0:T(8,128)(2,1)S(1)} collective-permute-done((bf16[4,96,640]{2,1,0:T(8,128)(2,1)S(1)}, bf16[4,96,640]{2,1,0:T(8,128)(2,1)S(1)}, u32[]{:S(2)}, u32[]{:S(2)}) %collective-permute-start.42) | collective-permute-done | bytes 491552 | tf_op jit(solution)/shard_map/ppermute | solution.py:26
  339.3 12.5 %collective-permute-done.47 = bf16[512,768]{1,0:T(8,128)(2,1)S(1)} collective-permute-done((bf16[512,768]{1,0:T(8,128)(2,1)S(1)}, bf16[512,768]{1,0:T(8,128)(2,1)S(1)}, u32[]{:S(2)}, u32[]{:S(2)}) %collective-permute-start.47) | collective-permute-done | bytes 786464 | tf_op jit(solution)/shard_map/ppermute | solution.py:26
  (300 shorter events, 150.5 us)
Async XLA Ops:
  28.4 21.4 %collective-permute-start.6 = (bf16[1024,384]{1,0:T(8,128)(2,1)}, bf16[1024,384]{1,0:T(8,128)(2,1)S(1)}, u32[]{:S(2)}, u32[]{:S(2)}) collective-permute-start(bf16[1024,384]{1,0:T(8,128)(2,1)} %get-tuple-element.85.rest_2_.kv_ref), channel_id=1, source_target_pairs={{0,8},{4,12},{8,16},{12,20},{16,24},{20,28},{1,9},{5,13},{9,17},{1... | collective-permute-start | bytes 2359304 | tf_op jit(solution)/shard_map/ppermute | solution.py:32
  31.9 22.0 %collective-permute-start.7 = (bf16[1024,384]{1,0:T(8,128)(2,1)}, bf16[1024,384]{1,0:T(8,128)(2,1)S(1)}, u32[]{:S(2)}, u32[]{:S(2)}) collective-permute-start(bf16[1024,384]{1,0:T(8,128)(2,1)} %get-tuple-element.85.rest_2_.kv_ref), channel_id=1, source_target_pairs={{8,0},{12,4},{16,8},{20,12},{24,16},{28,20},{9,1},{13,5},{17,9},{2... | collective-permute-start | bytes 2359304 | tf_op jit(solution)/shard_map/ppermute | solution.py:32
  33.9 62.9 %collective-permute-start.13 = (bf16[1744,768]{1,0:T(8,128)(2,1)}, bf16[1744,768]{1,0:T(8,128)(2,1)}, u32[]{:S(2)}, u32[]{:S(2)}) collective-permute-start(bf16[1744,768]{1,0:T(8,128)(2,1)} %slice_dynamic-update-slice_fusion.refs_8_), channel_id=1, source_target_pairs={{0,2},{1,3},{2,0},{3,1},{4,6},{5,7},{6,4},{7,5},{8,10},{9,11},{10,... | collective-permute-start | bytes 8036360 | tf_op jit(solution)/shard_map/ppermute | solution.py:26
  35.2 21.1 %collective-permute-start.8 = (bf16[1024,384]{1,0:T(8,128)(2,1)}, bf16[1024,384]{1,0:T(8,128)(2,1)S(1)}, u32[]{:S(2)}, u32[]{:S(2)}) collective-permute-start(bf16[1024,384]{1,0:T(8,128)(2,1)} %get-tuple-element.85.rest_2_.kv_ref), channel_id=1, source_target_pairs={{0,4},{4,0},{8,12},{12,8},{16,20},{20,16},{24,28},{28,24},{1,5},{5... | collective-permute-start | bytes 2359304 | tf_op jit(solution)/shard_map/ppermute | solution.py:26
  68.8 28.0 %collective-permute-start.11 = (bf16[1024,192]{1,0:T(8,128)(2,1)}, bf16[1024,192]{1,0:T(8,128)(2,1)}, u32[]{:S(2)}, u32[]{:S(2)}) collective-permute-start(bf16[1024,192]{1,0:T(8,128)(2,1)} %get-tuple-element.113.q_ref.rest_2_), channel_id=1, source_target_pairs={{0,4},{4,8},{8,12},{12,16},{16,20},{20,24},{24,28},{1,5},{5,9},{9,... | collective-permute-start | bytes 1179656 | tf_op jit(solution)/shard_map/ppermute | solution.py:32
  73.6 23.2 %collective-permute-start.12 = (bf16[1024,192]{1,0:T(8,128)(2,1)}, bf16[1024,192]{1,0:T(8,128)(2,1)}, u32[]{:S(2)}, u32[]{:S(2)}) collective-permute-start(bf16[1024,192]{1,0:T(8,128)(2,1)} %get-tuple-element.113.q_ref.rest_2_), channel_id=1, source_target_pairs={{4,0},{8,4},{12,8},{16,12},{20,16},{24,20},{28,24},{5,1},{9,5},{13... | collective-permute-start | bytes 1179656 | tf_op jit(solution)/shard_map/ppermute | solution.py:32
  75.0 25.7 %collective-permute-start.17 = (bf16[1744,768]{1,0:T(8,128)(2,1)}, bf16[1744,768]{1,0:T(8,128)(2,1)}, u32[]{:S(2)}, u32[]{:S(2)}) collective-permute-start(bf16[1744,768]{1,0:T(8,128)(2,1)} %slice_dynamic-update-slice_fusion.refs_8_), channel_id=1, source_target_pairs={{0,1},{1,0},{2,3},{3,2},{4,5},{5,4},{6,7},{7,6},{8,9},{9,8},{10,11... | collective-permute-start | bytes 8036360 | tf_op jit(solution)/shard_map/ppermute | solution.py:26
  96.8 22.5 %collective-permute-start.18 = (bf16[1744,768]{1,0:T(8,128)(2,1)}, bf16[1744,768]{1,0:T(8,128)(2,1)}, u32[]{:S(2)}, u32[]{:S(2)}) collective-permute-start(bf16[1744,768]{1,0:T(8,128)(2,1)} %collective-permute-done.13.refs_10_), channel_id=1, source_target_pairs={{0,1},{1,0},{2,3},{3,2},{4,5},{5,4},{6,7},{7,6},{8,9},{9,8},{10,11... | collective-permute-start | bytes 8036360 | tf_op jit(solution)/shard_map/ppermute | solution.py:26
  106.4 37.8 %collective-permute-start.19 = (bf16[1024,192]{1,0:T(8,128)(2,1)}, bf16[1024,192]{1,0:T(8,128)(2,1)}, u32[]{:S(2)}, u32[]{:S(2)}) collective-permute-start(bf16[1024,192]{1,0:T(8,128)(2,1)} %get-tuple-element.113.q_ref.rest_2_), channel_id=1, source_target_pairs={{0,8},{4,12},{8,16},{12,20},{16,24},{20,28},{1,9},{5,13},{9,17},{1... | collective-permute-start | bytes 1179656 | tf_op jit(solution)/shard_map/ppermute | solution.py:32
  117.9 26.4 %collective-permute-start.20 = (bf16[1024,192]{1,0:T(8,128)(2,1)}, bf16[1024,192]{1,0:T(8,128)(2,1)}, u32[]{:S(2)}, u32[]{:S(2)}) collective-permute-start(bf16[1024,192]{1,0:T(8,128)(2,1)} %get-tuple-element.113.q_ref.rest_2_), channel_id=1, source_target_pairs={{8,0},{12,4},{16,8},{20,12},{24,16},{28,20},{9,1},{13,5},{17,9},{2... | collective-permute-start | bytes 1179656 | tf_op jit(solution)/shard_map/ppermute | solution.py:32
  154.8 33.8 %collective-permute-start.30 = (bf16[768,768]{1,0:T(8,128)(2,1)S(1)}, bf16[768,768]{1,0:T(8,128)(2,1)S(1)}, u32[]{:S(2)}, u32[]{:S(2)}) collective-permute-start(bf16[768,768]{1,0:T(8,128)(2,1)S(1)} %get-tuple-element.157), channel_id=1, source_target_pairs={{0,2},{1,3},{2,0},{3,1},{4,6},{5,7},{6,4},{7,5},{8,10},{9,11},{10,... | collective-permute-start | bytes 3538952 | tf_op jit(solution)/shard_map/ppermute | solution.py:26
  158.9 29.7 %collective-permute-start.25 = (bf16[1024,256]{1,0:T(8,128)(2,1)S(1)}, bf16[1024,256]{1,0:T(8,128)(2,1)S(1)}, u32[]{:S(2)}, u32[]{:S(2)}) collective-permute-start(bf16[1024,256]{1,0:T(8,128)(2,1)S(1)} %layer_gather.1.grad_ref.rest_7_), channel_id=1, source_target_pairs={{0,8},{4,12},{8,16},{12,20},{16,24},{20,28},{1,9},{5,13},{9,17},{1... | collective-permute-start | bytes 1572872 | tf_op jit(solution)/shard_map/ppermute | solution.py:32
  163.5 28.5 %collective-permute-start.26 = (bf16[1024,256]{1,0:T(8,128)(2,1)S(1)}, bf16[1024,256]{1,0:T(8,128)(2,1)S(1)}, u32[]{:S(2)}, u32[]{:S(2)}) collective-permute-start(bf16[1024,256]{1,0:T(8,128)(2,1)S(1)} %layer_gather.1.grad_ref.rest_7_), channel_id=1, source_target_pairs={{0,4},{4,8},{8,12},{12,16},{16,20},{20,24},{24,28},{1,5},{5,9},{9,... | collective-permute-start | bytes 1572872 | tf_op jit(solution)/shard_map/ppermute | solution.py:32
  169.8 22.3 %collective-permute-start.27 = (bf16[1024,256]{1,0:T(8,128)(2,1)S(1)}, bf16[1024,256]{1,0:T(8,128)(2,1)S(1)}, u32[]{:S(2)}, u32[]{:S(2)}) collective-permute-start(bf16[1024,256]{1,0:T(8,128)(2,1)S(1)} %layer_gather.1.grad_ref.rest_7_), channel_id=1, source_target_pairs={{4,0},{8,4},{12,8},{16,12},{20,16},{24,20},{28,24},{5,1},{9,5},{13... | collective-permute-start | bytes 1572872 | tf_op jit(solution)/shard_map/ppermute | solution.py:32
  171.1 24.8 %collective-permute-start.28 = (bf16[1024,256]{1,0:T(8,128)(2,1)S(1)}, bf16[1024,256]{1,0:T(8,128)(2,1)S(1)}, u32[]{:S(2)}, u32[]{:S(2)}) collective-permute-start(bf16[1024,256]{1,0:T(8,128)(2,1)S(1)} %layer_gather.1.grad_ref.rest_7_), channel_id=1, source_target_pairs={{8,0},{12,4},{16,8},{20,12},{24,16},{28,20},{9,1},{13,5},{17,9},{2... | collective-permute-start | bytes 1572872 | tf_op jit(solution)/shard_map/ppermute | solution.py:32
  198.7 35.6 %collective-permute-start.32 = (bf16[1024,768]{1,0:T(8,128)(2,1)}, bf16[1024,768]{1,0:T(8,128)(2,1)}, u32[]{:S(2)}, u32[]{:S(2)}) collective-permute-start(bf16[1024,768]{1,0:T(8,128)(2,1)} %get-tuple-element.155), channel_id=1, source_target_pairs={{0,2},{1,3},{2,0},{3,1},{4,6},{5,7},{6,4},{7,5},{8,10},{9,11},{10,... | collective-permute-start | bytes 4718600 | tf_op jit(solution)/shard_map/ppermute | solution.py:26
  202.3 23.8 %collective-permute-start.31 = (bf16[384,768]{1,0:T(8,128)(2,1)}, bf16[384,768]{1,0:T(8,128)(2,1)}, u32[]{:S(2)}, u32[]{:S(2)}) collective-permute-start(bf16[384,768]{1,0:T(8,128)(2,1)} %get-tuple-element.161), channel_id=1, source_target_pairs={{0,4},{4,0},{8,12},{12,8},{16,20},{20,16},{24,28},{28,24},{1,5},{5... | collective-permute-start | bytes 1769480 | tf_op jit(solution)/shard_map/ppermute | solution.py:26
  245.6 22.6 %collective-permute-start.48 = (bf16[192,768]{1,0:T(8,128)(2,1)S(1)}, bf16[192,768]{1,0:T(8,128)(2,1)S(1)}, u32[]{:S(2)}, u32[]{:S(2)}) collective-permute-start(bf16[192,768]{1,0:T(8,128)(2,1)S(1)} %add_convert_fusion.16), channel_id=1, source_target_pairs={{0,8},{4,12},{8,0},{12,4},{16,24},{20,28},{24,16},{28,20},{1,9},{5... | collective-permute-start | bytes 884744 | tf_op jit(solution)/shard_map/ppermute | solution.py:26
  251.7 20.6 %collective-permute-start.43 = (bf16[512,768]{1,0:T(8,128)(2,1)S(1)}, bf16[512,768]{1,0:T(8,128)(2,1)S(1)}, u32[]{:S(2)}, u32[]{:S(2)}) collective-permute-start(bf16[512,768]{1,0:T(8,128)(2,1)S(1)} %get-tuple-element.160), channel_id=1, source_target_pairs={{0,4},{4,0},{8,12},{12,8},{16,20},{20,16},{24,28},{28,24},{1,5},{5... | collective-permute-start | bytes 2359304 | tf_op jit(solution)/shard_map/ppermute | solution.py:26
  261.9 33.9 %collective-permute-start.33 = (bf16[2,256,768]{2,1,0:T(8,128)(2,1)S(1)}, bf16[2,256,768]{2,1,0:T(8,128)(2,1)S(1)}, u32[]{:S(2)}, u32[]{:S(2)}) collective-permute-start(bf16[2,256,768]{2,1,0:T(8,128)(2,1)S(1)} %get-tuple-element.169), channel_id=1, source_target_pairs={{0,1},{1,0},{2,3},{3,2},{4,5},{5,4},{6,7},{7,6},{8,9},{9,8},{10,11... | collective-permute-start | bytes 2359304 | tf_op jit(solution)/shard_map/ppermute | solution.py:26
  269.3 21.1 %collective-permute-start.49 = (bf16[192,768]{1,0:T(8,128)(2,1)S(1)}, bf16[192,768]{1,0:T(8,128)(2,1)S(1)}, u32[]{:S(2)}, u32[]{:S(2)}) collective-permute-start(bf16[192,768]{1,0:T(8,128)(2,1)S(1)} %add_convert_fusion.15), channel_id=1, source_target_pairs={{0,16},{4,20},{8,24},{12,28},{16,0},{20,4},{24,8},{28,12},{1,17},{... | collective-permute-start | bytes 884744 | tf_op jit(solution)/shard_map/ppermute | solution.py:26
  272.4 22.6 %collective-permute-start.44 = (bf16[256,768]{1,0:T(8,128)(2,1)S(1)}, bf16[256,768]{1,0:T(8,128)(2,1)S(1)}, u32[]{:S(2)}, u32[]{:S(2)}) collective-permute-start(bf16[256,768]{1,0:T(8,128)(2,1)S(1)} %add_convert_fusion.10), channel_id=1, source_target_pairs={{0,8},{4,12},{8,0},{12,4},{16,24},{20,28},{24,16},{28,20},{1,9},{5... | collective-permute-start | bytes 1179656 | tf_op jit(solution)/shard_map/ppermute | solution.py:26
  295.1 20.5 %collective-permute-start.45 = (bf16[256,768]{1,0:T(8,128)(2,1)S(1)}, bf16[256,768]{1,0:T(8,128)(2,1)S(1)}, u32[]{:S(2)}, u32[]{:S(2)}) collective-permute-start(bf16[256,768]{1,0:T(8,128)(2,1)S(1)} %add_convert_fusion.9), channel_id=1, source_target_pairs={{0,16},{4,20},{8,24},{12,28},{16,0},{20,4},{24,8},{28,12},{1,17},{... | collective-permute-start | bytes 1179656 | tf_op jit(solution)/shard_map/ppermute | solution.py:26
  312.7 20.4 %collective-permute-start.42 = (bf16[4,96,640]{2,1,0:T(8,128)(2,1)S(1)}, bf16[4,96,640]{2,1,0:T(8,128)(2,1)S(1)}, u32[]{:S(2)}, u32[]{:S(2)}) collective-permute-start(bf16[4,96,640]{2,1,0:T(8,128)(2,1)S(1)} %maximum_select_fusion.5), channel_id=1, source_target_pairs={{0,4},{4,0},{8,12},{12,8},{16,20},{20,16},{24,28},{28,24},{1,5},{5... | collective-permute-start | bytes 1474568 | tf_op jit(solution)/shard_map/ppermute | solution.py:26
  (83 other events, 944.4 us)

commit v6 on v5

--- a/solution.py
+++ b/solution.py
@@ -14,6 +14,7 @@
 SPAN_K = 768
 TILE_K = 256
 SPAN_Q = 768
+CHUNK = 256
 
 masked_score = -1e30
 epsilon = 1e-06
@@ -50,10 +51,6 @@
     return copies
 
 
-def lanes_of(values, size):
-    return jnp.tile(values, (1, size // 128))
-
-
 def head_of(tile0, tile1, head):
     lane = lax.broadcasted_iota(jnp.int32, tile0.shape, 1)
     if head == 0:
@@ -63,21 +60,34 @@
     return tile1
 
 
+def turned(source, target, lanes, low, high):
+    def turn(i, carry):
+        rows = pl.ds(pl.multiple_of(i * 256, 256), 256)
+        target[:, rows] = source[rows, lanes].T
+        return carry
+
+    lax.fori_loop(low, high, turn, 0)
+
+
+def inside(span_ref, first, begin, rows):
+    own = pl.ds(first, TILE_Q)
+    place = begin + lax.broadcasted_iota(jnp.int32, (rows, TILE_Q), 0)
+    return (place >= span_ref[0:1, own]) & (place < span_ref[1:2, own])
+
+
 def forward_kernel(bounds, q_ref, span_ref, *rest):
-    pieces, rest = rest[:-11], rest[-11:]
-    outs, (wide_ref, stat_ref, kv, top, total, accum, sem) = rest[:4], rest[4:]
+    pieces, rest = rest[:-10], rest[-10:]
+    outs, (wide_ref, row_ref, stat_ref, kv, vt, sem) = rest[:4], rest[4:]
     step = pl.program_id(0)
 
     @pl.when(step == 0)
     def _():
-        for copy in load_window(pieces, kv, sem, [bounds[8 + i] for i in range(len(pieces))]):
+        for copy in load_window(pieces, kv, sem, [bounds[10 + i] for i in range(len(pieces))]):
             copy.wait()
+        turned(kv, vt, slice(192, 384), bounds[8], bounds[9])
 
     first = pl.multiple_of(step * TILE_Q, TILE_Q)
     here = pl.ds(first, TILE_Q)
-    top[...] = jnp.full_like(top, masked_score)
-    total[...] = jnp.zeros_like(total)
-    accum[...] = jnp.zeros_like(accum)
     q_tile = q_ref[here, :]
     heads = [head_of(q_tile[:, :128], q_tile[:, 128:], h) for h in range(3)]
     lower, count = bounds[2 * step], bounds[2 * step + 1]
@@ -85,42 +95,47 @@
     def run(i, carry):
         begin = pl.multiple_of(lower + i * SPAN_K, 128)
         rows = pl.ds(begin, SPAN_K)
-        keys = lax.broadcasted_iota(jnp.int32, (TILE_Q, SPAN_K), 1)
-        allowed = (keys >= span_ref[here, 0:1] - begin) & (keys < span_ref[here, 1:2] - begin)
-        scores = [rows_nt(heads[h], kv[rows, 0:128] if h < 2 else kv[rows, 128:192]) for h in range(3)]
+        allowed = inside(span_ref, first, begin, SPAN_K)
+        after = []
+
+        def ahead(h):
+            score = rows_nt(kv[rows, 0:128] if h < 2 else kv[rows, 128:192], heads[h])
+            return jnp.where(allowed, score, masked_score)
+
+        coming = ahead(0)
         for h in range(3):
-            score = scores[h]
-            score = jnp.where(allowed, score, masked_score)
-            before = top[h]
-            newest = jnp.maximum(before, jnp.max(score, axis=1, keepdims=True))
+            score = coming
+            if h < 2:
+                coming = ahead(h + 1)
+            before, total, accum = carry[3 * h : 3 * h + 3]
+            newest = jnp.maximum(before, jnp.max(score, axis=0, keepdims=True))
             factor = jnp.exp(before - newest)
-            weight = jnp.exp(score - lanes_of(newest, SPAN_K))
-            part = weight[:, 0:128]
-            for j in range(1, SPAN_K // 128):
-                part = part + weight[:, 128 * j : 128 * j + 128]
-            total[h] = total[h] * factor + part
-            values = kv[rows, 128:256] if h == 0 else kv[rows, 256:384]
-            accum[h] = accum[h] * factor + rows_nn(weight.astype(bf16), values)
-            top[h] = newest
-        return carry
-
-    lax.fori_loop(0, count, run, 0)
-    lane = lax.broadcasted_iota(jnp.int32, (TILE_Q, 128), 1)
-    mixed, stats = [], jnp.zeros((TILE_Q, 128), f32)
+            weight = jnp.exp(score - newest)
+            total = total * factor + jnp.sum(weight, axis=0, keepdims=True)
+            made = rows_nn(vt[h * HEAD_DIM : (h + 1) * HEAD_DIM, rows], weight.astype(bf16))
+            after += [newest, total, accum * factor + made]
+        return tuple(after)
+
+    start = (
+        jnp.full((1, TILE_Q), masked_score, f32),
+        jnp.zeros((1, TILE_Q), f32),
+        jnp.zeros((HEAD_DIM, TILE_Q), f32),
+    )
+    state = lax.fori_loop(0, count, run, start * 3)
+    mixed = jnp.concatenate([state[3 * h + 2] / state[3 * h + 1] for h in range(3)], axis=0).T
+    line = lax.broadcasted_iota(jnp.int32, (128, TILE_Q), 0)
+    stats = jnp.zeros((128, TILE_Q), f32)
     for h in range(3):
-        mass = jnp.sum(total[h], axis=1, keepdims=True)
-        mixed.append(pltpu.roll(accum[h] / mass, HEAD_DIM, 1))
-        stats = jnp.where(lane == h, top[h] + jnp.log(mass), stats)
-    pair = jnp.where(lane < HEAD_DIM, mixed[0], mixed[1])
-    wide_ref[here, 0:128] = pair
-    wide_ref[here, 128:192] = mixed[2][:, :HEAD_DIM]
-    stat_ref[here, :] = stats
+        stats = jnp.where(line == h, state[3 * h] + jnp.log(state[3 * h + 1]), stats)
+    wide_ref[here, :] = mixed
+    row_ref[:, here] = stats[0:8, :]
+    stat_ref[here, :] = stats.T
+    low = mixed.astype(bf16)
     for r, out_ref in enumerate(outs):
 
-        @pl.when(bounds[14 + step] == r)
+        @pl.when(bounds[16 + step] == r)
         def _(out_ref=out_ref):
-            out_ref[:, 0:128] = pair.astype(bf16)
-            out_ref[:, 128:192] = mixed[2][:, :HEAD_DIM].astype(bf16)
+            out_ref[...] = low
 
 
 def whole_spec(shape):
@@ -138,18 +153,20 @@
             in_specs=[whole_spec(queries.shape), whole_spec(spans.shape)]
             + [pl.BlockSpec(memory_space=pl.ANY)] * len(pieces),
             out_specs=[whole_spec((TILE_Q, 192))] * 4
-            + [whole_spec((block, 192)), whole_spec((block, 128))],
+            + [whole_spec((block, 192)), whole_spec((8, block)), whole_spec((block, 128))],
             scratch_shapes=[
                 pltpu.VMEM((window, 384), bf16),
-                pltpu.VMEM((3, TILE_Q, 128), f32),
-                pltpu.VMEM((3, TILE_Q, 128), f32),
-                pltpu.VMEM((3, TILE_Q, 128), f32),
+                pltpu.VMEM((192, window), bf16),
                 pltpu.SemaphoreType.DMA((len(pieces),)),
             ],
         ),
         out_shape=[jax.ShapeDtypeStruct((TILE_Q, 192), bf16)] * 4
-        + [jax.ShapeDtypeStruct((block, 192), f32), jax.ShapeDtypeStruct((block, 128), f32)],
-        compiler_params=pltpu.CompilerParams(vmem_limit_bytes=40 * 2**20),
+        + [
+            jax.ShapeDtypeStruct((block, 192), f32),
+            jax.ShapeDtypeStruct((8, block), f32),
+            jax.ShapeDtypeStruct((block, 128), f32),
+        ],
+        compiler_params=pltpu.CompilerParams(vmem_limit_bytes=60 * 2**20),
         cost_estimate=pl.CostEstimate(
             flops=4 * block * 2304 * 192, bytes_accessed=6 * 2**20, transcendentals=block * 2304 * 3
         ),
@@ -157,58 +174,59 @@
     )(bounds, queries, spans, *pieces)
 
 
-def query_kernel(bounds, q_ref, span_ref, grad_ref, wide_ref, stat_ref, *rest):
-    pieces, (out_ref, kv, accum, sem) = rest[:-4], rest[-4:]
+def query_kernel(bounds, q_ref, span_ref, grad_ref, wide_ref, row_ref, *rest):
+    pieces, (out_ref, kv, kt, sem) = rest[:-4], rest[-4:]
     step = pl.program_id(0)
 
     @pl.when(step == 0)
     def _():
-        for copy in load_window(pieces, kv, sem, [bounds[8 + i] for i in range(len(pieces))]):
+        for copy in load_window(pieces, kv, sem, [bounds[10 + i] for i in range(len(pieces))]):
             copy.wait()
+        turned(kv, kt, slice(0, 192), bounds[8], bounds[9])
 
     first = pl.multiple_of(step * TILE_Q, TILE_Q)
     here = pl.ds(first, TILE_Q)
-    accum[...] = jnp.zeros_like(accum)
     q_tile = q_ref[here, :]
     heads = [head_of(q_tile[:, :128], q_tile[:, 128:], h) for h in range(3)]
     g_tile = grad_ref[here, :]
     lane = lax.broadcasted_iota(jnp.int32, (TILE_Q, 128), 1)
-    g_pair = g_tile[:, :128]
-    g_last = g_tile[:, 128:256]
     none = jnp.zeros((TILE_Q, 128), bf16)
-    r_pair = pltpu.roll(g_pair.astype(f32), HEAD_DIM, 1).astype(bf16)
-    r_last = pltpu.roll(g_last.astype(f32), HEAD_DIM, 1).astype(bf16)
+    r_pair = pltpu.roll(g_tile[:, :128].astype(f32), HEAD_DIM, 1).astype(bf16)
+    r_last = pltpu.roll(g_tile[:, 128:256].astype(f32), HEAD_DIM, 1).astype(bf16)
     grads = [
         jnp.where(lane >= HEAD_DIM, r_pair, none),
         jnp.where(lane < HEAD_DIM, r_pair, none),
         jnp.where(lane >= HEAD_DIM, r_last, none),
     ]
-    product_pair = g_pair.astype(f32) * wide_ref[here, 0:128]
-    product_last = g_tile[:, 128:192].astype(f32) * wide_ref[here, 128:192]
+    product = (g_tile[:, 0:192].astype(f32) * wide_ref[here, :]).T
     deltas = [
-        jnp.sum(jnp.where(lane < HEAD_DIM, product_pair, 0.0), axis=1, keepdims=True),
-        jnp.sum(jnp.where(lane < HEAD_DIM, 0.0, product_pair), axis=1, keepdims=True),
-        jnp.sum(product_last, axis=1, keepdims=True),
+        jnp.sum(product[h * HEAD_DIM : (h + 1) * HEAD_DIM], axis=0, keepdims=True) for h in range(3)
     ]
-    logs = [stat_ref[here, h : h + 1] for h in range(3)]
+    logs = [row_ref[h : h + 1, here] for h in range(3)]
     lower, count = bounds[2 * step], bounds[2 * step + 1]
 
     def run(i, carry):
         begin = pl.multiple_of(lower + i * SPAN_K, 128)
         rows = pl.ds(begin, SPAN_K)
-        keys = lax.broadcasted_iota(jnp.int32, (TILE_Q, SPAN_K), 1)
-        allowed = (keys >= span_ref[here, 0:1] - begin) & (keys < span_ref[here, 1:2] - begin)
-        S = [rows_nt(heads[h], kv[rows, 0:128] if h < 2 else kv[rows, 128:192]) for h in range(3)]
-        B = [rows_nt(grads[h], kv[rows, 128:256] if h == 0 else kv[rows, 256:384]) for h in range(3)]
+        allowed = inside(span_ref, first, begin, SPAN_K)
+        after = []
+
+        def ahead(h):
+            score = rows_nt(kv[rows, 0:128] if h < 2 else kv[rows, 128:192], heads[h])
+            return score, rows_nt(kv[rows, 128:256] if h == 0 else kv[rows, 256:384], grads[h])
+
+        coming = ahead(0)
         for h in range(3):
-            chance = jnp.exp(jnp.where(allowed, S[h] - logs[h], masked_score))
-            change = (chance * (B[h] - deltas[h])).astype(bf16)
-            accum[h] += rows_nn(change, kv[rows, 0:128] if h < 2 else kv[rows, 128:256])
-        return carry
-
-    lax.fori_loop(0, count, run, 0)
-    out_ref[here, 0:128] = (jnp.where(lane < HEAD_DIM, accum[0], accum[1]) * 0.125).astype(bf16)
-    out_ref[here, 128:192] = (accum[2][:, :HEAD_DIM] * 0.125).astype(bf16)
+            score, back = coming
+            if h < 2:
+                coming = ahead(h + 1)
+            chance = jnp.exp(jnp.where(allowed, score - logs[h], masked_score))
+            change = (chance * (back - deltas[h])).astype(bf16)
+            after.append(carry[h] + rows_nn(kt[h * HEAD_DIM : (h + 1) * HEAD_DIM, rows], change))
+        return tuple(after)
+
+    sums = lax.fori_loop(0, count, run, (jnp.zeros((HEAD_DIM, TILE_Q), f32),) * 3)
+    out_ref[here, :] = (jnp.concatenate(sums, axis=0).T * 0.125).astype(bf16)
 
 
 def attention_queries(bounds, queries, spans, grads, wide, stats, pieces):
@@ -224,7 +242,7 @@
             out_specs=whole_spec((block, 192)),
             scratch_shapes=[
                 pltpu.VMEM((window, 384), bf16),
-                pltpu.VMEM((3, TILE_Q, 128), f32),
+                pltpu.VMEM((192, window), bf16),
                 pltpu.SemaphoreType.DMA((len(pieces),)),
             ],
         ),
@@ -277,17 +295,27 @@
         place = reach * block + first + lax.broadcasted_iota(jnp.int32, (TILE_K, SPAN_Q), 0)
         allowed = (place >= span_ref[0:1, columns]) & (place < span_ref[1:2, columns])
         lanes = [slice(0, 128), slice(0, 128), slice(128, 192)]
-        parts = gs[columns, 192:256]
-        stats = rows_nt(selector, parts)
-        S = [rows_nt(keys[h], qs[columns, lanes[h]]) for h in range(3)]
-        B = [rows_nt(values[h], gs[columns, lanes[h]]) for h in range(3)]
-        for h in range(3):
-            score = S[h] - stats[h : h + 1, :]
-            chance = jnp.exp(jnp.where(allowed, score, masked_score))
-            change = (chance * (B[h] - stats[h + 3 : h + 4, :])).astype(bf16)
+        stats = rows_nt(selector, gs[columns, 192:256])
+        items = [(h, ch) for h in range(3) for ch in range(SPAN_Q // CHUNK)]
+
+        def ahead(item):
+            h, ch = item
+            here = pl.ds(pl.multiple_of(begin + ch * CHUNK, 128), CHUNK)
+            q_tile, g_tile = qs[here, lanes[h]], gs[here, lanes[h]]
+            return q_tile, g_tile, rows_nt(keys[h], q_tile), rows_nt(values[h], g_tile)
+
+        coming = ahead(items[0])
+        for n, (h, ch) in enumerate(items):
+            q_tile, g_tile, score, back = coming
+            if n + 1 < len(items):
+                coming = ahead(items[n + 1])
+            cols = slice(ch * CHUNK, (ch + 1) * CHUNK)
+            score = jnp.where(allowed[:, cols], score - stats[h : h + 1, cols], masked_score)
+            chance = jnp.exp(score)
+            change = (chance * (back - stats[h + 3 : h + 4, cols])).astype(bf16)
             size = 128 if h < 2 else HEAD_DIM
-            key_sum[h, :, 0:size] += rows_nn(change, qs[columns, lanes[h]])
-            value_sum[h, :, 0:size] += rows_nn(chance.astype(bf16), gs[columns, lanes[h]])
+            key_sum[h, :, 0:size] += rows_nn(change, q_tile)
+            value_sum[h, :, 0:size] += rows_nn(chance.astype(bf16), g_tile)
         return carry
 
     lax.fori_loop(0, count, run, 0)
@@ -393,13 +421,13 @@
 
 def dense_kernel(place_ref, *refs):
     mixed = refs[0:4]
-    tokens_ref, up_ref, small_ref, inner_bias_ref = refs[4:8]
-    packs = refs[8:12]
-    out_ref, grad_ref = refs[12:14]
-    back_refs = refs[14:18]
-    outer_refs, inner_refs = refs[18:20], refs[20:22]
-    w_out, w_inner, w_outer, hidden, activated, slopes = refs[22:28]
-    outer_made, inner_made, tail_made, sem, sent = refs[28:]
+    tokens_ref, up_ref = refs[4:6]
+    packs = refs[6:10]
+    out_ref, grad_ref = refs[10:12]
+    back_refs = refs[12:16]
+    outer_refs, inner_refs = refs[16:18], refs[18:20]
+    w_out, w_inner, w_outer, hidden, activated, slopes = refs[20:26]
+    outer_made, inner_made, tail_made, lines, bias_rows, sem, sent = refs[26:]
     rows, width = tokens_ref.shape
     groups = w_inner.shape[0]
     part = width // groups
@@ -424,12 +452,25 @@
         )
         for r in range(groups)
     ]
-    for copy in out_copies + [x for g in range(groups) for x in inner_copies(g)] + outer_copies:
+    line_copies = [
+        pltpu.make_async_copy(
+            packs[r].at[pl.ds(width + part, 16), :], lines.at[place_ref[r]], sem.at[2 + groups, r]
+        )
+        for r in range(groups)
+    ]
+    for copy in line_copies + out_copies + [x for g in range(groups) for x in inner_copies(g)] + outer_copies:
         copy.start()
 
-    out_bias, gain_one, shift_one = small_ref[0:1], small_ref[1:2], small_ref[2:3]
-    outer_bias, gain_two, shift_two = small_ref[3:4], small_ref[4:5], small_ref[5:6]
-
+    for copy in line_copies:
+        copy.wait()
+    small = [lines[k][:, 0:part].astype(f32) for k in range(groups)]
+    out_bias, gain_one, shift_one, outer_bias, gain_two, shift_two = (
+        jnp.concatenate([x[i : i + 1] for x in small], axis=1) for i in range(6)
+    )
+    for k in range(groups):
+        bias_rows[k : k + 1, :] = jnp.concatenate(
+            [small[k][6 + i : 7 + i] for i in range(groups)], axis=1
+        )
     for copy in out_copies:
         copy.wait()
     residual = tokens_ref[...].astype(f32) + out_bias
@@ -442,7 +483,7 @@
     def ahead(g, carry):
         for copy in inner_copies(g):
             copy.wait()
-        value = rows_nn(first_low, w_inner[g]) + inner_bias_ref[pl.ds(g, 1), :]
+        value = rows_nn(first_low, w_inner[g]) + bias_rows[pl.ds(g, 1), :]
         chance = 0.5 * (1.0 + lax.erf(value * (2.0**-0.5)))
         density = jnp.exp(-0.5 * value * value) * (2.0 * jnp.pi) ** -0.5
         slopes[g] = chance + value * density
@@ -544,7 +585,7 @@
         copy.wait()
 
 
-def dense(places, mixed_pieces, tokens, cotangent, small, inner_bias, packs):
+def dense(places, mixed_pieces, tokens, cotangent, packs):
     rows, width = tokens.shape
     groups = len(packs)
     part = width // groups
@@ -552,7 +593,7 @@
     hbm = pl.BlockSpec(memory_space=pl.ANY)
     return pl.pallas_call(
         dense_kernel,
-        in_specs=[pl.BlockSpec(memory_space=pltpu.SMEM)] + [vmem] * (groups + 4) + [hbm] * groups,
+        in_specs=[pl.BlockSpec(memory_space=pltpu.SMEM)] + [vmem] * (groups + 2) + [hbm] * groups,
         out_specs=[vmem] * (2 + groups) + [hbm] * 4,
         out_shape=[
             jax.ShapeDtypeStruct((rows, width), bf16),
@@ -571,7 +612,9 @@
             pltpu.VMEM((groups, width, width), bf16),
             pltpu.VMEM((groups, width, width), bf16),
             pltpu.VMEM((groups, part + 64, width), bf16),
-            pltpu.SemaphoreType.DMA((groups + 2, groups)),
+            pltpu.VMEM((groups, 16, width), bf16),
+            pltpu.VMEM((8, width), f32),
+            pltpu.SemaphoreType.DMA((groups + 3, groups)),
             pltpu.SemaphoreType.DMA((groups + 2, groups)),
         ],
         compiler_params=pltpu.CompilerParams(vmem_limit_bytes=48 * 2**20),
@@ -581,7 +624,7 @@
             transcendentals=2 * rows * width * groups,
         ),
         name="layer_dense",
-    )(places, *mixed_pieces, tokens, cotangent, small, inner_bias, *packs)
+    )(places, *mixed_pieces, tokens, cotangent, *packs)
 
 
 def gather_kernel(place_ref, p0, p1, p2, p3, wide_ref, stat_ref, out_ref):
@@ -693,11 +736,6 @@
         kept = functools.reduce(both, [half_of(x, bit, axis) for x in terms])
         terms = [kept, swapped(sent, axis_name, step)]
     return terms
-
-
-def full_sum(terms, axis_name, step):
-    block = functools.reduce(both, terms)
-    return both(block, swapped(block, axis_name, step))
 
 
 def gather_back(block, axis_name, order, axis):
@@ -772,20 +810,16 @@
     next_begin = lax.cummin(begins, axis=0, reverse=True)
     stops = jnp.concatenate([next_begin[1:], jnp.full((1,), window, jnp.int32)])
     starts = marks - base
-    spans_row = jnp.stack([starts, stops] + [jnp.zeros_like(starts)] * 6)
-    spans_column = spans_row[:, pad : pad + block].T
     own_starts = starts[pad : pad + block]
     own_stops = stops[pad : pad + block]
-
-    def bounds_of(tile, span):
-        lowest = own_starts.reshape(-1, tile)[:, 0] // 128 * 128
-        highest = own_stops.reshape(-1, tile)[:, -1]
-        count = (highest - lowest + span - 1) // span
-        lowest = jnp.minimum(lowest, (window - count * span) // 128 * 128)
-        return jnp.stack([lowest, count], axis=1).reshape(-1)
-
-    query_bounds = bounds_of(TILE_Q, SPAN_K)
-    key_bounds = bounds_of(TILE_K, SPAN_Q)
+    spans_row = jnp.stack([starts, stops] + [jnp.zeros_like(starts)] * 6)
+    spans = spans_row[:, pad : pad + block]
+    lowest = own_starts.reshape(-1, TILE_Q)[:, 0] // 128 * 128
+    highest = own_stops.reshape(-1, TILE_Q)[:, -1]
+    count = (highest - lowest + SPAN_K - 1) // SPAN_K
+    lowest = jnp.minimum(lowest, (window - count * SPAN_K) // 128 * 128)
+    reached = jnp.stack([jnp.min(lowest) // 256, (jnp.max(lowest + count * SPAN_K) + 255) // 256])
+    bounds = jnp.concatenate([jnp.stack([lowest, count], axis=1).reshape(-1), reached])
 
     block_tokens, queries, pair = project(places, token_pieces, weight_pieces, head_bias)
 
@@ -795,22 +829,24 @@
         return [own if d == 0 else shifted(own, "ctx", d) for d in distances]
 
     even = c % 2 == 0
+    beside_at = jnp.where(even, reach + 1, reach - 1) * block
+    missing_at = jnp.where(even, reach - 1, reach + 1) * block
+    load_at = jnp.stack(
+        [0 * missing_at, 2 * reach * block + 0 * missing_at, reach * block + 0 * missing_at]
+        + [beside_at, missing_at, missing_at + block // 2]
+    )
+    bounds = jnp.concatenate([bounds, load_at, places]).astype(jnp.int32)
     beside = swapped(pair, "ctx", 1)
     before, after = shifted(pair, "ctx", 2), shifted(pair, "ctx", -2)
     half = block // 2
+    before, after, bounds, spans, spans_row = lax.optimization_barrier(
+        (before, after, bounds, spans, spans_row)
+    )
     route = [(i, i + 2 if i % 2 == 0 else i - 2) for i in range(cycle)]
     route = [(i, j) for i, j in route if 0 <= j < cycle]
     upper = swapped(jnp.where(even, after[:half], before[:half]), "ctx", 1)
     lower = lax.ppermute(beside[half:], "ctx", route)
     pairs = [before, after, pair, beside, upper, lower]
-    beside_at = jnp.where(even, reach + 1, reach - 1) * block
-    missing_at = jnp.where(even, reach - 1, reach + 1) * block
-    load_at = jnp.stack(
-        [0 * missing_at, 2 * reach * block + 0 * missing_at, reach * block + 0 * missing_at]
-        + [beside_at, missing_at, missing_at + half]
-    )
-    query_bounds = jnp.concatenate([query_bounds, load_at, places]).astype(jnp.int32)
-
     small_own = jnp.stack(
         [out_bias, first_gain, first_shift, outer_bias, second_gain, second_shift]
     )
@@ -820,8 +856,8 @@
     pack = jnp.concatenate([outer_weight, out_weight, small_own] + inner_parts, axis=0)
     pack, _ = lax.optimization_barrier((pack, token_pieces[2:] + weight_pieces[1:]))
     pack_near, pack_far = swapped(pack, "wt", 1), swapped(pack, "wt", 2)
-    *mixed_pieces, mixed_wide, stat_columns = attention_forward(
-        query_bounds, queries, spans_column, pairs
+    *mixed_pieces, mixed_wide, stat_rows, stat_columns = attention_forward(
+        bounds, queries, spans, pairs
     )
     ready, _ = lax.optimization_barrier((queries, pairs))
     query_halo = [queries if d == 0 else shifted(ready, "ctx", d) if d * d == 1 else None for d in distances]
@@ -830,17 +866,13 @@
         (mixed_pieces, mixed_wide, stat_columns, close, pack_far)
     )
     packs = [pack, pack_near, pack_far, swapped(pack_far, "wt", 1)]
-    small = jnp.stack([x[width + part : width + part + 16, :part] for x in packs]).astype(f32)
-    small = [lax.dynamic_index_in_dim(small, w ^ k, 0, keepdims=False) for k in range(shards)]
-    small_rows = jnp.concatenate([x[:8] for x in small], axis=1)
-    inner_bias_rows = jnp.stack([x[6:10].reshape(-1) for x in small])
 
     mixed_pieces = [mixed_pieces[0]] + [
         swapped(mixed_pieces[r], "wt", r) for r in range(1, shards)
     ]
     far_ready, mixed_pieces = lax.optimization_barrier((queries, mixed_pieces))
     results = dense(
-        places, mixed_pieces, tokens, cotangent, small_rows, inner_bias_rows, packs
+        places, mixed_pieces, tokens, cotangent, packs
     )
     remote = [shifted(far_ready, "ctx", d) for d in distances if d * d > 1]
     results, remote = lax.optimization_barrier((results, remote))
@@ -861,7 +893,7 @@
     grad_halo = halo(grads)
     outer_terms = far_terms(outer_keep, outer_got)
     grad_query = attention_queries(
-        query_bounds, queries, spans_column, grads, mixed_wide, stat_columns, pairs
+        bounds, queries, spans, grads, mixed_wide, stat_rows, pairs
     )
     grad_query, grad_halo, outer_terms, inner_keep, inner_got = lax.optimization_barrier(
         (grad_query, grad_halo, outer_terms, inner_keep, inner_got)
@@ -870,20 +902,19 @@
     near_first = [1 << i for i in range(cycle.bit_length() - 1)]
     outer_terms = scatter_sum(outer_terms, "ctx", near_first[:1], 0)
     inner_terms = far_terms(inner_keep, inner_got)
-    grad_pair = attention_keys(key_bounds, pair, spans_row, query_halo, grad_halo)
+    grad_pair = attention_keys(bounds, pair, spans_row, query_halo, grad_halo)
     grad_pair, outer_terms, inner_terms = lax.optimization_barrier(
         (grad_pair, outer_terms, inner_terms)
     )
 
     head_grad, token_partial = head_grads(places, block_tokens, grad_query, grad_pair, weight_pieces)
-    halved, last = near_first[:-1], near_first[-1]
-    outer_part = full_sum(scatter_sum(outer_terms, "ctx", halved[1:], 0), "ctx", last)
-    inner_part = full_sum(scatter_sum(inner_terms, "ctx", halved, 0), "ctx", last)
-    head_part = full_sum(scatter_sum([head_grad], "ctx", halved, 1), "ctx", last)
+    outer_part = both(*scatter_sum(outer_terms, "ctx", near_first[1:], 0))
+    inner_part = both(*scatter_sum(inner_terms, "ctx", near_first, 0))
+    head_part = both(*scatter_sum([head_grad], "ctx", near_first, 1))
     token_got = swapped(token_partial[1::2], "wt", 1)
     token_sum = both(*far_terms(token_partial[0::2], token_got))
-    outer_total = gather_back(outer_part, "ctx", halved, 0)
-    inner_total = gather_back(inner_part, "ctx", halved, 0)
+    outer_total = gather_back(outer_part, "ctx", near_first, 0)
+    inner_total = gather_back(inner_part, "ctx", near_first, 0)
     head_pieces = [
         lax.dynamic_index_in_dim(head_part, w ^ r, 0, keepdims=False) for r in range(shards)
     ]
@@ -894,7 +925,7 @@
             for k in range(shards)
         ]
     )
-    head_total = gather_back(head_parts, "ctx", halved, 1)
+    head_total = gather_back(head_parts, "ctx", near_first, 1)
 
     tokens_gradient = grad_one + token_sum.astype(f32)
     key_total, value_total, query_total = (

time: 355 us -> 334 us (0.941)
  starting transfers between devices: 90.9 us -> 55.7 us
    ppermute x41 -> x44, starting transfers between devices: 49.3 us -> 22.9 us  [swapped(): return lax.ppermute(block, axis, [(i, i ^ bit) for i in range(count)])]
    ppermute x10, starting transfers between devices: 37.5 us -> 29.1 us  [shifted(): return lax.ppermute(block, axis, route)]
    unnamed x116 -> x132, local copies, waits for them, and re-layouts: 15.8 us -> 19.4 us
    ppermute x41 -> x44, waiting for transfers between devices: 96.9 us -> 98.8 us  [swapped(): return lax.ppermute(block, axis, [(i, i ^ bit) for i in range(count)])]
  transfers between devices with their start and end apart: 52 -> 55, of which waited for: 26 -> 30; matrix products, arithmetic and copies ran while one was open for 11% -> 13% of each run, Pallas kernels for 21% -> 23%
where the time goes in v6:
time: 334 us
  waiting for transfers between devices  124 us (37%)
  Pallas kernels  86.6 us (26%)
  starting transfers between devices  55.7 us (17%)
  other arithmetic  34.5 us (10%)
  local copies, waits for them, and re-layouts  28.7 us (9%)
  between operations  5.12 us (2%)
    ppermute x44, waiting for transfers between devices, swapped(): return lax.ppermute(block, axis, [(i, i ^ bit) for i in range(count)])  98.8 us
    ppermute x10, starting transfers between devices, shifted(): return lax.ppermute(block, axis, route)  29.1 us
    ppermute x44, starting transfers between devices, swapped(): return lax.ppermute(block, axis, [(i, i ^ bit) for i in range(count)])  22.9 us
    ppermute x10, waiting for transfers between devices, shifted(): return lax.ppermute(block, axis, route)  22 us
    pallas_call x1, Pallas kernels, attention_forward(): pl.pallas_call(forward_kernel, grid_spec=pltpu.PrefetchScalarGridSpec(num...  20 us
    pallas_call x1, Pallas kernels, attention_keys(): pl.pallas_call(functools.partial(key_kernel, count // 2), grid_spec=pltpu...  20 us
    pallas_call x1, Pallas kernels, dense(): pl.pallas_call(dense_kernel, in_specs=[pl.BlockSpec(memory_space=pltpu.SM...  19.9 us
    unnamed x132, local copies, waits for them, and re-layouts  19.4 us
  transfers between devices with their start and end apart: 55, of which 30 were waited for; matrix products, arithmetic and copies ran while one was open for 13% of the time, Pallas kernels for 23%

profile of v6, /device:TPU:0, one launch (start us, length us, event | category | flops | bytes accessed | tf_op | source)
XLA Modules:
  0.0 334.0 jit_solution(3338287608832200870)
XLA Ops:
  23.3 4.1 %layer_projection.1 = (bf16[1024,768]{1,0:T(8,128)(2,1)S(1)}, bf16[1024,192]{1,0:T(8,128)(2,1)S(1)}, bf16[1024,384]{1,0:T(8,128)(2,1)}) custom-call(s32[4]{0:T(128)S(1)} %pad_add_fusion.2.place_ref, bf16[256,768]{1,0:T(8,128)(2,1)S(1)} %copy-done.26, bf16[256,768]{1,0:T(8,128)(2,1)S(1)} %collective-permute-done.near, ...), custom_call_target="tpu_custom_call" | custom-call | flops 905969664 | bytes 5242880 | tf_op jit(solution)/shard_map/layer_projection/pallas_call | solution.py:384
  41.7 8.0 %collective-permute-done.6.rest_0_ = bf16[1024,384]{1,0:T(8,128)(2,1)S(1)} collective-permute-done((bf16[1024,384]{1,0:T(8,128)(2,1)}, bf16[1024,384]{1,0:T(8,128)(2,1)S(1)}, u32[]{:S(2)}, u32[]{:S(2)}) %collective-permute-start.6) | collective-permute-done | bytes 786464 | tf_op jit(solution)/shard_map/ppermute | solution.py:33
  49.6 4.1 %collective-permute-done.7.rest_1_ = bf16[1024,384]{1,0:T(8,128)(2,1)S(1)} collective-permute-done((bf16[1024,384]{1,0:T(8,128)(2,1)}, bf16[1024,384]{1,0:T(8,128)(2,1)S(1)}, u32[]{:S(2)}, u32[]{:S(2)}) %collective-permute-start.7) | collective-permute-done | bytes 786464 | tf_op jit(solution)/shard_map/ppermute | solution.py:33
  59.0 5.2 %collective-permute-done.9.rest_4_ = bf16[512,384]{1,0:T(8,128)(2,1)S(1)} collective-permute-done((bf16[512,384]{1,0:T(8,128)(2,1)S(1)}, bf16[512,384]{1,0:T(8,128)(2,1)S(1)}, u32[]{:S(2)}, u32[]{:S(2)}) %collective-permute-start.9) | collective-permute-done | bytes 393248 | tf_op jit(solution)/shard_map/ppermute | solution.py:27
  66.9 4.2 %collective-permute-start.11 = (bf16[1024,192]{1,0:T(8,128)(2,1)S(1)}, bf16[1024,192]{1,0:T(8,128)(2,1)S(1)}, u32[]{:S(2)}, u32[]{:S(2)}) collective-permute-start(bf16[1024,192]{1,0:T(8,128)(2,1)S(1)} %get-tuple-element.123.q_ref.rest_2_), channel_id=1, source_target_pairs={{0,4},{4,8},{8,12},{12,16},{16,20},{20,24},{24,28},{1,5},{5,9},{9,... | collective-permute-start | bytes 1179656 | tf_op jit(solution)/shard_map/ppermute | solution.py:33
  72.5 20.0 %attention_forward.1 = (bf16[256,192]{1,0:T(8,128)(2,1)}, bf16[256,192]{1,0:T(8,128)(2,1)}, bf16[256,192]{1,0:T(8,128)(2,1)}, bf16[256,192]{1,0:T(8,128)(2,1)}, ...) custom-call(s32[20]{0:T(128)} %concatenate.99.bounds, bf16[1024,192]{1,0:T(8,128)(2,1)} %copy-done.12, ...), custom_call_target="tpu_custom_call" | custom-call | flops 1811939328 | bytes 6291456 | tf_op jit(solution)/shard_map/attention_forward/pallas_call | solution.py:148
  101.9 8.6 %collective-permute-start.19 = (bf16[1024,192]{1,0:T(8,128)(2,1)}, bf16[1024,192]{1,0:T(8,128)(2,1)S(1)}, u32[]{:S(2)}, u32[]{:S(2)}) collective-permute-start(bf16[1024,192]{1,0:T(8,128)(2,1)} %copy-done.12), channel_id=1, source_target_pairs={{0,8},{4,12},{8,16},{12,20},{16,24},{20,28},{1,9},{5,13},{9,17},{1... | collective-permute-start | bytes 1179656 | tf_op jit(solution)/shard_map/ppermute | solution.py:33
  116.5 19.9 %layer_dense.1 = (bf16[256,768]{1,0:T(8,128)(2,1)}, f32[256,768]{1,0:T(8,128)S(1)}, bf16[256,192]{1,0:T(8,128)(2,1)S(1)}, bf16[256,192]{1,0:T(8,128)(2,1)S(1)}, ...) custom-call(s32[4]{0:T(128)S(1)} %pad_add_fusion.2.place_ref, ...), custom_call_target="tpu_custom_call" | custom-call | flops 14495514624 | bytes 25165824 | tf_op jit(solution)/shard_map/layer_dense/pallas_call | solution.py:594
  151.8 4.6 %collective-permute-start.25 = (bf16[1024,256]{1,0:T(8,128)(2,1)S(1)}, bf16[1024,256]{1,0:T(8,128)(2,1)S(1)}, u32[]{:S(2)}, u32[]{:S(2)}) collective-permute-start(bf16[1024,256]{1,0:T(8,128)(2,1)S(1)} %layer_gather.1.grad_ref.rest_7_), channel_id=1, source_target_pairs={{0,8},{4,12},{8,16},{12,20},{16,24},{20,28},{1,9},{5,13},{9,17},{1... | collective-permute-start | bytes 1572872 | tf_op jit(solution)/shard_map/ppermute | solution.py:33
  160.7 15.1 %attention_queries.1.query_ref = bf16[1024,192]{1,0:T(8,128)(2,1)S(1)} custom-call(s32[20]{0:T(128)S(1)} %copy-done.11, bf16[1024,192]{1,0:T(8,128)(2,1)S(1)} %copy-done.13, s32[8,1024]{1,0:T(8,128)S(1)} %copy-done.10, bf16[1024,256]{1,0:T(8,128)(2,1)S(1)} %layer_gather.1.grad_ref.rest_7_, f32[1024,192]{1,0:T(8,128)S(1)} %copy-done, ...), custom_call_target="tpu_custom_call" | custom-call | flops 2717908992 | bytes 6291456 | tf_op jit(solution)/shard_map/attention_queries/pallas_call | solution.py:235
  175.9 4.3 %collective-permute-done.26.rest_6_ = bf16[1024,256]{1,0:T(8,128)(2,1)S(1)} collective-permute-done((bf16[1024,256]{1,0:T(8,128)(2,1)S(1)}, bf16[1024,256]{1,0:T(8,128)(2,1)S(1)}, u32[]{:S(2)}, u32[]{:S(2)}) %collective-permute-start.26) | collective-permute-done | bytes 524320 | tf_op jit(solution)/shard_map/ppermute | solution.py:33
  180.2 5.7 %collective-permute-done.28.rest_9_ = bf16[1024,256]{1,0:T(8,128)(2,1)S(1)} collective-permute-done((bf16[1024,256]{1,0:T(8,128)(2,1)S(1)}, bf16[1024,256]{1,0:T(8,128)(2,1)S(1)}, u32[]{:S(2)}, u32[]{:S(2)}) %collective-permute-start.28) | collective-permute-done | bytes 524320 | tf_op jit(solution)/shard_map/ppermute | solution.py:33
  197.1 20.0 %attention_keys.1.pair_ref = bf16[1024,384]{1,0:T(8,128)(2,1)S(1)} custom-call(s32[20]{0:T(128)S(1)} %copy-done.11, bf16[1024,384]{1,0:T(8,128)(2,1)} %get-tuple-element.91.rest_2_.kv_ref, s32[8,5120]{1,0:T(8,128)S(1)} %add_add_fusion.span_ref, bf16[1024,192]{1,0:T(8,128)(2,1)S(1)} %collective-permute-done.19.rest_0_, bf16[1024,192]{1,0:T(8,128)(2,1)S(1)} %copy-done.15, ...), custom_call_target="tpu_custom_call" | custom-call | flops 3623878656 | bytes 8388608 | tf_op jit(solution)/shard_map/attention_keys/pallas_call | solution.py:334
  217.1 6.7 %collective-permute-done.32 = bf16[1024,768]{1,0:T(8,128)(2,1)} collective-permute-done((bf16[1024,768]{1,0:T(8,128)(2,1)}, bf16[1024,768]{1,0:T(8,128)(2,1)}, u32[]{:S(2)}, u32[]{:S(2)}) %collective-permute-start.32) | collective-permute-done | bytes 1572896 | tf_op jit(solution)/shard_map/ppermute | solution.py:27
  223.9 5.0 %layer_heads.1 = (bf16[4,192,640]{2,1,0:T(8,128)(2,1)S(1)}, bf16[4,256,768]{2,1,0:T(8,128)(2,1)S(1)}) custom-call(s32[4]{0:T(128)S(1)} %pad_add_fusion.2.place_ref, bf16[1024,768]{1,0:T(8,128)(2,1)S(1)} %copy-done.40, bf16[1024,192]{1,0:T(8,128)(2,1)S(1)} %copy-done.42, bf16[1024,384]{1,0:T(8,128)(2,1)S(1)} %attention_keys.1.pair_ref, ...), custom_call_target="tpu_custom_call" | custom-call | flops 1811939328 | bytes 8388608 | tf_op jit(solution)/shard_map/layer_heads/pallas_call | solution.py:703
  239.9 4.3 %collective-permute-done.35 = bf16[4,96,640]{2,1,0:T(8,128)(2,1)} collective-permute-done((bf16[4,96,640]{2,1,0:T(8,128)(2,1)}, bf16[4,96,640]{2,1,0:T(8,128)(2,1)}, u32[]{:S(2)}, u32[]{:S(2)}) %collective-permute-start.35) | collective-permute-done | bytes 491552 | tf_op jit(solution)/shard_map/ppermute | solution.py:27
  248.4 4.8 %collective-permute-done.36 = bf16[4,48,640]{2,1,0:T(8,128)(2,1)S(1)} collective-permute-done((bf16[4,48,640]{2,1,0:T(8,128)(2,1)S(1)}, bf16[4,48,640]{2,1,0:T(8,128)(2,1)S(1)}, u32[]{:S(2)}, u32[]{:S(2)}) %collective-permute-start.36) | collective-permute-done | bytes 245792 | tf_op jit(solution)/shard_map/ppermute | solution.py:27
  253.4 4.4 %collective-permute-done.44 = bf16[512,768]{1,0:T(8,128)(2,1)S(1)} collective-permute-done((bf16[512,768]{1,0:T(8,128)(2,1)S(1)}, bf16[512,768]{1,0:T(8,128)(2,1)S(1)}, u32[]{:S(2)}, u32[]{:S(2)}) %collective-permute-start.44) | collective-permute-done | bytes 786464 | tf_op jit(solution)/shard_map/ppermute | solution.py:27
  258.1 4.4 %collective-permute-done.37 = bf16[4,24,640]{2,1,0:T(8,128)(2,1)S(1)} collective-permute-done((bf16[4,24,640]{2,1,0:T(8,128)(2,1)S(1)}, bf16[4,24,640]{2,1,0:T(8,128)(2,1)S(1)}, u32[]{:S(2)}, u32[]{:S(2)}) %collective-permute-start.37) | collective-permute-done | bytes 122912 | tf_op jit(solution)/shard_map/ppermute | solution.py:27
  272.6 8.5 %collective-permute-done.41 = bf16[4,24,640]{2,1,0:T(8,128)(2,1)S(1)} collective-permute-done((bf16[4,24,640]{2,1,0:T(8,128)(2,1)S(1)}, bf16[4,24,640]{2,1,0:T(8,128)(2,1)S(1)}, u32[]{:S(2)}, u32[]{:S(2)}) %collective-permute-start.41) | collective-permute-done | bytes 122912 | tf_op jit(solution)/shard_map/ppermute | solution.py:27
  290.0 5.2 %collective-permute-done.47 = bf16[128,768]{1,0:T(8,128)(2,1)S(1)} collective-permute-done((bf16[128,768]{1,0:T(8,128)(2,1)S(1)}, bf16[128,768]{1,0:T(8,128)(2,1)S(1)}, u32[]{:S(2)}, u32[]{:S(2)}) %collective-permute-start.47) | collective-permute-done | bytes 196640 | tf_op jit(solution)/shard_map/ppermute | solution.py:27
  297.6 4.0 %collective-permute-done.54 = bf16[384,768]{1,0:T(8,128)(2,1)} collective-permute-done((bf16[384,768]{1,0:T(8,128)(2,1)S(1)}, bf16[384,768]{1,0:T(8,128)(2,1)}, u32[]{:S(2)}, u32[]{:S(2)}) %collective-permute-start.54) | collective-permute-done | bytes 589856 | tf_op jit(solution)/shard_map/ppermute | solution.py:27
  304.4 6.1 %collective-permute-done.43 = bf16[4,96,640]{2,1,0:T(8,128)(2,1)S(1)} collective-permute-done((bf16[4,96,640]{2,1,0:T(8,128)(2,1)S(1)}, bf16[4,96,640]{2,1,0:T(8,128)(2,1)S(1)}, u32[]{:S(2)}, u32[]{:S(2)}) %collective-permute-start.43) | collective-permute-done | bytes 491552 | tf_op jit(solution)/shard_map/ppermute | solution.py:27
  315.5 14.0 %collective-permute-done.49 = bf16[512,768]{1,0:T(8,128)(2,1)S(1)} collective-permute-done((bf16[512,768]{1,0:T(8,128)(2,1)S(1)}, bf16[512,768]{1,0:T(8,128)(2,1)S(1)}, u32[]{:S(2)}, u32[]{:S(2)}) %collective-permute-start.49) | collective-permute-done | bytes 786464 | tf_op jit(solution)/shard_map/ppermute | solution.py:27
  (313 shorter events, 137.7 us)
Async XLA Ops:
  0.7 19.6 %collective-permute-start.1 = (bf16[256,768]{1,0:T(8,128)(2,1)}, bf16[256,768]{1,0:T(8,128)(2,1)S(1)}, u32[]{:S(2)}, u32[]{:S(2)}) collective-permute-start(bf16[256,768]{1,0:T(8,128)(2,1)} %refs_4_.1), channel_id=1, source_target_pairs={{0,2},{1,3},{2,0},{3,1},{4,6},{5,7},{6,4},{7,5},{8,10},{9,11},{10,... | collective-permute-start | bytes 1179656 | tf_op jit(solution)/shard_map/ppermute | solution.py:27
  3.7 19.5 %collective-permute-start = (bf16[256,768]{1,0:T(8,128)(2,1)}, bf16[256,768]{1,0:T(8,128)(2,1)S(1)}, u32[]{:S(2)}, u32[]{:S(2)}) collective-permute-start(bf16[256,768]{1,0:T(8,128)(2,1)} %refs_4_.1), channel_id=1, source_target_pairs={{0,1},{1,0},{2,3},{3,2},{4,5},{5,4},{6,7},{7,6},{8,9},{9,8},{10,11... | collective-permute-start | bytes 1179656 | tf_op jit(solution)/shard_map/ppermute | solution.py:27
  28.6 21.1 %collective-permute-start.6 = (bf16[1024,384]{1,0:T(8,128)(2,1)}, bf16[1024,384]{1,0:T(8,128)(2,1)S(1)}, u32[]{:S(2)}, u32[]{:S(2)}) collective-permute-start(bf16[1024,384]{1,0:T(8,128)(2,1)} %get-tuple-element.91.rest_2_.kv_ref), channel_id=1, source_target_pairs={{0,8},{4,12},{8,16},{12,20},{16,24},{20,28},{1,9},{5,13},{9,17},{1... | collective-permute-start | bytes 2359304 | tf_op jit(solution)/shard_map/ppermute | solution.py:33
  32.1 21.6 %collective-permute-start.7 = (bf16[1024,384]{1,0:T(8,128)(2,1)}, bf16[1024,384]{1,0:T(8,128)(2,1)S(1)}, u32[]{:S(2)}, u32[]{:S(2)}) collective-permute-start(bf16[1024,384]{1,0:T(8,128)(2,1)} %get-tuple-element.91.rest_2_.kv_ref), channel_id=1, source_target_pairs={{8,0},{12,4},{16,8},{20,12},{24,16},{28,20},{9,1},{13,5},{17,9},{2... | collective-permute-start | bytes 2359304 | tf_op jit(solution)/shard_map/ppermute | solution.py:33
  33.4 60.4 %collective-permute-start.13 = (bf16[1744,768]{1,0:T(8,128)(2,1)}, bf16[1744,768]{1,0:T(8,128)(2,1)}, u32[]{:S(2)}, u32[]{:S(2)}) collective-permute-start(bf16[1744,768]{1,0:T(8,128)(2,1)} %slice_dynamic-update-slice_fusion.refs_6_), channel_id=1, source_target_pairs={{0,2},{1,3},{2,0},{3,1},{4,6},{5,7},{6,4},{7,5},{8,10},{9,11},{10,... | collective-permute-start | bytes 8036360 | tf_op jit(solution)/shard_map/ppermute | solution.py:27
  34.5 20.8 %collective-permute-start.8 = (bf16[1024,384]{1,0:T(8,128)(2,1)}, bf16[1024,384]{1,0:T(8,128)(2,1)S(1)}, u32[]{:S(2)}, u32[]{:S(2)}) collective-permute-start(bf16[1024,384]{1,0:T(8,128)(2,1)} %get-tuple-element.91.rest_2_.kv_ref), channel_id=1, source_target_pairs={{0,4},{4,0},{8,12},{12,8},{16,20},{20,16},{24,28},{28,24},{1,5},{5... | collective-permute-start | bytes 2359304 | tf_op jit(solution)/shard_map/ppermute | solution.py:27
  66.9 25.6 %collective-permute-start.11 = (bf16[1024,192]{1,0:T(8,128)(2,1)S(1)}, bf16[1024,192]{1,0:T(8,128)(2,1)S(1)}, u32[]{:S(2)}, u32[]{:S(2)}) collective-permute-start(bf16[1024,192]{1,0:T(8,128)(2,1)S(1)} %get-tuple-element.123.q_ref.rest_2_), channel_id=1, source_target_pairs={{0,4},{4,8},{8,12},{12,16},{16,20},{20,24},{24,28},{1,5},{5,9},{9,... | collective-permute-start | bytes 1179656 | tf_op jit(solution)/shard_map/ppermute | solution.py:33
  71.1 21.5 %collective-permute-start.12 = (bf16[1024,192]{1,0:T(8,128)(2,1)S(1)}, bf16[1024,192]{1,0:T(8,128)(2,1)}, u32[]{:S(2)}, u32[]{:S(2)}) collective-permute-start(bf16[1024,192]{1,0:T(8,128)(2,1)S(1)} %get-tuple-element.123.q_ref.rest_2_), channel_id=1, source_target_pairs={{4,0},{8,4},{12,8},{16,12},{20,16},{24,20},{28,24},{5,1},{9,5},{13... | collective-permute-start | bytes 1179656 | tf_op jit(solution)/shard_map/ppermute | solution.py:33
  72.4 39.6 %collective-permute-start.17 = (bf16[1744,768]{1,0:T(8,128)(2,1)}, bf16[1744,768]{1,0:T(8,128)(2,1)}, u32[]{:S(2)}, u32[]{:S(2)}) collective-permute-start(bf16[1744,768]{1,0:T(8,128)(2,1)} %slice_dynamic-update-slice_fusion.refs_6_), channel_id=1, source_target_pairs={{0,1},{1,0},{2,3},{3,2},{4,5},{5,4},{6,7},{7,6},{8,9},{9,8},{10,11... | collective-permute-start | bytes 8036360 | tf_op jit(solution)/shard_map/ppermute | solution.py:27
  93.8 18.2 %collective-permute-start.18 = (bf16[1744,768]{1,0:T(8,128)(2,1)}, bf16[1744,768]{1,0:T(8,128)(2,1)S(1)}, u32[]{:S(2)}, u32[]{:S(2)}) collective-permute-start(bf16[1744,768]{1,0:T(8,128)(2,1)} %collective-permute-done.13.refs_8_), channel_id=1, source_target_pairs={{0,1},{1,0},{2,3},{3,2},{4,5},{5,4},{6,7},{7,6},{8,9},{9,8},{10,11... | collective-permute-start | bytes 8036360 | tf_op jit(solution)/shard_map/ppermute | solution.py:27
  101.9 34.5 %collective-permute-start.19 = (bf16[1024,192]{1,0:T(8,128)(2,1)}, bf16[1024,192]{1,0:T(8,128)(2,1)S(1)}, u32[]{:S(2)}, u32[]{:S(2)}) collective-permute-start(bf16[1024,192]{1,0:T(8,128)(2,1)} %copy-done.12), channel_id=1, source_target_pairs={{0,8},{4,12},{8,16},{12,20},{16,24},{20,28},{1,9},{5,13},{9,17},{1... | collective-permute-start | bytes 1179656 | tf_op jit(solution)/shard_map/ppermute | solution.py:33
  110.6 25.9 %collective-permute-start.20 = (bf16[1024,192]{1,0:T(8,128)(2,1)}, bf16[1024,192]{1,0:T(8,128)(2,1)S(1)}, u32[]{:S(2)}, u32[]{:S(2)}) collective-permute-start(bf16[1024,192]{1,0:T(8,128)(2,1)} %copy-done.12), channel_id=1, source_target_pairs={{8,0},{12,4},{16,8},{20,12},{24,16},{28,20},{9,1},{13,5},{17,9},{2... | collective-permute-start | bytes 1179656 | tf_op jit(solution)/shard_map/ppermute | solution.py:33
  147.8 28.1 %collective-permute-start.30 = (bf16[768,768]{1,0:T(8,128)(2,1)S(1)}, bf16[768,768]{1,0:T(8,128)(2,1)S(1)}, u32[]{:S(2)}, u32[]{:S(2)}) collective-permute-start(bf16[768,768]{1,0:T(8,128)(2,1)S(1)} %get-tuple-element.173), channel_id=1, source_target_pairs={{0,2},{1,3},{2,0},{3,1},{4,6},{5,7},{6,4},{7,5},{8,10},{9,11},{10,... | collective-permute-start | bytes 3538952 | tf_op jit(solution)/shard_map/ppermute | solution.py:27
  151.8 24.1 %collective-permute-start.25 = (bf16[1024,256]{1,0:T(8,128)(2,1)S(1)}, bf16[1024,256]{1,0:T(8,128)(2,1)S(1)}, u32[]{:S(2)}, u32[]{:S(2)}) collective-permute-start(bf16[1024,256]{1,0:T(8,128)(2,1)S(1)} %layer_gather.1.grad_ref.rest_7_), channel_id=1, source_target_pairs={{0,8},{4,12},{8,16},{12,20},{16,24},{20,28},{1,9},{5,13},{9,17},{1... | collective-permute-start | bytes 1572872 | tf_op jit(solution)/shard_map/ppermute | solution.py:33
  156.4 23.8 %collective-permute-start.26 = (bf16[1024,256]{1,0:T(8,128)(2,1)S(1)}, bf16[1024,256]{1,0:T(8,128)(2,1)S(1)}, u32[]{:S(2)}, u32[]{:S(2)}) collective-permute-start(bf16[1024,256]{1,0:T(8,128)(2,1)S(1)} %layer_gather.1.grad_ref.rest_7_), channel_id=1, source_target_pairs={{0,4},{4,8},{8,12},{12,16},{16,20},{20,24},{24,28},{1,5},{5,9},{9,... | collective-permute-start | bytes 1572872 | tf_op jit(solution)/shard_map/ppermute | solution.py:33
  157.8 22.5 %collective-permute-start.27 = (bf16[1024,256]{1,0:T(8,128)(2,1)S(1)}, bf16[1024,256]{1,0:T(8,128)(2,1)S(1)}, u32[]{:S(2)}, u32[]{:S(2)}) collective-permute-start(bf16[1024,256]{1,0:T(8,128)(2,1)S(1)} %layer_gather.1.grad_ref.rest_7_), channel_id=1, source_target_pairs={{4,0},{8,4},{12,8},{16,12},{20,16},{24,20},{28,24},{5,1},{9,5},{13... | collective-permute-start | bytes 1572872 | tf_op jit(solution)/shard_map/ppermute | solution.py:33
  159.1 26.8 %collective-permute-start.28 = (bf16[1024,256]{1,0:T(8,128)(2,1)S(1)}, bf16[1024,256]{1,0:T(8,128)(2,1)S(1)}, u32[]{:S(2)}, u32[]{:S(2)}) collective-permute-start(bf16[1024,256]{1,0:T(8,128)(2,1)S(1)} %layer_gather.1.grad_ref.rest_7_), channel_id=1, source_target_pairs={{8,0},{12,4},{16,8},{20,12},{24,16},{28,20},{9,1},{13,5},{17,9},{2... | collective-permute-start | bytes 1572872 | tf_op jit(solution)/shard_map/ppermute | solution.py:33
  188.3 35.5 %collective-permute-start.32 = (bf16[1024,768]{1,0:T(8,128)(2,1)}, bf16[1024,768]{1,0:T(8,128)(2,1)}, u32[]{:S(2)}, u32[]{:S(2)}) collective-permute-start(bf16[1024,768]{1,0:T(8,128)(2,1)} %get-tuple-element.171), channel_id=1, source_target_pairs={{0,2},{1,3},{2,0},{3,1},{4,6},{5,7},{6,4},{7,5},{8,10},{9,11},{10,... | collective-permute-start | bytes 4718600 | tf_op jit(solution)/shard_map/ppermute | solution.py:27
  191.8 25.3 %collective-permute-start.31 = (bf16[384,768]{1,0:T(8,128)(2,1)}, bf16[384,768]{1,0:T(8,128)(2,1)}, u32[]{:S(2)}, u32[]{:S(2)}) collective-permute-start(bf16[384,768]{1,0:T(8,128)(2,1)} %get-tuple-element.177), channel_id=1, source_target_pairs={{0,4},{4,0},{8,12},{12,8},{16,20},{20,16},{24,28},{28,24},{1,5},{5... | collective-permute-start | bytes 1769480 | tf_op jit(solution)/shard_map/ppermute | solution.py:27
  234.0 23.8 %collective-permute-start.44 = (bf16[512,768]{1,0:T(8,128)(2,1)S(1)}, bf16[512,768]{1,0:T(8,128)(2,1)S(1)}, u32[]{:S(2)}, u32[]{:S(2)}) collective-permute-start(bf16[512,768]{1,0:T(8,128)(2,1)S(1)} %get-tuple-element.176), channel_id=1, source_target_pairs={{0,4},{4,0},{8,12},{12,8},{16,20},{20,16},{24,28},{28,24},{1,5},{5... | collective-permute-start | bytes 2359304 | tf_op jit(solution)/shard_map/ppermute | solution.py:27
  245.7 25.5 %collective-permute-start.33 = (bf16[2,256,768]{2,1,0:T(8,128)(2,1)S(1)}, bf16[2,256,768]{2,1,0:T(8,128)(2,1)S(1)}, u32[]{:S(2)}, u32[]{:S(2)}) collective-permute-start(bf16[2,256,768]{2,1,0:T(8,128)(2,1)S(1)} %get-tuple-element.187), channel_id=1, source_target_pairs={{0,1},{1,0},{2,3},{3,2},{4,5},{5,4},{6,7},{7,6},{8,9},{9,8},{10,11... | collective-permute-start | bytes 2359304 | tf_op jit(solution)/shard_map/ppermute | solution.py:27
  264.6 20.3 %collective-permute-start.53 = (bf16[192,768]{1,0:T(8,128)(2,1)S(1)}, bf16[192,768]{1,0:T(8,128)(2,1)S(1)}, u32[]{:S(2)}, u32[]{:S(2)}) collective-permute-start(bf16[192,768]{1,0:T(8,128)(2,1)S(1)} %maximum_select_fusion.7), channel_id=1, source_target_pairs={{0,8},{4,12},{8,0},{12,4},{16,24},{20,28},{24,16},{28,20},{1,9},{5... | collective-permute-start | bytes 884744 | tf_op jit(solution)/shard_map/ppermute | solution.py:27
  272.1 23.3 %collective-permute-start.34 = (bf16[256,768]{1,0:T(8,128)(2,1)}, bf16[256,768]{1,0:T(8,128)(2,1)}, u32[]{:S(2)}, u32[]{:S(2)}) collective-permute-start(bf16[256,768]{1,0:T(8,128)(2,1)} %fusion.7), channel_id=1, source_target_pairs={{0,2},{1,3},{2,0},{3,1},{4,6},{5,7},{6,4},{7,5},{8,10},{9,11},{10,... | collective-permute-start | bytes 1179656 | tf_op jit(solution)/shard_map/ppermute | solution.py:27
  289.4 21.2 %collective-permute-start.43 = (bf16[4,96,640]{2,1,0:T(8,128)(2,1)S(1)}, bf16[4,96,640]{2,1,0:T(8,128)(2,1)S(1)}, u32[]{:S(2)}, u32[]{:S(2)}) collective-permute-start(bf16[4,96,640]{2,1,0:T(8,128)(2,1)S(1)} %maximum_select_fusion.5), channel_id=1, source_target_pairs={{0,4},{4,0},{8,12},{12,8},{16,20},{20,16},{24,28},{28,24},{1,5},{5... | collective-permute-start | bytes 1474568 | tf_op jit(solution)/shard_map/ppermute | solution.py:27
  (94 other events, 960.8 us)

commit v7 on v6

--- a/solution.py
+++ b/solution.py
@@ -255,10 +255,44 @@
     )(bounds, queries, spans, grads, wide, stats, *pieces)
 
 
-def key_kernel(reach, bounds, kv_ref, span_ref, *rest):
+def weight_copies(bounds, pieces, weight, sem):
+    part = pieces[0].shape[0]
+    copies = []
+    for r, piece in enumerate(pieces):
+        where = pl.ds(pl.multiple_of(bounds[16 + r] * part, part), part)
+        copies.append(pltpu.make_async_copy(piece, weight.at[where, :], sem.at[r]))
+    return copies
+
+
+def head_terms(bounds, tokens_ref, query_ref, pair_ref, weight, grad_ref, back_ref):
+    groups, part = grad_ref.shape[0], grad_ref.shape[1]
+    rows = back_ref.shape[1]
+    tokens = tokens_ref[...]
+    pair_grad = rows_tn(tokens, pair_ref[...]).astype(bf16)
+    query_grad = rows_tn(tokens, query_ref[...]).astype(bf16)
+    for k in range(groups):
+        here = slice(k * part, (k + 1) * part)
+        grad_ref[k, :, 0 : 2 * part] = pair_grad[here]
+        grad_ref[k, :, 2 * part : 3 * part] = query_grad[here]
+    ones = jnp.ones((tokens.shape[0], HEAD_DIM), bf16)
+    query_sum = rows_tn(query_ref[...], ones)
+    value_sum = rows_tn(pair_ref[:, part:], ones)
+    lane = lax.broadcasted_iota(jnp.int32, (part, HEAD_DIM), 1)
+    sums = jnp.where(lane == 0, query_sum, jnp.where(lane == 1, value_sum, 0.0))
+    grad_ref[:, :, 3 * part : 3 * part + HEAD_DIM] = jnp.zeros((groups, part, HEAD_DIM), bf16)
+    grad_ref[bounds[16], :, 3 * part : 3 * part + HEAD_DIM] = sums.astype(bf16)
+    for k in range(groups):
+        here = slice(k * rows, (k + 1) * rows)
+        made = rows_nt(pair_ref[here, :], weight[:, : 2 * part])
+        made = made + rows_nt(query_ref[here, :], weight[:, 2 * part :])
+        back_ref[bounds[16 + k]] = made.astype(bf16)
+
+
+def key_kernel(reach, bounds, kv_ref, span_ref, tokens_ref, query_ref, *rest):
     window = 2 * reach + 1
+    w_pieces, rest = rest[:4], rest[4:]
     q_pieces, g_pieces = rest[:window], rest[window : 2 * window]
-    out_ref, qs, gs, key_sum, value_sum, sem = rest[2 * window :]
+    grad_ref, back_ref, qs, gs, key_sum, value_sum, out_ref, weight, sem, w_sem = rest[2 * window :]
     step = pl.program_id(0)
     block = q_pieces[0].shape[0]
 
@@ -266,6 +300,8 @@
     def _():
         copies = load_window(q_pieces, qs, sem.at[0], [i * block for i in range(window)])
         copies += load_window(g_pieces, gs, sem.at[1], [i * block for i in range(window)])
+        for copy in weight_copies(bounds, w_pieces, weight, w_sem):
+            copy.start()
         for copy in copies:
             copy.wait()
 
@@ -327,33 +363,49 @@
     out_ref[here, 128:256] = jnp.where(lane < HEAD_DIM, key_sum[2], v_turn).astype(bf16)
     out_ref[here, 256:384] = jnp.where(lane < HEAD_DIM, v_turn, last_turn).astype(bf16)
 
-
-def attention_keys(bounds, pair, spans, q_pieces, g_pieces):
-    block = pair.shape[0]
+    @pl.when(step == pl.num_programs(0) - 1)
+    def _():
+        for copy in weight_copies(bounds, w_pieces, weight, w_sem):
+            copy.wait()
+        head_terms(bounds, tokens_ref, query_ref, out_ref, weight, grad_ref, back_ref)
+
+
+def attention_keys(bounds, pair, spans, tokens, grad_query, weight_pieces, q_pieces, g_pieces):
+    block, width = tokens.shape
     count = len(q_pieces)
+    groups, part = len(weight_pieces), weight_pieces[0].shape[0]
     return pl.pallas_call(
         functools.partial(key_kernel, count // 2),
         grid_spec=pltpu.PrefetchScalarGridSpec(
             num_scalar_prefetch=1,
             grid=(block // TILE_K,),
-            in_specs=[whole_spec(x.shape) for x in (pair, spans)]
-            + [pl.BlockSpec(memory_space=pl.ANY)] * (2 * count),
-            out_specs=whole_spec((block, 384)),
+            in_specs=[whole_spec(x.shape) for x in (pair, spans, tokens, grad_query)]
+            + [pl.BlockSpec(memory_space=pl.ANY)] * (groups + 2 * count),
+            out_specs=[
+                whole_spec((groups, part, 3 * part + HEAD_DIM)),
+                whole_spec((groups, block // groups, width)),
+            ],
             scratch_shapes=[
                 pltpu.VMEM((count * block, 192), bf16),
                 pltpu.VMEM((count * block, 256), bf16),
                 pltpu.VMEM((3, TILE_K, 128), f32),
                 pltpu.VMEM((3, TILE_K, 128), f32),
+                pltpu.VMEM((block, 384), bf16),
+                pltpu.VMEM((width, 3 * part), bf16),
                 pltpu.SemaphoreType.DMA((2, count)),
+                pltpu.SemaphoreType.DMA((groups,)),
             ],
         ),
-        out_shape=jax.ShapeDtypeStruct((block, 384), bf16),
-        compiler_params=pltpu.CompilerParams(vmem_limit_bytes=40 * 2**20),
+        out_shape=[
+            jax.ShapeDtypeStruct((groups, part, 3 * part + HEAD_DIM), bf16),
+            jax.ShapeDtypeStruct((groups, block // groups, width), bf16),
+        ],
+        compiler_params=pltpu.CompilerParams(vmem_limit_bytes=60 * 2**20),
         cost_estimate=pl.CostEstimate(
-            flops=8 * block * 2304 * 192, bytes_accessed=8 * 2**20, transcendentals=block * 2304 * 3
+            flops=10 * block * 2304 * 192, bytes_accessed=12 * 2**20, transcendentals=block * 2304 * 3
         ),
         name="attention_keys",
-    )(bounds, pair, spans, *q_pieces, *g_pieces)
+    )(bounds, pair, spans, tokens, grad_query, *weight_pieces, *q_pieces, *g_pieces)
 
 
 def projection_kernel(place_ref, own, near, far, corner, w_own, w_near, w_far, w_corner, bias_ref, *rest):
@@ -665,60 +717,6 @@
     )(places, *pieces, wide, stats)
 
 
-def heads_kernel(place_ref, tokens_ref, query_ref, pair_ref, w0, w1, w2, w3, grad_ref, back_ref, weight, sem):
-    groups, part = grad_ref.shape[0], w0.shape[0]
-    rows = back_ref.shape[1]
-    copies = []
-    for r, piece in enumerate((w0, w1, w2, w3)):
-        where = pl.multiple_of(place_ref[r] * part, part)
-        copies.append(pltpu.make_async_copy(piece, weight.at[pl.ds(where, part), :], sem.at[r]))
-        copies[-1].start()
-    tokens = tokens_ref[...]
-    pair_grad = rows_tn(tokens, pair_ref[...]).astype(bf16)
-    query_grad = rows_tn(tokens, query_ref[...]).astype(bf16)
-    for k in range(groups):
-        here = slice(k * part, (k + 1) * part)
-        grad_ref[k, :, 0 : 2 * part] = pair_grad[here]
-        grad_ref[k, :, 2 * part : 3 * part] = query_grad[here]
-    ones = jnp.ones((tokens.shape[0], HEAD_DIM), bf16)
-    query_sum = rows_tn(query_ref[...], ones)
-    value_sum = rows_tn(pair_ref[:, part:], ones)
-    lane = lax.broadcasted_iota(jnp.int32, (part, HEAD_DIM), 1)
-    sums = jnp.where(lane == 0, query_sum, jnp.where(lane == 1, value_sum, 0.0))
-    grad_ref[:, :, 3 * part : 3 * part + HEAD_DIM] = jnp.zeros((groups, part, HEAD_DIM), bf16)
-    grad_ref[place_ref[0], :, 3 * part : 3 * part + HEAD_DIM] = sums.astype(bf16)
-    for copy in copies:
-        copy.wait()
-    for k in range(groups):
-        here = slice(k * rows, (k + 1) * rows)
-        made = rows_nt(pair_ref[here, :], weight[:, : 2 * part])
-        made = made + rows_nt(query_ref[here, :], weight[:, 2 * part :])
-        back_ref[place_ref[k]] = made.astype(bf16)
-
-
-def head_grads(places, tokens, grad_query, grad_pair, weight_pieces):
-    block, width = tokens.shape
-    groups, part = len(weight_pieces), weight_pieces[0].shape[0]
-    vmem = pl.BlockSpec(memory_space=pltpu.VMEM)
-    return pl.pallas_call(
-        heads_kernel,
-        in_specs=[pl.BlockSpec(memory_space=pltpu.SMEM)]
-        + [vmem] * 3
-        + [pl.BlockSpec(memory_space=pl.ANY)] * groups,
-        out_specs=[vmem] * 2,
-        out_shape=[
-            jax.ShapeDtypeStruct((groups, part, 3 * part + HEAD_DIM), bf16),
-            jax.ShapeDtypeStruct((groups, block // groups, width), bf16),
-        ],
-        scratch_shapes=[pltpu.VMEM((width, 3 * part), bf16), pltpu.SemaphoreType.DMA((groups,))],
-        compiler_params=pltpu.CompilerParams(vmem_limit_bytes=32 * 2**20),
-        cost_estimate=pl.CostEstimate(
-            flops=4 * block * width * 3 * part, bytes_accessed=8 * 2**20, transcendentals=0
-        ),
-        name="layer_heads",
-    )(places, tokens, grad_query, grad_pair, *weight_pieces)
-
-
 def both(left, right):
     return (left.astype(f32) + right.astype(f32)).astype(bf16)
 
@@ -902,12 +900,13 @@
     near_first = [1 << i for i in range(cycle.bit_length() - 1)]
     outer_terms = scatter_sum(outer_terms, "ctx", near_first[:1], 0)
     inner_terms = far_terms(inner_keep, inner_got)
-    grad_pair = attention_keys(bounds, pair, spans_row, query_halo, grad_halo)
-    grad_pair, outer_terms, inner_terms = lax.optimization_barrier(
-        (grad_pair, outer_terms, inner_terms)
-    )
-
-    head_grad, token_partial = head_grads(places, block_tokens, grad_query, grad_pair, weight_pieces)
+    head_grad, token_partial = attention_keys(
+        bounds, pair, spans_row, block_tokens, grad_query, weight_pieces, query_halo, grad_halo
+    )
+    head_grad, token_partial, outer_terms, inner_terms = lax.optimization_barrier(
+        (head_grad, token_partial, outer_terms, inner_terms)
+    )
+
     outer_part = both(*scatter_sum(outer_terms, "ctx", near_first[1:], 0))
     inner_part = both(*scatter_sum(inner_terms, "ctx", near_first, 0))
     head_part = both(*scatter_sum([head_grad], "ctx", near_first, 1))

time: 334 us -> 331 us (level)
  starting transfers between devices: 55.7 us -> 86.6 us
  Pallas kernels: 86.6 us -> 68 us
  waiting for transfers between devices: 124 us -> 112 us
  local copies, waits for them, and re-layouts: 28.7 us -> 20.9 us
    ppermute x44, starting transfers between devices: 22.9 us -> 49 us  [swapped(): return lax.ppermute(block, axis, [(i, i ^ bit) for i in range(count)])]
    ppermute x44, waiting for transfers between devices: 98.8 us -> 81.9 us  [swapped(): return lax.ppermute(block, axis, [(i, i ^ bit) for i in range(count)])]
    unnamed x132 -> x118, local copies, waits for them, and re-layouts: 19.4 us -> 9.2 us
    pallas_call x1, Pallas kernels: 20 us -> 13.3 us  [attention_forward(): pl.pallas_call(forward_kernel, grid_spec=pltpu.PrefetchScalarGridSpec(num...]
    pallas_call x1, Pallas kernels: 15.1 us -> 9.39 us  [attention_queries(): pl.pallas_call(query_kernel, grid_spec=pltpu.PrefetchScalarGridSpec(num_s...]
    ppermute x10, waiting for transfers between devices: 22 us -> 27.1 us  [shifted(): return lax.ppermute(block, axis, route)]
    pallas_call x1 -> x0, Pallas kernels: 5.05 us -> none  [head_grads(): pl.pallas_call(heads_kernel, in_specs=[pl.BlockSpec(memory_space=pltpu.SM...]
    ppermute x10, starting transfers between devices: 29.1 us -> 33.1 us  [shifted(): return lax.ppermute(block, axis, route)]
  transfers between devices with their start and end apart: 55 -> 55, of which waited for: 30 -> 30; matrix products, arithmetic and copies ran while one was open for 13% -> 13% of each run, Pallas kernels for 23% -> 19%
where the time goes in v7:
time: 331 us; the launch traced here: 328 us
  waiting for transfers between devices  112 us (34%)
  starting transfers between devices  86.6 us (26%)
  Pallas kernels  68 us (21%)
  other arithmetic  35.2 us (11%)
  local copies, waits for them, and re-layouts  20.9 us (6%)
  between operations  4.96 us (1%)
    ppermute x44, waiting for transfers between devices, swapped(): return lax.ppermute(block, axis, [(i, i ^ bit) for i in range(count)])  81.9 us
    ppermute x44, starting transfers between devices, swapped(): return lax.ppermute(block, axis, [(i, i ^ bit) for i in range(count)])  49 us
    ppermute x10, starting transfers between devices, shifted(): return lax.ppermute(block, axis, route)  33.1 us
    ppermute x10, waiting for transfers between devices, shifted(): return lax.ppermute(block, axis, route)  27.1 us
    pallas_call x1, Pallas kernels, dense(): pl.pallas_call(dense_kernel, in_specs=[pl.BlockSpec(memory_space=pltpu.SM...  20 us
    pallas_call x1, Pallas kernels, attention_keys(): pl.pallas_call(functools.partial(key_kernel, count // 2), grid_spec=pltpu...  18.9 us
    pallas_call x1, Pallas kernels, attention_forward(): pl.pallas_call(forward_kernel, grid_spec=pltpu.PrefetchScalarGridSpec(num...  13.3 us
    convert_element_type x14, other arithmetic, both(): return (left.astype(f32) + right.astype(f32)).astype(bf16)  11.9 us
  transfers between devices with their start and end apart: 55, of which 30 were waited for; matrix products, arithmetic and copies ran while one was open for 13% of the time, Pallas kernels for 19%

profile of v7, /device:TPU:0, one launch (start us, length us, event | category | flops | bytes accessed | tf_op | source)
XLA Modules:
  0.0 328.0 jit_solution(1026392638554038811)
XLA Ops:
  23.8 4.1 %layer_projection.1 = (bf16[1024,768]{1,0:T(8,128)(2,1)S(1)}, bf16[1024,192]{1,0:T(8,128)(2,1)S(1)}, bf16[1024,384]{1,0:T(8,128)(2,1)}) custom-call(s32[4]{0:T(128)S(1)} %pad_add_fusion.2.place_ref, bf16[256,768]{1,0:T(8,128)(2,1)S(1)} %copy-done.14, bf16[256,768]{1,0:T(8,128)(2,1)S(1)} %collective-permute-done.near, ...), custom_call_target="tpu_custom_call" | custom-call | flops 905969664 | bytes 5242880 | tf_op jit(solution)/shard_map/layer_projection/pallas_call | solution.py:436
  43.2 6.7 %collective-permute-done.6.rest_0_ = bf16[1024,384]{1,0:T(8,128)(2,1)S(1)} collective-permute-done((bf16[1024,384]{1,0:T(8,128)(2,1)}, bf16[1024,384]{1,0:T(8,128)(2,1)S(1)}, u32[]{:S(2)}, u32[]{:S(2)}) %collective-permute-start.6) | collective-permute-done | bytes 786464 | tf_op jit(solution)/shard_map/ppermute | solution.py:33
  49.9 4.1 %collective-permute-done.7.rest_1_ = bf16[1024,384]{1,0:T(8,128)(2,1)S(1)} collective-permute-done((bf16[1024,384]{1,0:T(8,128)(2,1)}, bf16[1024,384]{1,0:T(8,128)(2,1)S(1)}, u32[]{:S(2)}, u32[]{:S(2)}) %collective-permute-start.7) | collective-permute-done | bytes 786464 | tf_op jit(solution)/shard_map/ppermute | solution.py:33
  55.6 4.6 %collective-permute-start.10 = (bf16[512,384]{1,0:T(8,128)(2,1)S(1)}, bf16[512,384]{1,0:T(8,128)(2,1)S(1)}, u32[]{:S(2)}, u32[]{:S(2)}) collective-permute-start(bf16[512,384]{1,0:T(8,128)(2,1)S(1)} %slice.254), channel_id=1, source_target_pairs={{0,8},{8,16},{12,4},{16,24},{20,12},{28,20},{1,9},{9,17},{13,5},{1... | collective-permute-start | bytes 1179656 | tf_op jit(solution)/shard_map/ppermute | solution.py:846
  60.2 3.8 %collective-permute-done.9.rest_4_ = bf16[512,384]{1,0:T(8,128)(2,1)S(1)} collective-permute-done((bf16[512,384]{1,0:T(8,128)(2,1)S(1)}, bf16[512,384]{1,0:T(8,128)(2,1)S(1)}, u32[]{:S(2)}, u32[]{:S(2)}) %collective-permute-start.9) | collective-permute-done | bytes 393248 | tf_op jit(solution)/shard_map/ppermute | solution.py:27
  67.4 5.1 %collective-permute-start.11 = (bf16[1024,192]{1,0:T(8,128)(2,1)S(1)}, bf16[1024,192]{1,0:T(8,128)(2,1)}, u32[]{:S(2)}, u32[]{:S(2)}) collective-permute-start(bf16[1024,192]{1,0:T(8,128)(2,1)S(1)} %get-tuple-element.124.q_ref.rest_6_), channel_id=1, source_target_pairs={{0,4},{4,8},{8,12},{12,16},{16,20},{20,24},{24,28},{1,5},{5,9},{9,... | collective-permute-start | bytes 1179656 | tf_op jit(solution)/shard_map/ppermute | solution.py:33
  73.9 13.3 %attention_forward.1 = (bf16[256,192]{1,0:T(8,128)(2,1)}, bf16[256,192]{1,0:T(8,128)(2,1)}, bf16[256,192]{1,0:T(8,128)(2,1)}, bf16[256,192]{1,0:T(8,128)(2,1)}, ...) custom-call(s32[20]{0:T(128)} %concatenate.99.bounds, bf16[1024,192]{1,0:T(8,128)(2,1)} %copy-done.12, ...), custom_call_target="tpu_custom_call" | custom-call | flops 1811939328 | bytes 6291456 | tf_op jit(solution)/shard_map/attention_forward/pallas_call | solution.py:148
  87.2 5.2 %collective-permute-done.11.rest_5_ = bf16[1024,192]{1,0:T(8,128)(2,1)} collective-permute-done((bf16[1024,192]{1,0:T(8,128)(2,1)S(1)}, bf16[1024,192]{1,0:T(8,128)(2,1)}, u32[]{:S(2)}, u32[]{:S(2)}) %collective-permute-start.11) | collective-permute-done | bytes 393248 | tf_op jit(solution)/shard_map/ppermute | solution.py:33
  95.9 3.5 %collective-permute-done.14.refs_1_ = bf16[256,192]{1,0:T(8,128)(2,1)S(1)} collective-permute-done((bf16[256,192]{1,0:T(8,128)(2,1)}, bf16[256,192]{1,0:T(8,128)(2,1)S(1)}, u32[]{:S(2)}, u32[]{:S(2)}) %collective-permute-start.14) | collective-permute-done | bytes 98336 | tf_op jit(solution)/shard_map/ppermute | solution.py:27
  102.0 8.3 %collective-permute-start.19 = (bf16[1024,192]{1,0:T(8,128)(2,1)}, bf16[1024,192]{1,0:T(8,128)(2,1)S(1)}, u32[]{:S(2)}, u32[]{:S(2)}) collective-permute-start(bf16[1024,192]{1,0:T(8,128)(2,1)} %copy-done.12), channel_id=1, source_target_pairs={{0,8},{4,12},{8,16},{12,20},{16,24},{20,28},{1,9},{5,13},{9,17},{1... | collective-permute-start | bytes 1179656 | tf_op jit(solution)/shard_map/ppermute | solution.py:33
  114.3 20.0 %layer_dense.1 = (bf16[256,768]{1,0:T(8,128)(2,1)}, f32[256,768]{1,0:T(8,128)S(1)}, bf16[256,192]{1,0:T(8,128)(2,1)S(1)}, bf16[256,192]{1,0:T(8,128)(2,1)S(1)}, ...) custom-call(s32[4]{0:T(128)S(1)} %pad_add_fusion.2.place_ref, ...), custom_call_target="tpu_custom_call" | custom-call | flops 14495514624 | bytes 25165824 | tf_op jit(solution)/shard_map/layer_dense/pallas_call | solution.py:646
  148.2 4.6 %collective-permute-start.25 = (bf16[1024,256]{1,0:T(8,128)(2,1)S(1)}, bf16[1024,256]{1,0:T(8,128)(2,1)S(1)}, u32[]{:S(2)}, u32[]{:S(2)}) collective-permute-start(bf16[1024,256]{1,0:T(8,128)(2,1)S(1)} %layer_gather.1.grad_ref.rest_11_), channel_id=1, source_target_pairs={{0,8},{4,12},{8,16},{12,20},{16,24},{20,28},{1,9},{5,13},{9,17},{1... | collective-permute-start | bytes 1572872 | tf_op jit(solution)/shard_map/ppermute | solution.py:33
  152.8 4.7 %collective-permute-start.26 = (bf16[1024,256]{1,0:T(8,128)(2,1)S(1)}, bf16[1024,256]{1,0:T(8,128)(2,1)S(1)}, u32[]{:S(2)}, u32[]{:S(2)}) collective-permute-start(bf16[1024,256]{1,0:T(8,128)(2,1)S(1)} %layer_gather.1.grad_ref.rest_11_), channel_id=1, source_target_pairs={{0,4},{4,8},{8,12},{12,16},{16,20},{20,24},{24,28},{1,5},{5,9},{9,... | collective-permute-start | bytes 1572872 | tf_op jit(solution)/shard_map/ppermute | solution.py:33
  160.4 9.4 %attention_queries.1.query_ref = bf16[1024,192]{1,0:T(8,128)(2,1)S(1)} custom-call(s32[20]{0:T(128)S(1)} %copy-done.11, bf16[1024,192]{1,0:T(8,128)(2,1)S(1)} %copy-done.13, s32[8,1024]{1,0:T(8,128)S(1)} %copy-done.10, bf16[1024,256]{1,0:T(8,128)(2,1)S(1)} %layer_gather.1.grad_ref.rest_11_, f32[1024,192]{1,0:T(8,128)S(1)} %copy-done, ...), custom_call_target="tpu_custom_call" | custom-call | flops 2717908992 | bytes 6291456 | tf_op jit(solution)/shard_map/attention_queries/pallas_call | solution.py:235
  169.8 3.5 %collective-permute-done.30 = bf16[768,768]{1,0:T(8,128)(2,1)S(1)} collective-permute-done((bf16[768,768]{1,0:T(8,128)(2,1)S(1)}, bf16[768,768]{1,0:T(8,128)(2,1)S(1)}, u32[]{:S(2)}, u32[]{:S(2)}) %collective-permute-start.30) | collective-permute-done | bytes 1179680 | tf_op jit(solution)/shard_map/ppermute | solution.py:27
  173.3 6.7 %collective-permute-done.26.rest_10_ = bf16[1024,256]{1,0:T(8,128)(2,1)S(1)} collective-permute-done((bf16[1024,256]{1,0:T(8,128)(2,1)S(1)}, bf16[1024,256]{1,0:T(8,128)(2,1)S(1)}, u32[]{:S(2)}, u32[]{:S(2)}) %collective-permute-start.26) | collective-permute-done | bytes 524320 | tf_op jit(solution)/shard_map/ppermute | solution.py:33
  180.1 4.4 %collective-permute-done.28.rest_13_ = bf16[1024,256]{1,0:T(8,128)(2,1)S(1)} collective-permute-done((bf16[1024,256]{1,0:T(8,128)(2,1)S(1)}, bf16[1024,256]{1,0:T(8,128)(2,1)S(1)}, u32[]{:S(2)}, u32[]{:S(2)}) %collective-permute-start.28) | collective-permute-done | bytes 524320 | tf_op jit(solution)/shard_map/ppermute | solution.py:33
  190.7 18.9 %attention_keys.1 = (bf16[4,192,640]{2,1,0:T(8,128)(2,1)}, bf16[4,256,768]{2,1,0:T(8,128)(2,1)}) custom-call(s32[20]{0:T(128)} %concatenate.99.bounds, bf16[1024,384]{1,0:T(8,128)(2,1)} %get-tuple-element.92.rest_2_.kv_ref, s32[8,5120]{1,0:T(8,128)} %add_add_fusion.span_ref, bf16[1024,768]{1,0:T(8,128)(2,1)} %copy-done.23, bf16[1024,192]{1,0:T(8,128)(2,1)} %copy-done.24, ...), custom_call_target="tpu_custom_call" | custom-call | flops 4529848320 | bytes 12582912 | tf_op jit(solution)/shard_map/attention_keys/pallas_call | solution.py:377
  209.7 12.8 %collective-permute-done.32 = bf16[1024,768]{1,0:T(8,128)(2,1)} collective-permute-done((bf16[1024,768]{1,0:T(8,128)(2,1)}, bf16[1024,768]{1,0:T(8,128)(2,1)}, u32[]{:S(2)}, u32[]{:S(2)}) %collective-permute-start.32) | collective-permute-done | bytes 1572896 | tf_op jit(solution)/shard_map/ppermute | solution.py:27
  233.3 5.6 %collective-permute-start.51 = (bf16[96,768]{1,0:T(8,128)(2,1)S(1)}, bf16[96,768]{1,0:T(8,128)(2,1)S(1)}, u32[]{:S(2)}, u32[]{:S(2)}) collective-permute-start(bf16[96,768]{1,0:T(8,128)(2,1)S(1)} %add_convert_fusion.20), channel_id=1, source_target_pairs={{0,16},{4,20},{8,24},{12,28},{16,0},{20,4},{24,8},{28,12},{1,17},{... | collective-permute-start | bytes 442376 | tf_op jit(solution)/shard_map/ppermute | solution.py:27
  271.9 5.4 %collective-permute-start.42 = (bf16[4,48,640]{2,1,0:T(8,128)(2,1)S(1)}, bf16[4,48,640]{2,1,0:T(8,128)(2,1)}, u32[]{:S(2)}, u32[]{:S(2)}) collective-permute-start(bf16[4,48,640]{2,1,0:T(8,128)(2,1)S(1)} %maximum_select_fusion.8), channel_id=1, source_target_pairs={{0,8},{4,12},{8,0},{12,4},{16,24},{20,28},{24,16},{28,20},{1,9},{5... | collective-permute-start | bytes 737288 | tf_op jit(solution)/shard_map/ppermute | solution.py:27
  286.3 5.3 %collective-permute-done.47 = bf16[128,768]{1,0:T(8,128)(2,1)} collective-permute-done((bf16[128,768]{1,0:T(8,128)(2,1)S(1)}, bf16[128,768]{1,0:T(8,128)(2,1)}, u32[]{:S(2)}, u32[]{:S(2)}) %collective-permute-start.47) | collective-permute-done | bytes 196640 | tf_op jit(solution)/shard_map/ppermute | solution.py:27
  300.4 5.2 %collective-permute-done.43 = bf16[4,96,640]{2,1,0:T(8,128)(2,1)S(1)} collective-permute-done((bf16[4,96,640]{2,1,0:T(8,128)(2,1)S(1)}, bf16[4,96,640]{2,1,0:T(8,128)(2,1)S(1)}, u32[]{:S(2)}, u32[]{:S(2)}) %collective-permute-start.43) | collective-permute-done | bytes 491552 | tf_op jit(solution)/shard_map/ppermute | solution.py:27
  310.5 13.0 %collective-permute-done.49 = bf16[512,768]{1,0:T(8,128)(2,1)S(1)} collective-permute-done((bf16[512,768]{1,0:T(8,128)(2,1)S(1)}, bf16[512,768]{1,0:T(8,128)(2,1)S(1)}, u32[]{:S(2)}, u32[]{:S(2)}) %collective-permute-start.49) | collective-permute-done | bytes 786464 | tf_op jit(solution)/shard_map/ppermute | solution.py:27
  (298 shorter events, 145.0 us)
Async XLA Ops:
  0.7 19.2 %collective-permute-start.1 = (bf16[256,768]{1,0:T(8,128)(2,1)}, bf16[256,768]{1,0:T(8,128)(2,1)S(1)}, u32[]{:S(2)}, u32[]{:S(2)}) collective-permute-start(bf16[256,768]{1,0:T(8,128)(2,1)} %refs_4_.1), channel_id=1, source_target_pairs={{0,2},{1,3},{2,0},{3,1},{4,6},{5,7},{6,4},{7,5},{8,10},{9,11},{10,... | collective-permute-start | bytes 1179656 | tf_op jit(solution)/shard_map/ppermute | solution.py:27
  3.7 20.1 %collective-permute-start = (bf16[256,768]{1,0:T(8,128)(2,1)}, bf16[256,768]{1,0:T(8,128)(2,1)S(1)}, u32[]{:S(2)}, u32[]{:S(2)}) collective-permute-start(bf16[256,768]{1,0:T(8,128)(2,1)} %refs_4_.1), channel_id=1, source_target_pairs={{0,1},{1,0},{2,3},{3,2},{4,5},{5,4},{6,7},{7,6},{8,9},{9,8},{10,11... | collective-permute-start | bytes 1179656 | tf_op jit(solution)/shard_map/ppermute | solution.py:27
  29.1 20.7 %collective-permute-start.6 = (bf16[1024,384]{1,0:T(8,128)(2,1)}, bf16[1024,384]{1,0:T(8,128)(2,1)S(1)}, u32[]{:S(2)}, u32[]{:S(2)}) collective-permute-start(bf16[1024,384]{1,0:T(8,128)(2,1)} %get-tuple-element.92.rest_2_.kv_ref), channel_id=1, source_target_pairs={{0,8},{4,12},{8,16},{12,20},{16,24},{20,28},{1,9},{5,13},{9,17},{1... | collective-permute-start | bytes 2359304 | tf_op jit(solution)/shard_map/ppermute | solution.py:33
  32.6 21.3 %collective-permute-start.7 = (bf16[1024,384]{1,0:T(8,128)(2,1)}, bf16[1024,384]{1,0:T(8,128)(2,1)S(1)}, u32[]{:S(2)}, u32[]{:S(2)}) collective-permute-start(bf16[1024,384]{1,0:T(8,128)(2,1)} %get-tuple-element.92.rest_2_.kv_ref), channel_id=1, source_target_pairs={{8,0},{12,4},{16,8},{20,12},{24,16},{28,20},{9,1},{13,5},{17,9},{2... | collective-permute-start | bytes 2359304 | tf_op jit(solution)/shard_map/ppermute | solution.py:33
  33.9 60.1 %collective-permute-start.13 = (bf16[1744,768]{1,0:T(8,128)(2,1)}, bf16[1744,768]{1,0:T(8,128)(2,1)}, u32[]{:S(2)}, u32[]{:S(2)}) collective-permute-start(bf16[1744,768]{1,0:T(8,128)(2,1)} %slice_dynamic-update-slice_fusion.refs_6_), channel_id=1, source_target_pairs={{0,2},{1,3},{2,0},{3,1},{4,6},{5,7},{6,4},{7,5},{8,10},{9,11},{10,... | collective-permute-start | bytes 8036360 | tf_op jit(solution)/shard_map/ppermute | solution.py:27
  35.4 20.2 %collective-permute-start.8 = (bf16[1024,384]{1,0:T(8,128)(2,1)}, bf16[1024,384]{1,0:T(8,128)(2,1)S(1)}, u32[]{:S(2)}, u32[]{:S(2)}) collective-permute-start(bf16[1024,384]{1,0:T(8,128)(2,1)} %get-tuple-element.92.rest_2_.kv_ref), channel_id=1, source_target_pairs={{0,4},{4,0},{8,12},{12,8},{16,20},{20,16},{24,28},{28,24},{1,5},{5... | collective-permute-start | bytes 2359304 | tf_op jit(solution)/shard_map/ppermute | solution.py:27
  67.4 25.0 %collective-permute-start.11 = (bf16[1024,192]{1,0:T(8,128)(2,1)S(1)}, bf16[1024,192]{1,0:T(8,128)(2,1)}, u32[]{:S(2)}, u32[]{:S(2)}) collective-permute-start(bf16[1024,192]{1,0:T(8,128)(2,1)S(1)} %get-tuple-element.124.q_ref.rest_6_), channel_id=1, source_target_pairs={{0,4},{4,8},{8,12},{12,16},{16,20},{20,24},{24,28},{1,5},{5,9},{9,... | collective-permute-start | bytes 1179656 | tf_op jit(solution)/shard_map/ppermute | solution.py:33
  72.5 19.9 %collective-permute-start.12 = (bf16[1024,192]{1,0:T(8,128)(2,1)S(1)}, bf16[1024,192]{1,0:T(8,128)(2,1)}, u32[]{:S(2)}, u32[]{:S(2)}) collective-permute-start(bf16[1024,192]{1,0:T(8,128)(2,1)S(1)} %get-tuple-element.124.q_ref.rest_6_), channel_id=1, source_target_pairs={{4,0},{8,4},{12,8},{16,12},{20,16},{24,20},{28,24},{5,1},{9,5},{13... | collective-permute-start | bytes 1179656 | tf_op jit(solution)/shard_map/ppermute | solution.py:33
  73.8 38.1 %collective-permute-start.17 = (bf16[1744,768]{1,0:T(8,128)(2,1)}, bf16[1744,768]{1,0:T(8,128)(2,1)}, u32[]{:S(2)}, u32[]{:S(2)}) collective-permute-start(bf16[1744,768]{1,0:T(8,128)(2,1)} %slice_dynamic-update-slice_fusion.refs_6_), channel_id=1, source_target_pairs={{0,1},{1,0},{2,3},{3,2},{4,5},{5,4},{6,7},{7,6},{8,9},{9,8},{10,11... | collective-permute-start | bytes 8036360 | tf_op jit(solution)/shard_map/ppermute | solution.py:27
  94.0 17.8 %collective-permute-start.18 = (bf16[1744,768]{1,0:T(8,128)(2,1)}, bf16[1744,768]{1,0:T(8,128)(2,1)S(1)}, u32[]{:S(2)}, u32[]{:S(2)}) collective-permute-start(bf16[1744,768]{1,0:T(8,128)(2,1)} %collective-permute-done.13.refs_8_), channel_id=1, source_target_pairs={{0,1},{1,0},{2,3},{3,2},{4,5},{5,4},{6,7},{7,6},{8,9},{9,8},{10,11... | collective-permute-start | bytes 8036360 | tf_op jit(solution)/shard_map/ppermute | solution.py:27
  102.0 32.2 %collective-permute-start.19 = (bf16[1024,192]{1,0:T(8,128)(2,1)}, bf16[1024,192]{1,0:T(8,128)(2,1)S(1)}, u32[]{:S(2)}, u32[]{:S(2)}) collective-permute-start(bf16[1024,192]{1,0:T(8,128)(2,1)} %copy-done.12), channel_id=1, source_target_pairs={{0,8},{4,12},{8,16},{12,20},{16,24},{20,28},{1,9},{5,13},{9,17},{1... | collective-permute-start | bytes 1179656 | tf_op jit(solution)/shard_map/ppermute | solution.py:33
  110.4 23.9 %collective-permute-start.20 = (bf16[1024,192]{1,0:T(8,128)(2,1)}, bf16[1024,192]{1,0:T(8,128)(2,1)S(1)}, u32[]{:S(2)}, u32[]{:S(2)}) collective-permute-start(bf16[1024,192]{1,0:T(8,128)(2,1)} %copy-done.12), channel_id=1, source_target_pairs={{8,0},{12,4},{16,8},{20,12},{24,16},{28,20},{9,1},{13,5},{17,9},{2... | collective-permute-start | bytes 1179656 | tf_op jit(solution)/shard_map/ppermute | solution.py:33
  144.6 28.7 %collective-permute-start.30 = (bf16[768,768]{1,0:T(8,128)(2,1)S(1)}, bf16[768,768]{1,0:T(8,128)(2,1)S(1)}, u32[]{:S(2)}, u32[]{:S(2)}) collective-permute-start(bf16[768,768]{1,0:T(8,128)(2,1)S(1)} %get-tuple-element.175), channel_id=1, source_target_pairs={{0,2},{1,3},{2,0},{3,1},{4,6},{5,7},{6,4},{7,5},{8,10},{9,11},{10,... | collective-permute-start | bytes 3538952 | tf_op jit(solution)/shard_map/ppermute | solution.py:27
  148.2 25.2 %collective-permute-start.25 = (bf16[1024,256]{1,0:T(8,128)(2,1)S(1)}, bf16[1024,256]{1,0:T(8,128)(2,1)S(1)}, u32[]{:S(2)}, u32[]{:S(2)}) collective-permute-start(bf16[1024,256]{1,0:T(8,128)(2,1)S(1)} %layer_gather.1.grad_ref.rest_11_), channel_id=1, source_target_pairs={{0,8},{4,12},{8,16},{12,20},{16,24},{20,28},{1,9},{5,13},{9,17},{1... | collective-permute-start | bytes 1572872 | tf_op jit(solution)/shard_map/ppermute | solution.py:33
  152.8 27.3 %collective-permute-start.26 = (bf16[1024,256]{1,0:T(8,128)(2,1)S(1)}, bf16[1024,256]{1,0:T(8,128)(2,1)S(1)}, u32[]{:S(2)}, u32[]{:S(2)}) collective-permute-start(bf16[1024,256]{1,0:T(8,128)(2,1)S(1)} %layer_gather.1.grad_ref.rest_11_), channel_id=1, source_target_pairs={{0,4},{4,8},{8,12},{12,16},{16,20},{20,24},{24,28},{1,5},{5,9},{9,... | collective-permute-start | bytes 1572872 | tf_op jit(solution)/shard_map/ppermute | solution.py:33
  157.5 22.6 %collective-permute-start.27 = (bf16[1024,256]{1,0:T(8,128)(2,1)S(1)}, bf16[1024,256]{1,0:T(8,128)(2,1)S(1)}, u32[]{:S(2)}, u32[]{:S(2)}) collective-permute-start(bf16[1024,256]{1,0:T(8,128)(2,1)S(1)} %layer_gather.1.grad_ref.rest_11_), channel_id=1, source_target_pairs={{4,0},{8,4},{12,8},{16,12},{20,16},{24,20},{28,24},{5,1},{9,5},{13... | collective-permute-start | bytes 1572872 | tf_op jit(solution)/shard_map/ppermute | solution.py:33
  158.8 25.7 %collective-permute-start.28 = (bf16[1024,256]{1,0:T(8,128)(2,1)S(1)}, bf16[1024,256]{1,0:T(8,128)(2,1)S(1)}, u32[]{:S(2)}, u32[]{:S(2)}) collective-permute-start(bf16[1024,256]{1,0:T(8,128)(2,1)S(1)} %layer_gather.1.grad_ref.rest_11_), channel_id=1, source_target_pairs={{8,0},{12,4},{16,8},{20,12},{24,16},{28,20},{9,1},{13,5},{17,9},{2... | collective-permute-start | bytes 1572872 | tf_op jit(solution)/shard_map/ppermute | solution.py:33
  186.5 36.0 %collective-permute-start.32 = (bf16[1024,768]{1,0:T(8,128)(2,1)}, bf16[1024,768]{1,0:T(8,128)(2,1)}, u32[]{:S(2)}, u32[]{:S(2)}) collective-permute-start(bf16[1024,768]{1,0:T(8,128)(2,1)} %get-tuple-element.173), channel_id=1, source_target_pairs={{0,2},{1,3},{2,0},{3,1},{4,6},{5,7},{6,4},{7,5},{8,10},{9,11},{10,... | collective-permute-start | bytes 4718600 | tf_op jit(solution)/shard_map/ppermute | solution.py:27
  190.7 18.9 %collective-permute-start.31 = (bf16[384,768]{1,0:T(8,128)(2,1)}, bf16[384,768]{1,0:T(8,128)(2,1)S(1)}, u32[]{:S(2)}, u32[]{:S(2)}) collective-permute-start(bf16[384,768]{1,0:T(8,128)(2,1)} %get-tuple-element.179), channel_id=1, source_target_pairs={{0,4},{4,0},{8,12},{12,8},{16,20},{20,16},{24,28},{28,24},{1,5},{5... | collective-permute-start | bytes 1769480 | tf_op jit(solution)/shard_map/ppermute | solution.py:27
  229.6 23.3 %collective-permute-start.44 = (bf16[512,768]{1,0:T(8,128)(2,1)S(1)}, bf16[512,768]{1,0:T(8,128)(2,1)S(1)}, u32[]{:S(2)}, u32[]{:S(2)}) collective-permute-start(bf16[512,768]{1,0:T(8,128)(2,1)S(1)} %get-tuple-element.178), channel_id=1, source_target_pairs={{0,4},{4,0},{8,12},{12,8},{16,20},{20,16},{24,28},{28,24},{1,5},{5... | collective-permute-start | bytes 2359304 | tf_op jit(solution)/shard_map/ppermute | solution.py:27
  241.7 26.5 %collective-permute-start.33 = (bf16[2,256,768]{2,1,0:T(8,128)(2,1)S(1)}, bf16[2,256,768]{2,1,0:T(8,128)(2,1)S(1)}, u32[]{:S(2)}, u32[]{:S(2)}) collective-permute-start(bf16[2,256,768]{2,1,0:T(8,128)(2,1)S(1)} %get-tuple-element.189), channel_id=1, source_target_pairs={{0,1},{1,0},{2,3},{3,2},{4,5},{5,4},{6,7},{7,6},{8,9},{9,8},{10,11... | collective-permute-start | bytes 2359304 | tf_op jit(solution)/shard_map/ppermute | solution.py:27
  259.7 21.2 %collective-permute-start.53 = (bf16[192,768]{1,0:T(8,128)(2,1)S(1)}, bf16[192,768]{1,0:T(8,128)(2,1)S(1)}, u32[]{:S(2)}, u32[]{:S(2)}) collective-permute-start(bf16[192,768]{1,0:T(8,128)(2,1)S(1)} %maximum_select_fusion.7), channel_id=1, source_target_pairs={{0,8},{4,12},{8,0},{12,4},{16,24},{20,28},{24,16},{28,20},{1,9},{5... | collective-permute-start | bytes 884744 | tf_op jit(solution)/shard_map/ppermute | solution.py:27
  269.2 23.6 %collective-permute-start.34 = (bf16[256,768]{1,0:T(8,128)(2,1)}, bf16[256,768]{1,0:T(8,128)(2,1)}, u32[]{:S(2)}, u32[]{:S(2)}) collective-permute-start(bf16[256,768]{1,0:T(8,128)(2,1)} %fusion.7), channel_id=1, source_target_pairs={{0,2},{1,3},{2,0},{3,1},{4,6},{5,7},{6,4},{7,5},{8,10},{9,11},{10,... | collective-permute-start | bytes 1179656 | tf_op jit(solution)/shard_map/ppermute | solution.py:27
  284.1 21.4 %collective-permute-start.43 = (bf16[4,96,640]{2,1,0:T(8,128)(2,1)S(1)}, bf16[4,96,640]{2,1,0:T(8,128)(2,1)S(1)}, u32[]{:S(2)}, u32[]{:S(2)}) collective-permute-start(bf16[4,96,640]{2,1,0:T(8,128)(2,1)S(1)} %maximum_select_fusion.5), channel_id=1, source_target_pairs={{0,4},{4,0},{8,12},{12,8},{16,20},{20,16},{24,28},{28,24},{1,5},{5... | collective-permute-start | bytes 1474568 | tf_op jit(solution)/shard_map/ppermute | solution.py:27
  (87 other events, 938.7 us)

commit v8 on v7

--- a/solution.py
+++ b/solution.py
@@ -749,6 +749,35 @@
     return block
 
 
+def gather_square(block, axis_name):
+    index = lax.axis_index(axis_name)
+    rows, width = block.shape
+    first, second = block[: rows // 2], block[rows // 2 :]
+    first_got = swapped(first, axis_name, 1)
+    second_got = swapped(second, axis_name, 2)
+    first_got, second_got = lax.optimization_barrier((first_got, second_got))
+    first_far = swapped(jnp.concatenate([first, first_got]), axis_name, 2)
+    second_far = swapped(jnp.concatenate([second, second_got]), axis_name, 1)
+    size = rows // 2
+    ours = [
+        (first, second),
+        (first_far[:size], second_got),
+        (first_got, second_far[:size]),
+        (first_far[size:], second_far[size:]),
+    ]
+    low, high = index % 2 == 1, (index // 2) % 2 == 1
+    placed = []
+    for x in range(2):
+        for z in range(2):
+            for half in range(2):
+                near = jnp.where(high, ours[2 * x + 1 - z][half], ours[2 * x + z][half])
+                across = jnp.where(
+                    high, ours[2 * (1 - x) + 1 - z][half], ours[2 * (1 - x) + z][half]
+                )
+                placed.append(jnp.where(low, across, near))
+    return jnp.concatenate(placed, axis=0)
+
+
 def on_device(
     tokens,
     doc_start,
@@ -913,7 +942,8 @@
     token_got = swapped(token_partial[1::2], "wt", 1)
     token_sum = both(*far_terms(token_partial[0::2], token_got))
     outer_total = gather_back(outer_part, "ctx", near_first, 0)
-    inner_total = gather_back(inner_part, "ctx", near_first, 0)
+    inner_part = gather_back(inner_part, "ctx", near_first[2:], 0)
+    inner_total = gather_square(inner_part, "ctx")
     head_pieces = [
         lax.dynamic_index_in_dim(head_part, w ^ r, 0, keepdims=False) for r in range(shards)
     ]

time: 331 us -> 322 us (0.973)
  starting transfers between devices: 86.6 us -> 80.1 us
  other arithmetic: 35.2 us -> 31.7 us
    ppermute x44 -> x46, starting transfers between devices: 49 us -> 44.5 us  [swapped(): return lax.ppermute(block, axis, [(i, i ^ bit) for i in range(count)])]
    unnamed x118 -> x116, local copies, waits for them, and re-layouts: 9.2 us -> 12.9 us
    ppermute x44 -> x46, waiting for transfers between devices: 81.9 us -> 82.2 us  [swapped(): return lax.ppermute(block, axis, [(i, i ^ bit) for i in range(count)])]
  transfers between devices with their start and end apart: 55 -> 57, of which waited for: 30 -> 29; matrix products, arithmetic and copies ran while one was open for 13% -> 14% of each run, Pallas kernels for 19% -> 20%
where the time goes in v8:
time: 322 us; the launch traced here: 321 us
  waiting for transfers between devices  112 us (35%)
  starting transfers between devices  80.1 us (25%)
  Pallas kernels  67.9 us (21%)
  other arithmetic  31.7 us (10%)
  local copies, waits for them, and re-layouts  24.1 us (7%)
  between operations  4.95 us (2%)
    ppermute x46, waiting for transfers between devices, swapped(): return lax.ppermute(block, axis, [(i, i ^ bit) for i in range(count)])  82.2 us
    ppermute x46, starting transfers between devices, swapped(): return lax.ppermute(block, axis, [(i, i ^ bit) for i in range(count)])  44.5 us
    ppermute x10, starting transfers between devices, shifted(): return lax.ppermute(block, axis, route)  32.2 us
    ppermute x10, waiting for transfers between devices, shifted(): return lax.ppermute(block, axis, route)  27.5 us
    pallas_call x1, Pallas kernels, dense(): pl.pallas_call(dense_kernel, in_specs=[pl.BlockSpec(memory_space=pltpu.SM...  19.9 us
    pallas_call x1, Pallas kernels, attention_keys(): pl.pallas_call(functools.partial(key_kernel, count // 2), grid_spec=pltpu...  18.9 us
    convert_element_type x14, other arithmetic, both(): return (left.astype(f32) + right.astype(f32)).astype(bf16)  13.6 us
    pallas_call x1, Pallas kernels, attention_forward(): pl.pallas_call(forward_kernel, grid_spec=pltpu.PrefetchScalarGridSpec(num...  13.3 us
  transfers between devices with their start and end apart: 57, of which 29 were waited for; matrix products, arithmetic and copies ran while one was open for 14% of the time, Pallas kernels for 20%

profile of v8, /device:TPU:0, one launch (start us, length us, event | category | flops | bytes accessed | tf_op | source)
XLA Modules:
  0.0 320.7 jit_solution(9233478293702311605)
XLA Ops:
  25.9 4.1 %layer_projection.1 = (bf16[1024,768]{1,0:T(8,128)(2,1)S(1)}, bf16[1024,192]{1,0:T(8,128)(2,1)S(1)}, bf16[1024,384]{1,0:T(8,128)(2,1)}) custom-call(s32[4]{0:T(128)S(1)} %pad_add_fusion.2.place_ref, bf16[256,768]{1,0:T(8,128)(2,1)S(1)} %copy-done.14, bf16[256,768]{1,0:T(8,128)(2,1)S(1)} %collective-permute-done.near, ...), custom_call_target="tpu_custom_call" | custom-call | flops 905969664 | bytes 5242880 | tf_op jit(solution)/shard_map/layer_projection/pallas_call | solution.py:436
  45.3 6.6 %collective-permute-done.6.rest_0_ = bf16[1024,384]{1,0:T(8,128)(2,1)S(1)} collective-permute-done((bf16[1024,384]{1,0:T(8,128)(2,1)}, bf16[1024,384]{1,0:T(8,128)(2,1)S(1)}, u32[]{:S(2)}, u32[]{:S(2)}) %collective-permute-start.6) | collective-permute-done | bytes 786464 | tf_op jit(solution)/shard_map/ppermute | solution.py:33
  51.9 4.1 %collective-permute-done.7.rest_1_ = bf16[1024,384]{1,0:T(8,128)(2,1)S(1)} collective-permute-done((bf16[1024,384]{1,0:T(8,128)(2,1)}, bf16[1024,384]{1,0:T(8,128)(2,1)S(1)}, u32[]{:S(2)}, u32[]{:S(2)}) %collective-permute-start.7) | collective-permute-done | bytes 786464 | tf_op jit(solution)/shard_map/ppermute | solution.py:33
  61.1 4.9 %collective-permute-done.9.rest_4_ = bf16[512,384]{1,0:T(8,128)(2,1)S(1)} collective-permute-done((bf16[512,384]{1,0:T(8,128)(2,1)S(1)}, bf16[512,384]{1,0:T(8,128)(2,1)S(1)}, u32[]{:S(2)}, u32[]{:S(2)}) %collective-permute-start.9) | collective-permute-done | bytes 393248 | tf_op jit(solution)/shard_map/ppermute | solution.py:27
  68.3 4.6 %collective-permute-start.11 = (bf16[1024,192]{1,0:T(8,128)(2,1)S(1)}, bf16[1024,192]{1,0:T(8,128)(2,1)}, u32[]{:S(2)}, u32[]{:S(2)}) collective-permute-start(bf16[1024,192]{1,0:T(8,128)(2,1)S(1)} %get-tuple-element.126.q_ref.rest_6_), channel_id=1, source_target_pairs={{0,4},{4,8},{8,12},{12,16},{16,20},{20,24},{24,28},{1,5},{5,9},{9,... | collective-permute-start | bytes 1179656 | tf_op jit(solution)/shard_map/ppermute | solution.py:33
  74.3 13.3 %attention_forward.1 = (bf16[256,192]{1,0:T(8,128)(2,1)}, bf16[256,192]{1,0:T(8,128)(2,1)}, bf16[256,192]{1,0:T(8,128)(2,1)}, bf16[256,192]{1,0:T(8,128)(2,1)}, ...) custom-call(s32[20]{0:T(128)} %concatenate.110.bounds, bf16[1024,192]{1,0:T(8,128)(2,1)} %copy-done.12, ...), custom_call_target="tpu_custom_call" | custom-call | flops 1811939328 | bytes 6291456 | tf_op jit(solution)/shard_map/attention_forward/pallas_call | solution.py:148
  87.5 4.9 %collective-permute-done.11.rest_5_ = bf16[1024,192]{1,0:T(8,128)(2,1)} collective-permute-done((bf16[1024,192]{1,0:T(8,128)(2,1)S(1)}, bf16[1024,192]{1,0:T(8,128)(2,1)}, u32[]{:S(2)}, u32[]{:S(2)}) %collective-permute-start.11) | collective-permute-done | bytes 393248 | tf_op jit(solution)/shard_map/ppermute | solution.py:33
  92.4 3.7 %collective-permute-done.13.refs_8_ = bf16[1744,768]{1,0:T(8,128)(2,1)} collective-permute-done((bf16[1744,768]{1,0:T(8,128)(2,1)}, bf16[1744,768]{1,0:T(8,128)(2,1)}, u32[]{:S(2)}, u32[]{:S(2)}) %collective-permute-start.13) | collective-permute-done | bytes 2678816 | tf_op jit(solution)/shard_map/ppermute | solution.py:27
  104.1 7.2 %collective-permute-start.19 = (bf16[1024,192]{1,0:T(8,128)(2,1)}, bf16[1024,192]{1,0:T(8,128)(2,1)S(1)}, u32[]{:S(2)}, u32[]{:S(2)}) collective-permute-start(bf16[1024,192]{1,0:T(8,128)(2,1)} %copy-done.12), channel_id=1, source_target_pairs={{0,8},{4,12},{8,16},{12,20},{16,24},{20,28},{1,9},{5,13},{9,17},{1... | collective-permute-start | bytes 1179656 | tf_op jit(solution)/shard_map/ppermute | solution.py:33
  115.2 19.9 %layer_dense.1 = (bf16[256,768]{1,0:T(8,128)(2,1)}, f32[256,768]{1,0:T(8,128)S(1)}, bf16[256,192]{1,0:T(8,128)(2,1)S(1)}, bf16[256,192]{1,0:T(8,128)(2,1)S(1)}, ...) custom-call(s32[4]{0:T(128)S(1)} %pad_add_fusion.2.place_ref, ...), custom_call_target="tpu_custom_call" | custom-call | flops 14495514624 | bytes 25165824 | tf_op jit(solution)/shard_map/layer_dense/pallas_call | solution.py:646
  149.2 4.6 %collective-permute-start.25 = (bf16[1024,256]{1,0:T(8,128)(2,1)S(1)}, bf16[1024,256]{1,0:T(8,128)(2,1)S(1)}, u32[]{:S(2)}, u32[]{:S(2)}) collective-permute-start(bf16[1024,256]{1,0:T(8,128)(2,1)S(1)} %layer_gather.1.grad_ref.rest_11_), channel_id=1, source_target_pairs={{0,8},{4,12},{8,16},{12,20},{16,24},{20,28},{1,9},{5,13},{9,17},{1... | collective-permute-start | bytes 1572872 | tf_op jit(solution)/shard_map/ppermute | solution.py:33
  153.8 5.4 %collective-permute-start.26 = (bf16[1024,256]{1,0:T(8,128)(2,1)S(1)}, bf16[1024,256]{1,0:T(8,128)(2,1)S(1)}, u32[]{:S(2)}, u32[]{:S(2)}) collective-permute-start(bf16[1024,256]{1,0:T(8,128)(2,1)S(1)} %layer_gather.1.grad_ref.rest_11_), channel_id=1, source_target_pairs={{0,4},{4,8},{8,12},{12,16},{16,20},{20,24},{24,28},{1,5},{5,9},{9,... | collective-permute-start | bytes 1572872 | tf_op jit(solution)/shard_map/ppermute | solution.py:33
  162.1 9.4 %attention_queries.1.query_ref = bf16[1024,192]{1,0:T(8,128)(2,1)S(1)} custom-call(s32[20]{0:T(128)S(1)} %copy-done.11, bf16[1024,192]{1,0:T(8,128)(2,1)S(1)} %copy-done.13, s32[8,1024]{1,0:T(8,128)S(1)} %copy-done.10, bf16[1024,256]{1,0:T(8,128)(2,1)S(1)} %layer_gather.1.grad_ref.rest_11_, f32[1024,192]{1,0:T(8,128)S(1)} %copy-done, ...), custom_call_target="tpu_custom_call" | custom-call | flops 2717908992 | bytes 6291456 | tf_op jit(solution)/shard_map/attention_queries/pallas_call | solution.py:235
  173.9 7.6 %collective-permute-done.26.rest_10_ = bf16[1024,256]{1,0:T(8,128)(2,1)S(1)} collective-permute-done((bf16[1024,256]{1,0:T(8,128)(2,1)S(1)}, bf16[1024,256]{1,0:T(8,128)(2,1)S(1)}, u32[]{:S(2)}, u32[]{:S(2)}) %collective-permute-start.26) | collective-permute-done | bytes 524320 | tf_op jit(solution)/shard_map/ppermute | solution.py:33
  181.5 4.4 %collective-permute-done.28.rest_13_ = bf16[1024,256]{1,0:T(8,128)(2,1)S(1)} collective-permute-done((bf16[1024,256]{1,0:T(8,128)(2,1)S(1)}, bf16[1024,256]{1,0:T(8,128)(2,1)S(1)}, u32[]{:S(2)}, u32[]{:S(2)}) %collective-permute-start.28) | collective-permute-done | bytes 524320 | tf_op jit(solution)/shard_map/ppermute | solution.py:33
  191.0 18.9 %attention_keys.1 = (bf16[4,192,640]{2,1,0:T(8,128)(2,1)}, bf16[4,256,768]{2,1,0:T(8,128)(2,1)}) custom-call(s32[20]{0:T(128)} %concatenate.110.bounds, bf16[1024,384]{1,0:T(8,128)(2,1)} %get-tuple-element.94.rest_2_.kv_ref, s32[8,5120]{1,0:T(8,128)} %add_add_fusion.span_ref, bf16[1024,768]{1,0:T(8,128)(2,1)} %copy-done.23, bf16[1024,192]{1,0:T(8,128)(2,1)} %copy-done.24, ...), custom_call_target="tpu_custom_call" | custom-call | flops 4529848320 | bytes 12582912 | tf_op jit(solution)/shard_map/attention_keys/pallas_call | solution.py:377
  210.0 13.5 %collective-permute-done.32 = bf16[1024,768]{1,0:T(8,128)(2,1)} collective-permute-done((bf16[1024,768]{1,0:T(8,128)(2,1)}, bf16[1024,768]{1,0:T(8,128)(2,1)}, u32[]{:S(2)}, u32[]{:S(2)}) %collective-permute-start.32) | collective-permute-done | bytes 1572896 | tf_op jit(solution)/shard_map/ppermute | solution.py:27
  227.4 4.2 %collective-permute-done.52 = bf16[192,768]{1,0:T(8,128)(2,1)S(1)} collective-permute-done((bf16[192,768]{1,0:T(8,128)(2,1)S(1)}, bf16[192,768]{1,0:T(8,128)(2,1)S(1)}, u32[]{:S(2)}, u32[]{:S(2)}) %collective-permute-start.52) | collective-permute-done | bytes 294944 | tf_op jit(solution)/shard_map/ppermute | solution.py:27
  247.6 4.1 %collective-permute-done.36 = bf16[4,48,640]{2,1,0:T(8,128)(2,1)S(1)} collective-permute-done((bf16[4,48,640]{2,1,0:T(8,128)(2,1)}, bf16[4,48,640]{2,1,0:T(8,128)(2,1)S(1)}, u32[]{:S(2)}, u32[]{:S(2)}) %collective-permute-start.36) | collective-permute-done | bytes 245792 | tf_op jit(solution)/shard_map/ppermute | solution.py:27
  268.2 5.2 %collective-permute-done.41 = bf16[4,24,640]{2,1,0:T(8,128)(2,1)S(1)} collective-permute-done((bf16[4,24,640]{2,1,0:T(8,128)(2,1)S(1)}, bf16[4,24,640]{2,1,0:T(8,128)(2,1)S(1)}, u32[]{:S(2)}, u32[]{:S(2)}) %collective-permute-start.41) | collective-permute-done | bytes 122912 | tf_op jit(solution)/shard_map/ppermute | solution.py:27
  278.3 5.2 %collective-permute-done.46 = bf16[128,768]{1,0:T(8,128)(2,1)S(1)} collective-permute-done((bf16[128,768]{1,0:T(8,128)(2,1)S(1)}, bf16[128,768]{1,0:T(8,128)(2,1)S(1)}, u32[]{:S(2)}, u32[]{:S(2)}) %collective-permute-start.46) | collective-permute-done | bytes 196640 | tf_op jit(solution)/shard_map/ppermute | solution.py:27
  290.6 5.2 %collective-permute-done.47 = bf16[128,768]{1,0:T(8,128)(2,1)S(1)} collective-permute-done((bf16[128,768]{1,0:T(8,128)(2,1)S(1)}, bf16[128,768]{1,0:T(8,128)(2,1)S(1)}, u32[]{:S(2)}, u32[]{:S(2)}) %collective-permute-start.47) | collective-permute-done | bytes 196640 | tf_op jit(solution)/shard_map/ppermute | solution.py:27
  297.7 3.7 %collective-permute-done.43 = bf16[4,96,640]{2,1,0:T(8,128)(2,1)S(1)} collective-permute-done((bf16[4,96,640]{2,1,0:T(8,128)(2,1)S(1)}, bf16[4,96,640]{2,1,0:T(8,128)(2,1)S(1)}, u32[]{:S(2)}, u32[]{:S(2)}) %collective-permute-start.43) | collective-permute-done | bytes 491552 | tf_op jit(solution)/shard_map/ppermute | solution.py:27
  308.4 4.9 %collective-permute-done.51 = bf16[256,768]{1,0:T(8,128)(2,1)S(1)} collective-permute-done((bf16[256,768]{1,0:T(8,128)(2,1)S(1)}, bf16[256,768]{1,0:T(8,128)(2,1)S(1)}, u32[]{:S(2)}, u32[]{:S(2)}) %collective-permute-start.51) | collective-permute-done | bytes 393248 | tf_op jit(solution)/shard_map/ppermute | solution.py:27
  (303 shorter events, 146.2 us)
Async XLA Ops:
  0.7 22.2 %collective-permute-start.1 = (bf16[256,768]{1,0:T(8,128)(2,1)}, bf16[256,768]{1,0:T(8,128)(2,1)S(1)}, u32[]{:S(2)}, u32[]{:S(2)}) collective-permute-start(bf16[256,768]{1,0:T(8,128)(2,1)} %refs_4_.1), channel_id=1, source_target_pairs={{0,2},{1,3},{2,0},{3,1},{4,6},{5,7},{6,4},{7,5},{8,10},{9,11},{10,... | collective-permute-start | bytes 1179656 | tf_op jit(solution)/shard_map/ppermute | solution.py:27
  3.7 22.2 %collective-permute-start = (bf16[256,768]{1,0:T(8,128)(2,1)}, bf16[256,768]{1,0:T(8,128)(2,1)S(1)}, u32[]{:S(2)}, u32[]{:S(2)}) collective-permute-start(bf16[256,768]{1,0:T(8,128)(2,1)} %refs_4_.1), channel_id=1, source_target_pairs={{0,1},{1,0},{2,3},{3,2},{4,5},{5,4},{6,7},{7,6},{8,9},{9,8},{10,11... | collective-permute-start | bytes 1179656 | tf_op jit(solution)/shard_map/ppermute | solution.py:27
  7.5 18.3 %collective-permute-start.3 = (bf16[192,576]{1,0:T(8,128)(2,1)}, bf16[192,576]{1,0:T(8,128)(2,1)S(1)}, u32[]{:S(2)}, u32[]{:S(2)}) collective-permute-start(bf16[192,576]{1,0:T(8,128)(2,1)} %pad_maximum_fusion.8), channel_id=1, source_target_pairs={{0,1},{1,0},{2,3},{3,2},{4,5},{5,4},{6,7},{7,6},{8,9},{9,8},{10,11... | collective-permute-start | bytes 663560 | tf_op jit(solution)/shard_map/ppermute | solution.py:27
  31.2 20.7 %collective-permute-start.6 = (bf16[1024,384]{1,0:T(8,128)(2,1)}, bf16[1024,384]{1,0:T(8,128)(2,1)S(1)}, u32[]{:S(2)}, u32[]{:S(2)}) collective-permute-start(bf16[1024,384]{1,0:T(8,128)(2,1)} %get-tuple-element.94.rest_2_.kv_ref), channel_id=1, source_target_pairs={{0,8},{4,12},{8,16},{12,20},{16,24},{20,28},{1,9},{5,13},{9,17},{1... | collective-permute-start | bytes 2359304 | tf_op jit(solution)/shard_map/ppermute | solution.py:33
  34.7 21.3 %collective-permute-start.7 = (bf16[1024,384]{1,0:T(8,128)(2,1)}, bf16[1024,384]{1,0:T(8,128)(2,1)S(1)}, u32[]{:S(2)}, u32[]{:S(2)}) collective-permute-start(bf16[1024,384]{1,0:T(8,128)(2,1)} %get-tuple-element.94.rest_2_.kv_ref), channel_id=1, source_target_pairs={{8,0},{12,4},{16,8},{20,12},{24,16},{28,20},{9,1},{13,5},{17,9},{2... | collective-permute-start | bytes 2359304 | tf_op jit(solution)/shard_map/ppermute | solution.py:33
  36.0 60.1 %collective-permute-start.13 = (bf16[1744,768]{1,0:T(8,128)(2,1)}, bf16[1744,768]{1,0:T(8,128)(2,1)}, u32[]{:S(2)}, u32[]{:S(2)}) collective-permute-start(bf16[1744,768]{1,0:T(8,128)(2,1)} %slice_dynamic-update-slice_fusion.refs_6_), channel_id=1, source_target_pairs={{0,2},{1,3},{2,0},{3,1},{4,6},{5,7},{6,4},{7,5},{8,10},{9,11},{10,... | collective-permute-start | bytes 8036360 | tf_op jit(solution)/shard_map/ppermute | solution.py:27
  37.4 20.2 %collective-permute-start.8 = (bf16[1024,384]{1,0:T(8,128)(2,1)}, bf16[1024,384]{1,0:T(8,128)(2,1)S(1)}, u32[]{:S(2)}, u32[]{:S(2)}) collective-permute-start(bf16[1024,384]{1,0:T(8,128)(2,1)} %get-tuple-element.94.rest_2_.kv_ref), channel_id=1, source_target_pairs={{0,4},{4,0},{8,12},{12,8},{16,20},{20,16},{24,28},{28,24},{1,5},{5... | collective-permute-start | bytes 2359304 | tf_op jit(solution)/shard_map/ppermute | solution.py:27
  68.3 24.2 %collective-permute-start.11 = (bf16[1024,192]{1,0:T(8,128)(2,1)S(1)}, bf16[1024,192]{1,0:T(8,128)(2,1)}, u32[]{:S(2)}, u32[]{:S(2)}) collective-permute-start(bf16[1024,192]{1,0:T(8,128)(2,1)S(1)} %get-tuple-element.126.q_ref.rest_6_), channel_id=1, source_target_pairs={{0,4},{4,8},{8,12},{12,16},{16,20},{20,24},{24,28},{1,5},{5,9},{9,... | collective-permute-start | bytes 1179656 | tf_op jit(solution)/shard_map/ppermute | solution.py:33
  72.9 19.5 %collective-permute-start.12 = (bf16[1024,192]{1,0:T(8,128)(2,1)S(1)}, bf16[1024,192]{1,0:T(8,128)(2,1)}, u32[]{:S(2)}, u32[]{:S(2)}) collective-permute-start(bf16[1024,192]{1,0:T(8,128)(2,1)S(1)} %get-tuple-element.126.q_ref.rest_6_), channel_id=1, source_target_pairs={{4,0},{8,4},{12,8},{16,12},{20,16},{24,20},{28,24},{5,1},{9,5},{13... | collective-permute-start | bytes 1179656 | tf_op jit(solution)/shard_map/ppermute | solution.py:33
  74.2 38.6 %collective-permute-start.17 = (bf16[1744,768]{1,0:T(8,128)(2,1)}, bf16[1744,768]{1,0:T(8,128)(2,1)}, u32[]{:S(2)}, u32[]{:S(2)}) collective-permute-start(bf16[1744,768]{1,0:T(8,128)(2,1)} %slice_dynamic-update-slice_fusion.refs_6_), channel_id=1, source_target_pairs={{0,1},{1,0},{2,3},{3,2},{4,5},{5,4},{6,7},{7,6},{8,9},{9,8},{10,11... | collective-permute-start | bytes 8036360 | tf_op jit(solution)/shard_map/ppermute | solution.py:27
  104.1 31.0 %collective-permute-start.19 = (bf16[1024,192]{1,0:T(8,128)(2,1)}, bf16[1024,192]{1,0:T(8,128)(2,1)S(1)}, u32[]{:S(2)}, u32[]{:S(2)}) collective-permute-start(bf16[1024,192]{1,0:T(8,128)(2,1)} %copy-done.12), channel_id=1, source_target_pairs={{0,8},{4,12},{8,16},{12,20},{16,24},{20,28},{1,9},{5,13},{9,17},{1... | collective-permute-start | bytes 1179656 | tf_op jit(solution)/shard_map/ppermute | solution.py:33
  111.3 23.9 %collective-permute-start.20 = (bf16[1024,192]{1,0:T(8,128)(2,1)}, bf16[1024,192]{1,0:T(8,128)(2,1)S(1)}, u32[]{:S(2)}, u32[]{:S(2)}) collective-permute-start(bf16[1024,192]{1,0:T(8,128)(2,1)} %copy-done.12), channel_id=1, source_target_pairs={{8,0},{12,4},{16,8},{20,12},{24,16},{28,20},{9,1},{13,5},{17,9},{2... | collective-permute-start | bytes 1179656 | tf_op jit(solution)/shard_map/ppermute | solution.py:33
  145.6 28.2 %collective-permute-start.30 = (bf16[768,768]{1,0:T(8,128)(2,1)S(1)}, bf16[768,768]{1,0:T(8,128)(2,1)S(1)}, u32[]{:S(2)}, u32[]{:S(2)}) collective-permute-start(bf16[768,768]{1,0:T(8,128)(2,1)S(1)} %get-tuple-element.179), channel_id=1, source_target_pairs={{0,2},{1,3},{2,0},{3,1},{4,6},{5,7},{6,4},{7,5},{8,10},{9,11},{10,... | collective-permute-start | bytes 3538952 | tf_op jit(solution)/shard_map/ppermute | solution.py:27
  149.2 24.7 %collective-permute-start.25 = (bf16[1024,256]{1,0:T(8,128)(2,1)S(1)}, bf16[1024,256]{1,0:T(8,128)(2,1)S(1)}, u32[]{:S(2)}, u32[]{:S(2)}) collective-permute-start(bf16[1024,256]{1,0:T(8,128)(2,1)S(1)} %layer_gather.1.grad_ref.rest_11_), channel_id=1, source_target_pairs={{0,8},{4,12},{8,16},{12,20},{16,24},{20,28},{1,9},{5,13},{9,17},{1... | collective-permute-start | bytes 1572872 | tf_op jit(solution)/shard_map/ppermute | solution.py:33
  153.8 27.7 %collective-permute-start.26 = (bf16[1024,256]{1,0:T(8,128)(2,1)S(1)}, bf16[1024,256]{1,0:T(8,128)(2,1)S(1)}, u32[]{:S(2)}, u32[]{:S(2)}) collective-permute-start(bf16[1024,256]{1,0:T(8,128)(2,1)S(1)} %layer_gather.1.grad_ref.rest_11_), channel_id=1, source_target_pairs={{0,4},{4,8},{8,12},{12,16},{16,20},{20,24},{24,28},{1,5},{5,9},{9,... | collective-permute-start | bytes 1572872 | tf_op jit(solution)/shard_map/ppermute | solution.py:33
  159.2 22.3 %collective-permute-start.27 = (bf16[1024,256]{1,0:T(8,128)(2,1)S(1)}, bf16[1024,256]{1,0:T(8,128)(2,1)S(1)}, u32[]{:S(2)}, u32[]{:S(2)}) collective-permute-start(bf16[1024,256]{1,0:T(8,128)(2,1)S(1)} %layer_gather.1.grad_ref.rest_11_), channel_id=1, source_target_pairs={{4,0},{8,4},{12,8},{16,12},{20,16},{24,20},{28,24},{5,1},{9,5},{13... | collective-permute-start | bytes 1572872 | tf_op jit(solution)/shard_map/ppermute | solution.py:33
  160.5 25.4 %collective-permute-start.28 = (bf16[1024,256]{1,0:T(8,128)(2,1)S(1)}, bf16[1024,256]{1,0:T(8,128)(2,1)S(1)}, u32[]{:S(2)}, u32[]{:S(2)}) collective-permute-start(bf16[1024,256]{1,0:T(8,128)(2,1)S(1)} %layer_gather.1.grad_ref.rest_11_), channel_id=1, source_target_pairs={{8,0},{12,4},{16,8},{20,12},{24,16},{28,20},{9,1},{13,5},{17,9},{2... | collective-permute-start | bytes 1572872 | tf_op jit(solution)/shard_map/ppermute | solution.py:33
  187.9 35.6 %collective-permute-start.32 = (bf16[1024,768]{1,0:T(8,128)(2,1)}, bf16[1024,768]{1,0:T(8,128)(2,1)}, u32[]{:S(2)}, u32[]{:S(2)}) collective-permute-start(bf16[1024,768]{1,0:T(8,128)(2,1)} %get-tuple-element.177), channel_id=1, source_target_pairs={{0,2},{1,3},{2,0},{3,1},{4,6},{5,7},{6,4},{7,5},{8,10},{9,11},{10,... | collective-permute-start | bytes 4718600 | tf_op jit(solution)/shard_map/ppermute | solution.py:27
  191.0 18.9 %collective-permute-start.31 = (bf16[384,768]{1,0:T(8,128)(2,1)}, bf16[384,768]{1,0:T(8,128)(2,1)}, u32[]{:S(2)}, u32[]{:S(2)}) collective-permute-start(bf16[384,768]{1,0:T(8,128)(2,1)} %get-tuple-element.183), channel_id=1, source_target_pairs={{0,4},{4,0},{8,12},{12,8},{16,20},{20,16},{24,28},{28,24},{1,5},{5... | collective-permute-start | bytes 1769480 | tf_op jit(solution)/shard_map/ppermute | solution.py:27
  236.5 18.3 %collective-permute-start.44 = (bf16[512,768]{1,0:T(8,128)(2,1)}, bf16[512,768]{1,0:T(8,128)(2,1)}, u32[]{:S(2)}, u32[]{:S(2)}) collective-permute-start(bf16[512,768]{1,0:T(8,128)(2,1)} %get-tuple-element.182), channel_id=1, source_target_pairs={{0,4},{4,0},{8,12},{12,8},{16,20},{20,16},{24,28},{28,24},{1,5},{5... | collective-permute-start | bytes 2359304 | tf_op jit(solution)/shard_map/ppermute | solution.py:27
  243.9 17.7 %collective-permute-start.33 = (bf16[2,256,768]{2,1,0:T(8,128)(2,1)}, bf16[2,256,768]{2,1,0:T(8,128)(2,1)}, u32[]{:S(2)}, u32[]{:S(2)}) collective-permute-start(bf16[2,256,768]{2,1,0:T(8,128)(2,1)} %get-tuple-element.188), channel_id=1, source_target_pairs={{0,1},{1,0},{2,3},{3,2},{4,5},{5,4},{6,7},{7,6},{8,9},{9,8},{10,11... | collective-permute-start | bytes 2359304 | tf_op jit(solution)/shard_map/ppermute | solution.py:27
  247.5 17.6 %collective-permute-start.55 = (bf16[192,768]{1,0:T(8,128)(2,1)S(1)}, bf16[192,768]{1,0:T(8,128)(2,1)S(1)}, u32[]{:S(2)}, u32[]{:S(2)}) collective-permute-start(bf16[192,768]{1,0:T(8,128)(2,1)S(1)} %maximum_select_fusion.5), channel_id=1, source_target_pairs={{0,8},{4,12},{8,0},{12,4},{16,24},{20,28},{24,16},{28,20},{1,9},{5... | collective-permute-start | bytes 884744 | tf_op jit(solution)/shard_map/ppermute | solution.py:27
  256.2 17.3 %collective-permute-start.45 = (bf16[256,768]{1,0:T(8,128)(2,1)S(1)}, bf16[256,768]{1,0:T(8,128)(2,1)S(1)}, u32[]{:S(2)}, u32[]{:S(2)}) collective-permute-start(bf16[256,768]{1,0:T(8,128)(2,1)S(1)} %get-tuple-element.186), channel_id=1, source_target_pairs={{0,8},{4,12},{8,0},{12,4},{16,24},{20,28},{24,16},{28,20},{1,9},{5... | collective-permute-start | bytes 1179656 | tf_op jit(solution)/shard_map/ppermute | solution.py:27
  265.3 23.6 %collective-permute-start.56 = (bf16[384,768]{1,0:T(8,128)(2,1)S(1)}, bf16[384,768]{1,0:T(8,128)(2,1)S(1)}, u32[]{:S(2)}, u32[]{:S(2)}) collective-permute-start(bf16[384,768]{1,0:T(8,128)(2,1)S(1)} %maximum_select_fusion.2), channel_id=1, source_target_pairs={{0,4},{4,0},{8,12},{12,8},{16,20},{20,16},{24,28},{28,24},{1,5},{5... | collective-permute-start | bytes 1769480 | tf_op jit(solution)/shard_map/ppermute | solution.py:27
  (88 other events, 992.5 us)

commit v9 on v8

--- a/solution.py
+++ b/solution.py
@@ -886,9 +886,9 @@
     *mixed_pieces, mixed_wide, stat_rows, stat_columns = attention_forward(
         bounds, queries, spans, pairs
     )
-    ready, _ = lax.optimization_barrier((queries, pairs))
-    query_halo = [queries if d == 0 else shifted(ready, "ctx", d) if d * d == 1 else None for d in distances]
-    close = [x for x, d in zip(query_halo, distances) if d * d == 1]
+    ready, _ = lax.optimization_barrier((queries, [before, after, beside]))
+    query_halo = [queries if d == 0 else shifted(ready, "ctx", d) if d * d > 1 else None for d in distances]
+    close = [x for x, d in zip(query_halo, distances) if d * d > 1]
     mixed_pieces, mixed_wide, stat_columns, close, pack_far = lax.optimization_barrier(
         (mixed_pieces, mixed_wide, stat_columns, close, pack_far)
     )
@@ -901,11 +901,11 @@
     results = dense(
         places, mixed_pieces, tokens, cotangent, packs
     )
-    remote = [shifted(far_ready, "ctx", d) for d in distances if d * d > 1]
+    remote = [shifted(far_ready, "ctx", d) for d in distances if d * d == 1]
     results, remote = lax.optimization_barrier((results, remote))
     layer_out, grad_one, *back = results[: 2 + shards]
     outer_keep, outer_send, inner_keep, inner_send = results[2 + shards :]
-    query_halo = [remote[0], close[0], queries, close[1], remote[1]]
+    query_halo = [close[0], remote[0], queries, remote[1], close[1]]
 
     back_pieces = [back[0]] + [swapped(back[r], "wt", r) for r in range(1, shards)]
     outer_got = swapped(outer_send, "wt", 1)

time: 322 us -> 316 us (0.981); the launches traced: 321 us -> 319 us
  Pallas kernels: 67.9 us -> 81.2 us
  waiting for transfers between devices: 112 us -> 104 us
  starting transfers between devices: 80.1 us -> 72.4 us
    ppermute x46, starting transfers between devices: 44.5 us -> 35.7 us  [swapped(): return lax.ppermute(block, axis, [(i, i ^ bit) for i in range(count)])]
    pallas_call x1, Pallas kernels: 18.9 us -> 23.6 us  [attention_keys(): pl.pallas_call(functools.partial(key_kernel, count // 2), grid_spec=pltpu...]
    pallas_call x1, Pallas kernels: 13.3 us -> 17.9 us  [attention_forward(): pl.pallas_call(forward_kernel, grid_spec=pltpu.PrefetchScalarGridSpec(num...]
    ppermute x10, waiting for transfers between devices: 27.5 us -> 23 us  [shifted(): return lax.ppermute(block, axis, route)]
    ppermute x46, waiting for transfers between devices: 82.2 us -> 77.8 us  [swapped(): return lax.ppermute(block, axis, [(i, i ^ bit) for i in range(count)])]
    pallas_call x1, Pallas kernels: 9.36 us -> 13.3 us  [attention_queries(): pl.pallas_call(query_kernel, grid_spec=pltpu.PrefetchScalarGridSpec(num_s...]
    unnamed x116 -> x108, local copies, waits for them, and re-layouts: 12.9 us -> 13.2 us
  transfers between devices with their start and end apart: 57 -> 57, of which waited for: 29 -> 26; matrix products, arithmetic and copies ran while one was open for 14% -> 14% of each run, Pallas kernels for 20% -> 25%
where the time goes in v9:
time: 316 us; the launch traced here: 319 us
  waiting for transfers between devices  104 us (33%)
  Pallas kernels  81.2 us (26%)
  starting transfers between devices  72.4 us (23%)
  other arithmetic  31.6 us (10%)
  local copies, waits for them, and re-layouts  24.3 us (8%)
  between operations  4.99 us (2%)
    ppermute x46, waiting for transfers between devices, swapped(): return lax.ppermute(block, axis, [(i, i ^ bit) for i in range(count)])  77.8 us
    ppermute x46, starting transfers between devices, swapped(): return lax.ppermute(block, axis, [(i, i ^ bit) for i in range(count)])  35.7 us
    ppermute x10, starting transfers between devices, shifted(): return lax.ppermute(block, axis, route)  32.4 us
    pallas_call x1, Pallas kernels, attention_keys(): pl.pallas_call(functools.partial(key_kernel, count // 2), grid_spec=pltpu...  23.6 us
    ppermute x10, waiting for transfers between devices, shifted(): return lax.ppermute(block, axis, route)  23 us
    pallas_call x1, Pallas kernels, dense(): pl.pallas_call(dense_kernel, in_specs=[pl.BlockSpec(memory_space=pltpu.SM...  19.9 us
    pallas_call x1, Pallas kernels, attention_forward(): pl.pallas_call(forward_kernel, grid_spec=pltpu.PrefetchScalarGridSpec(num...  17.9 us
    convert_element_type x14, other arithmetic, both(): return (left.astype(f32) + right.astype(f32)).astype(bf16)  13.5 us
  transfers between devices with their start and end apart: 57, of which 26 were waited for; matrix products, arithmetic and copies ran while one was open for 14% of the time, Pallas kernels for 25%

profile of v9, /device:TPU:0, one launch (start us, length us, event | category | flops | bytes accessed | tf_op | source)
XLA Modules:
  0.0 319.0 jit_solution(11264126054930318464)
XLA Ops:
  26.0 4.1 %layer_projection.1 = (bf16[1024,768]{1,0:T(8,128)(2,1)S(1)}, bf16[1024,192]{1,0:T(8,128)(2,1)S(1)}, bf16[1024,384]{1,0:T(8,128)(2,1)}) custom-call(s32[4]{0:T(128)S(1)} %pad_add_fusion.2.place_ref, bf16[256,768]{1,0:T(8,128)(2,1)S(1)} %copy-done.14, bf16[256,768]{1,0:T(8,128)(2,1)S(1)} %collective-permute-done.near, ...), custom_call_target="tpu_custom_call" | custom-call | flops 905969664 | bytes 5242880 | tf_op jit(solution)/shard_map/layer_projection/pallas_call | solution.py:436
  31.3 3.9 %collective-permute-start.6 = (bf16[1024,384]{1,0:T(8,128)(2,1)}, bf16[1024,384]{1,0:T(8,128)(2,1)S(1)}, u32[]{:S(2)}, u32[]{:S(2)}) collective-permute-start(bf16[1024,384]{1,0:T(8,128)(2,1)} %get-tuple-element.94.rest_2_.kv_ref), channel_id=1, source_target_pairs={{0,8},{4,12},{8,16},{12,20},{16,24},{20,28},{1,9},{5,13},{9,17},{1... | collective-permute-start | bytes 2359304 | tf_op jit(solution)/shard_map/ppermute | solution.py:33
  45.3 6.9 %collective-permute-done.6.rest_0_ = bf16[1024,384]{1,0:T(8,128)(2,1)S(1)} collective-permute-done((bf16[1024,384]{1,0:T(8,128)(2,1)}, bf16[1024,384]{1,0:T(8,128)(2,1)S(1)}, u32[]{:S(2)}, u32[]{:S(2)}) %collective-permute-start.6) | collective-permute-done | bytes 786464 | tf_op jit(solution)/shard_map/ppermute | solution.py:33
  52.2 4.1 %collective-permute-done.7.rest_1_ = bf16[1024,384]{1,0:T(8,128)(2,1)S(1)} collective-permute-done((bf16[1024,384]{1,0:T(8,128)(2,1)}, bf16[1024,384]{1,0:T(8,128)(2,1)S(1)}, u32[]{:S(2)}, u32[]{:S(2)}) %collective-permute-start.7) | collective-permute-done | bytes 786464 | tf_op jit(solution)/shard_map/ppermute | solution.py:33
  57.9 4.2 %collective-permute-start.10 = (bf16[512,384]{1,0:T(8,128)(2,1)S(1)}, bf16[512,384]{1,0:T(8,128)(2,1)}, u32[]{:S(2)}, u32[]{:S(2)}) collective-permute-start(bf16[512,384]{1,0:T(8,128)(2,1)S(1)} %slice.280), channel_id=1, source_target_pairs={{0,8},{8,16},{12,4},{16,24},{20,12},{28,20},{1,9},{9,17},{13,5},{1... | collective-permute-start | bytes 1179656 | tf_op jit(solution)/shard_map/ppermute | solution.py:875
  62.1 3.7 %collective-permute-start.11 = (bf16[1024,192]{1,0:T(8,128)(2,1)S(1)}, bf16[1024,192]{1,0:T(8,128)(2,1)}, u32[]{:S(2)}, u32[]{:S(2)}) collective-permute-start(bf16[1024,192]{1,0:T(8,128)(2,1)S(1)} %get-tuple-element.126.q_ref.rest_6_), channel_id=1, source_target_pairs={{0,8},{4,12},{8,16},{12,20},{16,24},{20,28},{1,9},{5,13},{9,17},{1... | collective-permute-start | bytes 1179656 | tf_op jit(solution)/shard_map/ppermute | solution.py:33
  70.9 17.9 %attention_forward.1 = (bf16[256,192]{1,0:T(8,128)(2,1)}, bf16[256,192]{1,0:T(8,128)(2,1)}, bf16[256,192]{1,0:T(8,128)(2,1)}, bf16[256,192]{1,0:T(8,128)(2,1)}, ...) custom-call(s32[20]{0:T(128)} %concatenate.110.bounds, bf16[1024,192]{1,0:T(8,128)(2,1)} %copy-done.12, ...), custom_call_target="tpu_custom_call" | custom-call | flops 1811939328 | bytes 6291456 | tf_op jit(solution)/shard_map/attention_forward/pallas_call | solution.py:148
  97.1 7.9 %collective-permute-start.19 = (bf16[1024,192]{1,0:T(8,128)(2,1)}, bf16[1024,192]{1,0:T(8,128)(2,1)S(1)}, u32[]{:S(2)}, u32[]{:S(2)}) collective-permute-start(bf16[1024,192]{1,0:T(8,128)(2,1)} %copy-done.12), channel_id=1, source_target_pairs={{0,4},{4,8},{8,12},{12,16},{16,20},{20,24},{24,28},{1,5},{5,9},{9,... | collective-permute-start | bytes 1179656 | tf_op jit(solution)/shard_map/ppermute | solution.py:33
  108.8 19.9 %layer_dense.1 = (bf16[256,768]{1,0:T(8,128)(2,1)}, f32[256,768]{1,0:T(8,128)S(1)}, bf16[256,192]{1,0:T(8,128)(2,1)S(1)}, bf16[256,192]{1,0:T(8,128)(2,1)S(1)}, ...) custom-call(s32[4]{0:T(128)S(1)} %pad_add_fusion.2.place_ref, ...), custom_call_target="tpu_custom_call" | custom-call | flops 14495514624 | bytes 25165824 | tf_op jit(solution)/shard_map/layer_dense/pallas_call | solution.py:646
  142.9 8.8 %collective-permute-start.25 = (bf16[1024,256]{1,0:T(8,128)(2,1)S(1)}, bf16[1024,256]{1,0:T(8,128)(2,1)S(1)}, u32[]{:S(2)}, u32[]{:S(2)}) collective-permute-start(bf16[1024,256]{1,0:T(8,128)(2,1)S(1)} %layer_gather.1.grad_ref.rest_11_), channel_id=1, source_target_pairs={{0,8},{4,12},{8,16},{12,20},{16,24},{20,28},{1,9},{5,13},{9,17},{1... | collective-permute-start | bytes 1572872 | tf_op jit(solution)/shard_map/ppermute | solution.py:33
  155.9 13.3 %attention_queries.1.query_ref = bf16[1024,192]{1,0:T(8,128)(2,1)S(1)} custom-call(s32[20]{0:T(128)S(1)} %copy-done.11, bf16[1024,192]{1,0:T(8,128)(2,1)S(1)} %copy-done.13, s32[8,1024]{1,0:T(8,128)S(1)} %copy-done.10, bf16[1024,256]{1,0:T(8,128)(2,1)S(1)} %layer_gather.1.grad_ref.rest_11_, f32[1024,192]{1,0:T(8,128)S(1)} %copy-done, ...), custom_call_target="tpu_custom_call" | custom-call | flops 2717908992 | bytes 6291456 | tf_op jit(solution)/shard_map/attention_queries/pallas_call | solution.py:235
  169.2 6.4 %collective-permute-done.26.rest_10_ = bf16[1024,256]{1,0:T(8,128)(2,1)S(1)} collective-permute-done((bf16[1024,256]{1,0:T(8,128)(2,1)S(1)}, bf16[1024,256]{1,0:T(8,128)(2,1)S(1)}, u32[]{:S(2)}, u32[]{:S(2)}) %collective-permute-start.26) | collective-permute-done | bytes 524320 | tf_op jit(solution)/shard_map/ppermute | solution.py:33
  175.6 5.7 %collective-permute-done.28.rest_13_ = bf16[1024,256]{1,0:T(8,128)(2,1)S(1)} collective-permute-done((bf16[1024,256]{1,0:T(8,128)(2,1)S(1)}, bf16[1024,256]{1,0:T(8,128)(2,1)S(1)}, u32[]{:S(2)}, u32[]{:S(2)}) %collective-permute-start.28) | collective-permute-done | bytes 524320 | tf_op jit(solution)/shard_map/ppermute | solution.py:33
  186.4 23.6 %attention_keys.1 = (bf16[4,192,640]{2,1,0:T(8,128)(2,1)}, bf16[4,256,768]{2,1,0:T(8,128)(2,1)}) custom-call(s32[20]{0:T(128)} %concatenate.110.bounds, bf16[1024,384]{1,0:T(8,128)(2,1)} %get-tuple-element.94.rest_2_.kv_ref, s32[8,5120]{1,0:T(8,128)} %add_add_fusion.span_ref, bf16[1024,768]{1,0:T(8,128)(2,1)} %copy-done.19, bf16[1024,192]{1,0:T(8,128)(2,1)} %copy-done.20, ...), custom_call_target="tpu_custom_call" | custom-call | flops 4529848320 | bytes 12582912 | tf_op jit(solution)/shard_map/attention_keys/pallas_call | solution.py:377
  210.0 8.8 %collective-permute-done.32 = bf16[1024,768]{1,0:T(8,128)(2,1)} collective-permute-done((bf16[1024,768]{1,0:T(8,128)(2,1)}, bf16[1024,768]{1,0:T(8,128)(2,1)}, u32[]{:S(2)}, u32[]{:S(2)}) %collective-permute-start.32) | collective-permute-done | bytes 1572896 | tf_op jit(solution)/shard_map/ppermute | solution.py:27
  220.0 3.7 %collective-permute-start.52 = (bf16[192,768]{1,0:T(8,128)(2,1)S(1)}, bf16[192,768]{1,0:T(8,128)(2,1)S(1)}, u32[]{:S(2)}, u32[]{:S(2)}) collective-permute-start(bf16[192,768]{1,0:T(8,128)(2,1)S(1)} %get-tuple-element.192), channel_id=1, source_target_pairs={{0,8},{4,12},{8,0},{12,4},{16,24},{20,28},{24,16},{28,20},{1,9},{5... | collective-permute-start | bytes 884744 | tf_op jit(solution)/shard_map/ppermute | solution.py:27
  224.9 3.7 %collective-permute-done.52 = bf16[192,768]{1,0:T(8,128)(2,1)S(1)} collective-permute-done((bf16[192,768]{1,0:T(8,128)(2,1)S(1)}, bf16[192,768]{1,0:T(8,128)(2,1)S(1)}, u32[]{:S(2)}, u32[]{:S(2)}) %collective-permute-start.52) | collective-permute-done | bytes 294944 | tf_op jit(solution)/shard_map/ppermute | solution.py:27
  233.5 5.3 %collective-permute-done.53 = bf16[96,768]{1,0:T(8,128)(2,1)S(1)} collective-permute-done((bf16[96,768]{1,0:T(8,128)(2,1)S(1)}, bf16[96,768]{1,0:T(8,128)(2,1)S(1)}, u32[]{:S(2)}, u32[]{:S(2)}) %collective-permute-start.53) | collective-permute-done | bytes 147488 | tf_op jit(solution)/shard_map/ppermute | solution.py:27
  246.8 5.2 %collective-permute-done.36 = bf16[4,48,640]{2,1,0:T(8,128)(2,1)S(1)} collective-permute-done((bf16[4,48,640]{2,1,0:T(8,128)(2,1)}, bf16[4,48,640]{2,1,0:T(8,128)(2,1)S(1)}, u32[]{:S(2)}, u32[]{:S(2)}) %collective-permute-start.36) | collective-permute-done | bytes 245792 | tf_op jit(solution)/shard_map/ppermute | solution.py:27
  266.3 6.4 %collective-permute-done.41 = bf16[4,24,640]{2,1,0:T(8,128)(2,1)S(1)} collective-permute-done((bf16[4,24,640]{2,1,0:T(8,128)(2,1)S(1)}, bf16[4,24,640]{2,1,0:T(8,128)(2,1)S(1)}, u32[]{:S(2)}, u32[]{:S(2)}) %collective-permute-start.41) | collective-permute-done | bytes 122912 | tf_op jit(solution)/shard_map/ppermute | solution.py:27
  276.5 8.5 %collective-permute-done.46 = bf16[128,768]{1,0:T(8,128)(2,1)S(1)} collective-permute-done((bf16[128,768]{1,0:T(8,128)(2,1)S(1)}, bf16[128,768]{1,0:T(8,128)(2,1)S(1)}, u32[]{:S(2)}, u32[]{:S(2)}) %collective-permute-start.46) | collective-permute-done | bytes 196640 | tf_op jit(solution)/shard_map/ppermute | solution.py:27
  288.2 6.6 %collective-permute-done.47 = bf16[128,768]{1,0:T(8,128)(2,1)S(1)} collective-permute-done((bf16[128,768]{1,0:T(8,128)(2,1)S(1)}, bf16[128,768]{1,0:T(8,128)(2,1)S(1)}, u32[]{:S(2)}, u32[]{:S(2)}) %collective-permute-start.47) | collective-permute-done | bytes 196640 | tf_op jit(solution)/shard_map/ppermute | solution.py:27
  295.0 5.3 %collective-permute-done.43 = bf16[4,96,640]{2,1,0:T(8,128)(2,1)S(1)} collective-permute-done((bf16[4,96,640]{2,1,0:T(8,128)(2,1)S(1)}, bf16[4,96,640]{2,1,0:T(8,128)(2,1)S(1)}, u32[]{:S(2)}, u32[]{:S(2)}) %collective-permute-start.43) | collective-permute-done | bytes 491552 | tf_op jit(solution)/shard_map/ppermute | solution.py:27
  306.5 6.4 %collective-permute-done.51 = bf16[256,768]{1,0:T(8,128)(2,1)S(1)} collective-permute-done((bf16[256,768]{1,0:T(8,128)(2,1)S(1)}, bf16[256,768]{1,0:T(8,128)(2,1)S(1)}, u32[]{:S(2)}, u32[]{:S(2)}) %collective-permute-start.51) | collective-permute-done | bytes 393248 | tf_op jit(solution)/shard_map/ppermute | solution.py:27
  (295 shorter events, 123.9 us)
Async XLA Ops:
  0.7 22.2 %collective-permute-start.1 = (bf16[256,768]{1,0:T(8,128)(2,1)}, bf16[256,768]{1,0:T(8,128)(2,1)S(1)}, u32[]{:S(2)}, u32[]{:S(2)}) collective-permute-start(bf16[256,768]{1,0:T(8,128)(2,1)} %refs_4_.1), channel_id=1, source_target_pairs={{0,2},{1,3},{2,0},{3,1},{4,6},{5,7},{6,4},{7,5},{8,10},{9,11},{10,... | collective-permute-start | bytes 1179656 | tf_op jit(solution)/shard_map/ppermute | solution.py:27
  3.7 22.3 %collective-permute-start = (bf16[256,768]{1,0:T(8,128)(2,1)}, bf16[256,768]{1,0:T(8,128)(2,1)S(1)}, u32[]{:S(2)}, u32[]{:S(2)}) collective-permute-start(bf16[256,768]{1,0:T(8,128)(2,1)} %refs_4_.1), channel_id=1, source_target_pairs={{0,1},{1,0},{2,3},{3,2},{4,5},{5,4},{6,7},{7,6},{8,9},{9,8},{10,11... | collective-permute-start | bytes 1179656 | tf_op jit(solution)/shard_map/ppermute | solution.py:27
  7.5 18.3 %collective-permute-start.3 = (bf16[192,576]{1,0:T(8,128)(2,1)}, bf16[192,576]{1,0:T(8,128)(2,1)S(1)}, u32[]{:S(2)}, u32[]{:S(2)}) collective-permute-start(bf16[192,576]{1,0:T(8,128)(2,1)} %pad_maximum_fusion.8), channel_id=1, source_target_pairs={{0,1},{1,0},{2,3},{3,2},{4,5},{5,4},{6,7},{7,6},{8,9},{9,8},{10,11... | collective-permute-start | bytes 663560 | tf_op jit(solution)/shard_map/ppermute | solution.py:27
  25.9 62.9 %collective-permute-start.13 = (bf16[1744,768]{1,0:T(8,128)(2,1)}, bf16[1744,768]{1,0:T(8,128)(2,1)}, u32[]{:S(2)}, u32[]{:S(2)}) collective-permute-start(bf16[1744,768]{1,0:T(8,128)(2,1)} %slice_dynamic-update-slice_fusion.refs_6_), channel_id=1, source_target_pairs={{0,2},{1,3},{2,0},{3,1},{4,6},{5,7},{6,4},{7,5},{8,10},{9,11},{10,... | collective-permute-start | bytes 8036360 | tf_op jit(solution)/shard_map/ppermute | solution.py:27
  31.3 20.9 %collective-permute-start.6 = (bf16[1024,384]{1,0:T(8,128)(2,1)}, bf16[1024,384]{1,0:T(8,128)(2,1)S(1)}, u32[]{:S(2)}, u32[]{:S(2)}) collective-permute-start(bf16[1024,384]{1,0:T(8,128)(2,1)} %get-tuple-element.94.rest_2_.kv_ref), channel_id=1, source_target_pairs={{0,8},{4,12},{8,16},{12,20},{16,24},{20,28},{1,9},{5,13},{9,17},{1... | collective-permute-start | bytes 2359304 | tf_op jit(solution)/shard_map/ppermute | solution.py:33
  35.2 21.0 %collective-permute-start.7 = (bf16[1024,384]{1,0:T(8,128)(2,1)}, bf16[1024,384]{1,0:T(8,128)(2,1)S(1)}, u32[]{:S(2)}, u32[]{:S(2)}) collective-permute-start(bf16[1024,384]{1,0:T(8,128)(2,1)} %get-tuple-element.94.rest_2_.kv_ref), channel_id=1, source_target_pairs={{8,0},{12,4},{16,8},{20,12},{24,16},{28,20},{9,1},{13,5},{17,9},{2... | collective-permute-start | bytes 2359304 | tf_op jit(solution)/shard_map/ppermute | solution.py:33
  37.4 20.4 %collective-permute-start.8 = (bf16[1024,384]{1,0:T(8,128)(2,1)}, bf16[1024,384]{1,0:T(8,128)(2,1)S(1)}, u32[]{:S(2)}, u32[]{:S(2)}) collective-permute-start(bf16[1024,384]{1,0:T(8,128)(2,1)} %get-tuple-element.94.rest_2_.kv_ref), channel_id=1, source_target_pairs={{0,4},{4,0},{8,12},{12,8},{16,20},{20,16},{24,28},{28,24},{1,5},{5... | collective-permute-start | bytes 2359304 | tf_op jit(solution)/shard_map/ppermute | solution.py:27
  62.1 26.7 %collective-permute-start.11 = (bf16[1024,192]{1,0:T(8,128)(2,1)S(1)}, bf16[1024,192]{1,0:T(8,128)(2,1)}, u32[]{:S(2)}, u32[]{:S(2)}) collective-permute-start(bf16[1024,192]{1,0:T(8,128)(2,1)S(1)} %get-tuple-element.126.q_ref.rest_6_), channel_id=1, source_target_pairs={{0,8},{4,12},{8,16},{12,20},{16,24},{20,28},{1,9},{5,13},{9,17},{1... | collective-permute-start | bytes 1179656 | tf_op jit(solution)/shard_map/ppermute | solution.py:33
  65.8 23.0 %collective-permute-start.12 = (bf16[1024,192]{1,0:T(8,128)(2,1)S(1)}, bf16[1024,192]{1,0:T(8,128)(2,1)}, u32[]{:S(2)}, u32[]{:S(2)}) collective-permute-start(bf16[1024,192]{1,0:T(8,128)(2,1)S(1)} %get-tuple-element.126.q_ref.rest_6_), channel_id=1, source_target_pairs={{8,0},{12,4},{16,8},{20,12},{24,16},{28,20},{9,1},{13,5},{17,9},{2... | collective-permute-start | bytes 1179656 | tf_op jit(solution)/shard_map/ppermute | solution.py:33
  67.1 39.3 %collective-permute-start.17 = (bf16[1744,768]{1,0:T(8,128)(2,1)}, bf16[1744,768]{1,0:T(8,128)(2,1)}, u32[]{:S(2)}, u32[]{:S(2)}) collective-permute-start(bf16[1744,768]{1,0:T(8,128)(2,1)} %slice_dynamic-update-slice_fusion.refs_6_), channel_id=1, source_target_pairs={{0,1},{1,0},{2,3},{3,2},{4,5},{5,4},{6,7},{7,6},{8,9},{9,8},{10,11... | collective-permute-start | bytes 8036360 | tf_op jit(solution)/shard_map/ppermute | solution.py:27
  88.8 17.6 %collective-permute-start.18 = (bf16[1744,768]{1,0:T(8,128)(2,1)}, bf16[1744,768]{1,0:T(8,128)(2,1)S(1)}, u32[]{:S(2)}, u32[]{:S(2)}) collective-permute-start(bf16[1744,768]{1,0:T(8,128)(2,1)} %collective-permute-done.13.refs_8_), channel_id=1, source_target_pairs={{0,1},{1,0},{2,3},{3,2},{4,5},{5,4},{6,7},{7,6},{8,9},{9,8},{10,11... | collective-permute-start | bytes 8036360 | tf_op jit(solution)/shard_map/ppermute | solution.py:27
  97.1 31.7 %collective-permute-start.19 = (bf16[1024,192]{1,0:T(8,128)(2,1)}, bf16[1024,192]{1,0:T(8,128)(2,1)S(1)}, u32[]{:S(2)}, u32[]{:S(2)}) collective-permute-start(bf16[1024,192]{1,0:T(8,128)(2,1)} %copy-done.12), channel_id=1, source_target_pairs={{0,4},{4,8},{8,12},{12,16},{16,20},{20,24},{24,28},{1,5},{5,9},{9,... | collective-permute-start | bytes 1179656 | tf_op jit(solution)/shard_map/ppermute | solution.py:33
  104.9 23.8 %collective-permute-start.20 = (bf16[1024,192]{1,0:T(8,128)(2,1)}, bf16[1024,192]{1,0:T(8,128)(2,1)S(1)}, u32[]{:S(2)}, u32[]{:S(2)}) collective-permute-start(bf16[1024,192]{1,0:T(8,128)(2,1)} %copy-done.12), channel_id=1, source_target_pairs={{4,0},{8,4},{12,8},{16,12},{20,16},{24,20},{28,24},{5,1},{9,5},{13... | collective-permute-start | bytes 1179656 | tf_op jit(solution)/shard_map/ppermute | solution.py:33
  138.9 30.3 %collective-permute-start.30 = (bf16[768,768]{1,0:T(8,128)(2,1)S(1)}, bf16[768,768]{1,0:T(8,128)(2,1)S(1)}, u32[]{:S(2)}, u32[]{:S(2)}) collective-permute-start(bf16[768,768]{1,0:T(8,128)(2,1)S(1)} %get-tuple-element.179), channel_id=1, source_target_pairs={{0,2},{1,3},{2,0},{3,1},{4,6},{5,7},{6,4},{7,5},{8,10},{9,11},{10,... | collective-permute-start | bytes 3538952 | tf_op jit(solution)/shard_map/ppermute | solution.py:27
  142.9 26.3 %collective-permute-start.25 = (bf16[1024,256]{1,0:T(8,128)(2,1)S(1)}, bf16[1024,256]{1,0:T(8,128)(2,1)S(1)}, u32[]{:S(2)}, u32[]{:S(2)}) collective-permute-start(bf16[1024,256]{1,0:T(8,128)(2,1)S(1)} %layer_gather.1.grad_ref.rest_11_), channel_id=1, source_target_pairs={{0,8},{4,12},{8,16},{12,20},{16,24},{20,28},{1,9},{5,13},{9,17},{1... | collective-permute-start | bytes 1572872 | tf_op jit(solution)/shard_map/ppermute | solution.py:33
  151.6 23.9 %collective-permute-start.26 = (bf16[1024,256]{1,0:T(8,128)(2,1)S(1)}, bf16[1024,256]{1,0:T(8,128)(2,1)S(1)}, u32[]{:S(2)}, u32[]{:S(2)}) collective-permute-start(bf16[1024,256]{1,0:T(8,128)(2,1)S(1)} %layer_gather.1.grad_ref.rest_11_), channel_id=1, source_target_pairs={{0,4},{4,8},{8,12},{12,16},{16,20},{20,24},{24,28},{1,5},{5,9},{9,... | collective-permute-start | bytes 1572872 | tf_op jit(solution)/shard_map/ppermute | solution.py:33
  153.0 22.6 %collective-permute-start.27 = (bf16[1024,256]{1,0:T(8,128)(2,1)S(1)}, bf16[1024,256]{1,0:T(8,128)(2,1)S(1)}, u32[]{:S(2)}, u32[]{:S(2)}) collective-permute-start(bf16[1024,256]{1,0:T(8,128)(2,1)S(1)} %layer_gather.1.grad_ref.rest_11_), channel_id=1, source_target_pairs={{4,0},{8,4},{12,8},{16,12},{20,16},{24,20},{28,24},{5,1},{9,5},{13... | collective-permute-start | bytes 1572872 | tf_op jit(solution)/shard_map/ppermute | solution.py:33
  154.3 27.0 %collective-permute-start.28 = (bf16[1024,256]{1,0:T(8,128)(2,1)S(1)}, bf16[1024,256]{1,0:T(8,128)(2,1)S(1)}, u32[]{:S(2)}, u32[]{:S(2)}) collective-permute-start(bf16[1024,256]{1,0:T(8,128)(2,1)S(1)} %layer_gather.1.grad_ref.rest_11_), channel_id=1, source_target_pairs={{8,0},{12,4},{16,8},{20,12},{24,16},{28,20},{9,1},{13,5},{17,9},{2... | collective-permute-start | bytes 1572872 | tf_op jit(solution)/shard_map/ppermute | solution.py:33
  183.2 35.6 %collective-permute-start.32 = (bf16[1024,768]{1,0:T(8,128)(2,1)}, bf16[1024,768]{1,0:T(8,128)(2,1)}, u32[]{:S(2)}, u32[]{:S(2)}) collective-permute-start(bf16[1024,768]{1,0:T(8,128)(2,1)} %get-tuple-element.177), channel_id=1, source_target_pairs={{0,2},{1,3},{2,0},{3,1},{4,6},{5,7},{6,4},{7,5},{8,10},{9,11},{10,... | collective-permute-start | bytes 4718600 | tf_op jit(solution)/shard_map/ppermute | solution.py:27
  186.3 23.7 %collective-permute-start.31 = (bf16[384,768]{1,0:T(8,128)(2,1)}, bf16[384,768]{1,0:T(8,128)(2,1)}, u32[]{:S(2)}, u32[]{:S(2)}) collective-permute-start(bf16[384,768]{1,0:T(8,128)(2,1)} %get-tuple-element.183), channel_id=1, source_target_pairs={{0,4},{4,0},{8,12},{12,8},{16,20},{20,16},{24,28},{28,24},{1,5},{5... | collective-permute-start | bytes 1769480 | tf_op jit(solution)/shard_map/ppermute | solution.py:27
  233.5 18.9 %collective-permute-start.44 = (bf16[512,768]{1,0:T(8,128)(2,1)}, bf16[512,768]{1,0:T(8,128)(2,1)}, u32[]{:S(2)}, u32[]{:S(2)}) collective-permute-start(bf16[512,768]{1,0:T(8,128)(2,1)} %get-tuple-element.182), channel_id=1, source_target_pairs={{0,4},{4,0},{8,12},{12,8},{16,20},{20,16},{24,28},{28,24},{1,5},{5... | collective-permute-start | bytes 2359304 | tf_op jit(solution)/shard_map/ppermute | solution.py:27
  246.7 19.3 %collective-permute-start.55 = (bf16[192,768]{1,0:T(8,128)(2,1)S(1)}, bf16[192,768]{1,0:T(8,128)(2,1)S(1)}, u32[]{:S(2)}, u32[]{:S(2)}) collective-permute-start(bf16[192,768]{1,0:T(8,128)(2,1)S(1)} %maximum_select_fusion.5), channel_id=1, source_target_pairs={{0,8},{4,12},{8,0},{12,4},{16,24},{20,28},{24,16},{28,20},{1,9},{5... | collective-permute-start | bytes 884744 | tf_op jit(solution)/shard_map/ppermute | solution.py:27
  254.1 18.8 %collective-permute-start.45 = (bf16[256,768]{1,0:T(8,128)(2,1)S(1)}, bf16[256,768]{1,0:T(8,128)(2,1)S(1)}, u32[]{:S(2)}, u32[]{:S(2)}) collective-permute-start(bf16[256,768]{1,0:T(8,128)(2,1)S(1)} %get-tuple-element.186), channel_id=1, source_target_pairs={{0,8},{4,12},{8,0},{12,4},{16,24},{20,28},{24,16},{28,20},{1,9},{5... | collective-permute-start | bytes 1179656 | tf_op jit(solution)/shard_map/ppermute | solution.py:27
  266.3 20.3 %collective-permute-start.56 = (bf16[384,768]{1,0:T(8,128)(2,1)S(1)}, bf16[384,768]{1,0:T(8,128)(2,1)S(1)}, u32[]{:S(2)}, u32[]{:S(2)}) collective-permute-start(bf16[384,768]{1,0:T(8,128)(2,1)S(1)} %maximum_select_fusion.2), channel_id=1, source_target_pairs={{0,4},{4,0},{8,12},{12,8},{16,20},{20,16},{24,28},{28,24},{1,5},{5... | collective-permute-start | bytes 1769480 | tf_op jit(solution)/shard_map/ppermute | solution.py:27
  (84 other events, 956.2 us)

commit v10 on v9

--- a/solution.py
+++ b/solution.py
@@ -669,7 +669,7 @@
             pltpu.SemaphoreType.DMA((groups + 3, groups)),
             pltpu.SemaphoreType.DMA((groups + 2, groups)),
         ],
-        compiler_params=pltpu.CompilerParams(vmem_limit_bytes=48 * 2**20),
+        compiler_params=pltpu.CompilerParams(vmem_limit_bytes=40 * 2**20),
         cost_estimate=pl.CostEstimate(
             flops=24 * rows * width * width * groups,
             bytes_accessed=24 * 2**20,

time: 316 us -> 320 us (1.013); the launches traced: 319 us -> 318 us
  waiting for transfers between devices: 104 us -> 108 us
  starting transfers between devices: 72.4 us -> 68.9 us
    ppermute x10, starting transfers between devices: 32.4 us -> 28.3 us  [shifted(): return lax.ppermute(block, axis, route)]
    ppermute x10, waiting for transfers between devices: 23 us -> 26.6 us  [shifted(): return lax.ppermute(block, axis, route)]
    unnamed x108 -> x94, local copies, waits for them, and re-layouts: 13.2 us -> 11.1 us
  transfers between devices with their start and end apart: 57 -> 57, of which waited for: 26 -> 27; matrix products, arithmetic and copies ran while one was open for 14% -> 14% of each run, Pallas kernels for 25% -> 25%
where the time goes in v10:
time: 320 us; the launch traced here: 318 us
  waiting for transfers between devices  108 us (34%)
  Pallas kernels  78.2 us (24%)
  starting transfers between devices  68.9 us (22%)
  other arithmetic  34.5 us (11%)
  local copies, waits for them, and re-layouts  23 us (7%)
  between operations  4.87 us (2%)
    ppermute x46, waiting for transfers between devices, swapped(): return lax.ppermute(block, axis, [(i, i ^ bit) for i in range(count)])  78.4 us
    ppermute x46, starting transfers between devices, swapped(): return lax.ppermute(block, axis, [(i, i ^ bit) for i in range(count)])  37.2 us
    ppermute x10, starting transfers between devices, shifted(): return lax.ppermute(block, axis, route)  28.3 us
    ppermute x10, waiting for transfers between devices, shifted(): return lax.ppermute(block, axis, route)  26.6 us
    pallas_call x1, Pallas kernels, attention_keys(): pl.pallas_call(functools.partial(key_kernel, count // 2), grid_spec=pltpu...  22.1 us
    pallas_call x1, Pallas kernels, dense(): pl.pallas_call(dense_kernel, in_specs=[pl.BlockSpec(memory_space=pltpu.SM...  20.9 us
    pallas_call x1, Pallas kernels, attention_forward(): pl.pallas_call(forward_kernel, grid_spec=pltpu.PrefetchScalarGridSpec(num...  15.8 us
    convert_element_type x14, other arithmetic, both(): return (left.astype(f32) + right.astype(f32)).astype(bf16)  13.5 us
  transfers between devices with their start and end apart: 57, of which 27 were waited for; matrix products, arithmetic and copies ran while one was open for 14% of the time, Pallas kernels for 25%

profile of v10, /device:TPU:0, one launch (start us, length us, event | category | flops | bytes accessed | tf_op | source)
XLA Modules:
  0.0 317.7 jit_solution(14985611022101254803)
XLA Ops:
  24.3 4.8 %layer_projection.1 = (bf16[1024,768]{1,0:T(8,128)(2,1)S(1)}, bf16[1024,192]{1,0:T(8,128)(2,1)S(1)}, bf16[1024,384]{1,0:T(8,128)(2,1)}) custom-call(s32[4]{0:T(128)S(1)} %pad_add_fusion.2.place_ref, bf16[256,768]{1,0:T(8,128)(2,1)S(1)} %copy-done.10, bf16[256,768]{1,0:T(8,128)(2,1)} %collective-permute-done.near, ...), custom_call_target="tpu_custom_call" | custom-call | flops 905969664 | bytes 5242880 | tf_op jit(solution)/shard_map/layer_projection/pallas_call | solution.py:436
  31.0 4.6 %collective-permute-start.6 = (bf16[1024,384]{1,0:T(8,128)(2,1)}, bf16[1024,384]{1,0:T(8,128)(2,1)}, u32[]{:S(2)}, u32[]{:S(2)}) collective-permute-start(bf16[1024,384]{1,0:T(8,128)(2,1)} %get-tuple-element.94.rest_2_.kv_ref), channel_id=1, source_target_pairs={{0,8},{4,12},{8,16},{12,20},{16,24},{20,28},{1,9},{5,13},{9,17},{1... | collective-permute-start | bytes 2359304 | tf_op jit(solution)/shard_map/ppermute | solution.py:33
  45.7 6.7 %collective-permute-done.6.rest_0_ = bf16[1024,384]{1,0:T(8,128)(2,1)} collective-permute-done((bf16[1024,384]{1,0:T(8,128)(2,1)}, bf16[1024,384]{1,0:T(8,128)(2,1)}, u32[]{:S(2)}, u32[]{:S(2)}) %collective-permute-start.6) | collective-permute-done | bytes 786464 | tf_op jit(solution)/shard_map/ppermute | solution.py:33
  52.4 5.0 %collective-permute-done.7.rest_1_ = bf16[1024,384]{1,0:T(8,128)(2,1)} collective-permute-done((bf16[1024,384]{1,0:T(8,128)(2,1)}, bf16[1024,384]{1,0:T(8,128)(2,1)}, u32[]{:S(2)}, u32[]{:S(2)}) %collective-permute-start.7) | collective-permute-done | bytes 786464 | tf_op jit(solution)/shard_map/ppermute | solution.py:33
  63.5 3.7 %collective-permute-start.11 = (bf16[1024,192]{1,0:T(8,128)(2,1)}, bf16[1024,192]{1,0:T(8,128)(2,1)}, u32[]{:S(2)}, u32[]{:S(2)}) collective-permute-start(bf16[1024,192]{1,0:T(8,128)(2,1)} %copy-done.8), channel_id=1, source_target_pairs={{0,8},{4,12},{8,16},{12,20},{16,24},{20,28},{1,9},{5,13},{9,17},{1... | collective-permute-start | bytes 1179656 | tf_op jit(solution)/shard_map/ppermute | solution.py:33
  72.3 15.8 %attention_forward.1 = (bf16[256,192]{1,0:T(8,128)(2,1)}, bf16[256,192]{1,0:T(8,128)(2,1)}, bf16[256,192]{1,0:T(8,128)(2,1)}, bf16[256,192]{1,0:T(8,128)(2,1)}, ...) custom-call(s32[20]{0:T(128)} %concatenate.110.bounds, bf16[1024,192]{1,0:T(8,128)(2,1)} %copy-done.8, ...), custom_call_target="tpu_custom_call" | custom-call | flops 1811939328 | bytes 6291456 | tf_op jit(solution)/shard_map/attention_forward/pallas_call | solution.py:148
  96.4 5.9 %collective-permute-start.19 = (bf16[1024,192]{1,0:T(8,128)(2,1)S(1)}, bf16[1024,192]{1,0:T(8,128)(2,1)S(1)}, u32[]{:S(2)}, u32[]{:S(2)}) collective-permute-start(bf16[1024,192]{1,0:T(8,128)(2,1)S(1)} %copy-done.9), channel_id=1, source_target_pairs={{0,4},{4,8},{8,12},{12,16},{16,20},{20,24},{24,28},{1,5},{5,9},{9,... | collective-permute-start | bytes 1179656 | tf_op jit(solution)/shard_map/ppermute | solution.py:33
  108.2 20.9 %layer_dense.1 = (bf16[256,768]{1,0:T(8,128)(2,1)}, f32[256,768]{1,0:T(8,128)S(1)}, bf16[256,192]{1,0:T(8,128)(2,1)S(1)}, bf16[256,192]{1,0:T(8,128)(2,1)S(1)}, ...) custom-call(s32[4]{0:T(128)S(1)} %pad_add_fusion.2.place_ref, ...), custom_call_target="tpu_custom_call" | custom-call | flops 14495514624 | bytes 25165824 | tf_op jit(solution)/shard_map/layer_dense/pallas_call | solution.py:646
  131.5 5.0 %collective-permute-done.21.p1 = bf16[256,192]{1,0:T(8,128)(2,1)S(1)} collective-permute-done((bf16[256,192]{1,0:T(8,128)(2,1)S(1)}, bf16[256,192]{1,0:T(8,128)(2,1)S(1)}, u32[]{:S(2)}, u32[]{:S(2)}) %collective-permute-start.21) | collective-permute-done | bytes 98336 | tf_op jit(solution)/shard_map/ppermute | solution.py:27
  142.7 4.0 %collective-permute-start.25 = (bf16[1024,256]{1,0:T(8,128)(2,1)S(1)}, bf16[1024,256]{1,0:T(8,128)(2,1)S(1)}, u32[]{:S(2)}, u32[]{:S(2)}) collective-permute-start(bf16[1024,256]{1,0:T(8,128)(2,1)S(1)} %layer_gather.1.grad_ref.rest_11_), channel_id=1, source_target_pairs={{0,8},{4,12},{8,16},{12,20},{16,24},{20,28},{1,9},{5,13},{9,17},{1... | collective-permute-start | bytes 1572872 | tf_op jit(solution)/shard_map/ppermute | solution.py:33
  152.9 12.2 %attention_queries.1.query_ref = bf16[1024,192]{1,0:T(8,128)(2,1)S(1)} custom-call(s32[20]{0:T(128)S(1)} %copy-done.7, bf16[1024,192]{1,0:T(8,128)(2,1)S(1)} %copy-done.9, s32[8,1024]{1,0:T(8,128)S(1)} %copy-done.6, bf16[1024,256]{1,0:T(8,128)(2,1)S(1)} %layer_gather.1.grad_ref.rest_11_, f32[1024,192]{1,0:T(8,128)S(1)} %copy-done, f32[8,1024]{1,0:T(8,128)S(1)} %copy-done.16, ...), custom_call_target="tpu_custom_call" | custom-call | flops 2717908992 | bytes 6291456 | tf_op jit(solution)/shard_map/attention_queries/pallas_call | solution.py:235
  167.8 5.0 %collective-permute-done.26.rest_10_ = bf16[1024,256]{1,0:T(8,128)(2,1)S(1)} collective-permute-done((bf16[1024,256]{1,0:T(8,128)(2,1)S(1)}, bf16[1024,256]{1,0:T(8,128)(2,1)S(1)}, u32[]{:S(2)}, u32[]{:S(2)}) %collective-permute-start.26) | collective-permute-done | bytes 524320 | tf_op jit(solution)/shard_map/ppermute | solution.py:33
  172.7 9.9 %collective-permute-done.28.rest_13_ = bf16[1024,256]{1,0:T(8,128)(2,1)S(1)} collective-permute-done((bf16[1024,256]{1,0:T(8,128)(2,1)S(1)}, bf16[1024,256]{1,0:T(8,128)(2,1)S(1)}, u32[]{:S(2)}, u32[]{:S(2)}) %collective-permute-start.28) | collective-permute-done | bytes 524320 | tf_op jit(solution)/shard_map/ppermute | solution.py:33
  187.7 22.1 %attention_keys.1 = (bf16[4,192,640]{2,1,0:T(8,128)(2,1)}, bf16[4,256,768]{2,1,0:T(8,128)(2,1)}) custom-call(s32[20]{0:T(128)} %concatenate.110.bounds, bf16[1024,384]{1,0:T(8,128)(2,1)} %get-tuple-element.94.rest_2_.kv_ref, s32[8,5120]{1,0:T(8,128)} %add_add_fusion.span_ref, bf16[1024,768]{1,0:T(8,128)(2,1)} %copy-done.13, bf16[1024,192]{1,0:T(8,128)(2,1)} %copy-done.14, ...), custom_call_target="tpu_custom_call" | custom-call | flops 4529848320 | bytes 12582912 | tf_op jit(solution)/shard_map/attention_keys/pallas_call | solution.py:377
  209.8 10.8 %collective-permute-done.32 = bf16[1024,768]{1,0:T(8,128)(2,1)} collective-permute-done((bf16[1024,768]{1,0:T(8,128)(2,1)}, bf16[1024,768]{1,0:T(8,128)(2,1)}, u32[]{:S(2)}, u32[]{:S(2)}) %collective-permute-start.32) | collective-permute-done | bytes 1572896 | tf_op jit(solution)/shard_map/ppermute | solution.py:27
  226.4 3.7 %collective-permute-done.52 = bf16[192,768]{1,0:T(8,128)(2,1)S(1)} collective-permute-done((bf16[192,768]{1,0:T(8,128)(2,1)S(1)}, bf16[192,768]{1,0:T(8,128)(2,1)S(1)}, u32[]{:S(2)}, u32[]{:S(2)}) %collective-permute-start.52) | collective-permute-done | bytes 294944 | tf_op jit(solution)/shard_map/ppermute | solution.py:27
  235.0 5.3 %collective-permute-done.53 = bf16[96,768]{1,0:T(8,128)(2,1)S(1)} collective-permute-done((bf16[96,768]{1,0:T(8,128)(2,1)S(1)}, bf16[96,768]{1,0:T(8,128)(2,1)S(1)}, u32[]{:S(2)}, u32[]{:S(2)}) %collective-permute-start.53) | collective-permute-done | bytes 147488 | tf_op jit(solution)/shard_map/ppermute | solution.py:27
  247.1 5.3 %collective-permute-done.36 = bf16[4,48,640]{2,1,0:T(8,128)(2,1)S(1)} collective-permute-done((bf16[4,48,640]{2,1,0:T(8,128)(2,1)}, bf16[4,48,640]{2,1,0:T(8,128)(2,1)S(1)}, u32[]{:S(2)}, u32[]{:S(2)}) %collective-permute-start.36) | collective-permute-done | bytes 245792 | tf_op jit(solution)/shard_map/ppermute | solution.py:27
  266.2 6.3 %collective-permute-done.41 = bf16[4,24,640]{2,1,0:T(8,128)(2,1)S(1)} collective-permute-done((bf16[4,24,640]{2,1,0:T(8,128)(2,1)S(1)}, bf16[4,24,640]{2,1,0:T(8,128)(2,1)S(1)}, u32[]{:S(2)}, u32[]{:S(2)}) %collective-permute-start.41) | collective-permute-done | bytes 122912 | tf_op jit(solution)/shard_map/ppermute | solution.py:27
  277.8 4.7 %collective-permute-done.46 = bf16[128,768]{1,0:T(8,128)(2,1)S(1)} collective-permute-done((bf16[128,768]{1,0:T(8,128)(2,1)S(1)}, bf16[128,768]{1,0:T(8,128)(2,1)S(1)}, u32[]{:S(2)}, u32[]{:S(2)}) %collective-permute-start.46) | collective-permute-done | bytes 196640 | tf_op jit(solution)/shard_map/ppermute | solution.py:27
  282.5 3.5 %collective-permute-start.47 = (bf16[128,768]{1,0:T(8,128)(2,1)S(1)}, bf16[128,768]{1,0:T(8,128)(2,1)S(1)}, u32[]{:S(2)}, u32[]{:S(2)}) collective-permute-start(bf16[128,768]{1,0:T(8,128)(2,1)S(1)} %add_convert_fusion.16), channel_id=1, source_target_pairs={{0,16},{4,20},{8,24},{12,28},{16,0},{20,4},{24,8},{28,12},{1,17},{... | collective-permute-start | bytes 589832 | tf_op jit(solution)/shard_map/ppermute | solution.py:27
  287.9 6.5 %collective-permute-done.47 = bf16[128,768]{1,0:T(8,128)(2,1)S(1)} collective-permute-done((bf16[128,768]{1,0:T(8,128)(2,1)S(1)}, bf16[128,768]{1,0:T(8,128)(2,1)S(1)}, u32[]{:S(2)}, u32[]{:S(2)}) %collective-permute-start.47) | collective-permute-done | bytes 196640 | tf_op jit(solution)/shard_map/ppermute | solution.py:27
  294.6 5.6 %collective-permute-done.43 = bf16[4,96,640]{2,1,0:T(8,128)(2,1)S(1)} collective-permute-done((bf16[4,96,640]{2,1,0:T(8,128)(2,1)S(1)}, bf16[4,96,640]{2,1,0:T(8,128)(2,1)S(1)}, u32[]{:S(2)}, u32[]{:S(2)}) %collective-permute-start.43) | collective-permute-done | bytes 491552 | tf_op jit(solution)/shard_map/ppermute | solution.py:27
  306.0 5.4 %collective-permute-done.51 = bf16[256,768]{1,0:T(8,128)(2,1)S(1)} collective-permute-done((bf16[256,768]{1,0:T(8,128)(2,1)S(1)}, bf16[256,768]{1,0:T(8,128)(2,1)S(1)}, u32[]{:S(2)}, u32[]{:S(2)}) %collective-permute-start.51) | collective-permute-done | bytes 393248 | tf_op jit(solution)/shard_map/ppermute | solution.py:27
  (281 shorter events, 130.2 us)
Async XLA Ops:
  0.7 19.9 %collective-permute-start.1 = (bf16[256,768]{1,0:T(8,128)(2,1)}, bf16[256,768]{1,0:T(8,128)(2,1)S(1)}, u32[]{:S(2)}, u32[]{:S(2)}) collective-permute-start(bf16[256,768]{1,0:T(8,128)(2,1)} %refs_4_.1), channel_id=1, source_target_pairs={{0,2},{1,3},{2,0},{3,1},{4,6},{5,7},{6,4},{7,5},{8,10},{9,11},{10,... | collective-permute-start | bytes 1179656 | tf_op jit(solution)/shard_map/ppermute | solution.py:27
  3.7 20.6 %collective-permute-start = (bf16[256,768]{1,0:T(8,128)(2,1)}, bf16[256,768]{1,0:T(8,128)(2,1)}, u32[]{:S(2)}, u32[]{:S(2)}) collective-permute-start(bf16[256,768]{1,0:T(8,128)(2,1)} %refs_4_.1), channel_id=1, source_target_pairs={{0,1},{1,0},{2,3},{3,2},{4,5},{5,4},{6,7},{7,6},{8,9},{9,8},{10,11... | collective-permute-start | bytes 1179656 | tf_op jit(solution)/shard_map/ppermute | solution.py:27
  8.8 15.0 %collective-permute-start.3 = (bf16[192,576]{1,0:T(8,128)(2,1)}, bf16[192,576]{1,0:T(8,128)(2,1)}, u32[]{:S(2)}, u32[]{:S(2)}) collective-permute-start(bf16[192,576]{1,0:T(8,128)(2,1)} %pad_maximum_fusion.8), channel_id=1, source_target_pairs={{0,1},{1,0},{2,3},{3,2},{4,5},{5,4},{6,7},{7,6},{8,9},{9,8},{10,11... | collective-permute-start | bytes 663560 | tf_op jit(solution)/shard_map/ppermute | solution.py:27
  23.9 64.3 %collective-permute-start.13 = (bf16[1744,768]{1,0:T(8,128)(2,1)S(1)}, bf16[1744,768]{1,0:T(8,128)(2,1)}, u32[]{:S(2)}, u32[]{:S(2)}) collective-permute-start(bf16[1744,768]{1,0:T(8,128)(2,1)S(1)} %slice_dynamic-update-slice_fusion.refs_6_), channel_id=1, source_target_pairs={{0,2},{1,3},{2,0},{3,1},{4,6},{5,7},{6,4},{7,5},{8,10},{9,11},{10,... | collective-permute-start | bytes 8036360 | tf_op jit(solution)/shard_map/ppermute | solution.py:27
  31.0 21.4 %collective-permute-start.6 = (bf16[1024,384]{1,0:T(8,128)(2,1)}, bf16[1024,384]{1,0:T(8,128)(2,1)}, u32[]{:S(2)}, u32[]{:S(2)}) collective-permute-start(bf16[1024,384]{1,0:T(8,128)(2,1)} %get-tuple-element.94.rest_2_.kv_ref), channel_id=1, source_target_pairs={{0,8},{4,12},{8,16},{12,20},{16,24},{20,28},{1,9},{5,13},{9,17},{1... | collective-permute-start | bytes 2359304 | tf_op jit(solution)/shard_map/ppermute | solution.py:33
  35.6 21.8 %collective-permute-start.7 = (bf16[1024,384]{1,0:T(8,128)(2,1)}, bf16[1024,384]{1,0:T(8,128)(2,1)}, u32[]{:S(2)}, u32[]{:S(2)}) collective-permute-start(bf16[1024,384]{1,0:T(8,128)(2,1)} %get-tuple-element.94.rest_2_.kv_ref), channel_id=1, source_target_pairs={{8,0},{12,4},{16,8},{20,12},{24,16},{28,20},{9,1},{13,5},{17,9},{2... | collective-permute-start | bytes 2359304 | tf_op jit(solution)/shard_map/ppermute | solution.py:33
  37.7 22.4 %collective-permute-start.8 = (bf16[1024,384]{1,0:T(8,128)(2,1)}, bf16[1024,384]{1,0:T(8,128)(2,1)S(1)}, u32[]{:S(2)}, u32[]{:S(2)}) collective-permute-start(bf16[1024,384]{1,0:T(8,128)(2,1)} %get-tuple-element.94.rest_2_.kv_ref), channel_id=1, source_target_pairs={{0,4},{4,0},{8,12},{12,8},{16,20},{20,16},{24,28},{28,24},{1,5},{5... | collective-permute-start | bytes 2359304 | tf_op jit(solution)/shard_map/ppermute | solution.py:27
  63.5 24.6 %collective-permute-start.11 = (bf16[1024,192]{1,0:T(8,128)(2,1)}, bf16[1024,192]{1,0:T(8,128)(2,1)}, u32[]{:S(2)}, u32[]{:S(2)}) collective-permute-start(bf16[1024,192]{1,0:T(8,128)(2,1)} %copy-done.8), channel_id=1, source_target_pairs={{0,8},{4,12},{8,16},{12,20},{16,24},{20,28},{1,9},{5,13},{9,17},{1... | collective-permute-start | bytes 1179656 | tf_op jit(solution)/shard_map/ppermute | solution.py:33
  67.2 21.0 %collective-permute-start.12 = (bf16[1024,192]{1,0:T(8,128)(2,1)}, bf16[1024,192]{1,0:T(8,128)(2,1)}, u32[]{:S(2)}, u32[]{:S(2)}) collective-permute-start(bf16[1024,192]{1,0:T(8,128)(2,1)} %copy-done.8), channel_id=1, source_target_pairs={{8,0},{12,4},{16,8},{20,12},{24,16},{28,20},{9,1},{13,5},{17,9},{2... | collective-permute-start | bytes 1179656 | tf_op jit(solution)/shard_map/ppermute | solution.py:33
  69.1 34.7 %collective-permute-start.17 = (bf16[1744,768]{1,0:T(8,128)(2,1)S(1)}, bf16[1744,768]{1,0:T(8,128)(2,1)}, u32[]{:S(2)}, u32[]{:S(2)}) collective-permute-start(bf16[1744,768]{1,0:T(8,128)(2,1)S(1)} %slice_dynamic-update-slice_fusion.refs_6_), channel_id=1, source_target_pairs={{0,1},{1,0},{2,3},{3,2},{4,5},{5,4},{6,7},{7,6},{8,9},{9,8},{10,11... | collective-permute-start | bytes 8036360 | tf_op jit(solution)/shard_map/ppermute | solution.py:27
  88.2 15.6 %collective-permute-start.18 = (bf16[1744,768]{1,0:T(8,128)(2,1)}, bf16[1744,768]{1,0:T(8,128)(2,1)S(1)}, u32[]{:S(2)}, u32[]{:S(2)}) collective-permute-start(bf16[1744,768]{1,0:T(8,128)(2,1)} %collective-permute-done.13.refs_8_), channel_id=1, source_target_pairs={{0,1},{1,0},{2,3},{3,2},{4,5},{5,4},{6,7},{7,6},{8,9},{9,8},{10,11... | collective-permute-start | bytes 8036360 | tf_op jit(solution)/shard_map/ppermute | solution.py:27
  96.4 32.6 %collective-permute-start.19 = (bf16[1024,192]{1,0:T(8,128)(2,1)S(1)}, bf16[1024,192]{1,0:T(8,128)(2,1)S(1)}, u32[]{:S(2)}, u32[]{:S(2)}) collective-permute-start(bf16[1024,192]{1,0:T(8,128)(2,1)S(1)} %copy-done.9), channel_id=1, source_target_pairs={{0,4},{4,8},{8,12},{12,16},{16,20},{20,24},{24,28},{1,5},{5,9},{9,... | collective-permute-start | bytes 1179656 | tf_op jit(solution)/shard_map/ppermute | solution.py:33
  102.3 26.8 %collective-permute-start.20 = (bf16[1024,192]{1,0:T(8,128)(2,1)S(1)}, bf16[1024,192]{1,0:T(8,128)(2,1)S(1)}, u32[]{:S(2)}, u32[]{:S(2)}) collective-permute-start(bf16[1024,192]{1,0:T(8,128)(2,1)S(1)} %copy-done.9), channel_id=1, source_target_pairs={{4,0},{8,4},{12,8},{16,12},{20,16},{24,20},{28,24},{5,1},{9,5},{13... | collective-permute-start | bytes 1179656 | tf_op jit(solution)/shard_map/ppermute | solution.py:33
  139.2 28.6 %collective-permute-start.30 = (bf16[768,768]{1,0:T(8,128)(2,1)S(1)}, bf16[768,768]{1,0:T(8,128)(2,1)S(1)}, u32[]{:S(2)}, u32[]{:S(2)}) collective-permute-start(bf16[768,768]{1,0:T(8,128)(2,1)S(1)} %get-tuple-element.179), channel_id=1, source_target_pairs={{0,2},{1,3},{2,0},{3,1},{4,6},{5,7},{6,4},{7,5},{8,10},{9,11},{10,... | collective-permute-start | bytes 3538952 | tf_op jit(solution)/shard_map/ppermute | solution.py:27
  142.7 25.1 %collective-permute-start.25 = (bf16[1024,256]{1,0:T(8,128)(2,1)S(1)}, bf16[1024,256]{1,0:T(8,128)(2,1)S(1)}, u32[]{:S(2)}, u32[]{:S(2)}) collective-permute-start(bf16[1024,256]{1,0:T(8,128)(2,1)S(1)} %layer_gather.1.grad_ref.rest_11_), channel_id=1, source_target_pairs={{0,8},{4,12},{8,16},{12,20},{16,24},{20,28},{1,9},{5,13},{9,17},{1... | collective-permute-start | bytes 1572872 | tf_op jit(solution)/shard_map/ppermute | solution.py:33
  146.7 26.0 %collective-permute-start.26 = (bf16[1024,256]{1,0:T(8,128)(2,1)S(1)}, bf16[1024,256]{1,0:T(8,128)(2,1)S(1)}, u32[]{:S(2)}, u32[]{:S(2)}) collective-permute-start(bf16[1024,256]{1,0:T(8,128)(2,1)S(1)} %layer_gather.1.grad_ref.rest_11_), channel_id=1, source_target_pairs={{0,4},{4,8},{8,12},{12,16},{16,20},{20,24},{24,28},{1,5},{5,9},{9,... | collective-permute-start | bytes 1572872 | tf_op jit(solution)/shard_map/ppermute | solution.py:33
  150.0 22.7 %collective-permute-start.27 = (bf16[1024,256]{1,0:T(8,128)(2,1)S(1)}, bf16[1024,256]{1,0:T(8,128)(2,1)S(1)}, u32[]{:S(2)}, u32[]{:S(2)}) collective-permute-start(bf16[1024,256]{1,0:T(8,128)(2,1)S(1)} %layer_gather.1.grad_ref.rest_11_), channel_id=1, source_target_pairs={{4,0},{8,4},{12,8},{16,12},{20,16},{24,20},{28,24},{5,1},{9,5},{13... | collective-permute-start | bytes 1572872 | tf_op jit(solution)/shard_map/ppermute | solution.py:33
  151.3 31.3 %collective-permute-start.28 = (bf16[1024,256]{1,0:T(8,128)(2,1)S(1)}, bf16[1024,256]{1,0:T(8,128)(2,1)S(1)}, u32[]{:S(2)}, u32[]{:S(2)}) collective-permute-start(bf16[1024,256]{1,0:T(8,128)(2,1)S(1)} %layer_gather.1.grad_ref.rest_11_), channel_id=1, source_target_pairs={{8,0},{12,4},{16,8},{20,12},{24,16},{28,20},{9,1},{13,5},{17,9},{2... | collective-permute-start | bytes 1572872 | tf_op jit(solution)/shard_map/ppermute | solution.py:33
  184.6 36.0 %collective-permute-start.32 = (bf16[1024,768]{1,0:T(8,128)(2,1)}, bf16[1024,768]{1,0:T(8,128)(2,1)}, u32[]{:S(2)}, u32[]{:S(2)}) collective-permute-start(bf16[1024,768]{1,0:T(8,128)(2,1)} %get-tuple-element.177), channel_id=1, source_target_pairs={{0,2},{1,3},{2,0},{3,1},{4,6},{5,7},{6,4},{7,5},{8,10},{9,11},{10,... | collective-permute-start | bytes 4718600 | tf_op jit(solution)/shard_map/ppermute | solution.py:27
  187.7 22.1 %collective-permute-start.31 = (bf16[384,768]{1,0:T(8,128)(2,1)}, bf16[384,768]{1,0:T(8,128)(2,1)}, u32[]{:S(2)}, u32[]{:S(2)}) collective-permute-start(bf16[384,768]{1,0:T(8,128)(2,1)} %get-tuple-element.183), channel_id=1, source_target_pairs={{0,4},{4,0},{8,12},{12,8},{16,20},{20,16},{24,28},{28,24},{1,5},{5... | collective-permute-start | bytes 1769480 | tf_op jit(solution)/shard_map/ppermute | solution.py:27
  235.0 18.9 %collective-permute-start.44 = (bf16[512,768]{1,0:T(8,128)(2,1)}, bf16[512,768]{1,0:T(8,128)(2,1)}, u32[]{:S(2)}, u32[]{:S(2)}) collective-permute-start(bf16[512,768]{1,0:T(8,128)(2,1)} %get-tuple-element.182), channel_id=1, source_target_pairs={{0,4},{4,0},{8,12},{12,8},{16,20},{20,16},{24,28},{28,24},{1,5},{5... | collective-permute-start | bytes 2359304 | tf_op jit(solution)/shard_map/ppermute | solution.py:27
  247.1 18.9 %collective-permute-start.55 = (bf16[192,768]{1,0:T(8,128)(2,1)S(1)}, bf16[192,768]{1,0:T(8,128)(2,1)S(1)}, u32[]{:S(2)}, u32[]{:S(2)}) collective-permute-start(bf16[192,768]{1,0:T(8,128)(2,1)S(1)} %maximum_select_fusion.5), channel_id=1, source_target_pairs={{0,8},{4,12},{8,0},{12,4},{16,24},{20,28},{24,16},{28,20},{1,9},{5... | collective-permute-start | bytes 884744 | tf_op jit(solution)/shard_map/ppermute | solution.py:27
  255.3 17.5 %collective-permute-start.45 = (bf16[256,768]{1,0:T(8,128)(2,1)S(1)}, bf16[256,768]{1,0:T(8,128)(2,1)S(1)}, u32[]{:S(2)}, u32[]{:S(2)}) collective-permute-start(bf16[256,768]{1,0:T(8,128)(2,1)S(1)} %get-tuple-element.186), channel_id=1, source_target_pairs={{0,8},{4,12},{8,0},{12,4},{16,24},{20,28},{24,16},{28,20},{1,9},{5... | collective-permute-start | bytes 1179656 | tf_op jit(solution)/shard_map/ppermute | solution.py:27
  266.1 20.1 %collective-permute-start.56 = (bf16[384,768]{1,0:T(8,128)(2,1)S(1)}, bf16[384,768]{1,0:T(8,128)(2,1)S(1)}, u32[]{:S(2)}, u32[]{:S(2)}) collective-permute-start(bf16[384,768]{1,0:T(8,128)(2,1)S(1)} %maximum_select_fusion.2), channel_id=1, source_target_pairs={{0,4},{4,0},{8,12},{12,8},{16,20},{20,16},{24,28},{28,24},{1,5},{5... | collective-permute-start | bytes 1769480 | tf_op jit(solution)/shard_map/ppermute | solution.py:27
  (77 other events, 724.7 us)
